TPU v7x, 32 devices: a whole 2x2x4 slice. The times are simulated.
32 devices in a mesh: fsdp: 8 (over y, x, core), tp: 4 (over z).
Axes of the slice: x: 2, y: 2, z: 4, core: 2. Of those that a mesh axis runs over, the one named last changes fastest.
Arguments:
- inputs: bfloat16 [32, 448, 768], P(('fsdp', 'tp')), may hold values from -6 to 6
- encoder: bfloat16 [32, 1500, 768], P('fsdp', 'tp'), may hold values from -6 to 6
- lengths: int32 [32], P('fsdp'), may hold values from 56 to 448, as said below
- self_qkv: bfloat16 [3, 768, 768], P(None, 'fsdp', 'tp'), may hold values from -0.21875 to 0.21875
- self_out: bfloat16 [768, 768], P('tp', 'fsdp'), may hold values from -0.875 to 0.875
- cross_q: bfloat16 [768, 768], P('fsdp', 'tp'), may hold values from -0.21875 to 0.21875
- cross_kv: bfloat16 [2, 768, 768], P(None, 'fsdp', 'tp'), may hold values from -0.21875 to 0.21875
- cross_out: bfloat16 [768, 768], P('tp', 'fsdp'), may hold values from -1.25 to 1.25
- fc_in: bfloat16 [768, 3072], P('fsdp', 'tp'), may hold values from -0.21875 to 0.21875
- fc_out: bfloat16 [3072, 768], P('tp', 'fsdp'), may hold values from -0.109375 to 0.109375
- norm_gain: float32 [4, 768], P(None, ('fsdp', 'tp')), may hold values from 0.5 to 1.5
- norm_bias: float32 [4, 768], P(None, ('fsdp', 'tp')), may hold values from -4 to 4
- proj_bias: float32 [7, 768], P(None, ('fsdp', 'tp')), may hold values from -4 to 4
- fc_in_bias: float32 [3072], P(('fsdp', 'tp')), may hold values from -4 to 4
- cotangent: bfloat16 [32, 448, 768], P(('fsdp', 'tp')), may hold values from -6 to 6
Outputs:
- layer_out: bfloat16 [32, 448, 768], P(('fsdp', 'tp'))
- grad_inputs: float32 [32, 448, 768], P(('fsdp', 'tp'))
- grad_encoder: float32 [32, 1500, 768], P('fsdp', 'tp')
- grad_self_qkv: float32 [3, 768, 768], P(None, 'fsdp', 'tp')
- grad_self_out: float32 [768, 768], P('tp', 'fsdp')
- grad_cross_q: float32 [768, 768], P('fsdp', 'tp')
- grad_cross_kv: float32 [2, 768, 768], P(None, 'fsdp', 'tp')
- grad_cross_out: float32 [768, 768], P('tp', 'fsdp')
- grad_fc_in: float32 [768, 3072], P('fsdp', 'tp')
- grad_fc_out: float32 [3072, 768], P('tp', 'fsdp')
- grad_norm_gain: float32 [4, 768], P(None, ('fsdp', 'tp'))
- grad_norm_bias: float32 [4, 768], P(None, ('fsdp', 'tp'))
- grad_proj_bias: float32 [7, 768], P(None, ('fsdp', 'tp'))
- grad_fc_in_bias: float32 [3072], P(('fsdp', 'tp'))
Inputs may be any that keep to these rules, and one draw needn't show every extreme that they name: `lengths`: valid tokens of each sequence; later positions are padding and never serve as keys.
All inputs are finite; a program needn't handle non-finite values.
Results may differ from a plain program's by a relative error of at most 0.035.
Values may be sent and summed in bfloat16 or wider, within the bound.
No kernel may reach another device: no remote copies, remote signals or barrier semaphores. Data moves between devices by JAX's collectives and lax.ppermute only.
A program may use at most 192 MiB of HBM per device.

v0:
```python
import jax
import jax.numpy as jnp
from jax import lax
from jax.sharding import PartitionSpec as P

HD = 64


EPSILON = 1e-05
NEGATIVE = -1e30


def normalize(row_block, gain_row, shift_row):
    center = row_block - jnp.mean(row_block, -1, keepdims=True)
    inverse = lax.rsqrt(jnp.mean(center * center, -1, keepdims=True) + EPSILON)
    unit_rows = center * inverse
    return (unit_rows * gain_row + shift_row, unit_rows, inverse)


def norm_back(grad_rows, unit_rows, inverse, gain_row):
    scaled = grad_rows * gain_row
    return inverse * (
        scaled
        - jnp.mean(scaled, -1, keepdims=True)
        - unit_rows * jnp.mean(scaled * unit_rows, -1, keepdims=True)
    )


def matmul(left_side, right_side):
    return jnp.dot(left_side, right_side, preferred_element_type=jnp.float32)


def transposed(left_side, right_side):
    return lax.dot_general(
        left_side, right_side, (((0,), (0,)), ((), ())), preferred_element_type=jnp.float32
    )


def against(left_side, right_side):
    return lax.dot_general(
        left_side, right_side, (((1,), (1,)), ((), ())), preferred_element_type=jnp.float32
    )


def exact_gelu(values):
    return jax.nn.gelu(values, approximate=False)


def row_sum(values):
    return jnp.sum(values.reshape(-1, values.shape[-1]), 0)


def attend_forward(query_seq, key_seq, value_seq, allowed):
    scores = jnp.einsum("qhd,khd->hqk", query_seq, key_seq, preferred_element_type=jnp.float32)
    if allowed is not None:
        scores = jnp.where(allowed[None], scores, NEGATIVE)
    highest = jnp.max(scores, -1, keepdims=True)
    shifted = jnp.exp(scores - highest)
    total = jnp.sum(shifted, -1, keepdims=True)
    weights = (shifted / total).astype(jnp.bfloat16)
    output = jnp.einsum("hqk,khd->qhd", weights, value_seq, preferred_element_type=jnp.float32)
    return (output, highest + jnp.log(total))


def attend_backward(query_seq, key_seq, value_seq, grad_out, log_total, allowed):
    scores = jnp.einsum("qhd,khd->hqk", query_seq, key_seq, preferred_element_type=jnp.float32)
    if allowed is not None:
        scores = jnp.where(allowed[None], scores, NEGATIVE)
    probs = jnp.exp(scores - log_total)
    grad_probs = jnp.einsum("qhd,khd->hqk", grad_out, value_seq, preferred_element_type=jnp.float32)
    grad_scores = (probs * (grad_probs - jnp.sum(probs * grad_probs, -1, keepdims=True))).astype(
        jnp.bfloat16
    )
    grad_query = jnp.einsum(
        "hqk,khd->qhd", grad_scores, key_seq, preferred_element_type=jnp.float32
    ).astype(jnp.bfloat16)
    grad_key = jnp.einsum(
        "hqk,qhd->khd", grad_scores, query_seq, preferred_element_type=jnp.float32
    ).astype(jnp.bfloat16)
    grad_value = jnp.einsum(
        "hqk,qhd->khd", probs.astype(jnp.bfloat16), grad_out, preferred_element_type=jnp.float32
    ).astype(jnp.bfloat16)
    return (grad_query, grad_key, grad_value)


def local(
    inputs,
    encoder,
    lengths,
    self_qkv,
    self_out,
    cross_q,
    cross_kv,
    cross_out,
    fc_in,
    fc_out,
    norm_gain,
    norm_bias,
    proj_bias,
    fc_in_bias,
    cotangent,
):
    tp_count = lax.axis_size("tp")
    tp_place = lax.axis_index("tp")
    local_seqs, seq_len, width_all = inputs.shape
    group_seqs = local_seqs * tp_count
    group_rows = group_seqs * seq_len
    head_width = width_all // tp_count
    local_heads = head_width // HD
    ff_width = fc_in.shape[1]
    own_frames = encoder.shape[1]
    frames_all = own_frames * tp_count
    head_scale = HD ** (-0.5)
    w_qkv, w_self_out, w_cross_q, w_cross_kv, w_cross_out, w_fc_in, w_fc_out = (
        lax.all_gather(self_qkv, "fsdp", axis=1, tiled=True),
        lax.all_gather(self_out, "fsdp", axis=1, tiled=True),
        lax.all_gather(cross_q, "fsdp", axis=0, tiled=True),
        lax.all_gather(cross_kv, "fsdp", axis=1, tiled=True),
        lax.all_gather(cross_out, "fsdp", axis=1, tiled=True),
        lax.all_gather(fc_in, "fsdp", axis=0, tiled=True),
        lax.all_gather(fc_out, "fsdp", axis=1, tiled=True),
    )
    gains, shifts, biases, fc_bias_all = (
        lax.all_gather(norm_gain, ("fsdp", "tp"), axis=1, tiled=True),
        lax.all_gather(norm_bias, ("fsdp", "tp"), axis=1, tiled=True),
        lax.all_gather(proj_bias, ("fsdp", "tp"), axis=1, tiled=True),
        lax.all_gather(fc_in_bias, ("fsdp", "tp"), axis=0, tiled=True),
    )
    head_start = tp_place * head_width
    ff_start = tp_place * ff_width

    def column(vector):
        return lax.dynamic_slice_in_dim(vector, head_start, head_width)

    def placed(vector):
        return lax.dynamic_update_slice_in_dim(
            jnp.zeros((width_all,), jnp.float32), vector, head_start, 0
        )

    fc_bias = lax.dynamic_slice_in_dim(fc_bias_all, ff_start, ff_width)

    def gather_rows(normed):
        whole = lax.all_gather(normed.astype(jnp.bfloat16), "tp", axis=0, tiled=True)
        return whole.reshape(group_rows, width_all)

    def scatter_rows(partial_out):
        return lax.psum_scatter(
            partial_out.reshape(group_seqs, seq_len, width_all).astype(jnp.bfloat16),
            "tp",
            scatter_dimension=0,
            tiled=True,
        ).astype(jnp.float32)

    def gather_grads(grad_rows):
        whole = lax.all_gather(grad_rows, "tp", axis=0, tiled=True)
        return whole.reshape(group_rows, width_all)

    def scatter_grads(partial_grad):
        return lax.psum_scatter(
            partial_grad.reshape(group_seqs, seq_len, width_all).astype(jnp.bfloat16),
            "tp",
            scatter_dimension=0,
            tiled=True,
        ).astype(jnp.float32)

    def split_heads(flat):
        return flat.reshape(group_seqs, seq_len, local_heads, HD)

    positions = jnp.arange(seq_len)

    def self_mask(length):
        return (positions[None, :] <= positions[:, None]) & (positions[None, :] < length)

    inputs_f = inputs.astype(jnp.float32)
    normed_one, unit_one, inv_one = normalize(inputs_f, gains[0], shifts[0])
    rows_one = gather_rows(normed_one)
    query_one = ((matmul(rows_one, w_qkv[0]) + column(biases[0])) * head_scale).astype(jnp.bfloat16)
    key_one = matmul(rows_one, w_qkv[1]).astype(jnp.bfloat16)
    value_one = (matmul(rows_one, w_qkv[2]) + column(biases[1])).astype(jnp.bfloat16)

    def self_forward(item):
        return attend_forward(item[0], item[1], item[2], self_mask(item[3]))

    attended_one, total_one = lax.map(
        self_forward,
        (split_heads(query_one), split_heads(key_one), split_heads(value_one), lengths),
    )
    mixed_one = attended_one.astype(jnp.bfloat16).reshape(group_rows, head_width)
    first = inputs_f + scatter_rows(matmul(mixed_one, w_self_out)) + biases[2]
    normed_two, unit_two, inv_two = normalize(first, gains[1], shifts[1])
    rows_two = gather_rows(normed_two)
    query_two = ((matmul(rows_two, w_cross_q) + column(biases[3])) * head_scale).astype(
        jnp.bfloat16
    )
    head_shape = (group_seqs, frames_all, local_heads, HD)
    frames = lax.all_gather(encoder, "tp", axis=1, tiled=True)
    flat_frames = frames.reshape(group_seqs * frames_all, width_all)
    key_two = matmul(flat_frames, w_cross_kv[0]).astype(jnp.bfloat16).reshape(head_shape)
    value_two = (
        (matmul(flat_frames, w_cross_kv[1]) + column(biases[4]))
        .astype(jnp.bfloat16)
        .reshape(head_shape)
    )

    def cross_forward(item):
        return attend_forward(item[0], item[1], item[2], None)

    attended_two, total_two = lax.map(cross_forward, (split_heads(query_two), key_two, value_two))
    mixed_two = attended_two.astype(jnp.bfloat16).reshape(group_rows, head_width)
    second = first + scatter_rows(matmul(mixed_two, w_cross_out)) + biases[5]
    normed_three, unit_three, inv_three = normalize(second, gains[2], shifts[2])
    rows_three = gather_rows(normed_three)
    before = matmul(rows_three, w_fc_in) + fc_bias
    hidden = exact_gelu(before).astype(jnp.bfloat16)
    third = second + scatter_rows(matmul(hidden, w_fc_out)) + biases[6]
    result, unit_four, inv_four = normalize(third, gains[3], shifts[3])
    grad_result = cotangent.astype(jnp.float32)
    gain_four = row_sum(grad_result * unit_four)
    shift_four = row_sum(grad_result)
    grad_third = norm_back(grad_result, unit_four, inv_four, gains[3])
    branch_three = grad_third.astype(jnp.bfloat16)
    bias_six = row_sum(branch_three.astype(jnp.float32))
    down_three = gather_grads(branch_three)
    grad_hidden = against(down_three, w_fc_out)
    grad_fc_out = transposed(hidden, down_three)
    grad_before = jax.vjp(exact_gelu, before)[1](grad_hidden)[0].astype(jnp.bfloat16)
    grad_fc_bias = jnp.sum(grad_before.astype(jnp.float32), 0)
    grad_fc_in = transposed(rows_three, grad_before)
    grad_normed_three = scatter_grads(against(grad_before, w_fc_in))
    gain_three = row_sum(grad_normed_three * unit_three)
    shift_three = row_sum(grad_normed_three)
    grad_second = grad_third + norm_back(grad_normed_three, unit_three, inv_three, gains[2])
    branch_two = grad_second.astype(jnp.bfloat16)
    bias_five = row_sum(branch_two.astype(jnp.float32))
    down_two = gather_grads(branch_two)
    grad_mixed_two = against(down_two, w_cross_out).astype(jnp.bfloat16)
    grad_cross_out = transposed(mixed_two, down_two)

    def cross_backward(item):
        return attend_backward(item[0], item[1], item[2], item[3], item[4], None)

    grad_query_two, grad_key_two, grad_value_two = lax.map(
        cross_backward,
        (split_heads(query_two), key_two, value_two, split_heads(grad_mixed_two), total_two),
    )
    flat_query_two = grad_query_two.reshape(group_rows, head_width)
    flat_key_two = grad_key_two.reshape(group_seqs * frames_all, head_width)
    flat_value_two = grad_value_two.reshape(group_seqs * frames_all, head_width)
    grad_cross_q = transposed(rows_two, flat_query_two) * head_scale
    bias_three = jnp.sum(flat_query_two.astype(jnp.float32), 0) * head_scale
    bias_four = jnp.sum(flat_value_two.astype(jnp.float32), 0)
    grad_cross_kv = jnp.stack(
        [transposed(flat_frames, flat_key_two), transposed(flat_frames, flat_value_two)]
    )
    grad_frames = against(flat_key_two, w_cross_kv[0]) + against(flat_value_two, w_cross_kv[1])
    grad_encoder = lax.psum_scatter(
        grad_frames.reshape(group_seqs, frames_all, width_all).astype(jnp.bfloat16),
        "tp",
        scatter_dimension=1,
        tiled=True,
    ).astype(jnp.float32)
    grad_normed_two = scatter_grads(against(flat_query_two, w_cross_q) * head_scale)
    gain_two = row_sum(grad_normed_two * unit_two)
    shift_two = row_sum(grad_normed_two)
    grad_first = grad_second + norm_back(grad_normed_two, unit_two, inv_two, gains[1])
    branch_one = grad_first.astype(jnp.bfloat16)
    bias_two = row_sum(branch_one.astype(jnp.float32))
    down_one = gather_grads(branch_one)
    grad_mixed_one = against(down_one, w_self_out).astype(jnp.bfloat16)
    grad_self_out = transposed(mixed_one, down_one)

    def self_backward(item):
        return attend_backward(item[0], item[1], item[2], item[3], item[4], self_mask(item[5]))

    grad_query_one, grad_key_one, grad_value_one = lax.map(
        self_backward,
        (
            split_heads(query_one),
            split_heads(key_one),
            split_heads(value_one),
            split_heads(grad_mixed_one),
            total_one,
            lengths,
        ),
    )
    flat_query_one = grad_query_one.reshape(group_rows, head_width)
    flat_key_one = grad_key_one.reshape(group_rows, head_width)
    flat_value_one = grad_value_one.reshape(group_rows, head_width)
    grad_qkv = jnp.stack(
        [
            transposed(rows_one, flat_query_one) * head_scale,
            transposed(rows_one, flat_key_one),
            transposed(rows_one, flat_value_one),
        ]
    )
    bias_zero = jnp.sum(flat_query_one.astype(jnp.float32), 0) * head_scale
    bias_one = jnp.sum(flat_value_one.astype(jnp.float32), 0)
    grad_normed_one = scatter_grads(
        against(flat_query_one, w_qkv[0]) * head_scale
        + against(flat_key_one, w_qkv[1])
        + against(flat_value_one, w_qkv[2])
    )
    gain_one = row_sum(grad_normed_one * unit_one)
    shift_one = row_sum(grad_normed_one)
    grad_inputs = grad_first + norm_back(grad_normed_one, unit_one, inv_one, gains[0])
    grad_gains = jnp.stack([gain_one, gain_two, gain_three, gain_four])
    grad_shifts = jnp.stack([shift_one, shift_two, shift_three, shift_four])
    grad_biases = jnp.stack(
        [
            placed(bias_zero),
            placed(bias_one),
            bias_two,
            placed(bias_three),
            placed(bias_four),
            bias_five,
            bias_six,
        ]
    )
    grad_fc_bias_all = lax.dynamic_update_slice_in_dim(
        jnp.zeros((ff_width * tp_count,), jnp.float32), grad_fc_bias, ff_start, 0
    )
    small_gain, small_shift, small_bias, small_fc_bias = (
        lax.psum_scatter(grad_gains, ("fsdp", "tp"), scatter_dimension=1, tiled=True),
        lax.psum_scatter(grad_shifts, ("fsdp", "tp"), scatter_dimension=1, tiled=True),
        lax.psum_scatter(grad_biases, ("fsdp", "tp"), scatter_dimension=1, tiled=True),
        lax.psum_scatter(grad_fc_bias_all, ("fsdp", "tp"), scatter_dimension=0, tiled=True),
    )
    (
        owned_qkv,
        owned_self_out,
        owned_cross_q,
        owned_cross_kv,
        owned_cross_out,
        owned_fc_in,
        owned_fc_out,
    ) = (
        lax.psum_scatter(grad_qkv, "fsdp", scatter_dimension=1, tiled=True),
        lax.psum_scatter(grad_self_out, "fsdp", scatter_dimension=1, tiled=True),
        lax.psum_scatter(grad_cross_q, "fsdp", scatter_dimension=0, tiled=True),
        lax.psum_scatter(grad_cross_kv, "fsdp", scatter_dimension=1, tiled=True),
        lax.psum_scatter(grad_cross_out, "fsdp", scatter_dimension=1, tiled=True),
        lax.psum_scatter(grad_fc_in, "fsdp", scatter_dimension=0, tiled=True),
        lax.psum_scatter(grad_fc_out, "fsdp", scatter_dimension=1, tiled=True),
    )
    return (
        result.astype(jnp.bfloat16),
        grad_inputs,
        grad_encoder,
        owned_qkv,
        owned_self_out,
        owned_cross_q,
        owned_cross_kv,
        owned_cross_out,
        owned_fc_in,
        owned_fc_out,
        small_gain,
        small_shift,
        small_bias,
        small_fc_bias,
    )


def solution(mesh):
    return jax.shard_map(
        local,
        mesh=mesh,
        in_specs=(
            P(("fsdp", "tp"), None, None),
            P("fsdp", "tp", None),
            P("fsdp"),
            P(None, "fsdp", "tp"),
            P("tp", "fsdp"),
            P("fsdp", "tp"),
            P(None, "fsdp", "tp"),
            P("tp", "fsdp"),
            P("fsdp", "tp"),
            P("tp", "fsdp"),
            P(None, ("fsdp", "tp")),
            P(None, ("fsdp", "tp")),
            P(None, ("fsdp", "tp")),
            P(("fsdp", "tp")),
            P(("fsdp", "tp"), None, None),
        ),
        out_specs=(
            P(("fsdp", "tp"), None, None),
            P(("fsdp", "tp"), None, None),
            P("fsdp", "tp", None),
            P(None, "fsdp", "tp"),
            P("tp", "fsdp"),
            P("fsdp", "tp"),
            P(None, "fsdp", "tp"),
            P("tp", "fsdp"),
            P("fsdp", "tp"),
            P("tp", "fsdp"),
            P(None, ("fsdp", "tp")),
            P(None, ("fsdp", "tp")),
            P(None, ("fsdp", "tp")),
            P(("fsdp", "tp")),
        ),
        check_vma=False,
    )
```

profile of v0, /device:TPU:0, one launch (start us, length us, event | category | flops | bytes accessed | tf_op | source)
XLA Modules:
  0.0 1686.5 jit_solution(319161292977433544)
XLA Ops:
  10.9 70.4 %all-gather = f32[32,24,4]{1,2,0:T(4,128)S(1)} all-gather(f32[1,24,4]{1,2,0:T(4,128)} %bitcast.408), channel_id=1, replica_groups=mesh['fsdp'=8,'tp'=4] {'fsdp','tp'}, dimensions={0}, use_global_device_ids=true | all-gather | bytes 12672 | tf_op jit(solution)/shard_map/all_gather | solution.py:124
  82.0 64.1 %all-gather.1 = f32[32,24,4]{1,2,0:T(4,128)S(1)} all-gather(f32[1,24,4]{1,2,0:T(4,128)} %bitcast.409), channel_id=1, replica_groups=mesh['fsdp'=8,'tp'=4] {'fsdp','tp'}, dimensions={0}, use_global_device_ids=true | all-gather | bytes 12672 | tf_op jit(solution)/shard_map/all_gather | solution.py:125
  149.3 69.4 %all-gather.2 = f32[32,24,7]{1,2,0:T(8,128)S(1)} all-gather(f32[1,24,7]{1,2,0:T(8,128)S(1)} %bitcast.407), channel_id=1, replica_groups=mesh['fsdp'=8,'tp'=4] {'fsdp','tp'}, dimensions={0}, use_global_device_ids=true | all-gather | bytes 22176 | tf_op jit(solution)/shard_map/all_gather | solution.py:126
  218.9 9.0 all_gather.59
  229.2 11.7 all_gather.57
  240.9 4.2 convolution_convert_fusion.9
  254.7 19.2 %while.58 = (s32[]{:T(128)}, bf16[4,448,3,64]{1,3,2,0:T(8,128)(2,1)S(1)}, f32[4,3,448,1]{2,1,3,0:T(4,128)}, bf16[4,448,3,64]{1,3,2,0:T(8,128)(2,1)S(1)}, s32[4]{...) while((s32[]{:T(128)}, ...), condition=%wide.region_5.6_spmd.clone.clone, body=%wide.region_2.5_spmd.clone.clone.sunk | while | flops 159960192 | bytes 9467121 | solution.py:184
  277.4 51.6 %reduce-scatter.27.cloned.1.call-done = bf16[1,448,768]{2,1,0:T(8,128)(2,1)} async-done(((bf16[4,448,768]{2,1,0:T(8,128)(2,1)}), bf16[1,448,768]{2,1,0:T(8,128)(2,1)}) %reduce-scatter.27.cloned.1.call-update) | async-done | bytes 688144 | tf_op jit(solution)/shard_map/reduce_scatter | solution.py:147
  334.1 9.5 all_gather.64
  343.7 19.2 %all_gather.63 = bf16[768,192]{1,0:T(8,128)(2,1)S(1)} all-gather(bf16[96,192]{1,0:T(8,128)(2,1)S(1)} %copy-done.60), channel_id=1, replica_groups=mesh['fsdp'=8,'tp'=4] {'fsdp'}, dimensions={0}, use_global_device_ids=true | all-gather | bytes 331776 | tf_op jit(solution)/shard_map/all_gather | solution.py:117
  364.3 10.8 all_gather.61
  375.1 15.0 all-gather.17.cloned.1.call-done
  394.8 158.6 %all-gather.15.cloned.1.call-done = bf16[4,1500,768]{2,0,1:T(4,128)(2,1)} async-done(((bf16[4,375,768]{2,0,1:T(4,128)(2,1)}), bf16[4,1500,768]{2,0,1:T(4,128)(2,1)}) %all-gather.15.cloned.1.call-update) | async-done | bytes 9216016 | tf_op jit(solution)/shard_map/all_gather | solution.py:196
  553.4 8.4 copy.99
  561.8 10.7 reshape.514
  572.5 6.7 convolution_convert_fusion.4
  579.2 4.4 fusion.106
  583.6 5.8 reshape.515
  589.4 3.6 copy.100
  593.0 4.4 reshape.518
  600.4 29.4 %while.56 = (s32[]{:T(128)}, bf16[4,448,3,64]{1,3,2,0:T(8,128)(2,1)}, f32[4,3,448,1]{2,1,3,0:T(4,128)S(1)}, bf16[4,1500,3,64]{1,3,2,0:T(8,128)(2,1)}, bf16[4,448...) while((s32[]{:T(128)}, bf16[4,448,3,64]{1,3,2,0:T(8,128)(2,1)}, ...), condition=%wide.region_12.13_spmd, body=%wide.region_9.12_spmd.sunk | while | flops 528190656 | bytes 31719312 | solution.py:208
  629.8 3.6 convolution_convert_fusion.10
  634.1 52.0 %reduce-scatter.29.cloned.1.call-done = bf16[1,448,768]{2,1,0:T(8,128)(2,1)} async-done(((bf16[4,448,768]{2,1,0:T(8,128)(2,1)}), bf16[1,448,768]{2,1,0:T(8,128)(2,1)}) %reduce-scatter.29.cloned.1.call-update) | async-done | bytes 688144 | tf_op jit(solution)/shard_map/reduce_scatter | solution.py:147
  691.0 43.9 %all-reduce = f32[3072]{0:T(1024)S(1)} all-reduce(f32[3072]{0:T(1024)S(1)} %dynamic-update-slice), channel_id=1, replica_groups=mesh['fsdp'=8,'tp'=4] {'fsdp','tp'}, use_global_device_ids=true, to_apply=%add | all-reduce | flops 3072 | bytes 24576
  735.0 12.6 all-gather.19.cloned.1.call-done
  747.6 17.3 %multiply_convert_fusion.3 = (bf16[1792,768]{1,0:T(8,128)(2,1)}, f32[1792,768]{1,0:T(8,128)}, f32[1792,768]{1,0:T(8,128)}) fusion(f32[768]{0:T(1024)S(1)} %dynamic_slice.77, bf16[1792,768]{1,0:T(8,128)(2,1)} %bitcast.416, bf16[768,768]{1,0:T(8,128)(2,1)} %all-gather.21.cloned.1.call-done), kind=kOutput, calls=%fused_computation.124 | convolution fusion | flops 2204762112 | bytes 17697792 | tf_op jit(solution)/shard_map/dot_general | solution.py:30
  764.9 7.0 all-gather.23.cloned.1.call-done
  771.9 6.0 convolution_convert_fusion.6
  778.0 54.3 %reduce-scatter.31.cloned.1.call-done = bf16[1,448,768]{2,1,0:T(8,128)(2,1)} async-done(((bf16[4,448,768]{2,1,0:T(8,128)(2,1)}), bf16[1,448,768]{2,1,0:T(8,128)(2,1)}) %reduce-scatter.31.cloned.1.call-update) | async-done | bytes 688144 | tf_op jit(solution)/shard_map/reduce_scatter | solution.py:147
  837.9 56.2 %all-gather.25.cloned.1.call-done = bf16[4,448,768]{2,1,0:T(8,128)(2,1)} async-done(((bf16[1,448,768]{2,1,0:T(8,128)(2,1)}), bf16[4,448,768]{2,1,0:T(8,128)(2,1)}) %all-gather.25.cloned.1.call-update) | async-done | bytes 2752528 | tf_op jit(solution)/shard_map/all_gather | solution.py:155
  894.1 10.0 convert_reduce_fusion
  904.1 3.9 convolution_convert_fusion.5
  908.2 53.0 %reduce-scatter.33.cloned.1.call-done = bf16[1,448,768]{2,1,0:T(8,128)(2,1)} async-done(((bf16[4,448,768]{2,1,0:T(8,128)(2,1)}), bf16[1,448,768]{2,1,0:T(8,128)(2,1)}) %reduce-scatter.33.cloned.1.call-update) | async-done | bytes 688144 | tf_op jit(solution)/shard_map/reduce_scatter | solution.py:159
  964.1 4.1 convert_reduce_fusion.11
  968.5 56.2 %all-gather.27.cloned.1.call-done = bf16[4,448,768]{2,1,0:T(8,128)(2,1)} async-done(((bf16[1,448,768]{2,1,0:T(8,128)(2,1)}), bf16[4,448,768]{2,1,0:T(8,128)(2,1)}) %all-gather.27.cloned.1.call-update) | async-done | bytes 2752528 | tf_op jit(solution)/shard_map/all_gather | solution.py:155
  1024.7 3.7 convolution_convert_fusion.8
  1028.4 3.4 reshape.522
  1035.0 48.7 %while.57 = (s32[]{:T(128)}, bf16[4,448,3,64]{1,3,2,0:T(8,128)(2,1)}, bf16[4,1500,3,64]{1,3,2,0:T(8,128)(2,1)}, bf16[4,1500,3,64]{1,3,2,0:T(8,128)(2,1)}, bf16[4...) while((s32[]{:T(128)}, ...), condition=%wide.region_26.27_spmd, body=%wide.region_24.26_spmd.sunk | while | flops 1309044736 | bytes 67793800 | solution.py:242
  1038.6 3.1 multiply_reduce_fusion.7
  1062.9 3.1 multiply_reduce_fusion.7
  1075.1 3.1 multiply_reduce_fusion.7
  1089.9 52.8 %reduce-scatter.35.cloned.1.call-done = bf16[1,448,768]{2,1,0:T(8,128)(2,1)} async-done(((bf16[4,448,768]{2,1,0:T(8,128)(2,1)}), bf16[1,448,768]{2,1,0:T(8,128)(2,1)}) %reduce-scatter.35.cloned.1.call-update) | async-done | bytes 688144 | tf_op jit(solution)/shard_map/reduce_scatter | solution.py:159
  1159.0 3.2 copy.118
  1162.3 4.1 reshape.530
  1166.4 4.9 convolution_bitcast_fusion
  1171.9 6.6 convolution_bitcast_fusion.4
  1178.6 3.2 copy.117
  1181.8 4.1 reshape.529
  1185.9 5.7 convolution_bitcast_fusion.5
  1192.8 3.5 copy.141
  1196.2 3.2 reshape.549
  1199.8 10.1 fusion.163
  1209.9 13.0 add_convert_fusion
  1222.9 10.6 convert_element_type.240
  1233.5 36.9 %copy.119 = bf16[4,1500,768]{2,0,1:T(4,128)(2,1)} copy(bf16[4,1500,768]{2,1,0:T(8,128)(2,1)} %convert_element_type.240) | data formatting | bytes 18432000 | tf_op jit(solution)/shard_map/convert_element_type | solution.py:257
  1280.2 35.1 %while.59 = (s32[]{:T(128)}, bf16[4,448,3,64]{1,3,2,0:T(8,128)(2,1)}, bf16[4,448,3,64]{1,3,2,0:T(8,128)(2,1)}, bf16[4,448,3,64]{1,3,2,0:T(8,128)(2,1)}, bf16[4,4...) while((s32[]{:T(128)}, ...), condition=%wide.region_32.33_spmd.clone.clone, body=%wide.region_30.32_spmd.clone.clone.sunk | while | flops 390827136 | bytes 21527560 | solution.py:275
  1318.0 4.2 convolution_bitcast_fusion.1
  1322.6 3.3 convolution_bitcast_fusion.2
  1337.8 4.7 reshape.543
  1347.4 6.7 fusion.173
  1354.4 6.6 fusion.174
  1372.5 249.1 %all-reduce.9.cloned.1.call-done = bf16[4,1500,768]{2,0,1:T(4,128)(2,1)} async-done(((bf16[4,1500,768]{2,0,1:T(4,128)(2,1)}), bf16[4,1500,768]{2,0,1:T(4,128)(2,1)}) %all-reduce.9.cloned.1.call-update) | async-done | bytes 9216016
  1621.6 4.4 dynamic-slice_convert_fusion
  1632.4 40.6 %all-reduce.6 = (f32[4,768]{1,0:T(4,128)S(1)}, f32[4,768]{1,0:T(4,128)S(1)}, f32[7,768]{1,0:T(8,128)S(1)}, f32[3072]{0:T(1024)S(1)}) all-reduce(f32[4,768]{1,0:T(4,128)S(1)} %pad_maximum_fusion.2, f32[4,768]{1,0:T(4,128)S(1)} %pad_maximum_fusion.3, f32[7,768]{1,0:T(8,128)S(1)} %stack.96, ...), channel_id=16, replica_groups=mesh['fsdp'=8,'tp'=4] {'fsdp','tp'}, use_global_device_ids=true, to_apply=%region_48.49.clone | all-reduce | flops 14592 | bytes 116736
  (498 shorter events, 251.9 us)
Async XLA Ops:
  8.0 141.2 %copy-start.61 = (bf16[192,96]{1,0:T(8,128)(2,1)S(1)}, bf16[192,96]{1,0:T(8,128)(2,1)}, u32[]{:S(2)}) copy-start(bf16[192,96]{1,0:T(8,128)(2,1)} %param.27) | copy-start | bytes 110596
  8.0 141.3 %copy-start.77 = (f32[7,24]{1,0:T(8,128)S(1)}, f32[7,24]{1,0:T(8,128)}, u32[]{:S(2)}) copy-start(f32[7,24]{1,0:T(8,128)} %param.35) | copy-start | bytes 2020
  8.0 221.2 %copy-start.49 = (bf16[3,96,192]{2,1,0:T(8,128)(2,1)S(1)}, bf16[3,96,192]{2,1,0:T(8,128)(2,1)}, u32[]{:S(2)}) copy-start(bf16[3,96,192]{2,1,0:T(8,128)(2,1)} %param.26) | copy-start | bytes 331780
  8.0 232.9 %all-gather.13.cloned.1.call-start = ((), (), s32[]{:S(2)}) async-start(), calls=%async_computation.13 | async-start | bytes 3440640 | tf_op jit(solution)/shard_map/all_gather | solution.py:143
  9.4 139.9 %copy-start.56 = (f32[448]{0:T(512)}, f32[448]{0:T(512)S(1)}, u32[]{:S(2)}) copy-start(f32[448]{0:T(512)S(1)} %broadcast_multiply_fusion.13) | copy-start | bytes 5380
  10.9 138.4 %copy-start.63 = (f32[448]{0:T(512)}, f32[448]{0:T(512)S(1)}, u32[]{:S(2)}) copy-start(f32[448]{0:T(512)S(1)} %add_rsqrt_fusion.3) | copy-start | bytes 5380
  82.0 67.3 %copy-start.51 = (f32[768]{0:T(1024)}, f32[768]{0:T(1024)S(1)}, u32[]{:S(2)}) copy-start(f32[768]{0:T(1024)S(1)} %get-tuple-element.458) | copy-start | bytes 9220
  82.0 250.0 %copy-start.53 = (f32[768]{0:T(1024)}, f32[768]{0:T(1024)S(1)}, u32[]{:S(2)}) copy-start(f32[768]{0:T(1024)S(1)} %get-tuple-element.457) | copy-start | bytes 9220
  149.1 179.9 %reduce-scatter.27.cloned.1.call-start = ((), (), s32[]{:S(2)}) async-start(), calls=%async_computation.14 | async-start | bytes 3440640 | tf_op jit(solution)/shard_map/reduce_scatter | solution.py:147
  227.9 46.9 %copy-start.33 = (bf16[192,768]{0,1:T(8,128)(2,1)}, bf16[192,768]{0,1:T(8,128)(2,1)S(1)}, u32[]{:S(2)}) copy-start(bf16[192,768]{0,1:T(8,128)(2,1)S(1)} %all_gather.59) | copy-start | bytes 884740
  229.1 457.0 %copy-start.47 = (f32[768]{0:T(1024)}, f32[768]{0:T(1024)S(1)}, u32[]{:S(2)}) copy-start(f32[768]{0:T(1024)S(1)} %get-tuple-element.558) | copy-start | bytes 9220
  274.8 54.3 %copy-start = (bf16[1,448,768]{2,1,0:T(8,128)(2,1)S(1)}, bf16[1,448,768]{2,1,0:T(8,128)(2,1)}, u32[]{:S(2)}) copy-start(bf16[1,448,768]{2,1,0:T(8,128)(2,1)} %param.23) | copy-start | bytes 2064388
  277.3 54.8 %copy-start.69 = (f32[768]{0:T(1024)S(1)}, f32[768]{0:T(1024)}, u32[]{:S(2)}) copy-start(f32[768]{0:T(1024)} %get-tuple-element.461) | copy-start | bytes 9220
  277.3 112.8 %all-gather.17.cloned.1.call-start = ((), (), s32[]{:S(2)}) async-start(), calls=%async_computation.16 | async-start | bytes 3440640 | tf_op jit(solution)/shard_map/all_gather | solution.py:143
  332.1 11.6 copy-start.60
  332.1 32.2 %copy-start.50 = (bf16[2,96,192]{2,1,0:T(8,128)(2,1)S(1)}, bf16[2,96,192]{2,1,0:T(8,128)(2,1)}, u32[]{:S(2)}) copy-start(bf16[2,96,192]{2,1,0:T(8,128)(2,1)} %param.29) | copy-start | bytes 221188
  333.4 220.0 %all-gather.15.cloned.1.call-start = ((), (), s32[]{:S(2)}) async-start(), calls=%async_computation.15 | async-start | bytes 11520000 | tf_op jit(solution)/shard_map/all_gather | solution.py:196
  334.0 352.1 %reduce-scatter.29.cloned.1.call-start = ((), (), s32[]{:S(2)}) async-start(), calls=%async_computation.17 | async-start | bytes 3440640 | tf_op jit(solution)/shard_map/reduce_scatter | solution.py:147
  362.8 27.3 %copy-start.45 = (bf16[768,192]{1,0:T(8,128)(2,1)}, bf16[768,192]{1,0:T(8,128)(2,1)S(1)}, u32[]{:S(2)}) copy-start(bf16[768,192]{1,0:T(8,128)(2,1)S(1)} %all_gather.63) | copy-start | bytes 884740
  629.8 56.3 %copy-start.68 = (f32[768]{0:T(1024)S(1)}, f32[768]{0:T(1024)}, u32[]{:S(2)}) copy-start(f32[768]{0:T(1024)} %get-tuple-element.559) | copy-start | bytes 9220
  633.5 101.5 %all-gather.21.cloned.1.call-start = ((), (), s32[]{:S(2)}) async-start(), calls=%async_computation.19 | async-start | bytes 1327104 | tf_op jit(solution)/shard_map/all_gather | solution.py:120
  634.0 113.5 %all-gather.19.cloned.1.call-start = ((), (), s32[]{:S(2)}) async-start(), calls=%async_computation.18 | async-start | bytes 3440640 | tf_op jit(solution)/shard_map/all_gather | solution.py:143
  690.1 81.8 %all-gather.23.cloned.1.call-start = ((), (), s32[]{:S(2)}) async-start(), calls=%async_computation.20 | async-start | bytes 1327104 | tf_op jit(solution)/shard_map/all_gather | solution.py:121
  690.7 141.7 %reduce-scatter.31.cloned.1.call-start = ((), (), s32[]{:S(2)}) async-start(), calls=%async_computation.21 | async-start | bytes 3440640 | tf_op jit(solution)/shard_map/reduce_scatter | solution.py:147
  777.9 54.4 %copy-start.67 = (f32[768]{0:T(1024)S(1)}, f32[768]{0:T(1024)}, u32[]{:S(2)}) copy-start(f32[768]{0:T(1024)} %get-tuple-element.560) | copy-start | bytes 9220
  777.9 56.5 %copy-start.26 = (bf16[1,448,768]{2,1,0:T(8,128)(2,1)S(1)}, bf16[1,448,768]{2,1,0:T(8,128)(2,1)}, u32[]{:S(2)}) copy-start(bf16[1,448,768]{2,1,0:T(8,128)(2,1)} %param.37) | copy-start | bytes 2064388
  777.9 56.5 %copy-start.55 = (f32[768]{0:T(1024)S(1)}, f32[768]{0:T(1024)}, u32[]{:S(2)}) copy-start(f32[768]{0:T(1024)} %get-tuple-element.455) | copy-start | bytes 9220
  777.9 116.2 %all-gather.25.cloned.1.call-start = ((), (), s32[]{:S(2)}) async-start(), calls=%async_computation.22 | async-start | bytes 3440640 | tf_op jit(solution)/shard_map/all_gather | solution.py:155
  837.6 123.6 %reduce-scatter.33.cloned.1.call-start = ((), (), s32[]{:S(2)}) async-start(), calls=%async_computation.23 | async-start | bytes 3440640 | tf_op jit(solution)/shard_map/reduce_scatter | solution.py:159
  894.1 10.0 copy-start.79
  908.1 56.1 %copy-start.75 = (f32[768]{0:T(1024)S(1)}, f32[768]{0:T(1024)}, u32[]{:S(2)}) copy-start(f32[768]{0:T(1024)} %get-tuple-element.459) | copy-start | bytes 9220
  908.1 116.6 %all-gather.27.cloned.1.call-start = ((), (), s32[]{:S(2)}) async-start(), calls=%async_computation.24 | async-start | bytes 3440640 | tf_op jit(solution)/shard_map/all_gather | solution.py:155
  968.2 174.5 %reduce-scatter.35.cloned.1.call-start = ((), (), s32[]{:S(2)}) async-start(), calls=%async_computation.25 | async-start | bytes 3440640 | tf_op jit(solution)/shard_map/reduce_scatter | solution.py:159
  1087.1 55.7 %copy-start.1 = (bf16[1,448,768]{2,1,0:T(8,128)(2,1)S(1)}, bf16[1,448,768]{2,1,0:T(8,128)(2,1)}, u32[]{:S(2)}) copy-start(bf16[1,448,768]{2,1,0:T(8,128)(2,1)} %param.23) | copy-start | bytes 2064388
  1087.1 55.7 %copy-start.7 = (bf16[1,448,768]{2,1,0:T(8,128)(2,1)S(1)}, bf16[1,448,768]{2,1,0:T(8,128)(2,1)}, u32[]{:S(2)}) copy-start(bf16[1,448,768]{2,1,0:T(8,128)(2,1)} %reduce-scatter.27.cloned.1.call-done) | copy-start | bytes 2064388
  1087.1 55.7 %copy-start.48 = (f32[768]{0:T(1024)S(1)}, f32[768]{0:T(1024)}, u32[]{:S(2)}) copy-start(f32[768]{0:T(1024)} %copy-done.47) | copy-start | bytes 9220
  1087.1 55.7 %copy-start.54 = (f32[768]{0:T(1024)S(1)}, f32[768]{0:T(1024)}, u32[]{:S(2)}) copy-start(f32[768]{0:T(1024)} %copy-done.53) | copy-start | bytes 9220
  1087.1 55.7 %copy-start.59 = (f32[448]{0:T(512)S(1)}, f32[448]{0:T(512)}, u32[]{:S(2)}) copy-start(f32[448]{0:T(512)} %copy-done.58) | copy-start | bytes 5380
  1087.1 55.7 %copy-start.66 = (f32[448]{0:T(512)S(1)}, f32[448]{0:T(512)}, u32[]{:S(2)}) copy-start(f32[448]{0:T(512)} %copy-done.65) | copy-start | bytes 5380
  1089.6 55.1 %copy-start.27 = (f32[1,448,768]{2,1,0:T(8,128)S(1)}, f32[1,448,768]{2,1,0:T(8,128)}, u32[]{:S(2)}) copy-start(f32[1,448,768]{2,1,0:T(8,128)} %get-tuple-element.537) | copy-start | bytes 4128772
  1089.6 181.1 %all-gather.29.cloned.1.call-start = ((), (), s32[]{:S(2)}) async-start(), calls=%async_computation.26 | async-start | bytes 3440640 | tf_op jit(solution)/shard_map/all_gather | solution.py:155
  1147.9 221.2 %reduce-scatter.51.cloned.1.call-start = ((), (), s32[]{:S(2)}) async-start(), calls=%async_computation.34 | async-start | bytes 884736
  1147.9 11.1 copy-start.14
  1171.4 199.3 %reduce-scatter.49.cloned.1.call-start = ((), (), s32[]{:S(2)}) async-start(), calls=%async_computation.33 | async-start | bytes 1327104
  1199.5 422.1 %all-reduce.9.cloned.1.call-start = ((), (), s32[]{:S(2)}) async-start(), calls=%async_computation.35 | async-start | bytes 18432000
  1199.7 10.2 copy-start.17
  1199.7 10.1 copy-start.31
  1270.4 356.5 %reduce-scatter.45.cloned.1.call-start = ((), (), s32[]{:S(2)}) async-start(), calls=%async_computation.31 | async-start | bytes 884736
  1322.1 7.4 copy-start.19
  1322.2 306.5 %reduce-scatter.43.cloned.1.call-start = ((), (), s32[]{:S(2)}) async-start(), calls=%async_computation.30 | async-start | bytes 2211840
  1342.6 287.9 %reduce-scatter.37.cloned.1.call-start = ((), (), s32[]{:S(2)}) async-start(), calls=%async_computation.27 | async-start | bytes 3440640 | tf_op jit(solution)/shard_map/reduce_scatter | solution.py:159
  1347.3 331.4 %reduce-scatter.39.cloned.1.call-start = ((), (), s32[]{:S(2)}) async-start(), calls=%async_computation.28 | async-start | bytes 2654208 | tf_op jit(solution)/shard_map/reduce_scatter | solution.py:342
  1354.1 7.0 copy-start.82
  1354.1 8.3 copy-start.71
  1354.1 8.3 copy-start.70
  1354.1 8.3 copy-start.72
  1354.1 8.3 copy-start.78
  1354.1 8.6 copy-start.74
  1354.1 8.6 copy-start.76
  1354.2 8.7 copy-start.73
  1354.2 324.5 %reduce-scatter.41.cloned.1.call-start = ((), (), s32[]{:S(2)}) async-start(), calls=%async_computation.29 | async-start | bytes 2654208 | tf_op jit(solution)/shard_map/reduce_scatter | solution.py:343
  1361.0 317.7 %reduce-scatter.47.cloned.1.call-start = ((), (), s32[]{:S(2)}) async-start(), calls=%async_computation.32 | async-start | bytes 884736
  1372.5 253.5 %copy-start.18 = (bf16[4,448,3,64]{1,3,2,0:T(8,128)(2,1)S(1)}, bf16[4,448,3,64]{1,3,2,0:T(8,128)(2,1)}, u32[]{:S(2)}) copy-start(bf16[4,448,3,64]{1,3,2,0:T(8,128)(2,1)} %get-tuple-element.211) | copy-start | bytes 2064388
  1372.5 253.7 %copy-start.20 = (bf16[4,448,3,64]{1,3,2,0:T(8,128)(2,1)S(1)}, bf16[4,448,3,64]{1,3,2,0:T(8,128)(2,1)}, u32[]{:S(2)}) copy-start(bf16[4,448,3,64]{1,3,2,0:T(8,128)(2,1)} %get-tuple-element.209) | copy-start | bytes 2064388
  (52 other events, 161.8 us)
Sparse Core Ops, SparseCore 0:
  149.2 56.4 all-gather.12
  277.4 51.5 reduce-scatter.26
  333.5 56.5 all-gather.16
  391.5 161.8 all-gather.14
  633.6 52.4 reduce-scatter.28
  1270.5 351.0 all-reduce.8
Sparse Core Ops, SparseCore 1:
  635.8 22.0 all-gather.20
  690.2 57.4 all-gather.18
  749.3 22.5 all-gather.22
  778.0 54.3 reduce-scatter.30
  837.7 56.3 all-gather.24
  908.2 53.0 reduce-scatter.32
  968.3 56.4 all-gather.26
  1089.7 53.0 reduce-scatter.34
  1148.0 56.4 all-gather.28
  1207.5 33.6 reduce-scatter.50
  1244.3 36.6 reduce-scatter.48
  1322.2 34.5 reduce-scatter.44
  1360.0 40.0 reduce-scatter.42
  1402.5 120.2 reduce-scatter.36
  1526.6 42.2 reduce-scatter.38
  1572.8 42.2 reduce-scatter.40
  1618.8 35.1 reduce-scatter.46
where the time goes:
time: 1690 us
  waiting for transfers between devices  821 us (49%)
  blocking collectives  349 us (21%)
  matrix products  238 us (14%)
  local copies, waits for them, and re-layouts  189 us (11%)
  other arithmetic  68.7 us (4%)
  between operations  18.1 us (1%)
    unnamed x29, waiting for transfers between devices  251 us
    all_gather x1, waiting for transfers between devices, local(): frames = lax.all_gather(encoder, 'tp', axis=1, tiled=True)  159 us
    reduce_scatter x3, waiting for transfers between devices, scatter_rows(): lax.psum_scatter(partial_out.reshape(group_seqs, seq_len, width_all).asty...  158 us
    all_gather x3, waiting for transfers between devices, gather_grads(): whole = lax.all_gather(grad_rows, 'tp', axis=0, tiled=True)  112 us
    reduce_scatter x3, waiting for transfers between devices, scatter_grads(): lax.psum_scatter(partial_grad.reshape(group_seqs, seq_len, width_all).ast...  106 us
    unnamed x2, blocking collectives  84.5 us
    all_gather x1, blocking collectives, local(): lax.all_gather(norm_gain, ('fsdp', 'tp'), axis=1, tiled=True)  70.4 us
    all_gather x1, blocking collectives, local(): lax.all_gather(proj_bias, ('fsdp', 'tp'), axis=1, tiled=True)  69.4 us
  transfers between devices with their start and end apart: 23, of which 12 were waited for; matrix products, arithmetic and copies ran while one was open for 16% of the time, Pallas kernels for 0%

commit v1 on v0

v1 whole, which is shorter than its diff:
```python
import functools

import jax
import jax.numpy as jnp
from jax import lax
from jax.experimental import pallas as pl
from jax.experimental.pallas import tpu as pltpu
from jax.sharding import PartitionSpec as P

HD = 64
EPSILON = 1e-05
NEGATIVE = -1e30
BF = jnp.bfloat16
F32 = jnp.float32


def dot(left, right, left_dim=1, right_dim=0):
    return lax.dot_general(
        left, right, (((left_dim,), (right_dim,)), ((), ())), preferred_element_type=F32
    )


def layer_norm_parts(rows):
    center = rows - jnp.mean(rows, -1, keepdims=True)
    inverse = lax.rsqrt(jnp.mean(center * center, -1, keepdims=True) + EPSILON)
    return center * inverse, inverse


def norm_back(grad_rows, unit, inverse, gain):
    scaled = grad_rows * gain
    return inverse * (
        scaled
        - jnp.mean(scaled, -1, keepdims=True)
        - unit * jnp.mean(scaled * unit, -1, keepdims=True)
    )


def column_sum(rows):
    return jnp.sum(rows, 0, keepdims=True)


def whole(shape):
    zeros = (0,) * len(shape)
    return pl.BlockSpec(shape, lambda t, *_: zeros)


def per_block(shape):
    rest = (0,) * (len(shape) - 1)
    return pl.BlockSpec((1,) + tuple(shape[1:]), lambda t, *_: (t,) + rest)


def packed(shape):
    return pl.BlockSpec((shape[0], 1) + tuple(shape[2:]), lambda t, *_: (0, t, 0, 0))


def sds(shape, dtype):
    return jax.ShapeDtypeStruct(tuple(shape), dtype)


def call(body, name, grid, ins, outs, scratch, flops, scalars=()):
    moved = sum(a.size * a.dtype.itemsize for a, _ in ins)
    moved += sum(o.size * o.dtype.itemsize for o, _ in outs)
    return pl.pallas_call(
        body,
        out_shape=[o for o, _ in outs],
        grid_spec=pltpu.PrefetchScalarGridSpec(
            num_scalar_prefetch=len(scalars),
            grid=(grid,),
            in_specs=[s for _, s in ins],
            out_specs=[s for _, s in outs],
            scratch_shapes=scratch,
        ),
        compiler_params=pltpu.CompilerParams(
            dimension_semantics=("arbitrary",), vmem_limit_bytes=60 * 2**20
        ),
        cost_estimate=pl.CostEstimate(flops=flops, bytes_accessed=moved, transcendentals=0),
        name=name,
    )(*scalars, *[a for a, _ in ins])


def head_lanes(rows, head, block):
    lane = lax.broadcasted_iota(jnp.int32, rows.shape, 1)
    return jnp.where((lane >= head * block) & (lane < (head + 1) * block), rows, jnp.zeros_like(rows))


def last_part(w, hw):
    start = (3 * hw) // 128 * 128
    return w[:, start:], 3 * hw - start


def project_out(mixed, w, hw):
    tail, extra = last_part(w, hw)
    if extra:
        mixed = jnp.concatenate([jnp.zeros((mixed.shape[0], extra), mixed.dtype), mixed], 1)
    return dot(mixed, tail, 1, 1)


def project_back(branch, w, hw):
    tail, extra = last_part(w, hw)
    return dot(branch, tail)[:, extra:]


def weight(ref, rows):
    parts = ref[:, 0, :rows, :]
    return parts.reshape(parts.shape[0] * rows, parts.shape[2])


def self_forward(length, rows, pack, own, params, head_bias, dims):
    seq, width, blocks, hw = dims
    heads = hw // HD

    def body(len_ref, x_ref, w_ref, prm_ref, hb_ref, n1_ref, q_ref, k_ref, v_ref, lse_ref, ot_ref,
             mix_ref, first_ref, n2_ref, bias_scr, acc_scr):
        t = pl.program_id(0)

        @pl.when(t == 0)
        def _():
            unit, _ = layer_norm_parts(x_ref[...].astype(F32))
            n1_ref[...] = (unit * prm_ref[0:1] + prm_ref[4:5]).astype(BF)
            key = lax.broadcasted_iota(jnp.int32, (seq, seq), 0)
            query = lax.broadcasted_iota(jnp.int32, (seq, seq), 1)
            bias_scr[...] = jnp.where((key <= query) & (key < len_ref[0]), 0.0, NEGATIVE)
            acc_scr[...] = x_ref[...].astype(F32) + prm_ref[10:11]

        w = weight(w_ref, own)
        qkv = dot(n1_ref[...], w[:, : 3 * hw])
        q = ((qkv[:, :hw] + hb_ref[0, 0:1]) * HD**-0.5).astype(BF)
        k = qkv[:, hw : 2 * hw].astype(BF)
        v = (qkv[:, 2 * hw :] + hb_ref[0, 1:2]).astype(BF)
        q_ref[0] = q
        k_ref[0] = k
        v_ref[0] = v
        vt = v.T
        for j in range(heads):
            s = dot(k, head_lanes(q, j, HD), 1, 1) + bias_scr[...]
            m = jnp.max(s, 0, keepdims=True)
            p = jnp.exp(s - m)
            total = jnp.sum(p, 0, keepdims=True)
            lse_ref[0, j : j + 1] = m + jnp.log(total)
            ot_ref[0, j * HD : (j + 1) * HD] = dot(vt[j * HD : (j + 1) * HD], p.astype(BF)) / total
        mixed = ot_ref[0].T.astype(BF)
        mix_ref[0] = mixed
        acc_scr[...] += project_out(mixed, w, hw)

        @pl.when(t == blocks - 1)
        def _():
            first = acc_scr[...]
            first_ref[...] = first
            unit, _ = layer_norm_parts(first)
            n2_ref[...] = (unit * prm_ref[1:2] + prm_ref[5:6]).astype(BF)

    full = whole((seq, width))
    hb = sds((blocks, seq, hw), BF)
    return call(
        body, "self_forward", blocks,
        [(rows, full), (pack, packed(pack.shape)), (params, whole(params.shape)),
         (head_bias, per_block(head_bias.shape))],
        [(sds((seq, width), BF), full)]
        + [(hb, per_block(hb.shape))] * 3
        + [(sds((blocks, 8, seq), F32), per_block((blocks, 8, seq))),
           (sds((blocks, hw, seq), F32), per_block((blocks, hw, seq))),
           (hb, per_block(hb.shape)),
           (sds((seq, width), F32), full),
           (sds((seq, width), BF), full)],
        [pltpu.VMEM((seq, seq), F32), pltpu.VMEM((seq, width), F32)],
        8 * seq * width * width + 16 * seq * seq * width,
        (length,),
    )


def frame_keys(frames, pack, own, head_bias, dims):
    seq, width, blocks, hw = dims
    pieces, piece, _ = frames.shape
    total = pieces * piece

    def body(e_ref, w_ref, hb_ref, k_ref, v_ref, kt_ref, vt_ref):
        w = weight(w_ref, own)[:, : 2 * hw]
        for c in range(pieces):
            kv = dot(e_ref[c], w)
            k = kv[:, :hw].astype(BF)
            v = (kv[:, hw:] + hb_ref[0, 3:4]).astype(BF)
            k_ref[0, c] = k
            v_ref[0, c] = v
            kt_ref[0, :, c * piece : (c + 1) * piece] = k.T
            vt_ref[0, :, c * piece : (c + 1) * piece] = v.T

    kv = sds((blocks, pieces, piece, hw), BF)
    kvt = sds((blocks, hw, total), BF)
    return call(
        body, "frame_keys", blocks,
        [(frames, whole(frames.shape)), (pack, packed(pack.shape)),
         (head_bias, per_block(head_bias.shape))],
        [(kv, per_block(kv.shape))] * 2 + [(kvt, per_block(kvt.shape))] * 2,
        [],
        4 * total * width * width,
    )


def cross_forward(n2, first, pack, own, params, head_bias, keys, values_t, valid, dims):
    seq, width, blocks, hw = dims
    heads = hw // HD
    _, pieces, piece, _ = keys.shape
    total_keys = pieces * piece

    def body(n2_ref, first_ref, w_ref, prm_ref, hb_ref, k_ref, vt_ref, q_ref, lse_ref, ot_ref,
             mix_ref, second_ref, n3_ref, s_scr, p_scr, acc_scr):
        t = pl.program_id(0)

        @pl.when(t == 0)
        def _():
            acc_scr[...] = first_ref[...] + prm_ref[13:14]

        q = ((dot(n2_ref[...], weight(w_ref, own)[:, 2 * hw : 3 * hw]) + hb_ref[0, 2:3]) * HD**-0.5).astype(BF)
        q_ref[0] = q
        row = lax.broadcasted_iota(jnp.int32, (piece, 1), 0)
        pad = jnp.where(row < valid, 0.0, NEGATIVE)

        for j in range(heads):
            qm = head_lanes(q, j, HD)

            def score(c, m):
                s = dot(k_ref[0, c], qm, 1, 1) + pad
                s_scr[c] = s
                return jnp.maximum(m, jnp.max(s, 0, keepdims=True))

            m = lax.fori_loop(0, pieces, score, jnp.full((1, seq), NEGATIVE, F32))

            def weigh(c, total):
                p = jnp.exp(s_scr[c] - m)
                p_scr[pl.ds(pl.multiple_of(c * piece, piece), piece)] = p.astype(BF)
                return total + jnp.sum(p, 0, keepdims=True)

            total = lax.fori_loop(0, pieces, weigh, jnp.zeros((1, seq), F32))
            lse_ref[0, j : j + 1] = m + jnp.log(total)
            at = j * HD
            ot_ref[0, at : at + HD] = dot(vt_ref[0, at : at + HD], p_scr[...]) / total

        mixed = ot_ref[0].T.astype(BF)
        mix_ref[0] = mixed
        acc_scr[...] += project_out(mixed, weight(w_ref, own), hw)

        @pl.when(t == blocks - 1)
        def _():
            second = acc_scr[...]
            second_ref[...] = second
            unit, _ = layer_norm_parts(second)
            n3_ref[...] = (unit * prm_ref[2:3] + prm_ref[6:7]).astype(BF)

    full = whole((seq, width))
    hb = sds((blocks, seq, hw), BF)
    return call(
        body, "cross_forward", blocks,
        [(n2, full), (first, full), (pack, packed(pack.shape)), (params, whole(params.shape)),
         (head_bias, per_block(head_bias.shape)), (keys, per_block(keys.shape)),
         (values_t, per_block(values_t.shape))],
        [(hb, per_block(hb.shape)),
         (sds((blocks, 8, seq), F32), per_block((blocks, 8, seq))),
         (sds((blocks, hw, seq), F32), per_block((blocks, hw, seq))),
         (hb, per_block(hb.shape)),
         (sds((seq, width), F32), full),
         (sds((seq, width), BF), full)],
        [pltpu.VMEM((pieces, piece, seq), F32), pltpu.VMEM((total_keys, seq), BF),
         pltpu.VMEM((seq, width), F32)],
        4 * seq * width * width + 16 * seq * total_keys * width,
    )


def feed_forward(n3, second, pack_in, pack_out, own, params, cotangent, dims):
    seq, width, blocks, hw = dims

    def body(n3_ref, second_ref, wi_ref, wo_ref, prm_ref, cot_ref, hid_ref, slope_ref, out_ref,
             g3_ref, b3_ref, sum_ref, acc_scr):
        t = pl.program_id(0)

        @pl.when(t == 0)
        def _():
            acc_scr[...] = second_ref[...] + prm_ref[14:15]

        before = dot(n3_ref[...], weight(wi_ref, own)) + prm_ref[pl.ds(15 + t, 1)]
        phi = 0.5 + 0.5 * lax.erf(before * 2**-0.5)
        hidden = (before * phi).astype(BF)
        hid_ref[0] = hidden
        slope_ref[0] = phi + before * (jnp.exp(-0.5 * before * before) * 0.3989422804014327)
        acc_scr[...] += dot(hidden, weight(wo_ref, own), 1, 1)

        @pl.when(t == blocks - 1)
        def _():
            unit, inverse = layer_norm_parts(acc_scr[...])
            out_ref[...] = (unit * prm_ref[3:4] + prm_ref[7:8]).astype(BF)
            cot = cot_ref[...].astype(F32)
            grad = norm_back(cot, unit, inverse, prm_ref[3:4])
            g3_ref[...] = grad
            branch = grad.astype(BF)
            b3_ref[...] = branch
            sum_ref[0:1] = column_sum(cot * unit)
            sum_ref[1:2] = column_sum(cot)
            sum_ref[2:3] = column_sum(branch.astype(F32))

    full = whole((seq, width))
    wide = (blocks, seq, width)
    return call(
        body, "feed_forward", blocks,
        [(n3, full), (second, full), (pack_in, packed(pack_in.shape)),
         (pack_out, packed(pack_out.shape)), (params, whole(params.shape)), (cotangent, full)],
        [(sds(wide, BF), per_block(wide)), (sds(wide, F32), per_block(wide)),
         (sds((seq, width), BF), full), (sds((seq, width), F32), full),
         (sds((seq, width), BF), full), (sds((8, width), F32), whole((8, width)))],
        [pltpu.VMEM((seq, width), F32)],
        16 * seq * width * width,
    )


def store_pack(ref, rows, value):
    ref[:, 0] = value.reshape(ref.shape[0], rows, value.shape[1]).astype(ref.dtype)


def feed_backward(b3, g3, hidden, slope, pack_in, pack_out, own, n3, second, params, grad_shape, dims):
    seq, width, blocks, hw = dims
    own_out = grad_shape[2]

    def body(b3_ref, g3_ref, hid_ref, slope_ref, wi_ref, wo_ref, n3_ref, second_ref, prm_ref,
             go_ref, gi_ref, fcb_ref, g2_ref, b2_ref, sum_ref, b3t_scr, n3t_scr, acc_scr):
        t = pl.program_id(0)

        @pl.when(t == 0)
        def _():
            b3t_scr[...] = b3_ref[...].T
            n3t_scr[...] = n3_ref[...].T
            acc_scr[...] = jnp.zeros_like(acc_scr)

        store_pack(go_ref, own_out, dot(b3t_scr[...], hid_ref[0]))
        grad_before = (dot(b3_ref[...], weight(wo_ref, own)) * slope_ref[0]).astype(BF)
        fcb_ref[0, 0:1] = column_sum(grad_before.astype(F32))
        store_pack(gi_ref, own_out, dot(n3t_scr[...], grad_before))
        acc_scr[...] += dot(grad_before, weight(wi_ref, own), 1, 1)

        @pl.when(t == blocks - 1)
        def _():
            grad = acc_scr[...]
            unit, inverse = layer_norm_parts(second_ref[...])
            sum_ref[0:1] = column_sum(grad * unit)
            sum_ref[1:2] = column_sum(grad)
            grad_second = g3_ref[...] + norm_back(grad, unit, inverse, prm_ref[2:3])
            g2_ref[...] = grad_second
            branch = grad_second.astype(BF)
            b2_ref[...] = branch
            sum_ref[2:3] = column_sum(branch.astype(F32))

    full = whole((seq, width))
    wide = (blocks, seq, width)
    grads = sds(grad_shape, BF)
    return call(
        body, "feed_backward", blocks,
        [(b3, full), (g3, full), (hidden, per_block(wide)), (slope, per_block(wide)),
         (pack_in, packed(pack_in.shape)), (pack_out, packed(pack_out.shape)), (n3, full),
         (second, full), (params, whole(params.shape))],
        [(grads, packed(grad_shape))] * 2
        + [(sds((blocks, 8, width), F32), per_block((blocks, 8, width))),
           (sds((seq, width), F32), full), (sds((seq, width), BF), full),
           (sds((8, width), F32), whole((8, width)))],
        [pltpu.VMEM((width, seq), BF), pltpu.VMEM((width, seq), BF), pltpu.VMEM((seq, width), F32)],
        32 * seq * width * width,
    )


def cross_backward(b2, g2, queries, keys, values, keys_t, lse, ot, mixed, frames, n2, first, pack,
                   own, params, valid, grad_shape, dims):
    seq, width, blocks, hw = dims
    heads = hw // HD
    _, pieces, piece, _ = keys.shape
    total_keys = pieces * piece
    own_out = grad_shape[2]

    def body(b2_ref, g2_ref, q_ref, k_ref, v_ref, kt_ref, lse_ref, ot_ref, mix_ref, e_ref, n2_ref,
             first_ref, w_ref, prm_ref, grad_ref, genc_ref, g1_ref, b1_ref, sum_ref, hsum_ref,
             et_scr, b2t_scr, n2t_scr, dk_scr, dv_scr, ds_scr, dqt_scr, genc_scr, acc_scr):
        t = pl.program_id(0)

        @pl.when(t == 0)
        def _():
            for c in range(pieces):
                et_scr[:, c * piece : (c + 1) * piece] = e_ref[c].T
            b2t_scr[...] = b2_ref[...].T
            n2t_scr[...] = n2_ref[...].T
            acc_scr[...] = jnp.zeros_like(acc_scr)
            genc_scr[...] = jnp.zeros_like(genc_scr)

        w = weight(w_ref, own)
        q = q_ref[0]
        gm = project_back(b2_ref[...], w, hw).astype(BF)
        weighted = gm.astype(F32).T * ot_ref[0]
        row = lax.broadcasted_iota(jnp.int32, (piece, 1), 0)
        pad = jnp.where(row < valid, 0.0, NEGATIVE)
        dk_scr[...] = jnp.zeros_like(dk_scr)
        dv_scr[...] = jnp.zeros_like(dv_scr)
        for j in range(heads):
            delta = jnp.sum(weighted[j * HD : (j + 1) * HD], 0, keepdims=True)
            shift = lse_ref[0, j : j + 1]
            qm = head_lanes(q, j, HD)
            gj = head_lanes(gm, j, HD)

            def one_piece(c, carry):
                s = dot(k_ref[0, c], qm, 1, 1) + pad
                p = jnp.exp(s - shift)
                ds = (p * (dot(v_ref[0, c], gj, 1, 1) - delta)).astype(BF)
                dv_scr[c] += dot(p.astype(BF), gj)
                dk_scr[c] += dot(ds, qm)
                ds_scr[pl.ds(pl.multiple_of(c * piece, piece), piece)] = ds
                return carry

            lax.fori_loop(0, pieces, one_piece, 0)
            dqt_scr[j * HD : (j + 1) * HD] = dot(kt_ref[0, j * HD : (j + 1) * HD], ds_scr[...])
        dq = dqt_scr[...].T.astype(BF)
        hsum_ref[0, 0:1] = column_sum(dq.astype(F32)) * HD**-0.5
        dq = (dq.astype(F32) * HD**-0.5).astype(BF)
        bias = jnp.zeros((1, hw), F32)
        wkv = w[:, : 2 * hw]
        grad_kv = jnp.zeros((width, 2 * hw), F32)
        for c in range(pieces):
            dv = dv_scr[c].astype(BF)
            bias += column_sum(dv.astype(F32))
            dkv = jnp.concatenate([dk_scr[c].astype(BF), dv], 1)
            genc_scr[c] += dot(dkv, wkv, 1, 1)
            grad_kv += dot(et_scr[:, c * piece : (c + 1) * piece], dkv)
        hsum_ref[0, 1:2] = bias
        grad_q = dot(n2t_scr[...], dq)
        grad_o = dot(b2t_scr[...], mix_ref[0])
        store_pack(grad_ref, own_out, jnp.concatenate([grad_kv, grad_q, grad_o], 1).astype(BF))
        acc_scr[...] += dot(dq, w[:, 2 * hw : 3 * hw], 1, 1)

        @pl.when(t == blocks - 1)
        def _():
            genc_ref[...] = genc_scr[...].astype(BF)
            grad = acc_scr[...]
            unit, inverse = layer_norm_parts(first_ref[...])
            sum_ref[0:1] = column_sum(grad * unit)
            sum_ref[1:2] = column_sum(grad)
            grad_first = g2_ref[...] + norm_back(grad, unit, inverse, prm_ref[1:2])
            g1_ref[...] = grad_first
            branch = grad_first.astype(BF)
            b1_ref[...] = branch
            sum_ref[2:3] = column_sum(branch.astype(F32))

    full = whole((seq, width))
    hb = per_block((blocks, seq, hw))
    once = lambda shape: pl.BlockSpec(shape, lambda t, *_: (0,) * len(shape), pipeline_mode=pl.Buffered(1))
    return call(
        body, "cross_backward", blocks,
        [(b2, full), (g2, full), (queries, hb), (keys, per_block(keys.shape)),
         (values, per_block(values.shape)), (keys_t, per_block(keys_t.shape)),
         (lse, per_block(lse.shape)), (ot, per_block(ot.shape)), (mixed, hb),
         (frames, once(frames.shape)), (n2, full), (first, full), (pack, packed(pack.shape)),
         (params, whole(params.shape))],
        [(sds(grad_shape, BF), packed(grad_shape)),
         (sds(frames.shape, BF), once(frames.shape)),
         (sds((seq, width), F32), full), (sds((seq, width), BF), full),
         (sds((8, width), F32), whole((8, width))),
         (sds((blocks, 8, hw), F32), per_block((blocks, 8, hw)))],
        [pltpu.VMEM((width, total_keys), BF), pltpu.VMEM((width, seq), BF),
         pltpu.VMEM((width, seq), BF), pltpu.VMEM((pieces, piece, hw), F32),
         pltpu.VMEM((pieces, piece, hw), F32), pltpu.VMEM((total_keys, seq), BF),
         pltpu.VMEM((hw, seq), F32), pltpu.VMEM(frames.shape, F32), pltpu.VMEM((seq, width), F32)],
        16 * seq * width * width + 8 * total_keys * width * width + 40 * seq * total_keys * width,
    )


def self_backward(length, b1, g1, queries, keys, values, lse, ot, mixed, n1, rows, pack, own, params,
                  grad_shape, dims):
    seq, width, blocks, hw = dims
    heads = hw // HD
    own_out = grad_shape[2]

    def body(len_ref, b1_ref, g1_ref, q_ref, k_ref, v_ref, lse_ref, ot_ref, mix_ref, n1_ref, x_ref,
             w_ref, prm_ref, grad_ref, gin_ref, sum_ref, hsum_ref, b1t_scr, n1t_scr, bias_scr,
             dqt_scr, acc_scr):
        t = pl.program_id(0)

        @pl.when(t == 0)
        def _():
            b1t_scr[...] = b1_ref[...].T
            n1t_scr[...] = n1_ref[...].T
            acc_scr[...] = jnp.zeros_like(acc_scr)
            key = lax.broadcasted_iota(jnp.int32, (seq, seq), 0)
            query = lax.broadcasted_iota(jnp.int32, (seq, seq), 1)
            bias_scr[...] = jnp.where((key <= query) & (key < len_ref[0]), 0.0, NEGATIVE)

        w = weight(w_ref, own)
        q = q_ref[0]
        k = k_ref[0]
        v = v_ref[0]
        kt = k.T
        gm = project_back(b1_ref[...], w, hw).astype(BF)
        weighted = gm.astype(F32).T * ot_ref[0]
        dk = jnp.zeros((seq, hw), F32)
        dv = jnp.zeros((seq, hw), F32)
        for j in range(heads):
            delta = jnp.sum(weighted[j * HD : (j + 1) * HD], 0, keepdims=True)
            qm = head_lanes(q, j, HD)
            gj = head_lanes(gm, j, HD)
            p = jnp.exp(dot(k, qm, 1, 1) + bias_scr[...] - lse_ref[0, j : j + 1])
            ds = (p * (dot(v, gj, 1, 1) - delta)).astype(BF)
            dv += dot(p.astype(BF), gj)
            dk += dot(ds, qm)
            dqt_scr[j * HD : (j + 1) * HD] = dot(kt[j * HD : (j + 1) * HD], ds)
        dq = dqt_scr[...].T.astype(BF).astype(F32) * HD**-0.5
        dv = dv.astype(BF)
        hsum_ref[0, 0:1] = column_sum(dq)
        hsum_ref[0, 1:2] = column_sum(dv.astype(F32))
        dqkv = jnp.concatenate([dq.astype(BF), dk.astype(BF), dv], 1)
        grad_qkv = dot(n1t_scr[...], dqkv)
        grad_o = dot(b1t_scr[...], mix_ref[0])
        store_pack(grad_ref, own_out, jnp.concatenate([grad_qkv, grad_o], 1).astype(BF))
        acc_scr[...] += dot(dqkv, w[:, : 3 * hw], 1, 1)

        @pl.when(t == blocks - 1)
        def _():
            grad = acc_scr[...]
            unit, inverse = layer_norm_parts(x_ref[...].astype(F32))
            sum_ref[0:1] = column_sum(grad * unit)
            sum_ref[1:2] = column_sum(grad)
            gin_ref[...] = g1_ref[...] + norm_back(grad, unit, inverse, prm_ref[0:1])

    full = whole((seq, width))
    hb = per_block((blocks, seq, hw))
    return call(
        body, "self_backward", blocks,
        [(b1, full), (g1, full), (queries, hb), (keys, hb), (values, hb),
         (lse, per_block(lse.shape)), (ot, per_block(ot.shape)), (mixed, hb), (n1, full),
         (rows, full), (pack, packed(pack.shape)), (params, whole(params.shape))],
        [(sds(grad_shape, BF), packed(grad_shape)),
         (sds((seq, width), F32), full),
         (sds((8, width), F32), whole((8, width))),
         (sds((blocks, 8, hw), F32), per_block((blocks, 8, hw)))],
        [pltpu.VMEM((width, seq), BF), pltpu.VMEM((width, seq), BF), pltpu.VMEM((seq, seq), F32),
         pltpu.VMEM((hw, seq), F32), pltpu.VMEM((seq, width), F32)],
        16 * seq * width * width + 40 * seq * seq * width,
        (length,),
    )


def pad_rows(rows, count):
    return jnp.pad(rows, ((0, count - rows.shape[0]),) + ((0, 0),) * (rows.ndim - 1))


def gather_pack(shard):
    whole_pack = lax.all_gather(shard, ("fsdp", "tp"), axis=0, tiled=False)
    return whole_pack.reshape((lax.axis_size("fsdp"), lax.axis_size("tp")) + shard.shape)


def kernel_form(pack, own):
    if own % 16 == 0:
        return pack, own
    outer, blocks, held, width = pack.shape
    flat = pack[:, :, :own].transpose(1, 0, 2, 3).reshape(1, blocks, outer * own, width)
    return flat, outer * own


def scatter_pack(grads, own):
    fsdp, tp = lax.axis_size("fsdp"), lax.axis_size("tp")
    if grads.shape[2] != own:
        blocks, width = grads.shape[1], grads.shape[3]
        grads = grads.reshape(blocks, fsdp, own, width).transpose(1, 0, 2, 3)
    place = lax.axis_index("fsdp")
    step = 1
    while step < fsdp:
        pairs = grads.reshape((grads.shape[0] // 2, 2) + grads.shape[1:])
        bit = (place // step) % 2
        kept = lax.dynamic_index_in_dim(pairs, bit, 1, keepdims=False)
        sent = lax.dynamic_index_in_dim(pairs, 1 - bit, 1, keepdims=False)
        come = lax.ppermute(sent, "fsdp", [(i, i ^ step) for i in range(fsdp)])
        grads = (kept.astype(F32) + come.astype(F32)).astype(BF)
        step *= 2
    grads = grads[0]
    here = lax.axis_index("tp")
    total = lax.dynamic_index_in_dim(grads, here, 0, keepdims=False).astype(F32)
    for hop in range(1, tp):
        sent = lax.dynamic_index_in_dim(grads, (here + hop) % tp, 0, keepdims=False)
        total += lax.ppermute(sent, "tp", [(i, (i + hop) % tp) for i in range(tp)]).astype(F32)
    return total


def local(
    inputs,
    encoder,
    lengths,
    self_qkv,
    self_out,
    cross_q,
    cross_kv,
    cross_out,
    fc_in,
    fc_out,
    norm_gain,
    norm_bias,
    proj_bias,
    fc_in_bias,
    cotangent,
):
    fsdp, tp = lax.axis_size("fsdp"), lax.axis_size("tp")
    devices = fsdp * tp
    tp_place = lax.axis_index("tp")
    seqs, seq, width = inputs.shape
    assert seqs == 1
    own, hw = cross_q.shape
    dims = (seq, width, tp, hw)
    frames_own = encoder.shape[1]
    small_own = norm_gain.shape[1]
    ff_own = fc_in_bias.shape[0]

    small = jnp.concatenate(
        [a.reshape(-1) for a in (norm_gain, norm_bias, proj_bias, fc_in_bias)]
    )
    small = jnp.pad(small, (0, width - small.size))
    high = small.astype(BF)
    low = (small - high.astype(F32)).astype(BF)
    extra = pad_rows(jnp.stack([high, low]), 16)

    pack_self = jnp.concatenate([self_qkv[0], self_qkv[1], self_qkv[2], self_out.T], 1)
    pack_self = jnp.concatenate([pack_self, extra], 0)
    pack_cross = jnp.concatenate([cross_kv[0], cross_kv[1], cross_q, cross_out.T], 1)
    w_self = gather_pack(pack_self)
    w_cross = gather_pack(pack_cross)
    w_in = gather_pack(fc_in)
    w_out = gather_pack(fc_out.T)

    table = w_self[:, :, own : own + 2].astype(F32).sum(2).reshape(devices, width)
    rows = (norm_gain.shape[0] + norm_bias.shape[0] + proj_bias.shape[0])
    params = table[:, : rows * small_own].reshape(devices, rows, small_own)
    params = params.transpose(1, 0, 2).reshape(rows, width)
    fc_bias = table[:, rows * small_own : rows * small_own + ff_own].reshape(tp, width)
    head_bias = jnp.stack([params[8], params[9], params[11], params[12]])
    head_bias = head_bias.reshape(4, tp, hw).transpose(1, 0, 2)
    head_bias = jnp.pad(head_bias, ((0, 0), (0, 4), (0, 0)))
    params = pad_rows(jnp.concatenate([params, fc_bias], 0), 24)

    w_self, own_rows = kernel_form(w_self, own)
    w_cross, _ = kernel_form(w_cross, own)
    w_in, _ = kernel_form(w_in, own)
    w_out, _ = kernel_form(w_out, own)
    grad_shape = (width // own_rows, tp, own_rows, width)

    piece = -(-frames_own // 128) * 128
    frames = lax.all_to_all(encoder, "tp", 0, 0, tiled=True)
    frames = jnp.pad(frames, ((0, 0), (0, piece - frames_own), (0, 0)))
    length = lax.dynamic_slice_in_dim(lengths, tp_place, 1)

    x = inputs[0]
    n1, q1, k1, v1, lse1, ot1, mixed1, first, n2 = self_forward(
        length, x, w_self, own_rows, params, head_bias, dims
    )
    k2, v2, k2t, v2t = frame_keys(frames, w_cross, own_rows, head_bias, dims)
    q2, lse2, ot2, mixed2, second, n3 = cross_forward(
        n2, first, w_cross, own_rows, params, head_bias, k2, v2t, frames_own, dims
    )
    hidden, slope, layer_out, g3, b3, sums3 = feed_forward(
        n3, second, w_in, w_out, own_rows, params, cotangent[0], dims
    )
    grad_out, grad_in, fcb, g2, b2, sums2 = feed_backward(
        b3, g3, hidden, slope, w_in, w_out, own_rows, n3, second, params, grad_shape, dims
    )
    grad_cross, grad_frames, g1, b1, sums1, hsum2 = cross_backward(
        b2, g2, q2, k2, v2, k2t, lse2, ot2, mixed2, frames, n2, first, w_cross, own_rows, params,
        frames_own, grad_shape, dims
    )
    grad_self, grad_inputs, sums0, hsum1 = self_backward(
        length, b1, g1, q1, k1, v1, lse1, ot1, mixed1, n1, x, w_self, own_rows, params, grad_shape,
        dims
    )

    grad_encoder = lax.all_to_all(grad_frames[:, :frames_own], "tp", 0, 0, tiled=True)

    def heads_row(block, row):
        return block[:, row].reshape(1, width)

    table = jnp.concatenate(
        [
            sums0[0:1], sums1[0:1], sums2[0:1], sums3[0:1],
            sums0[1:2], sums1[1:2], sums2[1:2], sums3[1:2],
            heads_row(hsum1, 0), heads_row(hsum1, 1), sums1[2:3],
            heads_row(hsum2, 0), heads_row(hsum2, 1), sums2[2:3], sums3[2:3],
        ],
        0,
    )
    table = table.reshape(rows, devices, small_own).transpose(1, 0, 2).reshape(devices, -1)
    table = jnp.concatenate([table, fcb[:, 0].reshape(devices, ff_own)], 1)
    mine = lax.psum_scatter(table, ("fsdp", "tp"), scatter_dimension=0, tiled=True)[0]
    rows4 = norm_gain.size
    own_gain = mine[:rows4].reshape(norm_gain.shape)
    own_shift = mine[rows4 : 2 * rows4].reshape(norm_bias.shape)
    own_bias = mine[2 * rows4 : rows * small_own].reshape(proj_bias.shape)
    own_fc_bias = mine[rows * small_own :]

    total_out = scatter_pack(grad_out, own)
    total_in = scatter_pack(grad_in, own)
    total_cross = scatter_pack(grad_cross, own)
    total_self = scatter_pack(grad_self, own)

    def part(total, index):
        return total[:, index * hw : (index + 1) * hw]

    return (
        layer_out[None],
        grad_inputs[None],
        grad_encoder.astype(F32),
        jnp.stack([part(total_self, 0), part(total_self, 1), part(total_self, 2)]),
        part(total_self, 3).T,
        part(total_cross, 2),
        jnp.stack([part(total_cross, 0), part(total_cross, 1)]),
        part(total_cross, 3).T,
        total_in,
        total_out.T,
        own_gain,
        own_shift,
        own_bias,
        own_fc_bias,
    )


def solution(mesh):
    return jax.shard_map(
        local,
        mesh=mesh,
        in_specs=(
            P(("fsdp", "tp"), None, None),
            P("fsdp", "tp", None),
            P("fsdp"),
            P(None, "fsdp", "tp"),
            P("tp", "fsdp"),
            P("fsdp", "tp"),
            P(None, "fsdp", "tp"),
            P("tp", "fsdp"),
            P("fsdp", "tp"),
            P("tp", "fsdp"),
            P(None, ("fsdp", "tp")),
            P(None, ("fsdp", "tp")),
            P(None, ("fsdp", "tp")),
            P(("fsdp", "tp")),
            P(("fsdp", "tp"), None, None),
        ),
        out_specs=(
            P(("fsdp", "tp"), None, None),
            P(("fsdp", "tp"), None, None),
            P("fsdp", "tp", None),
            P(None, "fsdp", "tp"),
            P("tp", "fsdp"),
            P("fsdp", "tp"),
            P(None, "fsdp", "tp"),
            P("tp", "fsdp"),
            P("fsdp", "tp"),
            P("tp", "fsdp"),
            P(None, ("fsdp", "tp")),
            P(None, ("fsdp", "tp")),
            P(None, ("fsdp", "tp")),
            P(("fsdp", "tp")),
        ),
        check_vma=False,
    )
```

time: 1690 us -> 698 us (0.41)
  waiting for transfers between devices: 821 us -> 307 us
  blocking collectives: 349 us -> 71.2 us
  matrix products: 238 us -> 0 us
  Pallas kernels: 0 us -> 175 us
  local copies, waits for them, and re-layouts: 189 us -> 47.7 us
  starting transfers between devices: 3.05 us -> 47.5 us
  other arithmetic: 68.7 us -> 25.9 us
    all_gather x8 -> x0, blocking collectives: 264 us -> none  [the longest x1 70.4 us: local(): lax.all_gather(norm_gain, ('fsdp', 'tp'), axis=1, tiled=True)]
    reduce_scatter x8 -> x0, waiting for transfers between devices: 264 us -> none  [the longest x3 158 us: scatter_rows(): lax.psum_scatter(partial_out.reshape(group_seqs, seq_len, width_all).asty...]
    unnamed x29 -> x4, waiting for transfers between devices: 251 us -> 1.24 us
    dot_general x84 -> x0, matrix products: 229 us -> none  [the longest x10 51.5 us: matmul(): return jnp.dot(left_side, right_side, preferred_element_type=jnp.float32)]
    pallas_call x0 -> x7, Pallas kernels: none -> 175 us  [call(): pl.pallas_call(body, out_shape=[o for o, _ in outs], grid_spec=pltpu.Pref...]
    all_gather x9 -> x4, waiting for transfers between devices: 306 us -> 143 us  [gather_pack(): whole_pack = lax.all_gather(shard, ('fsdp', 'tp'), axis=0, tiled=False)]
    ppermute x0 -> x24, waiting for transfers between devices: none -> 96.8 us  [the longest x12 75.2 us: scatter_pack(): come = lax.ppermute(sent, 'fsdp', [(i, i ^ step) for i in range(fsdp)])]
    all_to_all x0 -> x2, waiting for transfers between devices: none -> 65.9 us  [the longest x1 65.9 us: local(): frames = lax.all_to_all(encoder, 'tp', 0, 0, tiled=True)]
  transfers between devices with their start and end apart: 23 -> 30, of which waited for: 12 -> 15; matrix products, arithmetic and copies ran while one was open for 16% -> 8% of each run, Pallas kernels for 0% -> 9%
where the time goes in v1:
time: 698 us; the launch traced here: 689 us
  waiting for transfers between devices  307 us (44%)
  Pallas kernels  175 us (25%)
  blocking collectives  71.2 us (10%)
  local copies, waits for them, and re-layouts  47.7 us (7%)
  starting transfers between devices  47.5 us (7%)
  other arithmetic  25.9 us (4%)
  between operations  14.9 us (2%)
    pallas_call x7, Pallas kernels, call(): pl.pallas_call(body, out_shape=[o for o, _ in outs], grid_spec=pltpu.Pref...  175 us
    all_gather x4, waiting for transfers between devices, gather_pack(): whole_pack = lax.all_gather(shard, ('fsdp', 'tp'), axis=0, tiled=False)  143 us
    ppermute x12, waiting for transfers between devices, scatter_pack(): come = lax.ppermute(sent, 'fsdp', [(i, i ^ step) for i in range(fsdp)])  75.2 us
    unnamed x1, blocking collectives  71.2 us
    all_to_all x1, waiting for transfers between devices, local(): frames = lax.all_to_all(encoder, 'tp', 0, 0, tiled=True)  65.9 us
    ppermute x12, waiting for transfers between devices, scatter_pack(): lax.ppermute(sent, 'tp', [(i, (i + hop) % tp) for i in range(tp)])  21.6 us
    ppermute x12, starting transfers between devices, scatter_pack(): lax.ppermute(sent, 'tp', [(i, (i + hop) % tp) for i in range(tp)])  21.5 us
    convert_element_type x12, other arithmetic, scatter_pack(): grads = (kept.astype(F32) + come.astype(F32)).astype(BF)  16.9 us
  transfers between devices with their start and end apart: 30, of which 15 were waited for; matrix products, arithmetic and copies ran while one was open for 8% of the time, Pallas kernels for 9%

profile of v1, /device:TPU:0, one launch (start us, length us, event | category | flops | bytes accessed | tf_op | source)
XLA Modules:
  0.0 689.2 jit_solution(7817996132172678808)
XLA Ops:
  11.9 0.9 copy.67
  13.6 0.9 copy.73
  15.4 1.6 pad_maximum_fusion.3
  18.3 3.3 copy.74
  21.6 6.5 all-to-all-start
  28.7 65.9 %all-to-all-done = bf16[4,375,768]{2,1,0:T(8,128)(2,1)S(1)} async-done(((bf16[4,375,768]{2,1,0:T(8,128)(2,1)}), bf16[4,375,768]{2,1,0:T(8,128)(2,1)S(1)}, u32[]{:S(2)}, u32[]{:S(2)}) %all-to-all-start) | async-done | bytes 2304032 | tf_op jit(solution)/shard_map/all_to_all | solution.py:643
  94.5 1.6 pad.24.e_ref
  96.1 12.2 %all-gather.9.cloned.1.call-done = bf16[3584,768]{1,0:T(8,128)(2,1)} async-done(((bf16[112,768]{1,0:T(8,128)(2,1)}), bf16[3584,768]{1,0:T(8,128)(2,1)}) %all-gather.9.cloned.1.call-update) | async-done | bytes 5505040 | tf_op jit(solution)/shard_map/all_gather | solution.py:546
  108.3 1.3 convert_reduce_fusion
  112.0 62.0 %all-gather.11.cloned.1.call-done = bf16[3072,768]{1,0:T(8,128)(2,1)} async-done(((bf16[96,768]{1,0:T(8,128)(2,1)}), bf16[3072,768]{1,0:T(8,128)(2,1)}) %all-gather.11.cloned.1.call-update) | async-done | bytes 4718608 | tf_op jit(solution)/shard_map/all_gather | solution.py:546
  174.0 10.6 %frame_keys.1 = (bf16[4,4,384,192]{3,2,1,0:T(8,128)(2,1)}, bf16[4,4,384,192]{3,2,1,0:T(8,128)(2,1)}, bf16[4,192,1536]{2,1,0:T(8,128)(2,1)}, bf16[4,192,1536]{2,1,0:T(8,128)(2,1)}) custom-call(bf16[4,384,768]{2,1,0:T(8,128)(2,1)} %pad.24.e_ref, bf16[8,4,96,768]{3,2,1,0:T(8,128)(2,1)} %bitcast.166, f32[4,8,192]{2,1,0:T(8,128)} %pad.23.hb_ref), custom_call_target="tpu_custom_call" | custom-call | flops 3623878656 | bytes 16539648 | tf_op jit(solution)/shard_map/frame_keys/pallas_call | solution.py:63
  184.6 15.8 %self_forward.1 = (bf16[448,768]{1,0:T(8,128)(2,1)}, bf16[4,448,192]{2,1,0:T(8,128)(2,1)}, bf16[4,448,192]{2,1,0:T(8,128)(2,1)}, bf16[4,448,192]{2,1,0:T(8,128)(...) custom-call(s32[1]{0:T(128)} %dynamic_slice.111.len_ref, ...), custom_call_target="tpu_custom_call" | custom-call | flops 4580179968 | bytes 13230080 | tf_op jit(solution)/shard_map/self_forward/pallas_call | solution.py:63
  200.5 33.6 %cross_forward.1 = (bf16[4,448,192]{2,1,0:T(8,128)(2,1)}, f32[4,8,448]{2,1,0:T(8,128)}, f32[4,192,448]{2,1,0:T(8,128)}, bf16[4,448,192]{2,1,0:T(8,128)(2,1)}, f3...) custom-call(bf16[448,768]{1,0:T(8,128)(2,1)} %get-tuple-element.55.n2_ref, f32[448,768]{1,0:T(8,128)} %get-tuple-element.56.first_ref, ...), custom_call_target="tpu_custom_call" | custom-call | flops 9512681472 | bytes 16474112 | tf_op jit(solution)/shard_map/cross_forward/pallas_call | solution.py:63
  234.1 4.7 all-gather.13.cloned.1.call-done
  238.7 64.6 %all-gather.15.cloned.1.call-done = bf16[3072,768]{1,0:T(8,128)(2,1)} async-done(((bf16[96,768]{1,0:T(8,128)(2,1)}), bf16[3072,768]{1,0:T(8,128)(2,1)}) %all-gather.15.cloned.1.call-update) | async-done | bytes 4718608 | tf_op jit(solution)/shard_map/all_gather | solution.py:546
  303.3 13.9 %feed_forward.1 = (bf16[4,448,768]{2,1,0:T(8,128)(2,1)}, f32[4,448,768]{2,1,0:T(8,128)}, bf16[448,768]{1,0:T(8,128)(2,1)}, f32[448,768]{1,0:T(8,128)}, bf16[448,768]{1,0:T(8,128)(2,1)}, /*index=5*/f32[8,768]{1,0:T(8,128)}) custom-call(bf16[448,768]{1,0:T(8,128)(2,1)} %get-tuple-element.59.n3_ref, f32[448,768]{1,0:T(8,128)} %get-tuple-element.60.second_ref, ...), custom_call_target="tpu_custom_call" | custom-call | flops 4227858432 | bytes 23298048 | tf_op jit(solution)/shard_map/feed_forward/pallas_call | solution.py:63
  317.2 17.9 %feed_backward.1 = (bf16[8,4,96,768]{3,2,1,0:T(8,128)(2,1)}, bf16[8,4,96,768]{3,2,1,0:T(8,128)(2,1)}, f32[4,8,768]{2,1,0:T(8,128)}, f32[448,768]{1,0:T(8,128)}, ...) custom-call(bf16[448,768]{1,0:T(8,128)(2,1)} %get-tuple-element.62.b3_ref, f32[448,768]{1,0:T(8,128)} %get-tuple-element.63.g3_ref, ...), custom_call_target="tpu_custom_call" | custom-call | flops 8455716864 | bytes 33521664 | tf_op jit(solution)/shard_map/feed_backward/pallas_call | solution.py:63
  335.1 59.9 %cross_backward.1 = (bf16[8,4,96,768]{3,2,1,0:T(8,128)(2,1)}, bf16[4,384,768]{2,1,0:T(8,128)(2,1)}, f32[448,768]{1,0:T(8,128)}, bf16[448,768]{1,0:T(8,128)(2,1)}...) custom-call(bf16[448,768]{1,0:T(8,128)(2,1)} %get-tuple-element.66.b2_ref, f32[448,768]{1,0:T(8,128)} %get-tuple-element.67.g2_ref, ...), custom_call_target="tpu_custom_call" | custom-call | flops 32614907904 | bytes 30359552 | tf_op jit(solution)/shard_map/cross_backward/pallas_call | solution.py:63
  395.0 23.0 %self_backward.1 = (bf16[8,4,96,768]{3,2,1,0:T(8,128)(2,1)}, f32[448,768]{1,0:T(8,128)}, f32[8,768]{1,0:T(8,128)}, f32[4,8,192]{2,1,0:T(8,128)}) custom-call(s32[1]{0:T(128)} %dynamic_slice.111.len_ref, bf16[448,768]{1,0:T(8,128)(2,1)} %get-tuple-element.74.b1_ref, f32[448,768]{1,0:T(8,128)} %get-tuple-element.75.g1_ref, ...), custom_call_target="tpu_custom_call" | custom-call | flops 10393485312 | bytes 19349504 | tf_op jit(solution)/shard_map/self_backward/pallas_call | solution.py:63
  421.0 0.9 slice_reduce_fusion.9
  423.2 3.4 dynamic-slice_bitcast_fusion
  426.9 1.5 dynamic-slice_bitcast_fusion.1
  429.9 3.3 dynamic-slice_bitcast_fusion.2
  433.5 3.4 dynamic-slice_bitcast_fusion.3
  437.1 1.5 slice.145
  438.6 4.6 all-to-all-start.1
  443.9 0.9 slice_reduce_fusion.4
  445.0 71.2 %all-reduce.5 = f32[32,456]{1,0:T(8,128)S(1)} all-reduce(f32[32,456]{1,0:T(8,128)S(1)} %pad_maximum_fusion.4), channel_id=6, replica_groups=mesh['fsdp'=8,'tp'=4] {'fsdp','tp'}, use_global_device_ids=true, to_apply=%region_1.2.clone | all-reduce | flops 14592 | bytes 116736
  518.9 2.5 fusion
  521.5 2.3 collective-permute-start.19
  523.9 2.4 fusion.1
  526.3 1.1 dynamic-slice_bitcast_fusion.5
  527.4 1.2 collective-permute-start.13
  528.6 2.8 fusion.2
  531.3 1.3 dynamic-slice_bitcast_fusion.6
  532.7 1.1 collective-permute-start.7
  533.8 2.4 fusion.3
  536.1 1.1 dynamic-slice_bitcast_fusion.7
  537.3 0.9 collective-permute-start.1
  538.2 4.8 copy.80
  543.0 7.7 %collective-permute-done.19 = bf16[2,4,96,768]{3,2,1,0:T(8,128)(2,1)} collective-permute-done((bf16[2,4,96,768]{3,2,1,0:T(8,128)(2,1)S(1)}, bf16[2,4,96,768]{3,2,1,0:T(8,128)(2,1)}, u32[]{:S(2)}, u32[]{:S(2)}) %collective-permute-start.19) | collective-permute-done | bytes 1179680 | tf_op jit(solution)/shard_map/ppermute | solution.py:570
  550.8 1.6 fusion.4
  552.4 2.1 collective-permute-start.20
  554.5 21.5 %collective-permute-done.13 = bf16[2,4,96,768]{3,2,1,0:T(8,128)(2,1)} collective-permute-done((bf16[2,4,96,768]{3,2,1,0:T(8,128)(2,1)}, bf16[2,4,96,768]{3,2,1,0:T(8,128)(2,1)}, u32[]{:S(2)}, u32[]{:S(2)}) %collective-permute-start.13) | collective-permute-done | bytes 1179680 | tf_op jit(solution)/shard_map/ppermute | solution.py:570
  576.1 1.6 fusion.5
  577.7 2.1 collective-permute-start.14
  579.8 21.5 %collective-permute-done.7 = bf16[2,4,96,768]{3,2,1,0:T(8,128)(2,1)} collective-permute-done((bf16[2,4,96,768]{3,2,1,0:T(8,128)(2,1)}, bf16[2,4,96,768]{3,2,1,0:T(8,128)(2,1)}, u32[]{:S(2)}, u32[]{:S(2)}) %collective-permute-start.7) | collective-permute-done | bytes 1179680 | tf_op jit(solution)/shard_map/ppermute | solution.py:570
  601.3 1.6 fusion.6
  603.0 2.1 collective-permute-start.8
  605.1 19.9 %collective-permute-done.1 = bf16[2,4,96,768]{3,2,1,0:T(8,128)(2,1)} collective-permute-done((bf16[2,4,96,768]{3,2,1,0:T(8,128)(2,1)}, bf16[2,4,96,768]{3,2,1,0:T(8,128)(2,1)}, u32[]{:S(2)}, u32[]{:S(2)}) %collective-permute-start.1) | collective-permute-done | bytes 1179680 | tf_op jit(solution)/shard_map/ppermute | solution.py:570
  625.0 1.5 fusion.7
  626.6 1.8 collective-permute-start.2
  628.7 2.9 collective-permute-start.22
  631.9 3.7 collective-permute-start.11
  635.8 4.5 collective-permute-done.2
  640.6 9.4 %collective-permute-done.10 = bf16[96,768]{1,0:T(8,128)(2,1)S(1)} collective-permute-done((bf16[96,768]{1,0:T(8,128)(2,1)S(1)}, bf16[96,768]{1,0:T(8,128)(2,1)S(1)}, u32[]{:S(2)}, u32[]{:S(2)}) %collective-permute-start.10) | collective-permute-done | bytes 147488 | tf_op jit(solution)/shard_map/ppermute | solution.py:578
  650.0 3.1 collective-permute-start.4
  653.1 2.5 collective-permute-start.5
  656.3 2.2 collective-permute-done.3
  658.6 4.0 collective-permute-done.4
  662.5 5.6 collective-permute-start.15
  668.2 3.4 collective-permute-start.16
  675.5 1.2 collective-permute-done.15
  676.7 4.8 collective-permute-done.16
  (160 shorter events, 27.3 us)
Async XLA Ops:
  7.2 101.1 %all-gather.9.cloned.1.call-start = ((), (), s32[]{:S(2)}) async-start(), calls=%async_computation.2 | async-start | bytes 5677056 | tf_op jit(solution)/shard_map/all_gather | solution.py:546
  13.6 160.4 %all-gather.11.cloned.1.call-start = ((), (), s32[]{:S(2)}) async-start(), calls=%async_computation.3 | async-start | bytes 4866048 | tf_op jit(solution)/shard_map/all_gather | solution.py:546
  17.0 221.8 %all-gather.13.cloned.1.call-start = ((), (), s32[]{:S(2)}) async-start(), calls=%async_computation.4 | async-start | bytes 4866048 | tf_op jit(solution)/shard_map/all_gather | solution.py:546
  17.7 285.6 %all-gather.15.cloned.1.call-start = ((), (), s32[]{:S(2)}) async-start(), calls=%async_computation.5 | async-start | bytes 4866048 | tf_op jit(solution)/shard_map/all_gather | solution.py:546
  21.6 6.5 copy-start.8
  21.6 72.9 %all-to-all-start = ((bf16[4,375,768]{2,1,0:T(8,128)(2,1)}), bf16[4,375,768]{2,1,0:T(8,128)(2,1)S(1)}, u32[]{:S(2)}, u32[]{:S(2)}) async-start(bf16[4,375,768]{2,1,0:T(8,128)(2,1)} %copy.74), calls=%async_computation | async-start | bytes 4620288 | tf_op jit(solution)/shard_map/all_to_all | solution.py:643
  423.2 3.7 copy-start.6
  426.6 92.3 %collective-permute-start.18 = (bf16[4,4,96,768]{3,2,1,0:T(8,128)(2,1)}, bf16[4,4,96,768]{3,2,1,0:T(8,128)(2,1)S(1)}, u32[]{:S(2)}, u32[]{:S(2)}) collective-permute-start(bf16[4,4,96,768]{3,2,1,0:T(8,128)(2,1)} %dynamic-slice_bitcast_fusion), channel_id=1, source_target_pairs={{0,4},{4,0},{8,12},{12,8},{16,20},{20,16},{24,28},{28,24},{1,5},{5... | collective-permute-start | bytes 7077896 | tf_op jit(solution)/shard_map/ppermute | solution.py:570
  429.6 94.2 %collective-permute-start.12 = (bf16[4,4,96,768]{3,2,1,0:T(8,128)(2,1)}, bf16[4,4,96,768]{3,2,1,0:T(8,128)(2,1)}, u32[]{:S(2)}, u32[]{:S(2)}) collective-permute-start(bf16[4,4,96,768]{3,2,1,0:T(8,128)(2,1)} %dynamic-slice_bitcast_fusion.1), channel_id=1, source_target_pairs={{0,4},{4,0},{8,12},{12,8},{16,20},{20,16},{24,28},{28,24},{1,5},{5... | collective-permute-start | bytes 7077896 | tf_op jit(solution)/shard_map/ppermute | solution.py:570
  433.2 95.3 %collective-permute-start.6 = (bf16[4,4,96,768]{3,2,1,0:T(8,128)(2,1)}, bf16[4,4,96,768]{3,2,1,0:T(8,128)(2,1)}, u32[]{:S(2)}, u32[]{:S(2)}) collective-permute-start(bf16[4,4,96,768]{3,2,1,0:T(8,128)(2,1)} %dynamic-slice_bitcast_fusion.2), channel_id=1, source_target_pairs={{0,4},{4,0},{8,12},{12,8},{16,20},{20,16},{24,28},{28,24},{1,5},{5... | collective-permute-start | bytes 7077896 | tf_op jit(solution)/shard_map/ppermute | solution.py:570
  433.5 3.6 copy-start.7
  436.8 96.9 %collective-permute-start = (bf16[4,4,96,768]{3,2,1,0:T(8,128)(2,1)}, bf16[4,4,96,768]{3,2,1,0:T(8,128)(2,1)}, u32[]{:S(2)}, u32[]{:S(2)}) collective-permute-start(bf16[4,4,96,768]{3,2,1,0:T(8,128)(2,1)} %dynamic-slice_bitcast_fusion.3), channel_id=1, source_target_pairs={{0,4},{4,0},{8,12},{12,8},{16,20},{20,16},{24,28},{28,24},{1,5},{5... | collective-permute-start | bytes 7077896 | tf_op jit(solution)/shard_map/ppermute | solution.py:570
  438.6 85.3 %slice-start = ((s8[4718592]{0:T(1024)(128)(4,1)}), s8[524288]{0:T(1024)(128)(4,1)S(1)}, s32[]{:S(2)}) async-start(s8[4718592]{0:T(1024)(128)(4,1)} %bitcast.144), calls=%async_computation.6 | async-start | bytes 1048576
  438.6 99.6 %all-to-all-start.1 = ((bf16[4,375,768]{2,1,0:T(8,128)(2,1)}), bf16[4,375,768]{2,1,0:T(8,128)(2,1)}, u32[]{:S(2)}, u32[]{:S(2)}) async-start(bf16[4,375,768]{2,1,0:T(8,128)(2,1)} %slice.145), calls=%async_computation.1 | async-start | bytes 4620288 | tf_op jit(solution)/shard_map/all_to_all | solution.py:670
  518.9 5.0 slice-start.1
  521.4 4.8 copy-start
  521.4 7.1 %slice-start.2 = ((s8[4718592]{0:T(1024)(128)(4,1)}), s8[4194304]{0:T(1024)(128)(4,1)S(1)}, s32[]{:S(2)}) async-start(s8[4718592]{0:T(1024)(128)(4,1)} %bitcast.148), calls=%async_computation.8 | async-start | bytes 8388608
  521.5 7.0 %slice-start.3 = ((s8[4718592]{0:T(1024)(128)(4,1)}), s8[524288]{0:T(1024)(128)(4,1)S(1)}, s32[]{:S(2)}) async-start(s8[4718592]{0:T(1024)(128)(4,1)} %bitcast.148), calls=%async_computation.9 | async-start | bytes 1048576
  521.5 29.2 %collective-permute-start.19 = (bf16[2,4,96,768]{3,2,1,0:T(8,128)(2,1)S(1)}, bf16[2,4,96,768]{3,2,1,0:T(8,128)(2,1)}, u32[]{:S(2)}, u32[]{:S(2)}) collective-permute-start(bf16[2,4,96,768]{3,2,1,0:T(8,128)(2,1)S(1)} %dynamic-slice_bitcast_fusion.4), channel_id=1, source_target_pairs={{0,8},{4,12},{8,0},{12,4},{16,24},{20,28},{24,16},{28,20},{1,9},{5... | collective-permute-start | bytes 3538952 | tf_op jit(solution)/shard_map/ppermute | solution.py:570
  526.3 5.1 copy-start.2
  526.3 7.5 %slice-start.4 = ((s8[4718592]{0:T(1024)(128)(4,1)}), s8[4194304]{0:T(1024)(128)(4,1)S(1)}, s32[]{:S(2)}) async-start(s8[4718592]{0:T(1024)(128)(4,1)} %bitcast.152), calls=%async_computation.10 | async-start | bytes 8388608
  527.4 6.4 slice-start.5
  527.4 48.7 %collective-permute-start.13 = (bf16[2,4,96,768]{3,2,1,0:T(8,128)(2,1)}, bf16[2,4,96,768]{3,2,1,0:T(8,128)(2,1)}, u32[]{:S(2)}, u32[]{:S(2)}) collective-permute-start(bf16[2,4,96,768]{3,2,1,0:T(8,128)(2,1)} %dynamic-slice_bitcast_fusion.5), channel_id=1, source_target_pairs={{0,8},{4,12},{8,0},{12,4},{16,24},{20,28},{24,16},{28,20},{1,9},{5... | collective-permute-start | bytes 3538952 | tf_op jit(solution)/shard_map/ppermute | solution.py:570
  531.3 4.8 copy-start.4
  532.7 68.7 %collective-permute-start.7 = (bf16[2,4,96,768]{3,2,1,0:T(8,128)(2,1)}, bf16[2,4,96,768]{3,2,1,0:T(8,128)(2,1)}, u32[]{:S(2)}, u32[]{:S(2)}) collective-permute-start(bf16[2,4,96,768]{3,2,1,0:T(8,128)(2,1)} %dynamic-slice_bitcast_fusion.6), channel_id=1, source_target_pairs={{0,8},{4,12},{8,0},{12,4},{16,24},{20,28},{24,16},{28,20},{1,9},{5... | collective-permute-start | bytes 3538952 | tf_op jit(solution)/shard_map/ppermute | solution.py:570
  537.3 87.7 %collective-permute-start.1 = (bf16[2,4,96,768]{3,2,1,0:T(8,128)(2,1)}, bf16[2,4,96,768]{3,2,1,0:T(8,128)(2,1)}, u32[]{:S(2)}, u32[]{:S(2)}) collective-permute-start(bf16[2,4,96,768]{3,2,1,0:T(8,128)(2,1)} %dynamic-slice_bitcast_fusion.7), channel_id=1, source_target_pairs={{0,8},{4,12},{8,0},{12,4},{16,24},{20,28},{24,16},{28,20},{1,9},{5... | collective-permute-start | bytes 3538952 | tf_op jit(solution)/shard_map/ppermute | solution.py:570
  538.2 12.6 %copy-start.1 = (bf16[4,4,96,768]{3,2,1,0:T(8,128)(2,1)S(1)}, bf16[4,4,96,768]{3,2,1,0:T(8,128)(2,1)}, u32[]{:S(2)}) copy-start(bf16[4,4,96,768]{3,2,1,0:T(8,128)(2,1)} %copy-done) | copy-start | bytes 7077892
  543.0 33.0 %copy-start.3 = (bf16[4,4,96,768]{3,2,1,0:T(8,128)(2,1)S(1)}, bf16[4,4,96,768]{3,2,1,0:T(8,128)(2,1)}, u32[]{:S(2)}) copy-start(bf16[4,4,96,768]{3,2,1,0:T(8,128)(2,1)} %copy-done.2) | copy-start | bytes 7077892
  552.4 48.9 %copy-start.5 = (bf16[4,4,96,768]{3,2,1,0:T(8,128)(2,1)S(1)}, bf16[4,4,96,768]{3,2,1,0:T(8,128)(2,1)}, u32[]{:S(2)}) copy-start(bf16[4,4,96,768]{3,2,1,0:T(8,128)(2,1)} %copy-done.4) | copy-start | bytes 7077892
  552.4 76.0 %collective-permute-start.20 = (bf16[1,4,96,768]{3,2,1,0:T(8,128)(2,1)S(1)}, bf16[1,4,96,768]{3,2,1,0:T(8,128)(2,1)S(1)}, u32[]{:S(2)}, u32[]{:S(2)}) collective-permute-start(bf16[1,4,96,768]{3,2,1,0:T(8,128)(2,1)S(1)} %constant_dynamic-slice_fusion), channel_id=1, source_target_pairs={{0,16},{4,20},{8,24},{12,28},{16,0},{20,4},{24,8},{28,12},{1,17},{... | collective-permute-start | bytes 1769480 | tf_op jit(solution)/shard_map/ppermute | solution.py:570
  577.7 54.2 %collective-permute-start.14 = (bf16[1,4,96,768]{3,2,1,0:T(8,128)(2,1)S(1)}, bf16[1,4,96,768]{3,2,1,0:T(8,128)(2,1)S(1)}, u32[]{:S(2)}, u32[]{:S(2)}) collective-permute-start(bf16[1,4,96,768]{3,2,1,0:T(8,128)(2,1)S(1)} %constant_dynamic-slice_fusion.1), channel_id=1, source_target_pairs={{0,16},{4,20},{8,24},{12,28},{16,0},{20,4},{24,8},{28,12},{1,17},{... | collective-permute-start | bytes 1769480 | tf_op jit(solution)/shard_map/ppermute | solution.py:570
  603.0 28.6 %collective-permute-start.8 = (bf16[1,4,96,768]{3,2,1,0:T(8,128)(2,1)S(1)}, bf16[1,4,96,768]{3,2,1,0:T(8,128)(2,1)S(1)}, u32[]{:S(2)}, u32[]{:S(2)}) collective-permute-start(bf16[1,4,96,768]{3,2,1,0:T(8,128)(2,1)S(1)} %constant_dynamic-slice_fusion.2), channel_id=1, source_target_pairs={{0,16},{4,20},{8,24},{12,28},{16,0},{20,4},{24,8},{28,12},{1,17},{... | collective-permute-start | bytes 1769480 | tf_op jit(solution)/shard_map/ppermute | solution.py:570
  626.6 13.8 %collective-permute-start.2 = (bf16[1,4,96,768]{3,2,1,0:T(8,128)(2,1)S(1)}, bf16[1,4,96,768]{3,2,1,0:T(8,128)(2,1)S(1)}, u32[]{:S(2)}, u32[]{:S(2)}) collective-permute-start(bf16[1,4,96,768]{3,2,1,0:T(8,128)(2,1)S(1)} %constant_dynamic-slice_fusion.3), channel_id=1, source_target_pairs={{0,16},{4,20},{8,24},{12,28},{16,0},{20,4},{24,8},{28,12},{1,17},{... | collective-permute-start | bytes 1769480 | tf_op jit(solution)/shard_map/ppermute | solution.py:570
  628.6 43.1 %collective-permute-start.21 = (bf16[96,768]{1,0:T(8,128)(2,1)S(1)}, bf16[96,768]{1,0:T(8,128)(2,1)S(1)}, u32[]{:S(2)}, u32[]{:S(2)}) collective-permute-start(bf16[96,768]{1,0:T(8,128)(2,1)S(1)} %get-tuple-element.159), channel_id=1, source_target_pairs={{0,1},{1,2},{2,3},{3,0},{4,5},{5,6},{6,7},{7,4},{8,9},{9,10},{10,1... | collective-permute-start | bytes 442376 | tf_op jit(solution)/shard_map/ppermute | solution.py:578
  628.7 43.1 %collective-permute-start.22 = (bf16[96,768]{1,0:T(8,128)(2,1)S(1)}, bf16[96,768]{1,0:T(8,128)(2,1)S(1)}, u32[]{:S(2)}, u32[]{:S(2)}) collective-permute-start(bf16[96,768]{1,0:T(8,128)(2,1)S(1)} %get-tuple-element.161), channel_id=1, source_target_pairs={{0,2},{1,3},{2,0},{3,1},{4,6},{5,7},{6,4},{7,5},{8,10},{9,11},{10,... | collective-permute-start | bytes 442376 | tf_op jit(solution)/shard_map/ppermute | solution.py:578
  631.7 18.2 %collective-permute-start.10 = (bf16[96,768]{1,0:T(8,128)(2,1)S(1)}, bf16[96,768]{1,0:T(8,128)(2,1)S(1)}, u32[]{:S(2)}, u32[]{:S(2)}) collective-permute-start(bf16[96,768]{1,0:T(8,128)(2,1)S(1)} %get-tuple-element.167), channel_id=1, source_target_pairs={{0,2},{1,3},{2,0},{3,1},{4,6},{5,7},{6,4},{7,5},{8,10},{9,11},{10,... | collective-permute-start | bytes 442376 | tf_op jit(solution)/shard_map/ppermute | solution.py:578
  631.9 18.1 %collective-permute-start.11 = (bf16[96,768]{1,0:T(8,128)(2,1)S(1)}, bf16[96,768]{1,0:T(8,128)(2,1)S(1)}, u32[]{:S(2)}, u32[]{:S(2)}) collective-permute-start(bf16[96,768]{1,0:T(8,128)(2,1)S(1)} %get-tuple-element.166), channel_id=1, source_target_pairs={{0,3},{1,0},{2,1},{3,2},{4,7},{5,4},{6,5},{7,6},{8,11},{9,8},{10,9... | collective-permute-start | bytes 442376 | tf_op jit(solution)/shard_map/ppermute | solution.py:578
  640.3 12.8 %collective-permute-start.9 = (bf16[96,768]{1,0:T(8,128)(2,1)S(1)}, bf16[96,768]{1,0:T(8,128)(2,1)S(1)}, u32[]{:S(2)}, u32[]{:S(2)}) collective-permute-start(bf16[96,768]{1,0:T(8,128)(2,1)S(1)} %get-tuple-element.165), channel_id=1, source_target_pairs={{0,1},{1,2},{2,3},{3,0},{4,5},{5,6},{6,7},{7,4},{8,9},{9,10},{10,1... | collective-permute-start | bytes 442376 | tf_op jit(solution)/shard_map/ppermute | solution.py:578
  650.0 8.6 %collective-permute-start.3 = (bf16[96,768]{1,0:T(8,128)(2,1)S(1)}, bf16[96,768]{1,0:T(8,128)(2,1)S(1)}, u32[]{:S(2)}, u32[]{:S(2)}) collective-permute-start(bf16[96,768]{1,0:T(8,128)(2,1)S(1)} %get-tuple-element.168), channel_id=1, source_target_pairs={{0,1},{1,2},{2,3},{3,0},{4,5},{5,6},{6,7},{7,4},{8,9},{9,10},{10,1... | collective-permute-start | bytes 442376 | tf_op jit(solution)/shard_map/ppermute | solution.py:578
  650.0 12.5 %collective-permute-start.4 = (bf16[96,768]{1,0:T(8,128)(2,1)S(1)}, bf16[96,768]{1,0:T(8,128)(2,1)S(1)}, u32[]{:S(2)}, u32[]{:S(2)}) collective-permute-start(bf16[96,768]{1,0:T(8,128)(2,1)S(1)} %get-tuple-element.170), channel_id=1, source_target_pairs={{0,2},{1,3},{2,0},{3,1},{4,6},{5,7},{6,4},{7,5},{8,10},{9,11},{10,... | collective-permute-start | bytes 442376 | tf_op jit(solution)/shard_map/ppermute | solution.py:578
  653.1 15.1 %collective-permute-start.5 = (bf16[96,768]{1,0:T(8,128)(2,1)S(1)}, bf16[96,768]{1,0:T(8,128)(2,1)S(1)}, u32[]{:S(2)}, u32[]{:S(2)}) collective-permute-start(bf16[96,768]{1,0:T(8,128)(2,1)S(1)} %get-tuple-element.169), channel_id=1, source_target_pairs={{0,3},{1,0},{2,1},{3,2},{4,7},{5,4},{6,5},{7,6},{8,11},{9,8},{10,9... | collective-permute-start | bytes 442376 | tf_op jit(solution)/shard_map/ppermute | solution.py:578
  658.6 13.3 %collective-permute-start.23 = (bf16[96,768]{1,0:T(8,128)(2,1)S(1)}, bf16[96,768]{1,0:T(8,128)(2,1)S(1)}, u32[]{:S(2)}, u32[]{:S(2)}) collective-permute-start(bf16[96,768]{1,0:T(8,128)(2,1)S(1)} %get-tuple-element.160), channel_id=1, source_target_pairs={{0,3},{1,0},{2,1},{3,2},{4,7},{5,4},{6,5},{7,6},{8,11},{9,8},{10,9... | collective-permute-start | bytes 442376 | tf_op jit(solution)/shard_map/ppermute | solution.py:578
  662.5 14.2 %collective-permute-start.15 = (bf16[96,768]{1,0:T(8,128)(2,1)S(1)}, bf16[96,768]{1,0:T(8,128)(2,1)S(1)}, u32[]{:S(2)}, u32[]{:S(2)}) collective-permute-start(bf16[96,768]{1,0:T(8,128)(2,1)S(1)} %get-tuple-element.162), channel_id=1, source_target_pairs={{0,1},{1,2},{2,3},{3,0},{4,5},{5,6},{6,7},{7,4},{8,9},{9,10},{10,1... | collective-permute-start | bytes 442376 | tf_op jit(solution)/shard_map/ppermute | solution.py:578
  668.2 13.3 %collective-permute-start.16 = (bf16[96,768]{1,0:T(8,128)(2,1)S(1)}, bf16[96,768]{1,0:T(8,128)(2,1)S(1)}, u32[]{:S(2)}, u32[]{:S(2)}) collective-permute-start(bf16[96,768]{1,0:T(8,128)(2,1)S(1)} %get-tuple-element.164), channel_id=1, source_target_pairs={{0,2},{1,3},{2,0},{3,1},{4,6},{5,7},{6,4},{7,5},{8,10},{9,11},{10,... | collective-permute-start | bytes 442376 | tf_op jit(solution)/shard_map/ppermute | solution.py:578
  671.7 9.7 %collective-permute-start.17 = (bf16[96,768]{1,0:T(8,128)(2,1)S(1)}, bf16[96,768]{1,0:T(8,128)(2,1)S(1)}, u32[]{:S(2)}, u32[]{:S(2)}) collective-permute-start(bf16[96,768]{1,0:T(8,128)(2,1)S(1)} %get-tuple-element.163), channel_id=1, source_target_pairs={{0,3},{1,0},{2,1},{3,2},{4,7},{5,4},{6,5},{7,6},{8,11},{9,8},{10,9... | collective-permute-start | bytes 442376 | tf_op jit(solution)/shard_map/ppermute | solution.py:578
Sparse Core Ops, SparseCore 0:
  13.7 94.5 all-gather.8
  111.7 62.2 all-gather.10
  176.8 61.8 all-gather.12
  241.4 61.8 all-gather.14

commit v2 on v1

v2 whole, which is shorter than its diff:
```python
import functools

import jax
import jax.numpy as jnp
from jax import lax
from jax.experimental import pallas as pl
from jax.experimental.pallas import tpu as pltpu
from jax.sharding import PartitionSpec as P

HD = 64
EPSILON = 1e-05
NEGATIVE = -1e30
VMEM_LIMIT = 60 * 2**20
BF = jnp.bfloat16
F32 = jnp.float32


def dot(left, right, left_dim=1, right_dim=0):
    return lax.dot_general(
        left, right, (((left_dim,), (right_dim,)), ((), ())), preferred_element_type=F32
    )


def layer_norm_parts(rows):
    center = rows - jnp.mean(rows, -1, keepdims=True)
    inverse = lax.rsqrt(jnp.mean(center * center, -1, keepdims=True) + EPSILON)
    return center * inverse, inverse


def norm_back(grad_rows, unit, inverse, gain):
    scaled = grad_rows * gain
    return inverse * (
        scaled
        - jnp.mean(scaled, -1, keepdims=True)
        - unit * jnp.mean(scaled * unit, -1, keepdims=True)
    )


def put_heads(sum_ref, row, block, count, value):
    size = value.shape[1]
    for t in range(count):

        @pl.when(block == t)
        def _():
            sum_ref[row : row + 1, t * size : (t + 1) * size] = value


def column_sum(rows):
    return jnp.sum(rows, 0, keepdims=True)


def whole(shape):
    zeros = (0,) * len(shape)
    return pl.BlockSpec(shape, lambda t, *_: zeros)


def per_block(shape):
    rest = (0,) * (len(shape) - 1)
    return pl.BlockSpec((1,) + tuple(shape[1:]), lambda t, *_: (t,) + rest)


def packed(shape):
    return pl.BlockSpec((shape[0], 1) + tuple(shape[2:]), lambda t, *_: (0, t, 0, 0))


def sds(shape, dtype):
    return jax.ShapeDtypeStruct(tuple(shape), dtype)


def call(body, name, grid, ins, outs, scratch, flops, scalars=(), deps=(), carried=()):
    moved = sum(a.size * a.dtype.itemsize for a, _ in ins)
    moved += sum(o.size * o.dtype.itemsize for o, _ in outs)
    first = len(scalars) + len(ins)
    extra = list(carried) + list(deps)

    def inner(*refs):
        return body(*refs[:first], *refs[first + len(extra) :])

    return pl.pallas_call(
        inner,
        out_shape=[o for o, _ in outs],
        grid_spec=pltpu.PrefetchScalarGridSpec(
            num_scalar_prefetch=len(scalars),
            grid=(grid,),
            in_specs=[s for _, s in ins] + [pl.BlockSpec(memory_space=pl.ANY)] * len(extra),
            out_specs=[s for _, s in outs],
            scratch_shapes=scratch,
        ),
        compiler_params=pltpu.CompilerParams(
            dimension_semantics=("arbitrary",), vmem_limit_bytes=VMEM_LIMIT
        ),
        input_output_aliases={first + i: i for i in range(len(carried))},
        cost_estimate=pl.CostEstimate(flops=flops, bytes_accessed=moved, transcendentals=0),
        name=name,
    )(*scalars, *[a for a, _ in ins], *extra)


def head_lanes(rows, head, block):
    lane = lax.broadcasted_iota(jnp.int32, rows.shape, 1)
    return jnp.where((lane >= head * block) & (lane < (head + 1) * block), rows, jnp.zeros_like(rows))


def pack_in(pack):
    return [(array, packed(array.shape)) for array in pack]


def at_block(shape, start):
    rest = (0,) * (len(shape) - 1)
    return pl.BlockSpec((1,) + tuple(shape[1:]), lambda t, *_: (start + t,) + rest)


def pack_at(pack, start):
    return [
        (a, pl.BlockSpec((a.shape[0], 1) + a.shape[2:], lambda t, *_: (0, start + t, 0, 0))) for a in pack
    ]


def pack_scratch(width):
    return pltpu.VMEM((width, width), BF)


def assemble(refs, rows, place_ref, scr):
    if len(refs) == 1:
        parts = refs[0][:, 0, :rows, :]
        scr[...] = parts.reshape(parts.shape[0] * rows, parts.shape[2])
        return
    count = 2 * refs[0].shape[0]
    for f in range(count):
        distance = f ^ place_ref[0]
        source = distance >> 1
        for bit in range(2):

            @pl.when((distance & 1) == bit)
            def _():
                scr[f * rows : (f + 1) * rows] = refs[bit][source, 0, :rows, :]


def grad_outs(shape):
    return [(sds(shape, BF), packed(shape))] * (1 if shape[0] == 1 else 2)


def store_pack(refs, value, place_ref):
    rows = refs[0].shape[2]
    if len(refs) == 1:
        refs[0][0, 0] = value
        return
    for f in range(2 * refs[0].shape[0]):
        distance = f ^ place_ref[0]
        target = distance >> 1
        for bit in range(2):

            @pl.when((distance & 1) == bit)
            def _():
                refs[bit][target, 0] = value[f * rows : (f + 1) * rows]


def tail_start(hw):
    return (3 * hw) // 128 * 128


def project_out(mixed, w_scr, hw):
    start = tail_start(hw)
    extra = 3 * hw - start
    if extra:
        mixed = jnp.concatenate([jnp.zeros((mixed.shape[0], extra), mixed.dtype), mixed], 1)
    return dot(mixed, w_scr[:, start:], 1, 1)


def project_back(branch, w_scr, hw):
    start = tail_start(hw)
    return dot(branch, w_scr[:, start:])[:, 3 * hw - start :]


def self_forward(length, place, start, count, rows, part, pack, own, params, head_bias, dims, deps=(), carried=()):
    seq, width, blocks, hw = dims
    heads = hw // HD

    def body(len_ref, place_ref, x_ref, part_ref, *refs):
        w_refs, refs = refs[: len(pack)], refs[len(pack) :]
        (prm_ref, hb_ref, q_ref, k_ref, v_ref, lse_ref, ot_ref, mix_ref, n1_ref, first_ref, n2_ref,
         bias_scr, acc_scr, w_scr) = refs
        t = pl.program_id(0)
        assemble(w_refs, own, place_ref, w_scr)

        @pl.when(t == 0)
        def _():
            unit, _ = layer_norm_parts(x_ref[...].astype(F32))
            n1_ref[...] = (unit * prm_ref[0:1] + prm_ref[4:5]).astype(BF)
            key = lax.broadcasted_iota(jnp.int32, (seq, seq), 0)
            query = lax.broadcasted_iota(jnp.int32, (seq, seq), 1)
            bias_scr[...] = jnp.where((key <= query) & (key < len_ref[0]), 0.0, NEGATIVE)
            acc_scr[...] = part_ref[...].astype(F32) + prm_ref[10:11] if start == 0 else part_ref[...]

        qkv = dot(n1_ref[...], w_scr[:, : 3 * hw])
        q = ((qkv[:, :hw] + hb_ref[0, 0:1]) * HD**-0.5).astype(BF)
        k = qkv[:, hw : 2 * hw].astype(BF)
        v = (qkv[:, 2 * hw :] + hb_ref[0, 1:2]).astype(BF)
        q_ref[0] = q
        k_ref[0] = k
        v_ref[0] = v
        vt = v.T
        for j in range(heads):
            s = dot(k, head_lanes(q, j, HD), 1, 1) + bias_scr[...]
            m = jnp.max(s, 0, keepdims=True)
            p = jnp.exp(s - m)
            total = jnp.sum(p, 0, keepdims=True)
            lse_ref[0, j : j + 1] = m + jnp.log(total)
            ot_ref[0, j * HD : (j + 1) * HD] = dot(vt[j * HD : (j + 1) * HD], p.astype(BF)) / total
        mixed = ot_ref[0].T.astype(BF)
        mix_ref[0] = mixed
        acc_scr[...] += project_out(mixed, w_scr, hw)

        @pl.when(t == count - 1)
        def _():
            first = acc_scr[...]
            first_ref[...] = first
            unit, _ = layer_norm_parts(first)
            n2_ref[...] = (unit * prm_ref[1:2] + prm_ref[5:6]).astype(BF)

    full = whole((seq, width))
    hb = sds((blocks, seq, hw), BF)

    def block(shape):
        return at_block(shape, start)

    return call(
        body, "self_forward", count,
        [(rows, full), (part, full), *pack_at(pack, start), (params, whole(params.shape)),
         (head_bias, block(head_bias.shape))],
        [(hb, block(hb.shape))] * 3
        + [(sds((blocks, 8, seq), F32), block((blocks, 8, seq))),
           (sds((blocks, hw, seq), F32), block((blocks, hw, seq))),
           (hb, block(hb.shape)),
           (sds((seq, width), BF), full),
           (sds((seq, width), F32), full),
           (sds((seq, width), BF), full)],
        [pltpu.VMEM((seq, seq), F32), pltpu.VMEM((seq, width), F32), pack_scratch(width)],
        count * (8 * seq * width * hw + 16 * seq * seq * hw),
        (length, place),
        deps,
        carried,
    )


def frame_keys(place, frames, pack, own, head_bias, dims, deps=()):
    seq, width, blocks, hw = dims
    pieces, piece, _ = frames.shape
    total = pieces * piece

    def body(place_ref, e_ref, *refs):
        w_refs, refs = refs[: len(pack)], refs[len(pack) :]
        hb_ref, k_ref, v_ref, kt_ref, vt_ref, w_scr = refs
        assemble(w_refs, own, place_ref, w_scr)
        w = w_scr[:, : 2 * hw]
        for c in range(pieces):
            kv = dot(e_ref[c], w)
            k = kv[:, :hw].astype(BF)
            v = (kv[:, hw:] + hb_ref[0, 3:4]).astype(BF)
            k_ref[0, c] = k
            v_ref[0, c] = v
            kt_ref[0, :, c * piece : (c + 1) * piece] = k.T
            vt_ref[0, :, c * piece : (c + 1) * piece] = v.T

    kv = sds((blocks, pieces, piece, hw), BF)
    kvt = sds((blocks, hw, total), BF)
    return call(
        body, "frame_keys", blocks,
        [(frames, whole(frames.shape)), *pack_in(pack), (head_bias, per_block(head_bias.shape))],
        [(kv, per_block(kv.shape))] * 2 + [(kvt, per_block(kvt.shape))] * 2,
        [pack_scratch(width)],
        4 * total * width * width,
        (place,),
        deps,
    )


def cross_forward(place, start, count, n2, first, pack, own, params, head_bias, keys, values_t, valid, dims, deps=(),
                  carried=()):
    seq, width, blocks, hw = dims
    heads = hw // HD
    _, pieces, piece, _ = keys.shape
    total_keys = pieces * piece

    def body(place_ref, n2_ref, first_ref, *refs):
        w_refs, refs = refs[: len(pack)], refs[len(pack) :]
        (prm_ref, hb_ref, k_ref, vt_ref, q_ref, lse_ref, ot_ref, mix_ref, second_ref, n3_ref, s_scr,
         p_scr, acc_scr, w_scr) = refs
        t = pl.program_id(0)
        assemble(w_refs, own, place_ref, w_scr)

        @pl.when(t == 0)
        def _():
            acc_scr[...] = first_ref[...] + prm_ref[13:14] if start == 0 else first_ref[...]

        q = ((dot(n2_ref[...], w_scr[:, 2 * hw : 3 * hw]) + hb_ref[0, 2:3]) * HD**-0.5).astype(BF)
        q_ref[0] = q
        row = lax.broadcasted_iota(jnp.int32, (piece, 1), 0)
        pad = jnp.where(row < valid, 0.0, NEGATIVE)

        for j in range(heads):
            qm = head_lanes(q, j, HD)

            def score(c, m):
                s = dot(k_ref[0, c], qm, 1, 1) + pad
                s_scr[c] = s
                return jnp.maximum(m, jnp.max(s, 0, keepdims=True))

            m = lax.fori_loop(0, pieces, score, jnp.full((1, seq), NEGATIVE, F32))

            def weigh(c, total):
                p = jnp.exp(s_scr[c] - m)
                p_scr[pl.ds(pl.multiple_of(c * piece, piece), piece)] = p.astype(BF)
                return total + jnp.sum(p, 0, keepdims=True)

            total = lax.fori_loop(0, pieces, weigh, jnp.zeros((1, seq), F32))
            lse_ref[0, j : j + 1] = m + jnp.log(total)
            at = j * HD
            ot_ref[0, at : at + HD] = dot(vt_ref[0, at : at + HD], p_scr[...]) / total

        mixed = ot_ref[0].T.astype(BF)
        mix_ref[0] = mixed
        acc_scr[...] += project_out(mixed, w_scr, hw)

        @pl.when(t == count - 1)
        def _():
            second = acc_scr[...]
            second_ref[...] = second
            unit, _ = layer_norm_parts(second)
            n3_ref[...] = (unit * prm_ref[2:3] + prm_ref[6:7]).astype(BF)

    full = whole((seq, width))
    hb = sds((blocks, seq, hw), BF)

    def block(shape):
        return at_block(shape, start)

    packs = pack_at(pack, start)
    return call(
        body, "cross_forward", count,
        [(n2, full), (first, full), *packs, (params, whole(params.shape)), (head_bias, block(head_bias.shape)),
         (keys, block(keys.shape)), (values_t, block(values_t.shape))],
        [(hb, block(hb.shape)), (sds((blocks, 8, seq), F32), block((blocks, 8, seq))),
         (sds((blocks, hw, seq), F32), block((blocks, hw, seq))), (hb, block(hb.shape)),
         (sds((seq, width), F32), full), (sds((seq, width), BF), full)],
        [pltpu.VMEM((pieces, piece, seq), F32), pltpu.VMEM((total_keys, seq), BF),
         pltpu.VMEM((seq, width), F32), pack_scratch(width)],
        count * (4 * seq * width * hw + 4 * seq * total_keys * 256 * heads),
        (place,),
        deps,
        carried,
    )


def feed_forward(place, n3, second, w_in, w_out, own, params, cotangent, dims, deps=()):
    seq, width, blocks, hw = dims

    def body(place_ref, n3_ref, second_ref, *refs):
        wi_refs, wo_refs, refs = refs[: len(w_in)], refs[len(w_in) : 2 * len(w_in)], refs[2 * len(w_in) :]
        (prm_ref, cot_ref, hid_ref, slope_ref, out_ref, g3_ref, b3_ref, sum_ref, wi_scr, wo_scr,
         acc_scr) = refs
        t = pl.program_id(0)
        assemble(wi_refs, own, place_ref, wi_scr)
        assemble(wo_refs, own, place_ref, wo_scr)

        @pl.when(t == 0)
        def _():
            acc_scr[...] = second_ref[...] + prm_ref[14:15]

        before = dot(n3_ref[...], wi_scr[...]) + prm_ref[pl.ds(15 + t, 1)]
        phi = 0.5 + 0.5 * lax.erf(before * 2**-0.5)
        hidden = (before * phi).astype(BF)
        hid_ref[0] = hidden
        slope_ref[0] = phi + before * (jnp.exp(-0.5 * before * before) * 0.3989422804014327)
        acc_scr[...] += dot(hidden, wo_scr[...], 1, 1)

        @pl.when(t == blocks - 1)
        def _():
            unit, inverse = layer_norm_parts(acc_scr[...])
            out_ref[...] = (unit * prm_ref[3:4] + prm_ref[7:8]).astype(BF)
            cot = cot_ref[...].astype(F32)
            grad = norm_back(cot, unit, inverse, prm_ref[3:4])
            g3_ref[...] = grad
            branch = grad.astype(BF)
            b3_ref[...] = branch
            sum_ref[...] = jnp.zeros_like(sum_ref)
            sum_ref[3:4] = column_sum(cot * unit)
            sum_ref[7:8] = column_sum(cot)
            sum_ref[14:15] = column_sum(branch.astype(F32))

    full = whole((seq, width))
    wide = (blocks, seq, width)
    return call(
        body, "feed_forward", blocks,
        [(n3, full), (second, full), *pack_in(w_in), *pack_in(w_out),
         (params, whole(params.shape)), (cotangent, full)],
        [(sds(wide, BF), per_block(wide)), (sds(wide, F32), per_block(wide)),
         (sds((seq, width), BF), full), (sds((seq, width), F32), full),
         (sds((seq, width), BF), full), (sds(params.shape, F32), whole(params.shape))],
        [pack_scratch(width), pack_scratch(width), pltpu.VMEM((seq, width), F32)],
        16 * seq * width * width,
        (place,),
        deps,
    )


def feed_out_grads(place, b3, hidden, grad_shape, dims, deps=()):
    seq, width, blocks, hw = dims

    def body(place_ref, b3_ref, hid_ref, *refs):
        grad_refs, (b3t_scr,) = refs[:-1], refs[-1:]

        @pl.when(pl.program_id(0) == 0)
        def _():
            b3t_scr[...] = b3_ref[...].T

        store_pack(grad_refs, dot(b3t_scr[...], hid_ref[0]).astype(BF), place_ref)

    wide = (blocks, seq, width)
    return call(
        body, "feed_out_grads", blocks,
        [(b3, whole((seq, width))), (hidden, per_block(wide))],
        grad_outs(grad_shape),
        [pltpu.VMEM((width, seq), BF)],
        8 * seq * width * width,
        (place,),
        deps,
    )


def feed_backward(place, b3, g3, slope, w_in, w_out, own, n3, second, params, sums, grad_shape, dims, deps=()):
    seq, width, blocks, hw = dims
    grads = grad_outs(grad_shape)

    def body(place_ref, b3_ref, g3_ref, slope_ref, *refs):
        wi_refs, wo_refs, refs = refs[: len(w_in)], refs[len(w_in) : 2 * len(w_in)], refs[2 * len(w_in) :]
        (n3_ref, second_ref, prm_ref, old_ref), refs = refs[:4], refs[4:]
        grad_refs, refs = refs[: len(grads)], refs[len(grads) :]
        g2_ref, b2_ref, sum_ref, wi_scr, wo_scr, n3t_scr, acc_scr = refs
        t = pl.program_id(0)
        assemble(wi_refs, own, place_ref, wi_scr)
        assemble(wo_refs, own, place_ref, wo_scr)

        @pl.when(t == 0)
        def _():
            sum_ref[...] = old_ref[...]
            n3t_scr[...] = n3_ref[...].T
            acc_scr[...] = jnp.zeros_like(acc_scr)

        grad_before = (dot(b3_ref[...], wo_scr[...]) * slope_ref[0]).astype(BF)
        sum_ref[pl.ds(15 + t, 1)] = column_sum(grad_before.astype(F32))
        store_pack(grad_refs, dot(n3t_scr[...], grad_before).astype(BF), place_ref)
        acc_scr[...] += dot(grad_before, wi_scr[...], 1, 1)

        @pl.when(t == blocks - 1)
        def _():
            grad = acc_scr[...]
            unit, inverse = layer_norm_parts(second_ref[...])
            sum_ref[2:3] = column_sum(grad * unit)
            sum_ref[6:7] = column_sum(grad)
            grad_second = g3_ref[...] + norm_back(grad, unit, inverse, prm_ref[2:3])
            g2_ref[...] = grad_second
            branch = grad_second.astype(BF)
            b2_ref[...] = branch
            sum_ref[13:14] = column_sum(branch.astype(F32))

    full = whole((seq, width))
    wide = (blocks, seq, width)
    return call(
        body, "feed_backward", blocks,
        [(b3, full), (g3, full), (slope, per_block(wide)), *pack_in(w_in), *pack_in(w_out), (n3, full),
         (second, full), (params, whole(params.shape)), (sums, whole(sums.shape))],
        grads
        + [(sds((seq, width), F32), full), (sds((seq, width), BF), full),
           (sds(sums.shape, F32), whole(sums.shape))],
        [pack_scratch(width), pack_scratch(width), pltpu.VMEM((width, seq), BF), pltpu.VMEM((seq, width), F32)],
        24 * seq * width * width,
        (place,),
        deps,
    )


def cross_attend_back(place, start, count, sums, b2, queries, keys, values, keys_t, lse, ot, pack, own, valid,
                      dims, deps=(), carried=()):
    seq, width, blocks, hw = dims
    heads = hw // HD
    _, pieces, piece, _ = keys.shape
    total_keys = pieces * piece

    def body(place_ref, old_ref, b2_ref, q_ref, k_ref, v_ref, kt_ref, lse_ref, ot_ref, *refs):
        w_refs, refs = refs[: len(pack)], refs[len(pack) :]
        dq_ref, dkv_ref, sum_ref, w_scr, dk_scr, dv_scr, ds_scr, dqt_scr = refs
        t = pl.program_id(0)
        assemble(w_refs, own, place_ref, w_scr)

        @pl.when(t == 0)
        def _():
            sum_ref[...] = old_ref[...]

        q = q_ref[0]
        gm = project_back(b2_ref[...], w_scr, hw).astype(BF)
        weighted = gm.astype(F32).T * ot_ref[0]
        row = lax.broadcasted_iota(jnp.int32, (piece, 1), 0)
        pad = jnp.where(row < valid, 0.0, NEGATIVE)
        dk_scr[...] = jnp.zeros_like(dk_scr)
        dv_scr[...] = jnp.zeros_like(dv_scr)
        for j in range(heads):
            delta = jnp.sum(weighted[j * HD : (j + 1) * HD], 0, keepdims=True)
            shift = lse_ref[0, j : j + 1]
            qm = head_lanes(q, j, HD)
            gj = head_lanes(gm, j, HD)

            def one_piece(c, carry):
                s = dot(k_ref[0, c], qm, 1, 1) + pad
                p = jnp.exp(s - shift)
                ds = (p * (dot(v_ref[0, c], gj, 1, 1) - delta)).astype(BF)
                dv_scr[c] += dot(p.astype(BF), gj)
                dk_scr[c] += dot(ds, qm)
                ds_scr[pl.ds(pl.multiple_of(c * piece, piece), piece)] = ds
                return carry

            lax.fori_loop(0, pieces, one_piece, 0)
            dqt_scr[j * HD : (j + 1) * HD] = dot(kt_ref[0, j * HD : (j + 1) * HD], ds_scr[...])
        dq = dqt_scr[...].T.astype(BF).astype(F32) * HD**-0.5
        put_heads(sum_ref, 11, start + t, blocks, column_sum(dq))
        dq_ref[0] = dq.astype(BF)
        bias = jnp.zeros((1, hw), F32)
        for c in range(pieces):
            dv = dv_scr[c].astype(BF)
            bias += column_sum(dv.astype(F32))
            dkv_ref[0, c] = jnp.concatenate([dk_scr[c].astype(BF), dv], 1)
        put_heads(sum_ref, 12, start + t, blocks, bias)

    def block(shape):
        return at_block(shape, start)

    packs = pack_at(pack, start)
    dkv = (blocks, pieces, piece, 2 * hw)
    return call(
        body, "cross_attend_back", count,
        [(sums, whole(sums.shape)), (b2, whole((seq, width))), (queries, block(queries.shape)), (keys, block(keys.shape)),
         (values, block(values.shape)), (keys_t, block(keys_t.shape)), (lse, block(lse.shape)),
         (ot, block(ot.shape)), *packs],
        [(sds(queries.shape, BF), block(queries.shape)), (sds(dkv, BF), block(dkv)),
         (sds(sums.shape, F32), whole(sums.shape))],
        [pack_scratch(width), pltpu.VMEM((pieces, piece, hw), F32), pltpu.VMEM((pieces, piece, hw), F32),
         pltpu.VMEM((total_keys, seq), BF), pltpu.VMEM((hw, seq), F32)],
        count * (2 * seq * width * hw + 10 * seq * total_keys * 256 * heads // 2),
        (place,),
        deps,
        carried,
    )


def cross_rows_back(place, sums, dq, dkv, g2, first, pack, own, params, valid, dims, deps=()):
    seq, width, blocks, hw = dims
    _, pieces, piece, _ = dkv.shape
    frames = (pieces, piece, width)
    kept = (pieces, valid, width)

    def body(place_ref, old_ref, dq_ref, dkv_ref, g2_ref, first_ref, *refs):
        w_refs, refs = refs[: len(pack)], refs[len(pack) :]
        prm_ref, genc_ref, g1_ref, b1_ref, sum_ref, w_scr, genc_scr, acc_scr = refs
        t = pl.program_id(0)
        assemble(w_refs, own, place_ref, w_scr)

        @pl.when(t == 0)
        def _():
            acc_scr[...] = jnp.zeros_like(acc_scr)
            genc_scr[...] = jnp.zeros_like(genc_scr)
            sum_ref[...] = old_ref[...]

        wkv = w_scr[:, : 2 * hw]
        for c in range(pieces):
            genc_scr[c] += dot(dkv_ref[0, c], wkv, 1, 1)
        acc_scr[...] += dot(dq_ref[0], w_scr[:, 2 * hw : 3 * hw], 1, 1)

        @pl.when(t == blocks - 1)
        def _():
            genc_ref[...] = genc_scr[:, :valid].astype(BF)
            grad = acc_scr[...]
            unit, inverse = layer_norm_parts(first_ref[...])
            sum_ref[1:2] = column_sum(grad * unit)
            sum_ref[5:6] = column_sum(grad)
            grad_first = g2_ref[...] + norm_back(grad, unit, inverse, prm_ref[1:2])
            g1_ref[...] = grad_first
            branch = grad_first.astype(BF)
            b1_ref[...] = branch
            sum_ref[10:11] = column_sum(branch.astype(F32))

    full = whole((seq, width))
    return call(
        body, "cross_rows_back", blocks,
        [(sums, whole(sums.shape)), (dq, per_block(dq.shape)), (dkv, per_block(dkv.shape)), (g2, full), (first, full), *pack_in(pack),
         (params, whole(params.shape))],
        [(sds(kept, BF), whole(kept)), (sds((seq, width), F32), full), (sds((seq, width), BF), full),
         (sds(sums.shape, F32), whole(sums.shape))],
        [pack_scratch(width), pltpu.VMEM(frames, F32), pltpu.VMEM((seq, width), F32)],
        2 * seq * width * width + 4 * pieces * piece * width * width,
        (place,),
        deps,
    )


def cross_grads(place, dq, dkv, mixed, b2, n2, frames, grad_shape, dims, deps=()):
    seq, width, blocks, hw = dims
    _, pieces, piece, _ = dkv.shape
    total_keys = pieces * piece

    def body(place_ref, dq_ref, dkv_ref, mix_ref, b2_ref, n2_ref, e_ref, *refs):
        grad_refs, (et_scr, b2t_scr, n2t_scr) = refs[:-3], refs[-3:]

        @pl.when(pl.program_id(0) == 0)
        def _():
            for c in range(pieces):
                et_scr[:, c * piece : (c + 1) * piece] = e_ref[c].T
            b2t_scr[...] = b2_ref[...].T
            n2t_scr[...] = n2_ref[...].T

        grad_kv = dot(et_scr[...], dkv_ref[0].reshape(total_keys, 2 * hw))
        grad_q = dot(n2t_scr[...], dq_ref[0])
        grad_o = dot(b2t_scr[...], mix_ref[0])
        store_pack(grad_refs, jnp.concatenate([grad_kv, grad_q, grad_o], 1).astype(BF), place_ref)

    full = whole((seq, width))
    return call(
        body, "cross_grads", blocks,
        [(dq, per_block(dq.shape)), (dkv, per_block(dkv.shape)), (mixed, per_block(mixed.shape)), (b2, full),
         (n2, full), (frames, whole(frames.shape))],
        grad_outs(grad_shape),
        [pltpu.VMEM((width, total_keys), BF), pltpu.VMEM((width, seq), BF), pltpu.VMEM((width, seq), BF)],
        4 * seq * width * width + 4 * total_keys * width * width,
        (place,),
        deps,
    )


def self_attend_back(length, place, sums, b1, queries, keys, values, lse, ot, pack, own, dims, deps=()):
    seq, width, blocks, hw = dims
    heads = hw // HD

    def body(len_ref, place_ref, old_ref, b1_ref, q_ref, k_ref, v_ref, lse_ref, ot_ref, *refs):
        w_refs, refs = refs[: len(pack)], refs[len(pack) :]
        dqkv_ref, sum_ref, w_scr, bias_scr, dqt_scr = refs
        t = pl.program_id(0)
        assemble(w_refs, own, place_ref, w_scr)

        @pl.when(t == 0)
        def _():
            sum_ref[...] = old_ref[...]
            key = lax.broadcasted_iota(jnp.int32, (seq, seq), 0)
            query = lax.broadcasted_iota(jnp.int32, (seq, seq), 1)
            bias_scr[...] = jnp.where((key <= query) & (key < len_ref[0]), 0.0, NEGATIVE)

        q = q_ref[0]
        k = k_ref[0]
        v = v_ref[0]
        kt = k.T
        gm = project_back(b1_ref[...], w_scr, hw).astype(BF)
        weighted = gm.astype(F32).T * ot_ref[0]
        dk = jnp.zeros((seq, hw), F32)
        dv = jnp.zeros((seq, hw), F32)
        for j in range(heads):
            delta = jnp.sum(weighted[j * HD : (j + 1) * HD], 0, keepdims=True)
            qm = head_lanes(q, j, HD)
            gj = head_lanes(gm, j, HD)
            p = jnp.exp(dot(k, qm, 1, 1) + bias_scr[...] - lse_ref[0, j : j + 1])
            ds = (p * (dot(v, gj, 1, 1) - delta)).astype(BF)
            dv += dot(p.astype(BF), gj)
            dk += dot(ds, qm)
            dqt_scr[j * HD : (j + 1) * HD] = dot(kt[j * HD : (j + 1) * HD], ds)
        dq = dqt_scr[...].T.astype(BF).astype(F32) * HD**-0.5
        dv = dv.astype(BF)
        put_heads(sum_ref, 8, t, blocks, column_sum(dq))
        put_heads(sum_ref, 9, t, blocks, column_sum(dv.astype(F32)))
        dqkv_ref[0] = jnp.concatenate([dq.astype(BF), dk.astype(BF), dv], 1)

    hb = per_block((blocks, seq, hw))
    dqkv = (blocks, seq, 3 * hw)
    return call(
        body, "self_attend_back", blocks,
        [(sums, whole(sums.shape)), (b1, whole((seq, width))), (queries, hb), (keys, hb), (values, hb), (lse, per_block(lse.shape)),
         (ot, per_block(ot.shape)), *pack_in(pack)],
        [(sds(dqkv, BF), per_block(dqkv)), (sds(sums.shape, F32), whole(sums.shape))],
        [pack_scratch(width), pltpu.VMEM((seq, seq), F32), pltpu.VMEM((hw, seq), F32)],
        2 * seq * width * width + 40 * seq * seq * width,
        (length, place),
        deps,
    )


def self_grads(place, dqkv, mixed, b1, n1, grad_shape, dims, deps=()):
    seq, width, blocks, hw = dims

    def body(place_ref, dqkv_ref, mix_ref, b1_ref, n1_ref, *refs):
        grad_refs, (b1t_scr, n1t_scr) = refs[:-2], refs[-2:]

        @pl.when(pl.program_id(0) == 0)
        def _():
            b1t_scr[...] = b1_ref[...].T
            n1t_scr[...] = n1_ref[...].T

        grad_qkv = dot(n1t_scr[...], dqkv_ref[0])
        grad_o = dot(b1t_scr[...], mix_ref[0])
        store_pack(grad_refs, jnp.concatenate([grad_qkv, grad_o], 1).astype(BF), place_ref)

    full = whole((seq, width))
    return call(
        body, "self_grads", blocks,
        [(dqkv, per_block(dqkv.shape)), (mixed, per_block(mixed.shape)), (b1, full), (n1, full)],
        grad_outs(grad_shape),
        [pltpu.VMEM((width, seq), BF), pltpu.VMEM((width, seq), BF)],
        8 * seq * width * width,
        (place,),
        deps,
    )


def self_rows_back(place, sums, dqkv, g1, rows, pack, own, params, dims, deps=()):
    seq, width, blocks, hw = dims

    def body(place_ref, old_ref, dqkv_ref, g1_ref, x_ref, *refs):
        w_refs, refs = refs[: len(pack)], refs[len(pack) :]
        prm_ref, gin_ref, sum_ref, w_scr, acc_scr = refs
        t = pl.program_id(0)
        assemble(w_refs, own, place_ref, w_scr)

        @pl.when(t == 0)
        def _():
            acc_scr[...] = jnp.zeros_like(acc_scr)
            sum_ref[...] = old_ref[...]

        acc_scr[...] += dot(dqkv_ref[0], w_scr[:, : 3 * hw], 1, 1)

        @pl.when(t == blocks - 1)
        def _():
            grad = acc_scr[...]
            unit, inverse = layer_norm_parts(x_ref[...].astype(F32))
            sum_ref[0:1] = column_sum(grad * unit)
            sum_ref[4:5] = column_sum(grad)
            gin_ref[...] = g1_ref[...] + norm_back(grad, unit, inverse, prm_ref[0:1])

    full = whole((seq, width))
    return call(
        body, "self_rows_back", blocks,
        [(sums, whole(sums.shape)), (dqkv, per_block(dqkv.shape)), (g1, full), (rows, full), *pack_in(pack), (params, whole(params.shape))],
        [(sds((seq, width), F32), full), (sds(sums.shape, F32), whole(sums.shape))],
        [pack_scratch(width), pltpu.VMEM((seq, width), F32)],
        6 * seq * width * width,
        (place,),
        deps,
    )


def pad_rows(rows, count):
    return jnp.pad(rows, ((0, count - rows.shape[0]),) + ((0, 0),) * (rows.ndim - 1))


def swap(array, step):
    count = lax.axis_size("fsdp")
    return lax.ppermute(array, "fsdp", [(i, i ^ step) for i in range(count)])


def around(array, hop):
    count = lax.axis_size("tp")
    return lax.ppermute(array, "tp", [(i, (i + hop) % count) for i in range(count)])


def native_gather(shard):
    whole_pack = lax.all_gather(shard, ("fsdp", "tp"), axis=0, tiled=False)
    return whole_pack.reshape((lax.axis_size("fsdp"), lax.axis_size("tp")) + shard.shape)


def in_order(pieces, here):
    count = len(pieces)
    stacked = jnp.stack(pieces)
    return jnp.stack(
        [lax.dynamic_index_in_dim(stacked, (here - t) % count, 0, keepdims=False) for t in range(count)]
    )


def gate(array, things):
    return lax.optimization_barrier((array,) + tuple(things))[0] if things else array


class Gather:
    def __init__(self, shard):
        self.shard = shard
        self.here = lax.axis_index("tp")

    def after(self, names, things):
        for name in names.split():
            setattr(self, name, gate(getattr(self, name), things))

    def direct(self):
        self.line = in_order([self.shard] + [around(self.shard, hop) for hop in range(1, 4)], self.here)
        return (self.line,)

    def pair(self):
        self.come = lax.ppermute(self.shard, "tp", [(i, i ^ 1) for i in range(4)])
        return (self.come,)

    def middle(self):
        odd = self.here % 2 == 1
        first, last = jnp.where(odd, self.come, self.shard), jnp.where(odd, self.shard, self.come)
        self.near = jnp.stack([first, last])
        self.inner = lax.ppermute(self.near, "tp", [(1, 2), (2, 1)])
        return (self.inner,)

    def ends(self):
        outer = lax.ppermute(self.inner, "tp", [(1, 0), (2, 3)])
        far = jnp.where((self.here == 1) | (self.here == 2), self.inner, outer)
        upper = self.here >= 2
        self.line = jnp.concatenate([jnp.where(upper, far, self.near), jnp.where(upper, self.near, far)])
        return (outer,)

    def first(self):
        self.low, self.high = self.line[None, :2], self.line[None, 2:]
        self.low_x, self.high_y = swap(self.low, 2), swap(self.high, 4)
        return self.low_x, self.high_y

    def second(self):
        low = jnp.concatenate([self.low, self.low_x])
        high = jnp.concatenate([self.high, self.high_y])
        low_y, high_x = swap(low, 4), swap(high, 2)
        low = jnp.concatenate([low, low_y])
        high = jnp.stack([high[0], high_x[0], high[1], high_x[1]])
        self.mine = jnp.concatenate([low, high], 1)
        return low_y, high_x

    def core(self):
        self.pack = (self.mine, swap(self.mine, 1))
        return self.pack


def wide(array):
    return array.astype(F32)


class Scatter:
    def __init__(self, halves):
        self.kept, self.sent = halves
        self.tp = self.kept.shape[1]
        self.half = self.tp // 2

    def core(self):
        self.come = swap(self.sent, 1)
        return self.come

    def first(self):
        def both(q, t):
            return (wide(self.kept[q, t]) + wide(self.come[q, t])).astype(BF)

        low, high = slice(0, self.half), slice(self.half, self.tp)
        self.low_y = swap(both(slice(2, 4), low), 4)
        self.high_x = swap(both(slice(1, 4, 2), high), 2)
        return self.low_y, self.high_x

    def second(self):
        low, high = slice(0, self.half), slice(self.half, self.tp)

        def three(q, t, more):
            return wide(self.kept[q, t]) + wide(self.come[q, t]) + wide(more)

        self.low_x = swap(three(1, low, self.low_y[1]).astype(BF), 2)
        self.high_y = swap(three(2, high, self.high_x[1]).astype(BF), 4)
        return self.low_x, self.high_y

    def line(self):
        def total(t, more, last):
            return wide(self.kept[0, t]) + wide(self.come[0, t]) + wide(more) + wide(last)

        low, high = slice(0, self.half), slice(self.half, self.tp)
        sums = jnp.concatenate(
            [total(low, self.low_y[0], self.low_x), total(high, self.high_x[0], self.high_y)]
        ).astype(BF)
        here = lax.axis_index("tp")
        self.own = lax.dynamic_index_in_dim(sums, here, 0, keepdims=False)
        self.parts = [
            around(lax.dynamic_index_in_dim(sums, (here + hop) % self.tp, 0, keepdims=False), hop)
            for hop in range(1, self.tp)
        ]
        return tuple(self.parts)

    def total(self):
        result = wide(self.own)
        for part in self.parts:
            result += wide(part)
        return result


def butterfly_scatter(grads, own, narrow=BF):
    fsdp, tp = lax.axis_size("fsdp"), lax.axis_size("tp")
    if grads.shape[0] != fsdp:
        blocks, width = grads.shape[1], grads.shape[3]
        grads = grads.reshape(blocks, fsdp, own, width).transpose(1, 0, 2, 3)
    place = lax.axis_index("fsdp")
    step = 1
    while step < fsdp:
        pairs = grads.reshape((grads.shape[0] // 2, 2) + grads.shape[1:])
        bit = (place // step) % 2
        kept = lax.dynamic_index_in_dim(pairs, bit, 1, keepdims=False)
        sent = lax.dynamic_index_in_dim(pairs, 1 - bit, 1, keepdims=False)
        grads = (wide(kept) + wide(swap(sent, step))).astype(narrow)
        step *= 2
    grads = grads[0]
    here = lax.axis_index("tp")
    total = wide(lax.dynamic_index_in_dim(grads, here, 0, keepdims=False))
    for hop in range(1, tp):
        sent = lax.dynamic_index_in_dim(grads, (here + hop) % tp, 0, keepdims=False)
        total += wide(around(sent, hop))
    return total


def local(
    inputs,
    encoder,
    lengths,
    self_qkv,
    self_out,
    cross_q,
    cross_kv,
    cross_out,
    fc_in,
    fc_out,
    norm_gain,
    norm_bias,
    proj_bias,
    fc_in_bias,
    cotangent,
):
    fsdp, tp = lax.axis_size("fsdp"), lax.axis_size("tp")
    devices = fsdp * tp
    tp_place = lax.axis_index("tp")
    place = lax.axis_index("fsdp").reshape(1)
    seqs, seq, width = inputs.shape
    assert seqs == 1
    own, hw = cross_q.shape
    dims = (seq, width, tp, hw)
    frames_own = encoder.shape[1]
    small_own = norm_gain.shape[1]
    ff_own = fc_in_bias.shape[0]
    chained = fsdp == 8 and tp == 4 and own % 16 == 0

    small = jnp.concatenate(
        [a.reshape(-1) for a in (norm_gain, norm_bias, proj_bias, fc_in_bias)]
    )
    small = jnp.pad(small, (0, width - small.size))
    high = small.astype(BF)
    low = (small - high.astype(F32)).astype(BF)
    extra = pad_rows(jnp.stack([high, low]), 16)

    pack_self = jnp.concatenate([self_qkv[0], self_qkv[1], self_qkv[2], self_out.T], 1)
    pack_self = jnp.concatenate([pack_self, extra], 0)
    pack_cross = jnp.concatenate([cross_kv[0], cross_kv[1], cross_q, cross_out.T], 1)
    x = inputs[0]
    length = lax.dynamic_slice_in_dim(lengths, tp_place, 1)
    chains = {}
    sends = {"direct": "shard", "pair": "shard", "middle": "come", "ends": "inner", "first": "line",
             "second": "low_x high_y", "core": "mine"}

    def move(after, *steps):
        if not chained:
            return ()
        out = ()
        for text in steps:
            name, step = text.split(".")
            if step != "core":
                chains[name].after(sends[step], after)
            else:
                chains[name].mine = gate(chains[name].mine, after)
            out += tuple(getattr(chains[name], step)())
        return out

    frames = encoder
    if chained:
        for name, shard in (("self", pack_self), ("cross", pack_cross), ("in", fc_in), ("out", fc_out.T)):
            chains[name] = Gather(shard)
        moved = move((), "self.direct")
        side = move((), "cross.pair")
        frames = gate(frames, moved)
        more = move(moved, "self.first")
        side = move(moved + side, "cross.middle")
        moved = move(more, "self.second")
        side = move(more + side, "cross.ends", "in.pair")
        more = move(moved, "self.core")
        moved = move(moved + side, "cross.first", "in.middle", "out.pair") + more[1:]
        w_self = chains["self"].pack
        own_rows = own
        grad_shape = (fsdp // 2, tp, own, width)
        blocks = jnp.stack([part[:, :, own : own + 2] for part in w_self], 1)
        blocks = blocks.reshape(fsdp, tp, 2, width)
        table = jnp.stack(
            [lax.dynamic_index_in_dim(blocks, f ^ place[0], 0, keepdims=False) for f in range(fsdp)]
        )
        table = wide(table).sum(2).reshape(devices, width)
    else:
        moved = ()
        more = ()
        w_self = native_gather(pack_self)
        table = wide(w_self[:, :, own : own + 2]).sum(2).reshape(devices, width)
        own_rows = own * fsdp
        grad_shape = (1, tp, own_rows, width)

        def end_to_end(pack):
            return pack[:, :, :own].transpose(1, 0, 2, 3).reshape(1, tp, own_rows, width)

        w_self = (end_to_end(w_self),)
        w_cross = (end_to_end(native_gather(pack_cross)),)
        w_in = (end_to_end(native_gather(fc_in)),)
        w_out = (end_to_end(native_gather(fc_out.T)),)

    rows = norm_gain.shape[0] + norm_bias.shape[0] + proj_bias.shape[0]
    params = table[:, : rows * small_own].reshape(devices, rows, small_own)
    params = params.transpose(1, 0, 2).reshape(rows, width)
    fc_bias = table[:, rows * small_own : rows * small_own + ff_own].reshape(tp, width)
    head_bias = jnp.stack([params[8], params[9], params[11], params[12]])
    head_bias = head_bias.reshape(4, tp, hw).transpose(1, 0, 2)
    head_bias = jnp.pad(head_bias, ((0, 0), (0, 4), (0, 0)))
    params = pad_rows(jnp.concatenate([params, fc_bias], 0), 24)

    piece = -(-frames_own // 128) * 128
    frames = lax.all_to_all(frames, "tp", 0, 0, tiled=True)
    frames = jnp.pad(frames, ((0, 0), (0, piece - frames_own), (0, 0)))
    half = tp // 2

    later = move(moved, "cross.second", "in.ends", "out.middle")
    shared = (w_self, own_rows, params, head_bias, dims)
    *kept, part, _ = self_forward(length, place, 0, half, x, x, *shared, moved)
    moved = move(later + (part,), "cross.core", "in.first", "out.ends")
    q1, k1, v1, lse1, ot1, mixed1, n1, first, n2 = self_forward(
        length, place, half, tp - half, x, part, *shared, later, kept[:-1]
    )
    if chained:
        w_cross = chains["cross"].pack
    later = move(moved + (n2,), "in.second", "out.first")
    k2, v2, k2t, v2t = frame_keys(place, frames, w_cross, own_rows, head_bias, dims, (n2,) + moved)
    moved = move(later + (k2,), "in.core", "out.second")
    shared = (w_cross, own_rows, params, head_bias, k2, v2t, frames_own, dims)
    *kept, part, _ = cross_forward(place, 0, half, n2, first, *shared, later)
    later = move(moved + (part,), "out.core")
    q2, lse2, ot2, mixed2, second, n3 = cross_forward(
        place, half, tp - half, n2, part, *shared, moved, kept
    )
    if chained:
        w_in, w_out = chains["in"].pack, chains["out"].pack
    hidden, slope, layer_out, g3, b3, sums = feed_forward(
        place, n3, second, w_in, w_out, own_rows, params, cotangent[0], dims
    )
    scatters = {}

    def begin(name, halves):
        if chained:
            scatters[name] = Scatter(halves)

    def go(name, step):
        if not chained:
            return ()
        out = getattr(scatters[name], step)()
        return out if isinstance(out, tuple) else (out,)

    grad_out = feed_out_grads(place, b3, hidden, grad_shape, dims)
    begin("out", grad_out)
    step1 = go("out", "core")
    *grad_in, g2, b2, sums = feed_backward(
        place, b3, g3, slope, w_in, w_out, own_rows, n3, second, params, sums, grad_shape, dims, (grad_out[0],)
    )
    begin("in", grad_in)
    step2 = go("out", "first") + go("in", "core")
    shared = (b2, q2, k2, v2, k2t, lse2, ot2, w_cross, own_rows, frames_own, dims)
    *kept, sums = cross_attend_back(place, 0, half, sums, *shared, step1)
    step3 = go("out", "second") + go("in", "first")
    dq2, dkv2, sums = cross_attend_back(place, half, tp - half, sums, *shared, step2, kept)
    step4 = go("out", "line") + go("in", "second")
    grad_frames, g1, b1, sums = cross_rows_back(
        place, sums, dq2, dkv2, g2, first, w_cross, own_rows, params, frames_own, dims, step3
    )
    step5 = go("in", "line")
    grad_cross = cross_grads(place, dq2, dkv2, mixed2, b2, n2, frames, grad_shape, dims, step4 + (b1,))
    begin("cross", grad_cross)
    frames_back = lax.all_to_all(gate(grad_frames, (grad_cross[0],)), "tp", 0, 0, tiled=True)
    step6 = go("cross", "core")
    dqkv1, sums = self_attend_back(
        length, place, sums, b1, q1, k1, v1, lse1, ot1, w_self, own_rows, dims, step5 + (grad_cross[0],)
    )
    step7 = go("cross", "first")
    grad_self = self_grads(place, dqkv1, mixed1, b1, n1, grad_shape, dims, step6)
    begin("self", grad_self)
    go("self", "core")
    grad_inputs, sums = self_rows_back(
        place, sums, dqkv1, g1, x, w_self, own_rows, params, dims, step7 + (grad_self[0],)
    )
    go("cross", "second")

    for step in range(max(fsdp, tp)):
        if 2**step < fsdp:
            sums = sums + swap(sums, 2**step)
        if 2**step < tp:
            sums = sums + lax.ppermute(sums, "tp", [(i, i ^ 2**step) for i in range(tp)])
    device = lax.axis_index("fsdp") * tp + tp_place
    mine = lax.dynamic_slice_in_dim(sums[:rows], device * small_own, small_own, 1)
    gains = norm_gain.shape[0]
    own_gain, own_shift, own_bias = mine[:gains], mine[gains : 2 * gains], mine[2 * gains :]
    per_row = width // ff_own
    own_fc_bias = lax.dynamic_slice(
        sums, (rows + device // per_row, (device % per_row) * ff_own), (1, ff_own)
    )[0]

    if chained:
        go("self", "first")
        go("cross", "line")
        go("self", "second")
        go("self", "line")
        total_out, total_in, total_cross, total_self = (
            scatters[name].total() for name in ("out", "in", "cross", "self")
        )
    else:
        total_out, total_in, total_cross, total_self = (
            butterfly_scatter(grads[0], own) for grads in (grad_out, grad_in, grad_cross, grad_self)
        )

    def part(total, index):
        return total[:, index * hw : (index + 1) * hw]

    return (
        layer_out[None],
        grad_inputs[None],
        frames_back.astype(F32),
        jnp.stack([part(total_self, 0), part(total_self, 1), part(total_self, 2)]),
        part(total_self, 3).T,
        part(total_cross, 2),
        jnp.stack([part(total_cross, 0), part(total_cross, 1)]),
        part(total_cross, 3).T,
        total_in,
        total_out.T,
        own_gain,
        own_shift,
        own_bias,
        own_fc_bias,
    )


def solution(mesh):
    return jax.shard_map(
        local,
        mesh=mesh,
        in_specs=(
            P(("fsdp", "tp"), None, None),
            P("fsdp", "tp", None),
            P("fsdp"),
            P(None, "fsdp", "tp"),
            P("tp", "fsdp"),
            P("fsdp", "tp"),
            P(None, "fsdp", "tp"),
            P("tp", "fsdp"),
            P("fsdp", "tp"),
            P("tp", "fsdp"),
            P(None, ("fsdp", "tp")),
            P(None, ("fsdp", "tp")),
            P(None, ("fsdp", "tp")),
            P(("fsdp", "tp")),
            P(("fsdp", "tp"), None, None),
        ),
        out_specs=(
            P(("fsdp", "tp"), None, None),
            P(("fsdp", "tp"), None, None),
            P("fsdp", "tp", None),
            P(None, "fsdp", "tp"),
            P("tp", "fsdp"),
            P("fsdp", "tp"),
            P(None, "fsdp", "tp"),
            P("tp", "fsdp"),
            P("fsdp", "tp"),
            P("tp", "fsdp"),
            P(None, ("fsdp", "tp")),
            P(None, ("fsdp", "tp")),
            P(None, ("fsdp", "tp")),
            P(("fsdp", "tp")),
        ),
        check_vma=False,
    )
```

time: 698 us -> 552 us (0.79)
  waiting for transfers between devices: 307 us -> 132 us
  blocking collectives: 71.2 us -> 0 us
  starting transfers between devices: 47.5 us -> 107 us
  Pallas kernels: 175 us -> 220 us
  other arithmetic: 25.9 us -> 48.8 us
  local copies, waits for them, and re-layouts: 47.7 us -> 32.6 us
  between operations: 14.9 us -> 2.35 us
    all_gather x4 -> x0, waiting for transfers between devices: 143 us -> none  [gather_pack(): whole_pack = lax.all_gather(shard, ('fsdp', 'tp'), axis=0, tiled=False)]
    unnamed x1 -> x0, blocking collectives: 71.2 us -> none
    all_to_all x2, waiting for transfers between devices: 65.9 us -> 0.01 us  [the longest x1 0.01 us: local(): frames = lax.all_to_all(frames, 'tp', 0, 0, tiled=True)]
    ppermute x24 -> x69, starting transfers between devices: 36.2 us -> 88.5 us  [the longest x43 35.3 us: swap(): return lax.ppermute(array, 'fsdp', [(i, i ^ step) for i in range(count)])]
    pallas_call x7 -> x15, Pallas kernels: 175 us -> 220 us  [call(): pl.pallas_call(inner, out_shape=[o for o, _ in outs], grid_spec=pltpu.Pre...]
    ppermute x24 -> x69, waiting for transfers between devices: 96.8 us -> 132 us  [the longest x43 55.9 us: swap(): return lax.ppermute(array, 'fsdp', [(i, i ^ step) for i in range(count)])]
    squeeze x16 -> x1, local copies, waits for them, and re-layouts: 15.5 us -> 0.58 us  [local(): lax.dynamic_slice(sums, (rows + device // per_row, device % per_row * ff_...]
    concatenate x1 -> x15, other arithmetic: 0.08 us -> 12.6 us  [the longest x4 6.2 us: second(): self.mine = jnp.concatenate([low, high], 1)]
  transfers between devices with their start and end apart: 30 -> 71, of which waited for: 15 -> 21; matrix products, arithmetic and copies ran while one was open for 8% -> 12% of each run, Pallas kernels for 9% -> 32%
where the time goes in v2:
time: 552 us; the launch traced here: 543 us
  Pallas kernels  220 us (40%)
  waiting for transfers between devices  132 us (24%)
  starting transfers between devices  107 us (19%)
  other arithmetic  48.8 us (9%)
  local copies, waits for them, and re-layouts  32.6 us (6%)
    pallas_call x15, Pallas kernels, call(): pl.pallas_call(inner, out_shape=[o for o, _ in outs], grid_spec=pltpu.Pre...  220 us
    ppermute x43, waiting for transfers between devices, swap(): return lax.ppermute(array, 'fsdp', [(i, i ^ step) for i in range(count)])  55.9 us
    ppermute x3, waiting for transfers between devices, pair(): self.come = lax.ppermute(self.shard, 'tp', [(i, i ^ 1) for i in range(4)])  45.3 us
    ppermute x43, starting transfers between devices, swap(): return lax.ppermute(array, 'fsdp', [(i, i ^ step) for i in range(count)])  35.3 us
    ppermute x15, starting transfers between devices, around(): lax.ppermute(array, 'tp', [(i, (i + hop) % count) for i in range(count)])  31.8 us
    ppermute x15, waiting for transfers between devices, around(): lax.ppermute(array, 'tp', [(i, (i + hop) % count) for i in range(count)])  31.1 us
    unnamed x124, local copies, waits for them, and re-layouts  14.7 us
    all_to_all x1, starting transfers between devices, local(): frames = lax.all_to_all(frames, 'tp', 0, 0, tiled=True)  13.6 us
  transfers between devices with their start and end apart: 71, of which 21 were waited for; matrix products, arithmetic and copies ran while one was open for 12% of the time, Pallas kernels for 32%

profile of v2, /device:TPU:0, one launch (start us, length us, event | category | flops | bytes accessed | tf_op | source)
XLA Modules:
  0.0 542.5 jit_solution(8930469463509182778)
XLA Ops:
  6.3 5.1 collective-permute-start.2
  12.6 3.7 collective-permute-done.2
  16.3 9.8 %collective-permute-done.1 = bf16[112,768]{1,0:T(8,128)(2,1)S(1)} collective-permute-done((bf16[112,768]{1,0:T(8,128)(2,1)S(1)}, bf16[112,768]{1,0:T(8,128)(2,1)S(1)}, u32[]{:S(2)}, u32[]{:S(2)}) %collective-permute-start.1) | collective-permute-done | bytes 172064 | tf_op jit(solution)/shard_map/ppermute | solution.py:765
  26.4 1.6 collective-permute-start.4
  27.9 1.5 collective-permute-start.3
  29.4 6.6 %collective-permute-done.4 = bf16[1,2,112,768]{3,2,1,0:T(8,128)(2,1)S(1)} collective-permute-done((bf16[1,2,112,768]{3,2,1,0:T(8,128)(2,1)S(1)}, bf16[1,2,112,768]{3,2,1,0:T(8,128)(2,1)S(1)}, u32[]{:S(2)}, u32[]{:S(2)}) %collective-permute-start.4) | collective-permute-done | bytes 344096 | tf_op jit(solution)/shard_map/ppermute | solution.py:760
  37.3 1.6 collective-permute-start.6
  39.5 13.7 %collective-permute-done.6 = bf16[2,2,112,768]{3,2,1,0:T(8,128)(2,1)S(1)} collective-permute-done((bf16[2,2,112,768]{3,2,1,0:T(8,128)(2,1)S(1)}, bf16[2,2,112,768]{3,2,1,0:T(8,128)(2,1)S(1)}, u32[]{:S(2)}, u32[]{:S(2)}) %collective-permute-start.6) | collective-permute-done | bytes 688160 | tf_op jit(solution)/shard_map/ppermute | solution.py:760
  55.9 5.8 %collective-permute-done.8 = bf16[96,768]{1,0:T(8,128)(2,1)S(1)} collective-permute-done((bf16[96,768]{1,0:T(8,128)(2,1)S(1)}, bf16[96,768]{1,0:T(8,128)(2,1)S(1)}, u32[]{:S(2)}, u32[]{:S(2)}) %collective-permute-start.8) | collective-permute-done | bytes 147488 | tf_op jit(solution)/shard_map/ppermute | solution.py:799
  64.4 3.3 copy.56
  67.8 13.6 %all-to-all-start = ((bf16[4,375,768]{2,1,0:T(8,128)(2,1)}), bf16[4,375,768]{2,1,0:T(8,128)(2,1)}, u32[]{:S(2)}, u32[]{:S(2)}) async-start(bf16[4,375,768]{2,1,0:T(8,128)(2,1)} %copy.56), calls=%async_computation | async-start | bytes 4620288 | tf_op jit(solution)/shard_map/all_to_all | solution.py:1022
  81.4 2.1 collective-permute-start.11
  84.6 35.9 %collective-permute-done.11 = bf16[96,768]{1,0:T(8,128)(2,1)S(1)} collective-permute-done((bf16[96,768]{1,0:T(8,128)(2,1)S(1)}, bf16[96,768]{1,0:T(8,128)(2,1)S(1)}, u32[]{:S(2)}, u32[]{:S(2)}) %collective-permute-start.11) | collective-permute-done | bytes 147488 | tf_op jit(solution)/shard_map/ppermute | solution.py:799
  124.6 5.8 %collective-permute-start.15 = (bf16[96,768]{1,0:T(8,128)(2,1)}, bf16[96,768]{1,0:T(8,128)(2,1)}, u32[]{:S(2)}, u32[]{:S(2)}) collective-permute-start(bf16[96,768]{1,0:T(8,128)(2,1)} %bitcast.26), channel_id=1, source_target_pairs={{0,1},{1,0},{2,3},{3,2},{4,5},{5,4},{6,7},{7,6},{8,9},{9,8},{10,11... | collective-permute-start | bytes 442376 | tf_op jit(solution)/shard_map/ppermute | solution.py:799
  133.3 3.6 collective-permute-done.15.refs_11_
  146.2 11.6 %self_forward.2 = (bf16[4,448,192]{2,1,0:T(8,128)(2,1)}, bf16[4,448,192]{2,1,0:T(8,128)(2,1)}, bf16[4,448,192]{2,1,0:T(8,128)(2,1)}, f32[4,8,448]{2,1,0:T(8,128)...) custom-call(s32[1]{0:T(128)} %dynamic_slice.96.refs_0_, ...), custom_call_target="tpu_custom_call" | custom-call | flops 2290089984 | bytes 13918208 | tf_op jit(solution)/shard_map/self_forward/pallas_call | solution.py:79
  158.7 1.5 maximum_maximum_fusion.1.refs_2_.refs_6_.refs_3_.refs_9_
  160.3 4.0 pad.24.refs_1_.refs_6_
  165.5 1.5 collective-permute-start.23
  167.1 1.6 collective-permute-start.21
  170.1 11.4 %self_forward.3 = (bf16[4,448,192]{2,1,0:T(8,128)(2,1)}, bf16[4,448,192]{2,1,0:T(8,128)(2,1)}, bf16[4,448,192]{2,1,0:T(8,128)(2,1)}, f32[4,8,448]{2,1,0:T(8,128)...) custom-call(s32[1]{0:T(128)} %dynamic_slice.96.refs_0_, ...), custom_call_target="tpu_custom_call", output_to_operand_aliasing={{0}: (8, {}), {1}: (9, {}), {2}: (10, {}), {3}: (11, {}), {... | custom-call | flops 2290089984 | bytes 14606336 | tf_op jit(solution)/shard_map/self_forward/pallas_call | solution.py:79
  184.0 1.6 collective-permute-start.26
  187.0 11.0 %frame_keys.1 = (bf16[4,4,384,192]{3,2,1,0:T(8,128)(2,1)}, bf16[4,4,384,192]{3,2,1,0:T(8,128)(2,1)}, bf16[4,192,1536]{2,1,0:T(8,128)(2,1)}, bf16[4,192,1536]{2,1,0:T(8,128)(2,1)}) custom-call(s32[1]{0:T(128)} %bitcast.refs_1_.refs_0_, bf16[4,384,768]{2,1,0:T(8,128)(2,1)} %pad.24.refs_1_.refs_6_, bf16[4,4,96,768]{3,2,1,0:T(8,128)(2,1)} %copy-done.1, ...), custom_call_target="tpu_custom_call" | custom-call | flops 3623878656 | bytes 16539648 | tf_op jit(solution)/shard_map/frame_keys/pallas_call | solution.py:79
  201.9 1.6 collective-permute-done.26.refs_11_
  203.9 1.9 pad_maximum_fusion.12
  207.3 1.9 pad_maximum_fusion.11
  209.7 19.3 %cross_forward.2 = (bf16[4,448,192]{2,1,0:T(8,128)(2,1)}, f32[4,8,448]{2,1,0:T(8,128)}, f32[4,192,448]{2,1,0:T(8,128)}, bf16[4,448,192]{2,1,0:T(8,128)(2,1)}, f3...) custom-call(s32[1]{0:T(128)} %bitcast.refs_1_.refs_0_, bf16[448,768]{1,0:T(8,128)(2,1)} %get-tuple-element.123.refs_5_.refs_1_, ...), custom_call_target="tpu_custom_call" | custom-call | flops 4756340736 | bytes 16474112 | tf_op jit(solution)/shard_map/cross_forward/pallas_call | solution.py:79
  229.1 2.9 maximum_maximum_fusion.3.refs_5_.refs_6_
  232.1 19.7 %cross_forward.3 = (bf16[4,448,192]{2,1,0:T(8,128)(2,1)}, f32[4,8,448]{2,1,0:T(8,128)}, f32[4,192,448]{2,1,0:T(8,128)}, bf16[4,448,192]{2,1,0:T(8,128)(2,1)}, f3...) custom-call(s32[1]{0:T(128)} %bitcast.refs_1_.refs_0_, ...), custom_call_target="tpu_custom_call", output_to_operand_aliasing={{0}: (9, {}), {1}: (10, {}), {2}: (11, {}), {3}: (12, {})} | custom-call | flops 4756340736 | bytes 16474112 | tf_op jit(solution)/shard_map/cross_forward/pallas_call | solution.py:79
  253.2 14.3 %feed_forward.1 = (bf16[4,448,768]{2,1,0:T(8,128)(2,1)}, f32[4,448,768]{2,1,0:T(8,128)}, bf16[448,768]{1,0:T(8,128)(2,1)}, f32[448,768]{1,0:T(8,128)}, bf16[448,768]{1,0:T(8,128)(2,1)}, /*index=5*/f32[24,768]{1,0:T(8,128)}) custom-call(s32[1]{0:T(128)} %bitcast.refs_1_.refs_0_, bf16[448,768]{1,0:T(8,128)(2,1)} %get-tuple-element.142.refs_1_.refs_8_, ...), custom_call_target="tpu_custom_call" | custom-call | flops 4227858432 | bytes 23347200 | tf_op jit(solution)/shard_map/feed_forward/pallas_call | solution.py:79
  267.6 7.2 %feed_out_grads.1 = (bf16[4,4,96,768]{3,2,1,0:T(8,128)(2,1)}, bf16[4,4,96,768]{3,2,1,0:T(8,128)(2,1)}) custom-call(s32[1]{0:T(128)} %bitcast.refs_1_.refs_0_, bf16[448,768]{1,0:T(8,128)(2,1)} %get-tuple-element.146.refs_1_, bf16[4,448,768]{2,1,0:T(8,128)(2,1)} %get-tuple-element.150.refs_2_), custom_call_target="tpu_custom_call" | custom-call | flops 2113929216 | bytes 8159232 | tf_op jit(solution)/shard_map/feed_out_grads/pallas_call | solution.py:79
  275.2 18.8 %feed_backward.1 = (bf16[4,4,96,768]{3,2,1,0:T(8,128)(2,1)}, bf16[4,4,96,768]{3,2,1,0:T(8,128)(2,1)}, f32[448,768]{1,0:T(8,128)}, bf16[448,768]{1,0:T(8,128)(2,1)}, f32[24,768]{1,0:T(8,128)}) custom-call(s32[1]{0:T(128)} %bitcast.refs_1_.refs_0_, bf16[448,768]{1,0:T(8,128)(2,1)} %get-tuple-element.146.refs_1_, f32[448,768]{1,0:T(8,128)} %get-tuple-element.147.refs_2_, ...), custom_call_target="tpu_custom_call" | custom-call | flops 6341787648 | bytes 26075136 | tf_op jit(solution)/shard_map/feed_backward/pallas_call | solution.py:79
  294.1 3.1 add_convert_fusion.6
  299.2 1.6 add_convert_fusion.4
  302.8 23.0 %cross_attend_back.2 = (bf16[4,448,192]{2,1,0:T(8,128)(2,1)}, bf16[4,4,384,384]{3,2,1,0:T(8,128)(2,1)}, f32[24,768]{1,0:T(8,128)}) custom-call(s32[1]{0:T(128)} %bitcast.refs_1_.refs_0_, f32[24,768]{1,0:T(8,128)} %get-tuple-element.152.refs_1_, bf16[448,768]{1,0:T(8,128)(2,1)} %get-tuple-element.153.refs_2_.refs_4_, ...), custom_call_target="tpu_custom_call" | custom-call | flops 5549064192 | bytes 20160512 | tf_op jit(solution)/shard_map/cross_attend_back/pallas_call | solution.py:79
  325.9 2.7 fusion.9
  330.6 2.3 fusion.11
  334.9 23.1 %cross_attend_back.3 = (bf16[4,448,192]{2,1,0:T(8,128)(2,1)}, bf16[4,4,384,384]{3,2,1,0:T(8,128)(2,1)}, f32[24,768]{1,0:T(8,128)}) custom-call(s32[1]{0:T(128)} %bitcast.refs_1_.refs_0_, f32[24,768]{1,0:T(8,128)} %get-tuple-element.160.refs_1_, bf16[448,768]{1,0:T(8,128)(2,1)} %get-tuple-element.153.refs_2_.refs_4_, ...), custom_call_target="tpu_custom_call", output_to_operand_aliasing={{0}: (11, {}), {1}: (12, {})} | custom-call | flops 5549064192 | bytes 20160512 | tf_op jit(solution)/shard_map/cross_attend_back/pallas_call | solution.py:79
  358.1 1.7 fusion.4
  360.0 6.1 %collective-permute-start.45 = (bf16[96,768]{1,0:T(8,128)(2,1)S(1)}, bf16[96,768]{1,0:T(8,128)(2,1)S(1)}, u32[]{:S(2)}, u32[]{:S(2)}) collective-permute-start(bf16[96,768]{1,0:T(8,128)(2,1)S(1)} %get-tuple-element.267), channel_id=1, source_target_pairs={{0,1},{1,2},{2,3},{3,0},{4,5},{5,6},{6,7},{7,4},{8,9},{9,10},{10,1... | collective-permute-start | bytes 442376 | tf_op jit(solution)/shard_map/ppermute | solution.py:765
  367.1 2.8 collective-permute-start.47
  369.9 13.9 %cross_rows_back.1 = (bf16[4,375,768]{2,1,0:T(8,128)(2,1)}, f32[448,768]{1,0:T(8,128)}, bf16[448,768]{1,0:T(8,128)(2,1)}, f32[24,768]{1,0:T(8,128)}) custom-call(s32[1]{0:T(128)} %bitcast.refs_1_.refs_0_, f32[24,768]{1,0:T(8,128)} %get-tuple-element.164.refs_1_, bf16[4,448,192]{2,1,0:T(8,128)(2,1)} %get-tuple-element.165.refs_2_.refs_1_, ...), custom_call_target="tpu_custom_call" | custom-call | flops 4152360960 | bytes 17467392 | tf_op jit(solution)/shard_map/cross_rows_back/pallas_call | solution.py:79
  384.8 13.4 %cross_grads.1 = (bf16[4,4,96,768]{3,2,1,0:T(8,128)(2,1)}, bf16[4,4,96,768]{3,2,1,0:T(8,128)(2,1)}) custom-call(s32[1]{0:T(128)} %bitcast.refs_1_.refs_0_, bf16[4,448,192]{2,1,0:T(8,128)(2,1)} %get-tuple-element.165.refs_2_.refs_1_, bf16[4,4,384,384]{3,2,1,0:T(8,128)(2,1)} %get-tuple-element.166.refs_3_.refs_2_, ...), custom_call_target="tpu_custom_call" | custom-call | flops 4680843264 | bytes 14548992 | tf_op jit(solution)/shard_map/cross_grads/pallas_call | solution.py:79
  398.2 1.9 fusion.6
  401.4 2.7 collective-permute-start.44
  404.2 4.8 collective-permute-done.42.refs_11_
  409.0 5.4 collective-permute-done.43.refs_12_
  415.1 15.5 %self_attend_back.1 = (bf16[4,448,576]{2,1,0:T(8,128)(2,1)}, f32[24,768]{1,0:T(8,128)}) custom-call(s32[1]{0:T(128)} %dynamic_slice.96.refs_0_, s32[1]{0:T(128)} %bitcast.refs_1_.refs_0_, f32[24,768]{1,0:T(8,128)} %get-tuple-element.169.refs_2_, bf16[448,768]{1,0:T(8,128)(2,1)} %get-tuple-element.170.refs_12_.refs_3_, ...), custom_call_target="tpu_custom_call" | custom-call | flops 6694109184 | bytes 11902976 | tf_op jit(solution)/shard_map/self_attend_back/pallas_call | solution.py:79
  432.1 8.5 %self_grads.1 = (bf16[4,4,96,768]{3,2,1,0:T(8,128)(2,1)}, bf16[4,4,96,768]{3,2,1,0:T(8,128)(2,1)}) custom-call(s32[1]{0:T(128)} %bitcast.refs_1_.refs_0_, bf16[4,448,576]{2,1,0:T(8,128)(2,1)} %get-tuple-element.179.refs_1_.refs_2_, bf16[4,448,192]{2,1,0:T(8,128)(2,1)} %get-tuple-element.182.refs_2_, bf16[448,768]{1,0:T(8,128)(2,1)} %get-tuple-element.170.refs_12_.refs_3_, ...), custom_call_target="tpu_custom_call" | custom-call | flops 2113929216 | bytes 8847360 | tf_op jit(solution)/shard_map/self_grads/pallas_call | solution.py:79
  440.5 4.9 all-to-all-start.1
  445.4 2.5 add_convert_fusion.2
  450.0 13.8 %collective-permute-done.49.refs_8_ = bf16[2,2,96,768]{3,2,1,0:T(8,128)(2,1)S(1)} collective-permute-done((bf16[2,2,96,768]{3,2,1,0:T(8,128)(2,1)}, bf16[2,2,96,768]{3,2,1,0:T(8,128)(2,1)S(1)}, u32[]{:S(2)}, u32[]{:S(2)}) %collective-permute-start.49) | collective-permute-done | bytes 589856 | tf_op jit(solution)/shard_map/ppermute | solution.py:760
  465.8 8.9 %self_rows_back.1 = (f32[448,768]{1,0:T(8,128)}, f32[24,768]{1,0:T(8,128)}) custom-call(s32[1]{0:T(128)} %bitcast.refs_1_.refs_0_, f32[24,768]{1,0:T(8,128)} %get-tuple-element.178.refs_1_, bf16[4,448,576]{2,1,0:T(8,128)(2,1)} %get-tuple-element.179.refs_1_.refs_2_, f32[448,768]{1,0:T(8,128)} %get-tuple-element.180.refs_3_, bf16[448,768]{1,0:T(8,128)(2,1)} %bitcast.172, ...), custom_call_target="tpu_custom_call" | custom-call | flops 1585446912 | bytes 11231232 | tf_op jit(solution)/shard_map/self_rows_back/pallas_call | solution.py:79
  474.8 1.7 add_convert_fusion
  479.0 3.3 collective-permute-start.65
  487.6 12.7 %collective-permute-done.66 = f32[24,768]{1,0:T(8,128)S(1)} collective-permute-done((f32[24,768]{1,0:T(8,128)S(1)}, f32[24,768]{1,0:T(8,128)S(1)}, u32[]{:S(2)}, u32[]{:S(2)}) %collective-permute-start.66) | collective-permute-done | bytes 73760 | tf_op jit(solution)/shard_map/ppermute | solution.py:760
  500.3 2.4 collective-permute-start.67
  507.9 3.7 collective-permute-start.63
  512.0 1.7 collective-permute-done.68
  516.8 2.4 collective-permute-start.58
  519.5 3.6 collective-permute-start.56
  525.1 4.7 copy.57
  529.8 2.4 collective-permute-done.62
  532.2 5.0 collective-permute-done.57
  (321 shorter events, 88.7 us)
Async XLA Ops:
  6.3 9.9 %collective-permute-start.2 = (bf16[112,768]{1,0:T(8,128)(2,1)S(1)}, bf16[112,768]{1,0:T(8,128)(2,1)S(1)}, u32[]{:S(2)}, u32[]{:S(2)}) collective-permute-start(bf16[112,768]{1,0:T(8,128)(2,1)S(1)} %pad_maximum_fusion.18), channel_id=1, source_target_pairs={{0,3},{1,0},{2,1},{3,2},{4,7},{5,4},{6,5},{7,6},{8,11},{9,8},{10,9... | collective-permute-start | bytes 516104 | tf_op jit(solution)/shard_map/ppermute | solution.py:765
  11.5 14.6 %collective-permute-start.1 = (bf16[112,768]{1,0:T(8,128)(2,1)S(1)}, bf16[112,768]{1,0:T(8,128)(2,1)S(1)}, u32[]{:S(2)}, u32[]{:S(2)}) collective-permute-start(bf16[112,768]{1,0:T(8,128)(2,1)S(1)} %pad_maximum_fusion.18), channel_id=1, source_target_pairs={{0,2},{1,3},{2,0},{3,1},{4,6},{5,7},{6,4},{7,5},{8,10},{9,11},{10,... | collective-permute-start | bytes 516104 | tf_op jit(solution)/shard_map/ppermute | solution.py:765
  11.5 14.6 %collective-permute-start = (bf16[112,768]{1,0:T(8,128)(2,1)S(1)}, bf16[112,768]{1,0:T(8,128)(2,1)S(1)}, u32[]{:S(2)}, u32[]{:S(2)}) collective-permute-start(bf16[112,768]{1,0:T(8,128)(2,1)S(1)} %pad_maximum_fusion.18), channel_id=1, source_target_pairs={{0,1},{1,2},{2,3},{3,0},{4,5},{5,6},{6,7},{7,4},{8,9},{9,10},{10,1... | collective-permute-start | bytes 516104 | tf_op jit(solution)/shard_map/ppermute | solution.py:765
  26.4 9.7 %collective-permute-start.4 = (bf16[1,2,112,768]{3,2,1,0:T(8,128)(2,1)S(1)}, bf16[1,2,112,768]{3,2,1,0:T(8,128)(2,1)S(1)}, u32[]{:S(2)}, u32[]{:S(2)}) collective-permute-start(bf16[1,2,112,768]{3,2,1,0:T(8,128)(2,1)S(1)} %get-tuple-element.255), channel_id=1, source_target_pairs={{0,16},{4,20},{8,24},{12,28},{16,0},{20,4},{24,8},{28,12},{1,17},{... | collective-permute-start | bytes 1032200 | tf_op jit(solution)/shard_map/ppermute | solution.py:760
  27.9 9.3 %collective-permute-start.3 = (bf16[1,2,112,768]{3,2,1,0:T(8,128)(2,1)S(1)}, bf16[1,2,112,768]{3,2,1,0:T(8,128)(2,1)S(1)}, u32[]{:S(2)}, u32[]{:S(2)}) collective-permute-start(bf16[1,2,112,768]{3,2,1,0:T(8,128)(2,1)S(1)} %get-tuple-element.254), channel_id=1, source_target_pairs={{0,8},{4,12},{8,0},{12,4},{16,24},{20,28},{24,16},{28,20},{1,9},{5... | collective-permute-start | bytes 1032200 | tf_op jit(solution)/shard_map/ppermute | solution.py:760
  37.3 15.9 %collective-permute-start.6 = (bf16[2,2,112,768]{3,2,1,0:T(8,128)(2,1)S(1)}, bf16[2,2,112,768]{3,2,1,0:T(8,128)(2,1)S(1)}, u32[]{:S(2)}, u32[]{:S(2)}) collective-permute-start(bf16[2,2,112,768]{3,2,1,0:T(8,128)(2,1)S(1)} %pad_maximum_fusion.3), channel_id=1, source_target_pairs={{0,8},{4,12},{8,0},{12,4},{16,24},{20,28},{24,16},{28,20},{1,9},{5... | collective-permute-start | bytes 2064392 | tf_op jit(solution)/shard_map/ppermute | solution.py:760
  39.0 15.6 %collective-permute-start.5 = (bf16[2,2,112,768]{3,2,1,0:T(8,128)(2,1)S(1)}, bf16[2,2,112,768]{3,2,1,0:T(8,128)(2,1)S(1)}, u32[]{:S(2)}, u32[]{:S(2)}) collective-permute-start(bf16[2,2,112,768]{3,2,1,0:T(8,128)(2,1)S(1)} %pad_maximum_fusion.2), channel_id=1, source_target_pairs={{0,16},{4,20},{8,24},{12,28},{16,0},{20,4},{24,8},{28,12},{1,17},{... | collective-permute-start | bytes 2064392 | tf_op jit(solution)/shard_map/ppermute | solution.py:760
  55.0 75.5 %collective-permute-start.7 = (bf16[4,4,112,768]{3,2,1,0:T(8,128)(2,1)S(1)}, bf16[4,4,112,768]{3,2,1,0:T(8,128)(2,1)}, u32[]{:S(2)}, u32[]{:S(2)}) collective-permute-start(bf16[4,4,112,768]{3,2,1,0:T(8,128)(2,1)S(1)} %maximum_maximum_fusion.refs_4_.refs_9_.refs_5_), channel_id=1, source_target_pairs={{0,4},{4,0},{8,12},{12,8},{16,20},{20,16},{24,28},{28,24},{1,5},{5... | collective-permute-start | bytes 8257544 | tf_op jit(solution)/shard_map/ppermute | solution.py:760
  62.5 21.0 %collective-permute-start.10 = (bf16[2,96,768]{2,1,0:T(8,128)(2,1)S(1)}, bf16[2,96,768]{2,1,0:T(8,128)(2,1)}, u32[]{:S(2)}, u32[]{:S(2)}) collective-permute-start(bf16[2,96,768]{2,1,0:T(8,128)(2,1)S(1)} %collective-permute-done.9), channel_id=1, source_target_pairs={{1,0},{2,3},{5,4},{6,7},{9,8},{10,11},{13,12},{14,15},{17,16},{18,... | collective-permute-start | bytes 884744 | tf_op jit(solution)/shard_map/ppermute | solution.py:810
  67.8 92.6 %all-to-all-start = ((bf16[4,375,768]{2,1,0:T(8,128)(2,1)}), bf16[4,375,768]{2,1,0:T(8,128)(2,1)}, u32[]{:S(2)}, u32[]{:S(2)}) async-start(bf16[4,375,768]{2,1,0:T(8,128)(2,1)} %copy.56), calls=%async_computation | async-start | bytes 4620288 | tf_op jit(solution)/shard_map/all_to_all | solution.py:1022
  81.4 39.1 %collective-permute-start.11 = (bf16[96,768]{1,0:T(8,128)(2,1)S(1)}, bf16[96,768]{1,0:T(8,128)(2,1)S(1)}, u32[]{:S(2)}, u32[]{:S(2)}) collective-permute-start(bf16[96,768]{1,0:T(8,128)(2,1)S(1)} %copy-done.49), channel_id=1, source_target_pairs={{0,1},{1,0},{2,3},{3,2},{4,5},{5,4},{6,7},{7,6},{8,9},{9,8},{10,11... | collective-permute-start | bytes 442376 | tf_op jit(solution)/shard_map/ppermute | solution.py:799
  121.4 15.6 %collective-permute-start.12 = (bf16[1,2,96,768]{3,2,1,0:T(8,128)(2,1)}, bf16[1,2,96,768]{3,2,1,0:T(8,128)(2,1)S(1)}, u32[]{:S(2)}, u32[]{:S(2)}) collective-permute-start(bf16[1,2,96,768]{3,2,1,0:T(8,128)(2,1)} %get-tuple-element.283), channel_id=1, source_target_pairs={{0,8},{4,12},{8,0},{12,4},{16,24},{20,28},{24,16},{28,20},{1,9},{5... | collective-permute-start | bytes 884744 | tf_op jit(solution)/shard_map/ppermute | solution.py:760
  121.9 15.0 %collective-permute-start.13 = (bf16[1,2,96,768]{3,2,1,0:T(8,128)(2,1)}, bf16[1,2,96,768]{3,2,1,0:T(8,128)(2,1)S(1)}, u32[]{:S(2)}, u32[]{:S(2)}) collective-permute-start(bf16[1,2,96,768]{3,2,1,0:T(8,128)(2,1)} %get-tuple-element.282), channel_id=1, source_target_pairs={{0,16},{4,20},{8,24},{12,28},{16,0},{20,4},{24,8},{28,12},{1,17},{... | collective-permute-start | bytes 884744 | tf_op jit(solution)/shard_map/ppermute | solution.py:760
  123.3 13.7 %collective-permute-start.14 = (bf16[2,96,768]{2,1,0:T(8,128)(2,1)}, bf16[2,96,768]{2,1,0:T(8,128)(2,1)}, u32[]{:S(2)}, u32[]{:S(2)}) collective-permute-start(bf16[2,96,768]{2,1,0:T(8,128)(2,1)} %pad_maximum_fusion.14), channel_id=1, source_target_pairs={{1,2},{2,1},{5,6},{6,5},{9,10},{10,9},{13,14},{14,13},{17,18},{18,... | collective-permute-start | bytes 884744 | tf_op jit(solution)/shard_map/ppermute | solution.py:806
  124.6 12.3 %collective-permute-start.15 = (bf16[96,768]{1,0:T(8,128)(2,1)}, bf16[96,768]{1,0:T(8,128)(2,1)}, u32[]{:S(2)}, u32[]{:S(2)}) collective-permute-start(bf16[96,768]{1,0:T(8,128)(2,1)} %bitcast.26), channel_id=1, source_target_pairs={{0,1},{1,0},{2,3},{3,2},{4,5},{5,4},{6,7},{7,6},{8,9},{9,8},{10,11... | collective-permute-start | bytes 442376 | tf_op jit(solution)/shard_map/ppermute | solution.py:799
  138.2 19.7 %collective-permute-start.16 = (bf16[2,2,96,768]{3,2,1,0:T(8,128)(2,1)S(1)}, bf16[2,2,96,768]{3,2,1,0:T(8,128)(2,1)S(1)}, u32[]{:S(2)}, u32[]{:S(2)}) collective-permute-start(bf16[2,2,96,768]{3,2,1,0:T(8,128)(2,1)S(1)} %pad_maximum_fusion.5), channel_id=1, source_target_pairs={{0,16},{4,20},{8,24},{12,28},{16,0},{20,4},{24,8},{28,12},{1,17},{... | collective-permute-start | bytes 1769480 | tf_op jit(solution)/shard_map/ppermute | solution.py:760
  139.8 18.0 %collective-permute-start.17 = (bf16[2,2,96,768]{3,2,1,0:T(8,128)(2,1)S(1)}, bf16[2,2,96,768]{3,2,1,0:T(8,128)(2,1)S(1)}, u32[]{:S(2)}, u32[]{:S(2)}) collective-permute-start(bf16[2,2,96,768]{3,2,1,0:T(8,128)(2,1)S(1)} %pad_maximum_fusion.6), channel_id=1, source_target_pairs={{0,8},{4,12},{8,0},{12,4},{16,24},{20,28},{24,16},{28,20},{1,9},{5... | collective-permute-start | bytes 1769480 | tf_op jit(solution)/shard_map/ppermute | solution.py:760
  140.4 19.8 %collective-permute-start.18 = (bf16[2,96,768]{2,1,0:T(8,128)(2,1)}, bf16[2,96,768]{2,1,0:T(8,128)(2,1)}, u32[]{:S(2)}, u32[]{:S(2)}) collective-permute-start(bf16[2,96,768]{2,1,0:T(8,128)(2,1)} %collective-permute-done.14.refs_10_), channel_id=1, source_target_pairs={{1,0},{2,3},{5,4},{6,7},{9,8},{10,11},{13,12},{14,15},{17,16},{18,... | collective-permute-start | bytes 884744 | tf_op jit(solution)/shard_map/ppermute | solution.py:810
  143.5 16.7 %collective-permute-start.19 = (bf16[2,96,768]{2,1,0:T(8,128)(2,1)}, bf16[2,96,768]{2,1,0:T(8,128)(2,1)}, u32[]{:S(2)}, u32[]{:S(2)}) collective-permute-start(bf16[2,96,768]{2,1,0:T(8,128)(2,1)} %pad_maximum_fusion.15), channel_id=1, source_target_pairs={{1,2},{2,1},{5,6},{6,5},{9,10},{10,9},{13,14},{14,13},{17,18},{18,... | collective-permute-start | bytes 884744 | tf_op jit(solution)/shard_map/ppermute | solution.py:806
  160.3 22.4 %collective-permute-start.20 = (bf16[4,4,96,768]{3,2,1,0:T(8,128)(2,1)S(1)}, bf16[4,4,96,768]{3,2,1,0:T(8,128)(2,1)}, u32[]{:S(2)}, u32[]{:S(2)}) collective-permute-start(bf16[4,4,96,768]{3,2,1,0:T(8,128)(2,1)S(1)} %maximum_maximum_fusion.1.refs_2_.refs_6_.refs_3_.refs_9_), channel_id=1, source_target_pairs={{0,4},{4,0},{8,12},{12,8},{16,20},{20,16},{24,28},{28,24},{1,5},{5... | collective-permute-start | bytes 7077896 | tf_op jit(solution)/shard_map/ppermute | solution.py:760
  165.5 16.0 %collective-permute-start.23 = (bf16[2,96,768]{2,1,0:T(8,128)(2,1)}, bf16[2,96,768]{2,1,0:T(8,128)(2,1)}, u32[]{:S(2)}, u32[]{:S(2)}) collective-permute-start(bf16[2,96,768]{2,1,0:T(8,128)(2,1)} %collective-permute-done.19.refs_17_), channel_id=1, source_target_pairs={{1,0},{2,3},{5,4},{6,7},{9,8},{10,11},{13,12},{14,15},{17,16},{18,... | collective-permute-start | bytes 884744 | tf_op jit(solution)/shard_map/ppermute | solution.py:810
  167.1 15.5 %collective-permute-start.21 = (bf16[1,2,96,768]{3,2,1,0:T(8,128)(2,1)S(1)}, bf16[1,2,96,768]{3,2,1,0:T(8,128)(2,1)S(1)}, u32[]{:S(2)}, u32[]{:S(2)}) collective-permute-start(bf16[1,2,96,768]{3,2,1,0:T(8,128)(2,1)S(1)} %get-tuple-element.279), channel_id=1, source_target_pairs={{0,8},{4,12},{8,0},{12,4},{16,24},{20,28},{24,16},{28,20},{1,9},{5... | collective-permute-start | bytes 884744 | tf_op jit(solution)/shard_map/ppermute | solution.py:760
  168.6 14.0 %collective-permute-start.22 = (bf16[1,2,96,768]{3,2,1,0:T(8,128)(2,1)S(1)}, bf16[1,2,96,768]{3,2,1,0:T(8,128)(2,1)S(1)}, u32[]{:S(2)}, u32[]{:S(2)}) collective-permute-start(bf16[1,2,96,768]{3,2,1,0:T(8,128)(2,1)S(1)} %get-tuple-element.278), channel_id=1, source_target_pairs={{0,16},{4,20},{8,24},{12,28},{16,0},{20,4},{24,8},{28,12},{1,17},{... | collective-permute-start | bytes 884744 | tf_op jit(solution)/shard_map/ppermute | solution.py:760
  182.7 16.3 %collective-permute-start.25 = (bf16[2,2,96,768]{3,2,1,0:T(8,128)(2,1)S(1)}, bf16[2,2,96,768]{3,2,1,0:T(8,128)(2,1)S(1)}, u32[]{:S(2)}, u32[]{:S(2)}) collective-permute-start(bf16[2,2,96,768]{3,2,1,0:T(8,128)(2,1)S(1)} %pad_maximum_fusion.9), channel_id=1, source_target_pairs={{0,8},{4,12},{8,0},{12,4},{16,24},{20,28},{24,16},{28,20},{1,9},{5... | collective-permute-start | bytes 1769480 | tf_op jit(solution)/shard_map/ppermute | solution.py:760
  183.3 16.3 %collective-permute-start.24 = (bf16[2,2,96,768]{3,2,1,0:T(8,128)(2,1)S(1)}, bf16[2,2,96,768]{3,2,1,0:T(8,128)(2,1)S(1)}, u32[]{:S(2)}, u32[]{:S(2)}) collective-permute-start(bf16[2,2,96,768]{3,2,1,0:T(8,128)(2,1)S(1)} %pad_maximum_fusion.8), channel_id=1, source_target_pairs={{0,16},{4,20},{8,24},{12,28},{16,0},{20,4},{24,8},{28,12},{1,17},{... | collective-permute-start | bytes 1769480 | tf_op jit(solution)/shard_map/ppermute | solution.py:760
  184.0 19.5 %collective-permute-start.26 = (bf16[1,2,96,768]{3,2,1,0:T(8,128)(2,1)S(1)}, bf16[1,2,96,768]{3,2,1,0:T(8,128)(2,1)}, u32[]{:S(2)}, u32[]{:S(2)}) collective-permute-start(bf16[1,2,96,768]{3,2,1,0:T(8,128)(2,1)S(1)} %get-tuple-element.277), channel_id=1, source_target_pairs={{0,8},{4,12},{8,0},{12,4},{16,24},{20,28},{24,16},{28,20},{1,9},{5... | collective-permute-start | bytes 884744 | tf_op jit(solution)/shard_map/ppermute | solution.py:760
  185.6 18.3 %collective-permute-start.27 = (bf16[1,2,96,768]{3,2,1,0:T(8,128)(2,1)S(1)}, bf16[1,2,96,768]{3,2,1,0:T(8,128)(2,1)}, u32[]{:S(2)}, u32[]{:S(2)}) collective-permute-start(bf16[1,2,96,768]{3,2,1,0:T(8,128)(2,1)S(1)} %get-tuple-element.276), channel_id=1, source_target_pairs={{0,16},{4,20},{8,24},{12,28},{16,0},{20,4},{24,8},{28,12},{1,17},{... | collective-permute-start | bytes 884744 | tf_op jit(solution)/shard_map/ppermute | solution.py:760
  203.9 28.0 %collective-permute-start.28 = (bf16[4,4,96,768]{3,2,1,0:T(8,128)(2,1)S(1)}, bf16[4,4,96,768]{3,2,1,0:T(8,128)(2,1)}, u32[]{:S(2)}, u32[]{:S(2)}) collective-permute-start(bf16[4,4,96,768]{3,2,1,0:T(8,128)(2,1)S(1)} %maximum_maximum_fusion.2.refs_13_.refs_3_.refs_4_), channel_id=1, source_target_pairs={{0,4},{4,0},{8,12},{12,8},{16,20},{20,16},{24,28},{28,24},{1,5},{5... | collective-permute-start | bytes 7077896 | tf_op jit(solution)/shard_map/ppermute | solution.py:760
  205.8 23.2 %collective-permute-start.30 = (bf16[2,2,96,768]{3,2,1,0:T(8,128)(2,1)}, bf16[2,2,96,768]{3,2,1,0:T(8,128)(2,1)S(1)}, u32[]{:S(2)}, u32[]{:S(2)}) collective-permute-start(bf16[2,2,96,768]{3,2,1,0:T(8,128)(2,1)} %pad_maximum_fusion.12), channel_id=1, source_target_pairs={{0,8},{4,12},{8,0},{12,4},{16,24},{20,28},{24,16},{28,20},{1,9},{5... | collective-permute-start | bytes 1769480 | tf_op jit(solution)/shard_map/ppermute | solution.py:760
  209.1 19.9 %collective-permute-start.29 = (bf16[2,2,96,768]{3,2,1,0:T(8,128)(2,1)}, bf16[2,2,96,768]{3,2,1,0:T(8,128)(2,1)S(1)}, u32[]{:S(2)}, u32[]{:S(2)}) collective-permute-start(bf16[2,2,96,768]{3,2,1,0:T(8,128)(2,1)} %pad_maximum_fusion.11), channel_id=1, source_target_pairs={{0,16},{4,20},{8,24},{12,28},{16,0},{20,4},{24,8},{28,12},{1,17},{... | collective-permute-start | bytes 1769480 | tf_op jit(solution)/shard_map/ppermute | solution.py:760
  232.0 19.8 %collective-permute-start.31 = (bf16[4,4,96,768]{3,2,1,0:T(8,128)(2,1)}, bf16[4,4,96,768]{3,2,1,0:T(8,128)(2,1)S(1)}, u32[]{:S(2)}, u32[]{:S(2)}) collective-permute-start(bf16[4,4,96,768]{3,2,1,0:T(8,128)(2,1)} %maximum_maximum_fusion.3.refs_5_.refs_6_), channel_id=1, source_target_pairs={{0,4},{4,0},{8,12},{12,8},{16,20},{20,16},{24,28},{28,24},{1,5},{5... | collective-permute-start | bytes 7077896 | tf_op jit(solution)/shard_map/ppermute | solution.py:760
  274.7 19.4 %collective-permute-start.32 = (bf16[4,4,96,768]{3,2,1,0:T(8,128)(2,1)}, bf16[4,4,96,768]{3,2,1,0:T(8,128)(2,1)}, u32[]{:S(2)}, u32[]{:S(2)}) collective-permute-start(bf16[4,4,96,768]{3,2,1,0:T(8,128)(2,1)} %get-tuple-element.159), channel_id=1, source_target_pairs={{0,4},{4,0},{8,12},{12,8},{16,20},{20,16},{24,28},{28,24},{1,5},{5... | collective-permute-start | bytes 7077896 | tf_op jit(solution)/shard_map/ppermute | solution.py:760
  297.2 28.7 %collective-permute-start.33 = (bf16[2,2,96,768]{3,2,1,0:T(8,128)(2,1)}, bf16[2,2,96,768]{3,2,1,0:T(8,128)(2,1)S(1)}, u32[]{:S(2)}, u32[]{:S(2)}) collective-permute-start(bf16[2,2,96,768]{3,2,1,0:T(8,128)(2,1)} %get-tuple-element.245), channel_id=1, source_target_pairs={{0,16},{4,20},{8,24},{12,28},{16,0},{20,4},{24,8},{28,12},{1,17},{... | collective-permute-start | bytes 1769480 | tf_op jit(solution)/shard_map/ppermute | solution.py:760
  298.6 27.2 %collective-permute-start.34 = (bf16[2,2,96,768]{3,2,1,0:T(8,128)(2,1)}, bf16[2,2,96,768]{3,2,1,0:T(8,128)(2,1)S(1)}, u32[]{:S(2)}, u32[]{:S(2)}) collective-permute-start(bf16[2,2,96,768]{3,2,1,0:T(8,128)(2,1)} %get-tuple-element.244), channel_id=1, source_target_pairs={{0,8},{4,12},{8,0},{12,4},{16,24},{20,28},{24,16},{28,20},{1,9},{5... | collective-permute-start | bytes 1769480 | tf_op jit(solution)/shard_map/ppermute | solution.py:760
  300.8 29.8 %collective-permute-start.38 = (bf16[2,2,96,768]{3,2,1,0:T(8,128)(2,1)}, bf16[2,2,96,768]{3,2,1,0:T(8,128)(2,1)}, u32[]{:S(2)}, u32[]{:S(2)}) collective-permute-start(bf16[2,2,96,768]{3,2,1,0:T(8,128)(2,1)} %get-tuple-element.241), channel_id=1, source_target_pairs={{0,16},{4,20},{8,24},{12,28},{16,0},{20,4},{24,8},{28,12},{1,17},{... | collective-permute-start | bytes 1769480 | tf_op jit(solution)/shard_map/ppermute | solution.py:760
  301.8 28.7 %collective-permute-start.39 = (bf16[2,2,96,768]{3,2,1,0:T(8,128)(2,1)}, bf16[2,2,96,768]{3,2,1,0:T(8,128)(2,1)}, u32[]{:S(2)}, u32[]{:S(2)}) collective-permute-start(bf16[2,2,96,768]{3,2,1,0:T(8,128)(2,1)} %get-tuple-element.240), channel_id=1, source_target_pairs={{0,8},{4,12},{8,0},{12,4},{16,24},{20,28},{24,16},{28,20},{1,9},{5... | collective-permute-start | bytes 1769480 | tf_op jit(solution)/shard_map/ppermute | solution.py:760
  328.6 29.5 %collective-permute-start.36 = (bf16[2,96,768]{2,1,0:T(8,128)(2,1)}, bf16[2,96,768]{2,1,0:T(8,128)(2,1)}, u32[]{:S(2)}, u32[]{:S(2)}) collective-permute-start(bf16[2,96,768]{2,1,0:T(8,128)(2,1)} %get-tuple-element.243), channel_id=1, source_target_pairs={{0,8},{4,12},{8,0},{12,4},{16,24},{20,28},{24,16},{28,20},{1,9},{5... | collective-permute-start | bytes 884744 | tf_op jit(solution)/shard_map/ppermute | solution.py:760
  329.6 28.5 %collective-permute-start.37 = (bf16[2,96,768]{2,1,0:T(8,128)(2,1)}, bf16[2,96,768]{2,1,0:T(8,128)(2,1)}, u32[]{:S(2)}, u32[]{:S(2)}) collective-permute-start(bf16[2,96,768]{2,1,0:T(8,128)(2,1)} %get-tuple-element.242), channel_id=1, source_target_pairs={{0,16},{4,20},{8,24},{12,28},{16,0},{20,4},{24,8},{28,12},{1,17},{... | collective-permute-start | bytes 884744 | tf_op jit(solution)/shard_map/ppermute | solution.py:760
  332.9 51.0 %collective-permute-start.41 = (bf16[2,96,768]{2,1,0:T(8,128)(2,1)}, bf16[2,96,768]{2,1,0:T(8,128)(2,1)S(1)}, u32[]{:S(2)}, u32[]{:S(2)}) collective-permute-start(bf16[2,96,768]{2,1,0:T(8,128)(2,1)} %get-tuple-element.238), channel_id=1, source_target_pairs={{0,16},{4,20},{8,24},{12,28},{16,0},{20,4},{24,8},{28,12},{1,17},{... | collective-permute-start | bytes 884744 | tf_op jit(solution)/shard_map/ppermute | solution.py:760
  334.0 49.9 %collective-permute-start.40 = (bf16[2,96,768]{2,1,0:T(8,128)(2,1)}, bf16[2,96,768]{2,1,0:T(8,128)(2,1)S(1)}, u32[]{:S(2)}, u32[]{:S(2)}) collective-permute-start(bf16[2,96,768]{2,1,0:T(8,128)(2,1)} %get-tuple-element.239), channel_id=1, source_target_pairs={{0,8},{4,12},{8,0},{12,4},{16,24},{20,28},{24,16},{28,20},{1,9},{5... | collective-permute-start | bytes 884744 | tf_op jit(solution)/shard_map/ppermute | solution.py:760
  360.0 23.9 %collective-permute-start.45 = (bf16[96,768]{1,0:T(8,128)(2,1)S(1)}, bf16[96,768]{1,0:T(8,128)(2,1)S(1)}, u32[]{:S(2)}, u32[]{:S(2)}) collective-permute-start(bf16[96,768]{1,0:T(8,128)(2,1)S(1)} %get-tuple-element.267), channel_id=1, source_target_pairs={{0,1},{1,2},{2,3},{3,0},{4,5},{5,6},{6,7},{7,4},{8,9},{9,10},{10,1... | collective-permute-start | bytes 442376 | tf_op jit(solution)/shard_map/ppermute | solution.py:765
  366.1 17.8 %collective-permute-start.46 = (bf16[96,768]{1,0:T(8,128)(2,1)S(1)}, bf16[96,768]{1,0:T(8,128)(2,1)S(1)}, u32[]{:S(2)}, u32[]{:S(2)}) collective-permute-start(bf16[96,768]{1,0:T(8,128)(2,1)S(1)} %get-tuple-element.268), channel_id=1, source_target_pairs={{0,2},{1,3},{2,0},{3,1},{4,6},{5,7},{6,4},{7,5},{8,10},{9,11},{10,... | collective-permute-start | bytes 442376 | tf_op jit(solution)/shard_map/ppermute | solution.py:765
  367.1 16.9 %collective-permute-start.47 = (bf16[96,768]{1,0:T(8,128)(2,1)S(1)}, bf16[96,768]{1,0:T(8,128)(2,1)S(1)}, u32[]{:S(2)}, u32[]{:S(2)}) collective-permute-start(bf16[96,768]{1,0:T(8,128)(2,1)S(1)} %get-tuple-element.266), channel_id=1, source_target_pairs={{0,3},{1,0},{2,1},{3,2},{4,7},{5,4},{6,5},{7,6},{8,11},{9,8},{10,9... | collective-permute-start | bytes 442376 | tf_op jit(solution)/shard_map/ppermute | solution.py:765
  398.2 32.4 %collective-permute-start.48 = (bf16[4,4,96,768]{3,2,1,0:T(8,128)(2,1)}, bf16[4,4,96,768]{3,2,1,0:T(8,128)(2,1)S(1)}, u32[]{:S(2)}, u32[]{:S(2)}) collective-permute-start(bf16[4,4,96,768]{3,2,1,0:T(8,128)(2,1)} %get-tuple-element.181), channel_id=1, source_target_pairs={{0,4},{4,0},{8,12},{12,8},{16,20},{20,16},{24,28},{28,24},{1,5},{5... | collective-permute-start | bytes 7077896 | tf_op jit(solution)/shard_map/ppermute | solution.py:760
  400.3 8.7 %collective-permute-start.42 = (bf16[96,768]{1,0:T(8,128)(2,1)S(1)}, bf16[96,768]{1,0:T(8,128)(2,1)S(1)}, u32[]{:S(2)}, u32[]{:S(2)}) collective-permute-start(bf16[96,768]{1,0:T(8,128)(2,1)S(1)} %get-tuple-element.270), channel_id=1, source_target_pairs={{0,1},{1,2},{2,3},{3,0},{4,5},{5,6},{6,7},{7,4},{8,9},{9,10},{10,1... | collective-permute-start | bytes 442376 | tf_op jit(solution)/shard_map/ppermute | solution.py:765
  400.3 14.0 %collective-permute-start.43 = (bf16[96,768]{1,0:T(8,128)(2,1)S(1)}, bf16[96,768]{1,0:T(8,128)(2,1)S(1)}, u32[]{:S(2)}, u32[]{:S(2)}) collective-permute-start(bf16[96,768]{1,0:T(8,128)(2,1)S(1)} %get-tuple-element.271), channel_id=1, source_target_pairs={{0,2},{1,3},{2,0},{3,1},{4,6},{5,7},{6,4},{7,5},{8,10},{9,11},{10,... | collective-permute-start | bytes 442376 | tf_op jit(solution)/shard_map/ppermute | solution.py:765
  401.4 13.0 %collective-permute-start.44 = (bf16[96,768]{1,0:T(8,128)(2,1)S(1)}, bf16[96,768]{1,0:T(8,128)(2,1)S(1)}, u32[]{:S(2)}, u32[]{:S(2)}) collective-permute-start(bf16[96,768]{1,0:T(8,128)(2,1)S(1)} %get-tuple-element.269), channel_id=1, source_target_pairs={{0,3},{1,0},{2,1},{3,2},{4,7},{5,4},{6,5},{7,6},{8,11},{9,8},{10,9... | collective-permute-start | bytes 442376 | tf_op jit(solution)/shard_map/ppermute | solution.py:765
  440.5 34.2 %collective-permute-start.51 = (bf16[4,4,96,768]{3,2,1,0:T(8,128)(2,1)}, bf16[4,4,96,768]{3,2,1,0:T(8,128)(2,1)}, u32[]{:S(2)}, u32[]{:S(2)}) collective-permute-start(bf16[4,4,96,768]{3,2,1,0:T(8,128)(2,1)} %get-tuple-element.188), channel_id=1, source_target_pairs={{0,4},{4,0},{8,12},{12,8},{16,20},{20,16},{24,28},{28,24},{1,5},{5... | collective-permute-start | bytes 7077896 | tf_op jit(solution)/shard_map/ppermute | solution.py:760
  440.5 84.6 %all-to-all-start.1 = ((bf16[4,375,768]{2,1,0:T(8,128)(2,1)}), bf16[4,375,768]{2,1,0:T(8,128)(2,1)}, u32[]{:S(2)}, u32[]{:S(2)}) async-start(bf16[4,375,768]{2,1,0:T(8,128)(2,1)} %get-tuple-element.187), calls=%async_computation.1 | async-start | bytes 4620288 | tf_op jit(solution)/shard_map/all_to_all | solution.py:1080
  448.0 15.8 %collective-permute-start.49 = (bf16[2,2,96,768]{3,2,1,0:T(8,128)(2,1)}, bf16[2,2,96,768]{3,2,1,0:T(8,128)(2,1)S(1)}, u32[]{:S(2)}, u32[]{:S(2)}) collective-permute-start(bf16[2,2,96,768]{3,2,1,0:T(8,128)(2,1)} %get-tuple-element.233), channel_id=1, source_target_pairs={{0,16},{4,20},{8,24},{12,28},{16,0},{20,4},{24,8},{28,12},{1,17},{... | collective-permute-start | bytes 1769480 | tf_op jit(solution)/shard_map/ppermute | solution.py:760
  449.4 15.5 %collective-permute-start.50 = (bf16[2,2,96,768]{3,2,1,0:T(8,128)(2,1)}, bf16[2,2,96,768]{3,2,1,0:T(8,128)(2,1)S(1)}, u32[]{:S(2)}, u32[]{:S(2)}) collective-permute-start(bf16[2,2,96,768]{3,2,1,0:T(8,128)(2,1)} %get-tuple-element.232), channel_id=1, source_target_pairs={{0,8},{4,12},{8,0},{12,4},{16,24},{20,28},{24,16},{28,20},{1,9},{5... | collective-permute-start | bytes 1769480 | tf_op jit(solution)/shard_map/ppermute | solution.py:760
  476.5 26.2 %collective-permute-start.54 = (bf16[2,2,96,768]{3,2,1,0:T(8,128)(2,1)S(1)}, bf16[2,2,96,768]{3,2,1,0:T(8,128)(2,1)S(1)}, u32[]{:S(2)}, u32[]{:S(2)}) collective-permute-start(bf16[2,2,96,768]{3,2,1,0:T(8,128)(2,1)S(1)} %get-tuple-element.230), channel_id=1, source_target_pairs={{0,8},{4,12},{8,0},{12,4},{16,24},{20,28},{24,16},{28,20},{1,9},{5... | collective-permute-start | bytes 1769480 | tf_op jit(solution)/shard_map/ppermute | solution.py:760
  477.1 25.6 %collective-permute-start.52 = (bf16[2,2,96,768]{3,2,1,0:T(8,128)(2,1)S(1)}, bf16[2,2,96,768]{3,2,1,0:T(8,128)(2,1)S(1)}, u32[]{:S(2)}, u32[]{:S(2)}) collective-permute-start(bf16[2,2,96,768]{3,2,1,0:T(8,128)(2,1)S(1)} %get-tuple-element.231), channel_id=1, source_target_pairs={{0,16},{4,20},{8,24},{12,28},{16,0},{20,4},{24,8},{28,12},{1,17},{... | collective-permute-start | bytes 1769480 | tf_op jit(solution)/shard_map/ppermute | solution.py:760
  483.6 22.1 %collective-permute-start.60 = (bf16[2,96,768]{2,1,0:T(8,128)(2,1)S(1)}, bf16[2,96,768]{2,1,0:T(8,128)(2,1)S(1)}, u32[]{:S(2)}, u32[]{:S(2)}) collective-permute-start(bf16[2,96,768]{2,1,0:T(8,128)(2,1)S(1)} %get-tuple-element.224), channel_id=1, source_target_pairs={{0,16},{4,20},{8,24},{12,28},{16,0},{20,4},{24,8},{28,12},{1,17},{... | collective-permute-start | bytes 884744 | tf_op jit(solution)/shard_map/ppermute | solution.py:760
  484.6 21.1 %collective-permute-start.59 = (bf16[2,96,768]{2,1,0:T(8,128)(2,1)S(1)}, bf16[2,96,768]{2,1,0:T(8,128)(2,1)S(1)}, u32[]{:S(2)}, u32[]{:S(2)}) collective-permute-start(bf16[2,96,768]{2,1,0:T(8,128)(2,1)S(1)} %get-tuple-element.225), channel_id=1, source_target_pairs={{0,8},{4,12},{8,0},{12,4},{16,24},{20,28},{24,16},{28,20},{1,9},{5... | collective-permute-start | bytes 884744 | tf_op jit(solution)/shard_map/ppermute | solution.py:760
  486.1 14.2 %collective-permute-start.66 = (f32[24,768]{1,0:T(8,128)S(1)}, f32[24,768]{1,0:T(8,128)S(1)}, u32[]{:S(2)}, u32[]{:S(2)}) collective-permute-start(f32[24,768]{1,0:T(8,128)S(1)} %add.488), channel_id=1, source_target_pairs={{0,8},{4,12},{8,0},{12,4},{16,24},{20,28},{24,16},{28,20},{1,9},{5... | collective-permute-start | bytes 221192 | tf_op jit(solution)/shard_map/ppermute | solution.py:760
  504.0 11.2 %collective-permute-start.55 = (bf16[2,96,768]{2,1,0:T(8,128)(2,1)S(1)}, bf16[2,96,768]{2,1,0:T(8,128)(2,1)S(1)}, u32[]{:S(2)}, u32[]{:S(2)}) collective-permute-start(bf16[2,96,768]{2,1,0:T(8,128)(2,1)S(1)} %get-tuple-element.228), channel_id=1, source_target_pairs={{0,16},{4,20},{8,24},{12,28},{16,0},{20,4},{24,8},{28,12},{1,17},{... | collective-permute-start | bytes 884744 | tf_op jit(solution)/shard_map/ppermute | solution.py:760
  504.8 10.4 %collective-permute-start.53 = (bf16[2,96,768]{2,1,0:T(8,128)(2,1)S(1)}, bf16[2,96,768]{2,1,0:T(8,128)(2,1)S(1)}, u32[]{:S(2)}, u32[]{:S(2)}) collective-permute-start(bf16[2,96,768]{2,1,0:T(8,128)(2,1)S(1)} %get-tuple-element.229), channel_id=1, source_target_pairs={{0,8},{4,12},{8,0},{12,4},{16,24},{20,28},{24,16},{28,20},{1,9},{5... | collective-permute-start | bytes 884744 | tf_op jit(solution)/shard_map/ppermute | solution.py:760
  507.9 11.6 %collective-permute-start.63 = (bf16[96,768]{1,0:T(8,128)(2,1)S(1)}, bf16[96,768]{1,0:T(8,128)(2,1)S(1)}, u32[]{:S(2)}, u32[]{:S(2)}) collective-permute-start(bf16[96,768]{1,0:T(8,128)(2,1)S(1)} %get-tuple-element.262), channel_id=1, source_target_pairs={{0,3},{1,0},{2,1},{3,2},{4,7},{5,4},{6,5},{7,6},{8,11},{9,8},{10,9... | collective-permute-start | bytes 442376 | tf_op jit(solution)/shard_map/ppermute | solution.py:765
  511.6 20.6 %collective-permute-start.62 = (bf16[96,768]{1,0:T(8,128)(2,1)}, bf16[96,768]{1,0:T(8,128)(2,1)}, u32[]{:S(2)}, u32[]{:S(2)}) collective-permute-start(bf16[96,768]{1,0:T(8,128)(2,1)} %get-tuple-element.261), channel_id=1, source_target_pairs={{0,2},{1,3},{2,0},{3,1},{4,6},{5,7},{6,4},{7,5},{8,10},{9,11},{10,... | collective-permute-start | bytes 442376 | tf_op jit(solution)/shard_map/ppermute | solution.py:765
  513.7 18.5 %collective-permute-start.61 = (bf16[96,768]{1,0:T(8,128)(2,1)}, bf16[96,768]{1,0:T(8,128)(2,1)}, u32[]{:S(2)}, u32[]{:S(2)}) collective-permute-start(bf16[96,768]{1,0:T(8,128)(2,1)} %get-tuple-element.260), channel_id=1, source_target_pairs={{0,1},{1,2},{2,3},{3,0},{4,5},{5,6},{6,7},{7,4},{8,9},{9,10},{10,1... | collective-permute-start | bytes 442376 | tf_op jit(solution)/shard_map/ppermute | solution.py:765
  516.8 15.4 %collective-permute-start.58 = (bf16[96,768]{1,0:T(8,128)(2,1)S(1)}, bf16[96,768]{1,0:T(8,128)(2,1)S(1)}, u32[]{:S(2)}, u32[]{:S(2)}) collective-permute-start(bf16[96,768]{1,0:T(8,128)(2,1)S(1)} %get-tuple-element.265), channel_id=1, source_target_pairs={{0,3},{1,0},{2,1},{3,2},{4,7},{5,4},{6,5},{7,6},{8,11},{9,8},{10,9... | collective-permute-start | bytes 442376 | tf_op jit(solution)/shard_map/ppermute | solution.py:765
  519.2 18.0 %collective-permute-start.57 = (bf16[96,768]{1,0:T(8,128)(2,1)S(1)}, bf16[96,768]{1,0:T(8,128)(2,1)S(1)}, u32[]{:S(2)}, u32[]{:S(2)}) collective-permute-start(bf16[96,768]{1,0:T(8,128)(2,1)S(1)} %get-tuple-element.264), channel_id=1, source_target_pairs={{0,2},{1,3},{2,0},{3,1},{4,6},{5,7},{6,4},{7,5},{8,10},{9,11},{10,... | collective-permute-start | bytes 442376 | tf_op jit(solution)/shard_map/ppermute | solution.py:765
  519.5 17.7 %collective-permute-start.56 = (bf16[96,768]{1,0:T(8,128)(2,1)S(1)}, bf16[96,768]{1,0:T(8,128)(2,1)S(1)}, u32[]{:S(2)}, u32[]{:S(2)}) collective-permute-start(bf16[96,768]{1,0:T(8,128)(2,1)S(1)} %get-tuple-element.263), channel_id=1, source_target_pairs={{0,1},{1,2},{2,3},{3,0},{4,5},{5,6},{6,7},{7,4},{8,9},{9,10},{10,1... | collective-permute-start | bytes 442376 | tf_op jit(solution)/shard_map/ppermute | solution.py:765
  (63 other events, 544.5 us)

commit v3 on v2

--- a/solution.py
+++ b/solution.py
@@ -11,6 +11,7 @@
 EPSILON = 1e-05
 NEGATIVE = -1e30
 VMEM_LIMIT = 60 * 2**20
+HINT = 20
 BF = jnp.bfloat16
 F32 = jnp.float32
 
@@ -90,7 +91,7 @@
             dimension_semantics=("arbitrary",), vmem_limit_bytes=VMEM_LIMIT
         ),
         input_output_aliases={first + i: i for i in range(len(carried))},
-        cost_estimate=pl.CostEstimate(flops=flops, bytes_accessed=moved, transcendentals=0),
+        cost_estimate=pl.CostEstimate(flops=HINT * flops, bytes_accessed=moved, transcendentals=0),
         name=name,
     )(*scalars, *[a for a, _ in ins], *extra)
 
@@ -101,7 +102,7 @@
 
 
 def pack_in(pack):
-    return [(array, packed(array.shape)) for array in pack]
+    return pack_at(pack, 0)
 
 
 def at_block(shape, start):
@@ -242,15 +243,29 @@
     )
 
 
-def frame_keys(place, frames, pack, own, head_bias, dims, deps=()):
+def frame_keys(place, frames, pack, own, head_bias, piece, dims, deps=()):
     seq, width, blocks, hw = dims
-    pieces, piece, _ = frames.shape
+    pieces = len(frames)
+    valid = sum(part.shape[0] for part in frames[0])
+    parts = [part for group in frames for part in group]
     total = pieces * piece
-
-    def body(place_ref, e_ref, *refs):
+    edge = valid // 16 * 16
+
+    def body(place_ref, *refs):
+        f_refs, refs = list(refs[: len(parts)]), refs[len(parts) :]
         w_refs, refs = refs[: len(pack)], refs[len(pack) :]
-        hb_ref, k_ref, v_ref, kt_ref, vt_ref, w_scr = refs
+        hb_ref, k_ref, v_ref, kt_ref, vt_ref, e_ref, w_scr = refs
         assemble(w_refs, own, place_ref, w_scr)
+
+        @pl.when(pl.program_id(0) == 0)
+        def _():
+            for c in range(pieces):
+                e_ref[c, edge:] = jnp.zeros((piece - edge, width), BF)
+                at = 0
+                for part in frames[c]:
+                    e_ref[c, at : at + part.shape[0]] = f_refs.pop(0)[...]
+                    at += part.shape[0]
+
         w = w_scr[:, : 2 * hw]
         for c in range(pieces):
             kv = dot(e_ref[c], w)
@@ -263,10 +278,11 @@
 
     kv = sds((blocks, pieces, piece, hw), BF)
     kvt = sds((blocks, hw, total), BF)
+    padded = sds((pieces, piece, width), BF)
     return call(
         body, "frame_keys", blocks,
-        [(frames, whole(frames.shape)), *pack_in(pack), (head_bias, per_block(head_bias.shape))],
-        [(kv, per_block(kv.shape))] * 2 + [(kvt, per_block(kvt.shape))] * 2,
+        [(part, whole(part.shape)) for part in parts] + [*pack_in(pack), (head_bias, per_block(head_bias.shape))],
+        [(kv, per_block(kv.shape))] * 2 + [(kvt, per_block(kvt.shape))] * 2 + [(padded, whole(padded.shape))],
         [pack_scratch(width)],
         4 * total * width * width,
         (place,),
@@ -576,7 +592,8 @@
 
         @pl.when(t == blocks - 1)
         def _():
-            genc_ref[...] = genc_scr[:, :valid].astype(BF)
+            for c in range(pieces):
+                genc_ref[lax.rem(place_ref[1] + pieces - c, pieces)] = genc_scr[c, :valid].astype(BF)
             grad = acc_scr[...]
             unit, inverse = layer_norm_parts(first_ref[...])
             sum_ref[1:2] = column_sum(grad * unit)
@@ -785,51 +802,29 @@
 class Gather:
     def __init__(self, shard):
         self.shard = shard
-        self.here = lax.axis_index("tp")
-
-    def after(self, names, things):
-        for name in names.split():
-            setattr(self, name, gate(getattr(self, name), things))
 
     def direct(self):
-        self.line = in_order([self.shard] + [around(self.shard, hop) for hop in range(1, 4)], self.here)
-        return (self.line,)
-
-    def pair(self):
-        self.come = lax.ppermute(self.shard, "tp", [(i, i ^ 1) for i in range(4)])
-        return (self.come,)
-
-    def middle(self):
-        odd = self.here % 2 == 1
-        first, last = jnp.where(odd, self.come, self.shard), jnp.where(odd, self.shard, self.come)
-        self.near = jnp.stack([first, last])
-        self.inner = lax.ppermute(self.near, "tp", [(1, 2), (2, 1)])
-        return (self.inner,)
-
-    def ends(self):
-        outer = lax.ppermute(self.inner, "tp", [(1, 0), (2, 3)])
-        far = jnp.where((self.here == 1) | (self.here == 2), self.inner, outer)
-        upper = self.here >= 2
-        self.line = jnp.concatenate([jnp.where(upper, far, self.near), jnp.where(upper, self.near, far)])
-        return (outer,)
+        come = [around(self.shard, hop) for hop in range(1, 4)]
+        line = in_order([self.shard] + come, lax.axis_index("tp"))
+        self.low, self.high = line[None, :2], line[None, 2:]
+        return tuple(come)
 
     def first(self):
-        self.low, self.high = self.line[None, :2], self.line[None, 2:]
         self.low_x, self.high_y = swap(self.low, 2), swap(self.high, 4)
         return self.low_x, self.high_y
 
     def second(self):
-        low = jnp.concatenate([self.low, self.low_x])
-        high = jnp.concatenate([self.high, self.high_y])
-        low_y, high_x = swap(low, 4), swap(high, 2)
-        low = jnp.concatenate([low, low_y])
-        high = jnp.stack([high[0], high_x[0], high[1], high_x[1]])
-        self.mine = jnp.concatenate([low, high], 1)
-        return low_y, high_x
+        self.low_two = jnp.concatenate([self.low, self.low_x])
+        self.high_two = jnp.concatenate([self.high, self.high_y])
+        self.low_y, self.high_x = swap(self.low_two, 4), swap(self.high_two, 2)
+        return self.low_y, self.high_x
 
     def core(self):
-        self.pack = (self.mine, swap(self.mine, 1))
-        return self.pack
+        low = jnp.concatenate([self.low_two, self.low_y])
+        high = jnp.stack([self.high_two[0], self.high_x[0], self.high_two[1], self.high_x[1]])
+        mine = jnp.concatenate([low, high], 1)
+        self.pack = (mine, swap(mine, 1))
+        return self.pack[1:]
 
 
 def wide(array):
@@ -931,7 +926,7 @@
     fsdp, tp = lax.axis_size("fsdp"), lax.axis_size("tp")
     devices = fsdp * tp
     tp_place = lax.axis_index("tp")
-    place = lax.axis_index("fsdp").reshape(1)
+    place = jnp.stack([lax.axis_index("fsdp"), tp_place])
     seqs, seq, width = inputs.shape
     assert seqs == 1
     own, hw = cross_q.shape
@@ -955,35 +950,36 @@
     x = inputs[0]
     length = lax.dynamic_slice_in_dim(lengths, tp_place, 1)
     chains = {}
-    sends = {"direct": "shard", "pair": "shard", "middle": "come", "ends": "inner", "first": "line",
-             "second": "low_x high_y", "core": "mine"}
+    sends = {"direct": "shard", "first": "low high", "second": "low_x high_y", "core": "low_y high_x"}
 
     def move(after, *steps):
-        if not chained:
-            return ()
         out = ()
-        for text in steps:
+        for text in steps if chained else ():
             name, step = text.split(".")
-            if step != "core":
-                chains[name].after(sends[step], after)
-            else:
-                chains[name].mine = gate(chains[name].mine, after)
-            out += tuple(getattr(chains[name], step)())
+            chain = chains[name]
+            for array in sends[step].split():
+                setattr(chain, array, gate(getattr(chain, array), after))
+            out += getattr(chain, step)()
         return out
 
-    frames = encoder
+    frames = [
+        lax.dynamic_index_in_dim(encoder, (tp_place + hop) % tp, 0, keepdims=False) for hop in range(tp)
+    ]
+    before = turn = ()
     if chained:
         for name, shard in (("self", pack_self), ("cross", pack_cross), ("in", fc_in), ("out", fc_out.T)):
             chains[name] = Gather(shard)
-        moved = move((), "self.direct")
-        side = move((), "cross.pair")
-        frames = gate(frames, moved)
-        more = move(moved, "self.first")
-        side = move(moved + side, "cross.middle")
-        moved = move(more, "self.second")
-        side = move(more + side, "cross.ends", "in.pair")
-        more = move(moved, "self.core")
-        moved = move(moved + side, "cross.first", "in.middle", "out.pair") + more[1:]
+        turn = move((), "self.direct") + tuple(frames)
+        turn = move(turn, "self.first", "cross.direct")
+        turn = move(turn, "self.second", "in.direct")
+        frames[1] = around(gate(frames[1], turn), 1)
+        turn = move(turn, "self.core", "cross.first") + (frames[1],)
+        before = turn
+        edge = frames_own // 32 * 16
+        frames[3] = around(gate(frames[3], turn), 3)
+        near, far = frames[2][:edge], frames[2][edge:]
+        near = around(gate(near, turn), 2)
+        turn = move(turn, "cross.second", "in.first") + (frames[3], near)
         w_self = chains["self"].pack
         own_rows = own
         grad_shape = (fsdp // 2, tp, own, width)
@@ -994,8 +990,6 @@
         )
         table = wide(table).sum(2).reshape(devices, width)
     else:
-        moved = ()
-        more = ()
         w_self = native_gather(pack_self)
         table = wide(w_self[:, :, own : own + 2]).sum(2).reshape(devices, width)
         own_rows = own * fsdp
@@ -1019,28 +1013,27 @@
     params = pad_rows(jnp.concatenate([params, fc_bias], 0), 24)
 
     piece = -(-frames_own // 128) * 128
-    frames = lax.all_to_all(frames, "tp", 0, 0, tiled=True)
-    frames = jnp.pad(frames, ((0, 0), (0, piece - frames_own), (0, 0)))
     half = tp // 2
 
-    later = move(moved, "cross.second", "in.ends", "out.middle")
-    shared = (w_self, own_rows, params, head_bias, dims)
-    *kept, part, _ = self_forward(length, place, 0, half, x, x, *shared, moved)
-    moved = move(later + (part,), "cross.core", "in.first", "out.ends")
     q1, k1, v1, lse1, ot1, mixed1, n1, first, n2 = self_forward(
-        length, place, half, tp - half, x, part, *shared, later, kept[:-1]
-    )
+        length, place, 0, tp, x, x, w_self, own_rows, params, head_bias, dims, before
+    )
+    turn += (n2,)
     if chained:
+        far = around(gate(far, turn), 2)
+        turn = move(turn, "cross.core", "in.second") + (far,)
         w_cross = chains["cross"].pack
-    later = move(moved + (n2,), "in.second", "out.first")
-    k2, v2, k2t, v2t = frame_keys(place, frames, w_cross, own_rows, head_bias, dims, (n2,) + moved)
-    moved = move(later + (k2,), "in.core", "out.second")
+        frames = [(frames[0],), (frames[1],), (near, far), (frames[3],)]
+    else:
+        frames = [(around(array, hop) if hop else array,) for hop, array in enumerate(frames)]
+    k2, v2, k2t, v2t, frames = frame_keys(place, frames, w_cross, own_rows, head_bias, piece, dims, turn)
+    turn = move(turn, "in.core", "out.direct") + (k2,)
     shared = (w_cross, own_rows, params, head_bias, k2, v2t, frames_own, dims)
-    *kept, part, _ = cross_forward(place, 0, half, n2, first, *shared, later)
-    later = move(moved + (part,), "out.core")
-    q2, lse2, ot2, mixed2, second, n3 = cross_forward(
-        place, half, tp - half, n2, part, *shared, moved, kept
-    )
+    *kept, part, _ = cross_forward(place, 0, half, n2, first, *shared, turn)
+    turn = move(turn, "out.first") + (part,)
+    q2, lse2, ot2, mixed2, second, n3 = cross_forward(place, half, tp - half, n2, part, *shared, turn, kept)
+    turn = move(turn, "out.second") + (n3,)
+    move(turn, "out.core")
     if chained:
         w_in, w_out = chains["in"].pack, chains["out"].pack
     hidden, slope, layer_out, g3, b3, sums = feed_forward(
@@ -1074,10 +1067,10 @@
     grad_frames, g1, b1, sums = cross_rows_back(
         place, sums, dq2, dkv2, g2, first, w_cross, own_rows, params, frames_own, dims, step3
     )
+    grad_cross = cross_grads(place, dq2, dkv2, mixed2, b2, n2, frames, grad_shape, dims, step4 + (b1,))
     step5 = go("in", "line")
-    grad_cross = cross_grads(place, dq2, dkv2, mixed2, b2, n2, frames, grad_shape, dims, step4 + (b1,))
     begin("cross", grad_cross)
-    frames_back = lax.all_to_all(gate(grad_frames, (grad_cross[0],)), "tp", 0, 0, tiled=True)
+    frames_back = lax.all_to_all(gate(grad_frames, (grad_cross[0], *step5)), "tp", 0, 0, tiled=True)
     step6 = go("cross", "core")
     dqkv1, sums = self_attend_back(
         length, place, sums, b1, q1, k1, v1, lse1, ot1, w_self, own_rows, dims, step5 + (grad_cross[0],)
@@ -1089,13 +1082,21 @@
     grad_inputs, sums = self_rows_back(
         place, sums, dqkv1, g1, x, w_self, own_rows, params, dims, step7 + (grad_self[0],)
     )
-    go("cross", "second")
-
-    for step in range(max(fsdp, tp)):
-        if 2**step < fsdp:
-            sums = sums + swap(sums, 2**step)
-        if 2**step < tp:
-            sums = sums + lax.ppermute(sums, "tp", [(i, i ^ 2**step) for i in range(tp)])
+    turns = [(), (), (), ()]
+    if chained:
+        scatters["cross"].low_y = gate(scatters["cross"].low_y, (grad_self[0],))
+        step8 = go("cross", "second")
+        scatters["self"].come = gate(scatters["self"].come, (sums, *step8))
+        scatters["cross"].low_x = gate(scatters["cross"].low_x, (sums, *step8))
+        turns[2] = go("self", "first") + go("cross", "line")
+        scatters["self"].low_y = gate(scatters["self"].low_y, turns[2])
+        turns[3] = go("self", "second")
+    step = 1
+    while step < fsdp:
+        sums = sums + swap(gate(sums, turns.pop(0) if turns else ()), step)
+        step *= 2
+    sums = gate(sums, turns.pop(0) if turns else ())
+    sums = sum([around(sums, hop) for hop in range(1, tp)], sums)
     device = lax.axis_index("fsdp") * tp + tp_place
     mine = lax.dynamic_slice_in_dim(sums[:rows], device * small_own, small_own, 1)
     gains = norm_gain.shape[0]
@@ -1106,9 +1107,6 @@
     )[0]
 
     if chained:
-        go("self", "first")
-        go("cross", "line")
-        go("self", "second")
         go("self", "line")
         total_out, total_in, total_cross, total_self = (
             scatters[name].total() for name in ("out", "in", "cross", "self")

time: 552 us -> 494 us (0.89)
  waiting for transfers between devices: 132 us -> 80.1 us
  starting transfers between devices: 107 us -> 93.1 us
    ppermute x11 -> x0, waiting for transfers between devices: 45.3 us -> none  [the longest x3 45.3 us: pair(): self.come = lax.ppermute(self.shard, 'tp', [(i, i ^ 1) for i in range(4)])]
    ppermute x43, waiting for transfers between devices: 55.9 us -> 14.5 us  [swap(): return lax.ppermute(array, 'fsdp', [(i, i ^ step) for i in range(count)])]
    ppermute x15 -> x31, waiting for transfers between devices: 31.1 us -> 65.5 us  [around(): lax.ppermute(array, 'tp', [(i, (i + hop) % count) for i in range(count)])]
    ppermute x11 -> x0, starting transfers between devices: 21.3 us -> none  [the longest x3 8.16 us: pair(): self.come = lax.ppermute(self.shard, 'tp', [(i, i ^ 1) for i in range(4)])]
    ppermute x15 -> x31, starting transfers between devices: 31.8 us -> 52.8 us  [around(): lax.ppermute(array, 'tp', [(i, (i + hop) % count) for i in range(count)])]
    all_to_all x2 -> x1, starting transfers between devices: 18.5 us -> 4.72 us  [local(): lax.all_to_all(gate(grad_frames, (grad_cross[0], *step5)), 'tp', 0, 0, ti...]
    dynamic_slice x0 -> x1, local copies, waits for them, and re-layouts: none -> 8.41 us  [local(): lax.dynamic_index_in_dim(encoder, (tp_place + hop) % tp, 0, keepdims=False)]
    concatenate x15 -> x12, other arithmetic: 12.6 us -> 7.09 us  [the longest x4 4.99 us: core(): mine = jnp.concatenate([low, high], 1)]
  transfers between devices with their start and end apart: 71 -> 75, of which waited for: 21 -> 20; matrix products, arithmetic and copies ran while one was open for 12% -> 14% of each run, Pallas kernels for 32% -> 41%
where the time goes in v3:
time: 494 us; the launch traced here: 486 us
  Pallas kernels  224 us (45%)
  starting transfers between devices  93.1 us (19%)
  waiting for transfers between devices  80.1 us (16%)
  other arithmetic  49.5 us (10%)
  local copies, waits for them, and re-layouts  36.8 us (7%)
    pallas_call x14, Pallas kernels, call(): pl.pallas_call(inner, out_shape=[o for o, _ in outs], grid_spec=pltpu.Pre...  224 us
    ppermute x31, waiting for transfers between devices, around(): lax.ppermute(array, 'tp', [(i, (i + hop) % count) for i in range(count)])  65.5 us
    ppermute x31, starting transfers between devices, around(): lax.ppermute(array, 'tp', [(i, (i + hop) % count) for i in range(count)])  52.8 us
    ppermute x43, starting transfers between devices, swap(): return lax.ppermute(array, 'fsdp', [(i, i ^ step) for i in range(count)])  35.5 us
    unnamed x126, local copies, waits for them, and re-layouts  15.9 us
    ppermute x43, waiting for transfers between devices, swap(): return lax.ppermute(array, 'fsdp', [(i, i ^ step) for i in range(count)])  14.5 us
  transfers between devices with their start and end apart: 75, of which 20 were waited for; matrix products, arithmetic and copies ran while one was open for 14% of the time, Pallas kernels for 41%

profile of v3, /device:TPU:0, one launch (start us, length us, event | category | flops | bytes accessed | tf_op | source)
XLA Modules:
  0.0 485.7 jit_solution(446206041232133766)
XLA Ops:
  7.6 5.1 %collective-permute-start.2 = (bf16[112,768]{1,0:T(8,128)(2,1)}, bf16[112,768]{1,0:T(8,128)(2,1)}, u32[]{:S(2)}, u32[]{:S(2)}) collective-permute-start(bf16[112,768]{1,0:T(8,128)(2,1)} %pad_maximum_fusion.14), channel_id=1, source_target_pairs={{0,3},{1,0},{2,1},{3,2},{4,7},{5,4},{6,5},{7,6},{8,11},{9,8},{10,9... | collective-permute-start | bytes 516104 | tf_op jit(solution)/shard_map/ppermute | solution.py:782
  13.7 8.4 %constant_dynamic-slice_fusion.23 = (bf16[1,375,768]{2,0,1:T(2,128)(2,1)S(1)}, bf16[1,375,768]{2,0,1:T(2,128)(2,1)S(1)}, bf16[1,375,768]{2,0,1:T(2,128)(2,1)S(1)}, bf16[1,375,768]{2,0,1:T(2,128)(2,1)}) fusion(bf16[4,375,768]{2,0,1:T(4,128)(2,1)} %param.16, s32[]{:T(128)S(6)} %select_n.189, s32[]{:T(128)S(6)} %select_n.187, s32[]{:T(128)S(6)} %select_n.185, ...), kind=kLoop, calls=%fused_computation.209 | loop fusion | bytes 4608016 | tf_op jit(solution)/shard_map/jit(dynamic_index_in_dim)/dynamic_slice | solution.py:966
  22.1 2.2 copy.67
  28.9 1.6 collective-permute-start.4
  30.5 1.6 collective-permute-start.3
  32.3 2.0 collective-permute-start.5
  35.2 2.8 collective-permute-start.7
  38.1 2.8 collective-permute-done.5
  40.9 4.5 collective-permute-done.6
  46.7 3.6 collective-permute-start.10
  50.3 1.6 collective-permute-start.11
  52.7 3.4 collective-permute-done.10
  56.1 4.6 collective-permute-done.11
  60.7 2.1 collective-permute-done.9
  63.3 1.9 maximum_maximum_fusion.refs_4_.refs_9_.refs_5_
  67.6 1.6 collective-permute-start.14
  69.6 3.7 collective-permute-start.16
  78.3 8.7 %collective-permute-done.16.refs_11_.refs_2_ = bf16[375,768]{1,0:T(8,128)(2,1)} collective-permute-done((bf16[375,768]{1,0:T(8,128)(2,1)S(1)}, bf16[375,768]{1,0:T(8,128)(2,1)}, u32[]{:S(2)}, u32[]{:S(2)}) %collective-permute-start.16) | collective-permute-done | bytes 576032 | tf_op jit(solution)/shard_map/ppermute | solution.py:782
  95.2 7.6 %collective-permute-done.22.refs_3_ = bf16[176,768]{1,0:T(8,128)(2,1)S(1)} collective-permute-done((bf16[176,768]{1,0:T(8,128)(2,1)}, bf16[176,768]{1,0:T(8,128)(2,1)S(1)}, u32[]{:S(2)}, u32[]{:S(2)}) %collective-permute-start.22) | collective-permute-done | bytes 270368 | tf_op jit(solution)/shard_map/ppermute | solution.py:782
  102.8 1.7 collective-permute-start.21
  104.4 17.9 %self_forward.1 = (bf16[4,448,192]{2,1,0:T(8,128)(2,1)}, bf16[4,448,192]{2,1,0:T(8,128)(2,1)}, bf16[4,448,192]{2,1,0:T(8,128)(2,1)}, f32[4,8,448]{2,1,0:T(8,128)...) custom-call(s32[1]{0:T(128)} %dynamic_slice.145.refs_0_, ...), custom_call_target="tpu_custom_call" | custom-call | flops 91603599360 | bytes 13918208 | tf_op jit(solution)/shard_map/self_forward/pallas_call | solution.py:80
  126.1 1.6 collective-permute-start.26
  127.8 16.4 %collective-permute-done.24.refs_4_.refs_12_ = bf16[199,768]{1,0:T(8,128)(2,1)S(1)} collective-permute-done((bf16[199,768]{1,0:T(8,128)(2,1)S(1)}, bf16[199,768]{1,0:T(8,128)(2,1)S(1)}, u32[]{:S(2)}, u32[]{:S(2)}) %collective-permute-start.24) | collective-permute-done | bytes 305696 | tf_op jit(solution)/shard_map/ppermute | solution.py:782
  145.2 3.0 collective-permute-start.30
  148.7 12.3 %frame_keys.1 = (bf16[4,4,384,192]{3,2,1,0:T(8,128)(2,1)}, bf16[4,4,384,192]{3,2,1,0:T(8,128)(2,1)}, bf16[4,192,1536]{2,1,0:T(8,128)(2,1)}, bf16[4,192,1536]{2,1,0:T(8,128)(2,1)}, bf16[4,384,768]{2,1,0:T(8,128)(2,1)}) custom-call(s32[2]{0:T(128)} %pad_add_fusion.refs_1_.refs_0_, bf16[375,768]{1,0:T(8,128)(2,1)} %bitcast.189, ...), custom_call_target="tpu_custom_call" | custom-call | flops 72477573120 | bytes 18843648 | tf_op jit(solution)/shard_map/frame_keys/pallas_call | solution.py:80
  164.2 19.9 %cross_forward.2 = (bf16[4,448,192]{2,1,0:T(8,128)(2,1)}, f32[4,8,448]{2,1,0:T(8,128)}, f32[4,192,448]{2,1,0:T(8,128)}, bf16[4,448,192]{2,1,0:T(8,128)(2,1)}, f3...) custom-call(s32[2]{0:T(128)} %pad_add_fusion.refs_1_.refs_0_, bf16[448,768]{1,0:T(8,128)(2,1)} %get-tuple-element.119.refs_1_.refs_5_, ...), custom_call_target="tpu_custom_call" | custom-call | flops 95126814720 | bytes 16474112 | tf_op jit(solution)/shard_map/cross_forward/pallas_call | solution.py:80
  186.6 19.9 %cross_forward.3 = (bf16[4,448,192]{2,1,0:T(8,128)(2,1)}, f32[4,8,448]{2,1,0:T(8,128)}, f32[4,192,448]{2,1,0:T(8,128)}, bf16[4,448,192]{2,1,0:T(8,128)(2,1)}, f3...) custom-call(s32[2]{0:T(128)} %pad_add_fusion.refs_1_.refs_0_, ...), custom_call_target="tpu_custom_call", output_to_operand_aliasing={{0}: (9, {}), {1}: (10, {}), {2}: (11, {}), {3}: (12, {})} | custom-call | flops 95126814720 | bytes 16474112 | tf_op jit(solution)/shard_map/cross_forward/pallas_call | solution.py:80
  208.1 4.5 collective-permute-done.35.refs_6_.refs_7_
  214.0 15.5 %feed_forward.1 = (bf16[4,448,768]{2,1,0:T(8,128)(2,1)}, f32[4,448,768]{2,1,0:T(8,128)}, bf16[448,768]{1,0:T(8,128)(2,1)}, f32[448,768]{1,0:T(8,128)}, bf16[448,768]{1,0:T(8,128)(2,1)}, /*index=5*/f32[24,768]{1,0:T(8,128)}) custom-call(s32[2]{0:T(128)} %pad_add_fusion.refs_1_.refs_0_, bf16[448,768]{1,0:T(8,128)(2,1)} %get-tuple-element.144.refs_1_.refs_8_, ...), custom_call_target="tpu_custom_call" | custom-call | flops 84557168640 | bytes 23347200 | tf_op jit(solution)/shard_map/feed_forward/pallas_call | solution.py:80
  229.5 7.8 %feed_out_grads.1 = (bf16[4,4,96,768]{3,2,1,0:T(8,128)(2,1)}, bf16[4,4,96,768]{3,2,1,0:T(8,128)(2,1)}) custom-call(s32[2]{0:T(128)} %pad_add_fusion.refs_1_.refs_0_, bf16[448,768]{1,0:T(8,128)(2,1)} %get-tuple-element.151.refs_1_, bf16[4,448,768]{2,1,0:T(8,128)(2,1)} %get-tuple-element.155.refs_2_), custom_call_target="tpu_custom_call" | custom-call | flops 42278584320 | bytes 8159232 | tf_op jit(solution)/shard_map/feed_out_grads/pallas_call | solution.py:80
  237.4 19.5 %feed_backward.1 = (bf16[4,4,96,768]{3,2,1,0:T(8,128)(2,1)}, bf16[4,4,96,768]{3,2,1,0:T(8,128)(2,1)}, f32[448,768]{1,0:T(8,128)}, bf16[448,768]{1,0:T(8,128)(2,1)}, f32[24,768]{1,0:T(8,128)}) custom-call(s32[2]{0:T(128)} %pad_add_fusion.refs_1_.refs_0_, bf16[448,768]{1,0:T(8,128)(2,1)} %get-tuple-element.151.refs_1_, f32[448,768]{1,0:T(8,128)} %get-tuple-element.152.refs_2_, ...), custom_call_target="tpu_custom_call" | custom-call | flops 126835752960 | bytes 26075136 | tf_op jit(solution)/shard_map/feed_backward/pallas_call | solution.py:80
  257.4 2.7 add_convert_fusion.6
  261.9 2.6 add_convert_fusion.4
  266.7 23.9 %cross_attend_back.2 = (bf16[4,448,192]{2,1,0:T(8,128)(2,1)}, bf16[4,4,384,384]{3,2,1,0:T(8,128)(2,1)}, f32[24,768]{1,0:T(8,128)}) custom-call(s32[2]{0:T(128)} %pad_add_fusion.refs_1_.refs_0_, f32[24,768]{1,0:T(8,128)} %get-tuple-element.157.refs_1_, bf16[448,768]{1,0:T(8,128)(2,1)} %get-tuple-element.158.refs_2_.refs_4_, ...), custom_call_target="tpu_custom_call" | custom-call | flops 110981283840 | bytes 20160512 | tf_op jit(solution)/shard_map/cross_attend_back/pallas_call | solution.py:80
  290.6 2.3 fusion.9
  294.8 2.7 fusion.11
  299.6 23.7 %cross_attend_back.3 = (bf16[4,448,192]{2,1,0:T(8,128)(2,1)}, bf16[4,4,384,384]{3,2,1,0:T(8,128)(2,1)}, f32[24,768]{1,0:T(8,128)}) custom-call(s32[2]{0:T(128)} %pad_add_fusion.refs_1_.refs_0_, f32[24,768]{1,0:T(8,128)} %get-tuple-element.165.refs_1_, ...), custom_call_target="tpu_custom_call", output_to_operand_aliasing={{0}: (11, {}), {1}: (12, {})} | custom-call | flops 110981283840 | bytes 20160512 | tf_op jit(solution)/shard_map/cross_attend_back/pallas_call | solution.py:80
  323.4 1.7 fusion.6
  328.1 1.7 fusion.4
  330.8 2.4 collective-permute-start.49
  335.6 14.4 %cross_rows_back.1 = (bf16[4,375,768]{2,1,0:T(8,128)(2,1)}, f32[448,768]{1,0:T(8,128)}, bf16[448,768]{1,0:T(8,128)(2,1)}, f32[24,768]{1,0:T(8,128)}) custom-call(s32[2]{0:T(128)} %pad_add_fusion.refs_1_.refs_0_, f32[24,768]{1,0:T(8,128)} %get-tuple-element.169.refs_1_, bf16[4,448,192]{2,1,0:T(8,128)(2,1)} %get-tuple-element.170.refs_2_.refs_1_, ...), custom_call_target="tpu_custom_call" | custom-call | flops 83047219200 | bytes 17467392 | tf_op jit(solution)/shard_map/cross_rows_back/pallas_call | solution.py:80
  350.0 2.0 collective-permute-start.48
  352.7 14.1 %cross_grads.1 = (bf16[4,4,96,768]{3,2,1,0:T(8,128)(2,1)}, bf16[4,4,96,768]{3,2,1,0:T(8,128)(2,1)}) custom-call(s32[2]{0:T(128)} %pad_add_fusion.refs_1_.refs_0_, bf16[4,448,192]{2,1,0:T(8,128)(2,1)} %get-tuple-element.170.refs_2_.refs_1_, bf16[4,4,384,384]{3,2,1,0:T(8,128)(2,1)} %get-tuple-element.171.refs_3_.refs_2_, ...), custom_call_target="tpu_custom_call" | custom-call | flops 93616865280 | bytes 14548992 | tf_op jit(solution)/shard_map/cross_grads/pallas_call | solution.py:80
  366.9 4.7 all-to-all-start
  371.6 16.4 %self_attend_back.1 = (bf16[4,448,576]{2,1,0:T(8,128)(2,1)}, f32[24,768]{1,0:T(8,128)}) custom-call(s32[1]{0:T(128)} %dynamic_slice.145.refs_0_, s32[2]{0:T(128)} %pad_add_fusion.refs_1_.refs_0_, f32[24,768]{1,0:T(8,128)} %get-tuple-element.174.refs_2_, bf16[448,768]{1,0:T(8,128)(2,1)} %get-tuple-element.175.refs_12_.refs_3_, ...), custom_call_target="tpu_custom_call" | custom-call | flops 133882183680 | bytes 11902976 | tf_op jit(solution)/shard_map/self_attend_back/pallas_call | solution.py:80
  388.0 2.5 add_convert_fusion.2
  392.4 9.2 %self_grads.1 = (bf16[4,4,96,768]{3,2,1,0:T(8,128)(2,1)}, bf16[4,4,96,768]{3,2,1,0:T(8,128)(2,1)}) custom-call(s32[2]{0:T(128)} %pad_add_fusion.refs_1_.refs_0_, bf16[4,448,576]{2,1,0:T(8,128)(2,1)} %get-tuple-element.185.refs_1_.refs_2_, bf16[4,448,192]{2,1,0:T(8,128)(2,1)} %get-tuple-element.188.refs_2_, ...), custom_call_target="tpu_custom_call" | custom-call | flops 42278584320 | bytes 8847360 | tf_op jit(solution)/shard_map/self_grads/pallas_call | solution.py:80
  401.6 4.9 %collective-permute-done.53.refs_8_ = bf16[2,2,96,768]{3,2,1,0:T(8,128)(2,1)S(1)} collective-permute-done((bf16[2,2,96,768]{3,2,1,0:T(8,128)(2,1)}, bf16[2,2,96,768]{3,2,1,0:T(8,128)(2,1)S(1)}, u32[]{:S(2)}, u32[]{:S(2)}) %collective-permute-start.53) | collective-permute-done | bytes 589856 | tf_op jit(solution)/shard_map/ppermute | solution.py:777
  407.5 2.3 fusion.13
  411.6 9.5 %self_rows_back.1 = (f32[448,768]{1,0:T(8,128)}, f32[24,768]{1,0:T(8,128)}) custom-call(s32[2]{0:T(128)} %pad_add_fusion.refs_1_.refs_0_, f32[24,768]{1,0:T(8,128)} %get-tuple-element.184.refs_1_, bf16[4,448,576]{2,1,0:T(8,128)(2,1)} %get-tuple-element.185.refs_1_.refs_2_, f32[448,768]{1,0:T(8,128)} %get-tuple-element.186.refs_3_, ...), custom_call_target="tpu_custom_call" | custom-call | flops 31708938240 | bytes 11231232 | tf_op jit(solution)/shard_map/self_rows_back/pallas_call | solution.py:80
  421.2 2.0 fusion.20
  425.1 1.8 fusion.2
  426.9 1.6 add_convert_fusion
  430.6 1.8 collective-permute-start.60
  432.4 2.4 collective-permute-start.61
  437.7 1.6 collective-permute-done.60
  439.3 4.8 collective-permute-done.61
  444.7 2.1 fusion.15
  449.8 1.6 copy.56
  452.3 1.6 pad_maximum_fusion.13
  453.9 4.7 copy.54
  459.6 4.8 collective-permute-start.73
  466.8 3.5 collective-permute-start.67
  474.6 9.0 %collective-permute-done.66 = bf16[96,768]{1,0:T(8,128)(2,1)S(1)} collective-permute-done((bf16[96,768]{1,0:T(8,128)(2,1)S(1)}, bf16[96,768]{1,0:T(8,128)(2,1)S(1)}, u32[]{:S(2)}, u32[]{:S(2)}) %collective-permute-start.66) | collective-permute-done | bytes 147488 | tf_op jit(solution)/shard_map/ppermute | solution.py:782
  (328 shorter events, 86.7 us)
Async XLA Ops:
  7.6 19.5 %collective-permute-start.2 = (bf16[112,768]{1,0:T(8,128)(2,1)}, bf16[112,768]{1,0:T(8,128)(2,1)}, u32[]{:S(2)}, u32[]{:S(2)}) collective-permute-start(bf16[112,768]{1,0:T(8,128)(2,1)} %pad_maximum_fusion.14), channel_id=1, source_target_pairs={{0,3},{1,0},{2,1},{3,2},{4,7},{5,4},{6,5},{7,6},{8,11},{9,8},{10,9... | collective-permute-start | bytes 516104 | tf_op jit(solution)/shard_map/ppermute | solution.py:782
  12.7 14.9 %collective-permute-start.1 = (bf16[112,768]{1,0:T(8,128)(2,1)}, bf16[112,768]{1,0:T(8,128)(2,1)}, u32[]{:S(2)}, u32[]{:S(2)}) collective-permute-start(bf16[112,768]{1,0:T(8,128)(2,1)} %pad_maximum_fusion.14), channel_id=1, source_target_pairs={{0,2},{1,3},{2,0},{3,1},{4,6},{5,7},{6,4},{7,5},{8,10},{9,11},{10,... | collective-permute-start | bytes 516104 | tf_op jit(solution)/shard_map/ppermute | solution.py:782
  12.7 14.9 %collective-permute-start = (bf16[112,768]{1,0:T(8,128)(2,1)}, bf16[112,768]{1,0:T(8,128)(2,1)}, u32[]{:S(2)}, u32[]{:S(2)}) collective-permute-start(bf16[112,768]{1,0:T(8,128)(2,1)} %pad_maximum_fusion.14), channel_id=1, source_target_pairs={{0,1},{1,2},{2,3},{3,0},{4,5},{5,6},{6,7},{7,4},{8,9},{9,10},{10,1... | collective-permute-start | bytes 516104 | tf_op jit(solution)/shard_map/ppermute | solution.py:782
  28.9 16.5 %collective-permute-start.4 = (bf16[1,2,112,768]{3,2,1,0:T(8,128)(2,1)S(1)}, bf16[1,2,112,768]{3,2,1,0:T(8,128)(2,1)S(1)}, u32[]{:S(2)}, u32[]{:S(2)}) collective-permute-start(bf16[1,2,112,768]{3,2,1,0:T(8,128)(2,1)S(1)} %maximum_bitcast_fusion.1), channel_id=1, source_target_pairs={{0,16},{4,20},{8,24},{12,28},{16,0},{20,4},{24,8},{28,12},{1,17},{... | collective-permute-start | bytes 1032200 | tf_op jit(solution)/shard_map/ppermute | solution.py:777
  30.5 14.9 %collective-permute-start.3 = (bf16[1,2,112,768]{3,2,1,0:T(8,128)(2,1)S(1)}, bf16[1,2,112,768]{3,2,1,0:T(8,128)(2,1)S(1)}, u32[]{:S(2)}, u32[]{:S(2)}) collective-permute-start(bf16[1,2,112,768]{3,2,1,0:T(8,128)(2,1)S(1)} %maximum_bitcast_fusion), channel_id=1, source_target_pairs={{0,8},{4,12},{8,0},{12,4},{16,24},{20,28},{24,16},{28,20},{1,9},{5... | collective-permute-start | bytes 1032200 | tf_op jit(solution)/shard_map/ppermute | solution.py:777
  34.3 11.1 %collective-permute-start.6 = (bf16[96,768]{1,0:T(8,128)(2,1)S(1)}, bf16[96,768]{1,0:T(8,128)(2,1)S(1)}, u32[]{:S(2)}, u32[]{:S(2)}) collective-permute-start(bf16[96,768]{1,0:T(8,128)(2,1)S(1)} %pad_maximum_fusion.15), channel_id=1, source_target_pairs={{0,2},{1,3},{2,0},{3,1},{4,6},{5,7},{6,4},{7,5},{8,10},{9,11},{10,... | collective-permute-start | bytes 442376 | tf_op jit(solution)/shard_map/ppermute | solution.py:782
  35.2 10.2 %collective-permute-start.7 = (bf16[96,768]{1,0:T(8,128)(2,1)S(1)}, bf16[96,768]{1,0:T(8,128)(2,1)S(1)}, u32[]{:S(2)}, u32[]{:S(2)}) collective-permute-start(bf16[96,768]{1,0:T(8,128)(2,1)S(1)} %pad_maximum_fusion.15), channel_id=1, source_target_pairs={{0,3},{1,0},{2,1},{3,2},{4,7},{5,4},{6,5},{7,6},{8,11},{9,8},{10,9... | collective-permute-start | bytes 442376 | tf_op jit(solution)/shard_map/ppermute | solution.py:782
  45.5 17.3 %collective-permute-start.9 = (bf16[2,2,112,768]{3,2,1,0:T(8,128)(2,1)S(1)}, bf16[2,2,112,768]{3,2,1,0:T(8,128)(2,1)S(1)}, u32[]{:S(2)}, u32[]{:S(2)}) collective-permute-start(bf16[2,2,112,768]{3,2,1,0:T(8,128)(2,1)S(1)} %pad_maximum_fusion.2), channel_id=1, source_target_pairs={{0,8},{4,12},{8,0},{12,4},{16,24},{20,28},{24,16},{28,20},{1,9},{5... | collective-permute-start | bytes 2064392 | tf_op jit(solution)/shard_map/ppermute | solution.py:777
  46.1 17.0 %collective-permute-start.8 = (bf16[2,2,112,768]{3,2,1,0:T(8,128)(2,1)S(1)}, bf16[2,2,112,768]{3,2,1,0:T(8,128)(2,1)S(1)}, u32[]{:S(2)}, u32[]{:S(2)}) collective-permute-start(bf16[2,2,112,768]{3,2,1,0:T(8,128)(2,1)S(1)} %pad_maximum_fusion.1), channel_id=1, source_target_pairs={{0,16},{4,20},{8,24},{12,28},{16,0},{20,4},{24,8},{28,12},{1,17},{... | collective-permute-start | bytes 2064392 | tf_op jit(solution)/shard_map/ppermute | solution.py:777
  46.7 9.4 %collective-permute-start.10 = (bf16[96,768]{1,0:T(8,128)(2,1)S(1)}, bf16[96,768]{1,0:T(8,128)(2,1)S(1)}, u32[]{:S(2)}, u32[]{:S(2)}) collective-permute-start(bf16[96,768]{1,0:T(8,128)(2,1)S(1)} %copy-done.31), channel_id=1, source_target_pairs={{0,1},{1,2},{2,3},{3,0},{4,5},{5,6},{6,7},{7,4},{8,9},{9,10},{10,1... | collective-permute-start | bytes 442376 | tf_op jit(solution)/shard_map/ppermute | solution.py:782
  50.3 10.4 %collective-permute-start.11 = (bf16[96,768]{1,0:T(8,128)(2,1)S(1)}, bf16[96,768]{1,0:T(8,128)(2,1)S(1)}, u32[]{:S(2)}, u32[]{:S(2)}) collective-permute-start(bf16[96,768]{1,0:T(8,128)(2,1)S(1)} %copy-done.31), channel_id=1, source_target_pairs={{0,2},{1,3},{2,0},{3,1},{4,6},{5,7},{6,4},{7,5},{8,10},{9,11},{10,... | collective-permute-start | bytes 442376 | tf_op jit(solution)/shard_map/ppermute | solution.py:782
  65.2 9.2 %collective-permute-start.13 = (bf16[4,4,112,768]{3,2,1,0:T(8,128)(2,1)}, bf16[4,4,112,768]{3,2,1,0:T(8,128)(2,1)}, u32[]{:S(2)}, u32[]{:S(2)}) collective-permute-start(bf16[4,4,112,768]{3,2,1,0:T(8,128)(2,1)} %maximum_maximum_fusion.refs_4_.refs_9_.refs_5_), channel_id=1, source_target_pairs={{0,4},{4,0},{8,12},{12,8},{16,20},{20,16},{24,28},{28,24},{1,5},{5... | collective-permute-start | bytes 8257544 | tf_op jit(solution)/shard_map/ppermute | solution.py:777
  67.6 9.6 %collective-permute-start.14 = (bf16[1,2,96,768]{3,2,1,0:T(8,128)(2,1)S(1)}, bf16[1,2,96,768]{3,2,1,0:T(8,128)(2,1)S(1)}, u32[]{:S(2)}, u32[]{:S(2)}) collective-permute-start(bf16[1,2,96,768]{3,2,1,0:T(8,128)(2,1)S(1)} %maximum_bitcast_fusion.2), channel_id=1, source_target_pairs={{0,8},{4,12},{8,0},{12,4},{16,24},{20,28},{24,16},{28,20},{1,9},{5... | collective-permute-start | bytes 884744 | tf_op jit(solution)/shard_map/ppermute | solution.py:777
  69.6 17.4 %collective-permute-start.16 = (bf16[375,768]{1,0:T(8,128)(2,1)S(1)}, bf16[375,768]{1,0:T(8,128)(2,1)}, u32[]{:S(2)}, u32[]{:S(2)}) collective-permute-start(bf16[375,768]{1,0:T(8,128)(2,1)S(1)} %bitcast.191), channel_id=1, source_target_pairs={{0,1},{1,2},{2,3},{3,0},{4,5},{5,6},{6,7},{7,4},{8,9},{9,10},{10,1... | collective-permute-start | bytes 1728008 | tf_op jit(solution)/shard_map/ppermute | solution.py:782
  87.9 34.5 %collective-permute-start.18 = (bf16[2,2,96,768]{3,2,1,0:T(8,128)(2,1)}, bf16[2,2,96,768]{3,2,1,0:T(8,128)(2,1)}, u32[]{:S(2)}, u32[]{:S(2)}) collective-permute-start(bf16[2,2,96,768]{3,2,1,0:T(8,128)(2,1)} %pad_maximum_fusion.5), channel_id=1, source_target_pairs={{0,8},{4,12},{8,0},{12,4},{16,24},{20,28},{24,16},{28,20},{1,9},{5... | collective-permute-start | bytes 1769480 | tf_op jit(solution)/shard_map/ppermute | solution.py:777
  88.4 14.4 %collective-permute-start.22 = (bf16[176,768]{1,0:T(8,128)(2,1)}, bf16[176,768]{1,0:T(8,128)(2,1)S(1)}, u32[]{:S(2)}, u32[]{:S(2)}) collective-permute-start(bf16[176,768]{1,0:T(8,128)(2,1)} %slice_bitcast_fusion.1), channel_id=1, source_target_pairs={{0,2},{1,3},{2,0},{3,1},{4,6},{5,7},{6,4},{7,5},{8,10},{9,11},{10,... | collective-permute-start | bytes 811016 | tf_op jit(solution)/shard_map/ppermute | solution.py:782
  90.6 31.8 %collective-permute-start.17 = (bf16[2,2,96,768]{3,2,1,0:T(8,128)(2,1)}, bf16[2,2,96,768]{3,2,1,0:T(8,128)(2,1)}, u32[]{:S(2)}, u32[]{:S(2)}) collective-permute-start(bf16[2,2,96,768]{3,2,1,0:T(8,128)(2,1)} %pad_maximum_fusion.4), channel_id=1, source_target_pairs={{0,16},{4,20},{8,24},{12,28},{16,0},{20,4},{24,8},{28,12},{1,17},{... | collective-permute-start | bytes 1769480 | tf_op jit(solution)/shard_map/ppermute | solution.py:777
  91.9 30.5 %collective-permute-start.19 = (bf16[1,2,96,768]{3,2,1,0:T(8,128)(2,1)S(1)}, bf16[1,2,96,768]{3,2,1,0:T(8,128)(2,1)S(1)}, u32[]{:S(2)}, u32[]{:S(2)}) collective-permute-start(bf16[1,2,96,768]{3,2,1,0:T(8,128)(2,1)S(1)} %maximum_bitcast_fusion.4), channel_id=1, source_target_pairs={{0,8},{4,12},{8,0},{12,4},{16,24},{20,28},{24,16},{28,20},{1,9},{5... | collective-permute-start | bytes 884744 | tf_op jit(solution)/shard_map/ppermute | solution.py:777
  93.4 29.0 %collective-permute-start.20 = (bf16[1,2,96,768]{3,2,1,0:T(8,128)(2,1)S(1)}, bf16[1,2,96,768]{3,2,1,0:T(8,128)(2,1)S(1)}, u32[]{:S(2)}, u32[]{:S(2)}) collective-permute-start(bf16[1,2,96,768]{3,2,1,0:T(8,128)(2,1)S(1)} %maximum_bitcast_fusion.5), channel_id=1, source_target_pairs={{0,16},{4,20},{8,24},{12,28},{16,0},{20,4},{24,8},{28,12},{1,17},{... | collective-permute-start | bytes 884744 | tf_op jit(solution)/shard_map/ppermute | solution.py:777
  102.8 19.6 %collective-permute-start.21 = (bf16[375,768]{1,0:T(8,128)(2,1)}, bf16[375,768]{1,0:T(8,128)(2,1)}, u32[]{:S(2)}, u32[]{:S(2)}) collective-permute-start(bf16[375,768]{1,0:T(8,128)(2,1)} %bitcast.190), channel_id=1, source_target_pairs={{0,3},{1,0},{2,1},{3,2},{4,7},{5,4},{6,5},{7,6},{8,11},{9,8},{10,9... | collective-permute-start | bytes 1728008 | tf_op jit(solution)/shard_map/ppermute | solution.py:782
  125.0 19.2 %collective-permute-start.23 = (bf16[4,4,96,768]{3,2,1,0:T(8,128)(2,1)S(1)}, bf16[4,4,96,768]{3,2,1,0:T(8,128)(2,1)S(1)}, u32[]{:S(2)}, u32[]{:S(2)}) collective-permute-start(bf16[4,4,96,768]{3,2,1,0:T(8,128)(2,1)S(1)} %maximum_maximum_fusion.1.refs_6_.refs_3_.refs_9_), channel_id=1, source_target_pairs={{0,4},{4,0},{8,12},{12,8},{16,20},{20,16},{24,28},{28,24},{1,5},{5... | collective-permute-start | bytes 7077896 | tf_op jit(solution)/shard_map/ppermute | solution.py:777
  125.1 19.1 %collective-permute-start.25 = (bf16[2,2,96,768]{3,2,1,0:T(8,128)(2,1)S(1)}, bf16[2,2,96,768]{3,2,1,0:T(8,128)(2,1)S(1)}, u32[]{:S(2)}, u32[]{:S(2)}) collective-permute-start(bf16[2,2,96,768]{3,2,1,0:T(8,128)(2,1)S(1)} %pad_maximum_fusion.7), channel_id=1, source_target_pairs={{0,16},{4,20},{8,24},{12,28},{16,0},{20,4},{24,8},{28,12},{1,17},{... | collective-permute-start | bytes 1769480 | tf_op jit(solution)/shard_map/ppermute | solution.py:777
  126.1 18.1 %collective-permute-start.26 = (bf16[2,2,96,768]{3,2,1,0:T(8,128)(2,1)S(1)}, bf16[2,2,96,768]{3,2,1,0:T(8,128)(2,1)S(1)}, u32[]{:S(2)}, u32[]{:S(2)}) collective-permute-start(bf16[2,2,96,768]{3,2,1,0:T(8,128)(2,1)S(1)} %pad_maximum_fusion.8), channel_id=1, source_target_pairs={{0,8},{4,12},{8,0},{12,4},{16,24},{20,28},{24,16},{28,20},{1,9},{5... | collective-permute-start | bytes 1769480 | tf_op jit(solution)/shard_map/ppermute | solution.py:777
  127.7 16.5 %collective-permute-start.24 = (bf16[199,768]{1,0:T(8,128)(2,1)S(1)}, bf16[199,768]{1,0:T(8,128)(2,1)S(1)}, u32[]{:S(2)}, u32[]{:S(2)}) collective-permute-start(bf16[199,768]{1,0:T(8,128)(2,1)S(1)} %slice_bitcast_fusion), channel_id=1, source_target_pairs={{0,2},{1,3},{2,0},{3,1},{4,6},{5,7},{6,4},{7,5},{8,10},{9,11},{10,... | collective-permute-start | bytes 917000 | tf_op jit(solution)/shard_map/ppermute | solution.py:782
  144.3 16.7 %collective-permute-start.28 = (bf16[96,768]{1,0:T(8,128)(2,1)S(1)}, bf16[96,768]{1,0:T(8,128)(2,1)S(1)}, u32[]{:S(2)}, u32[]{:S(2)}) collective-permute-start(bf16[96,768]{1,0:T(8,128)(2,1)S(1)} %bitcast.204), channel_id=1, source_target_pairs={{0,1},{1,2},{2,3},{3,0},{4,5},{5,6},{6,7},{7,4},{8,9},{9,10},{10,1... | collective-permute-start | bytes 442376 | tf_op jit(solution)/shard_map/ppermute | solution.py:782
  144.3 16.7 %collective-permute-start.29 = (bf16[96,768]{1,0:T(8,128)(2,1)S(1)}, bf16[96,768]{1,0:T(8,128)(2,1)S(1)}, u32[]{:S(2)}, u32[]{:S(2)}) collective-permute-start(bf16[96,768]{1,0:T(8,128)(2,1)S(1)} %bitcast.205), channel_id=1, source_target_pairs={{0,2},{1,3},{2,0},{3,1},{4,6},{5,7},{6,4},{7,5},{8,10},{9,11},{10,... | collective-permute-start | bytes 442376 | tf_op jit(solution)/shard_map/ppermute | solution.py:782
  145.2 15.9 %collective-permute-start.30 = (bf16[96,768]{1,0:T(8,128)(2,1)S(1)}, bf16[96,768]{1,0:T(8,128)(2,1)}, u32[]{:S(2)}, u32[]{:S(2)}) collective-permute-start(bf16[96,768]{1,0:T(8,128)(2,1)S(1)} %bitcast.206), channel_id=1, source_target_pairs={{0,3},{1,0},{2,1},{3,2},{4,7},{5,4},{6,5},{7,6},{8,11},{9,8},{10,9... | collective-permute-start | bytes 442376 | tf_op jit(solution)/shard_map/ppermute | solution.py:782
  148.6 13.7 %collective-permute-start.27 = (bf16[4,4,96,768]{3,2,1,0:T(8,128)(2,1)S(1)}, bf16[4,4,96,768]{3,2,1,0:T(8,128)(2,1)}, u32[]{:S(2)}, u32[]{:S(2)}) collective-permute-start(bf16[4,4,96,768]{3,2,1,0:T(8,128)(2,1)S(1)} %maximum_maximum_fusion.2.refs_3_.refs_4_), channel_id=1, source_target_pairs={{0,4},{4,0},{8,12},{12,8},{16,20},{20,16},{24,28},{28,24},{1,5},{5... | collective-permute-start | bytes 7077896 | tf_op jit(solution)/shard_map/ppermute | solution.py:777
  162.3 21.9 %collective-permute-start.31 = (bf16[1,2,96,768]{3,2,1,0:T(8,128)(2,1)S(1)}, bf16[1,2,96,768]{3,2,1,0:T(8,128)(2,1)S(1)}, u32[]{:S(2)}, u32[]{:S(2)}) collective-permute-start(bf16[1,2,96,768]{3,2,1,0:T(8,128)(2,1)S(1)} %maximum_bitcast_fusion.6), channel_id=1, source_target_pairs={{0,8},{4,12},{8,0},{12,4},{16,24},{20,28},{24,16},{28,20},{1,9},{5... | collective-permute-start | bytes 884744 | tf_op jit(solution)/shard_map/ppermute | solution.py:777
  162.8 21.3 %collective-permute-start.32 = (bf16[1,2,96,768]{3,2,1,0:T(8,128)(2,1)S(1)}, bf16[1,2,96,768]{3,2,1,0:T(8,128)(2,1)S(1)}, u32[]{:S(2)}, u32[]{:S(2)}) collective-permute-start(bf16[1,2,96,768]{3,2,1,0:T(8,128)(2,1)S(1)} %maximum_bitcast_fusion.7), channel_id=1, source_target_pairs={{0,16},{4,20},{8,24},{12,28},{16,0},{20,4},{24,8},{28,12},{1,17},{... | collective-permute-start | bytes 884744 | tf_op jit(solution)/shard_map/ppermute | solution.py:777
  184.2 22.4 %collective-permute-start.34 = (bf16[2,2,96,768]{3,2,1,0:T(8,128)(2,1)S(1)}, bf16[2,2,96,768]{3,2,1,0:T(8,128)(2,1)S(1)}, u32[]{:S(2)}, u32[]{:S(2)}) collective-permute-start(bf16[2,2,96,768]{3,2,1,0:T(8,128)(2,1)S(1)} %pad_maximum_fusion.11), channel_id=1, source_target_pairs={{0,8},{4,12},{8,0},{12,4},{16,24},{20,28},{24,16},{28,20},{1,9},{5... | collective-permute-start | bytes 1769480 | tf_op jit(solution)/shard_map/ppermute | solution.py:777
  185.8 20.7 %collective-permute-start.33 = (bf16[2,2,96,768]{3,2,1,0:T(8,128)(2,1)S(1)}, bf16[2,2,96,768]{3,2,1,0:T(8,128)(2,1)S(1)}, u32[]{:S(2)}, u32[]{:S(2)}) collective-permute-start(bf16[2,2,96,768]{3,2,1,0:T(8,128)(2,1)S(1)} %pad_maximum_fusion.10), channel_id=1, source_target_pairs={{0,16},{4,20},{8,24},{12,28},{16,0},{20,4},{24,8},{28,12},{1,17},{... | collective-permute-start | bytes 1769480 | tf_op jit(solution)/shard_map/ppermute | solution.py:777
  237.3 20.1 %collective-permute-start.36 = (bf16[4,4,96,768]{3,2,1,0:T(8,128)(2,1)}, bf16[4,4,96,768]{3,2,1,0:T(8,128)(2,1)}, u32[]{:S(2)}, u32[]{:S(2)}) collective-permute-start(bf16[4,4,96,768]{3,2,1,0:T(8,128)(2,1)} %get-tuple-element.164), channel_id=1, source_target_pairs={{0,4},{4,0},{8,12},{12,8},{16,20},{20,16},{24,28},{28,24},{1,5},{5... | collective-permute-start | bytes 7077896 | tf_op jit(solution)/shard_map/ppermute | solution.py:777
  260.1 30.5 %collective-permute-start.37 = (bf16[2,2,96,768]{3,2,1,0:T(8,128)(2,1)}, bf16[2,2,96,768]{3,2,1,0:T(8,128)(2,1)}, u32[]{:S(2)}, u32[]{:S(2)}) collective-permute-start(bf16[2,2,96,768]{3,2,1,0:T(8,128)(2,1)} %get-tuple-element.257), channel_id=1, source_target_pairs={{0,16},{4,20},{8,24},{12,28},{16,0},{20,4},{24,8},{28,12},{1,17},{... | collective-permute-start | bytes 1769480 | tf_op jit(solution)/shard_map/ppermute | solution.py:777
  261.4 29.2 %collective-permute-start.38 = (bf16[2,2,96,768]{3,2,1,0:T(8,128)(2,1)}, bf16[2,2,96,768]{3,2,1,0:T(8,128)(2,1)}, u32[]{:S(2)}, u32[]{:S(2)}) collective-permute-start(bf16[2,2,96,768]{3,2,1,0:T(8,128)(2,1)} %get-tuple-element.256), channel_id=1, source_target_pairs={{0,8},{4,12},{8,0},{12,4},{16,24},{20,28},{24,16},{28,20},{1,9},{5... | collective-permute-start | bytes 1769480 | tf_op jit(solution)/shard_map/ppermute | solution.py:777
  264.5 30.2 %collective-permute-start.42 = (bf16[2,2,96,768]{3,2,1,0:T(8,128)(2,1)}, bf16[2,2,96,768]{3,2,1,0:T(8,128)(2,1)S(1)}, u32[]{:S(2)}, u32[]{:S(2)}) collective-permute-start(bf16[2,2,96,768]{3,2,1,0:T(8,128)(2,1)} %get-tuple-element.253), channel_id=1, source_target_pairs={{0,16},{4,20},{8,24},{12,28},{16,0},{20,4},{24,8},{28,12},{1,17},{... | collective-permute-start | bytes 1769480 | tf_op jit(solution)/shard_map/ppermute | solution.py:777
  265.8 29.0 %collective-permute-start.43 = (bf16[2,2,96,768]{3,2,1,0:T(8,128)(2,1)}, bf16[2,2,96,768]{3,2,1,0:T(8,128)(2,1)S(1)}, u32[]{:S(2)}, u32[]{:S(2)}) collective-permute-start(bf16[2,2,96,768]{3,2,1,0:T(8,128)(2,1)} %get-tuple-element.252), channel_id=1, source_target_pairs={{0,8},{4,12},{8,0},{12,4},{16,24},{20,28},{24,16},{28,20},{1,9},{5... | collective-permute-start | bytes 1769480 | tf_op jit(solution)/shard_map/ppermute | solution.py:777
  292.9 35.2 %collective-permute-start.40 = (bf16[2,96,768]{2,1,0:T(8,128)(2,1)}, bf16[2,96,768]{2,1,0:T(8,128)(2,1)}, u32[]{:S(2)}, u32[]{:S(2)}) collective-permute-start(bf16[2,96,768]{2,1,0:T(8,128)(2,1)} %get-tuple-element.255), channel_id=1, source_target_pairs={{0,8},{4,12},{8,0},{12,4},{16,24},{20,28},{24,16},{28,20},{1,9},{5... | collective-permute-start | bytes 884744 | tf_op jit(solution)/shard_map/ppermute | solution.py:777
  293.9 34.2 %collective-permute-start.41 = (bf16[2,96,768]{2,1,0:T(8,128)(2,1)}, bf16[2,96,768]{2,1,0:T(8,128)(2,1)}, u32[]{:S(2)}, u32[]{:S(2)}) collective-permute-start(bf16[2,96,768]{2,1,0:T(8,128)(2,1)} %get-tuple-element.254), channel_id=1, source_target_pairs={{0,16},{4,20},{8,24},{12,28},{16,0},{20,4},{24,8},{28,12},{1,17},{... | collective-permute-start | bytes 884744 | tf_op jit(solution)/shard_map/ppermute | solution.py:777
  297.4 25.9 %collective-permute-start.45 = (bf16[2,96,768]{2,1,0:T(8,128)(2,1)}, bf16[2,96,768]{2,1,0:T(8,128)(2,1)S(1)}, u32[]{:S(2)}, u32[]{:S(2)}) collective-permute-start(bf16[2,96,768]{2,1,0:T(8,128)(2,1)} %get-tuple-element.250), channel_id=1, source_target_pairs={{0,16},{4,20},{8,24},{12,28},{16,0},{20,4},{24,8},{28,12},{1,17},{... | collective-permute-start | bytes 884744 | tf_op jit(solution)/shard_map/ppermute | solution.py:777
  298.7 24.7 %collective-permute-start.44 = (bf16[2,96,768]{2,1,0:T(8,128)(2,1)}, bf16[2,96,768]{2,1,0:T(8,128)(2,1)}, u32[]{:S(2)}, u32[]{:S(2)}) collective-permute-start(bf16[2,96,768]{2,1,0:T(8,128)(2,1)} %get-tuple-element.251), channel_id=1, source_target_pairs={{0,8},{4,12},{8,0},{12,4},{16,24},{20,28},{24,16},{28,20},{1,9},{5... | collective-permute-start | bytes 884744 | tf_op jit(solution)/shard_map/ppermute | solution.py:777
  326.1 40.8 %collective-permute-start.46 = (bf16[96,768]{1,0:T(8,128)(2,1)}, bf16[96,768]{1,0:T(8,128)(2,1)}, u32[]{:S(2)}, u32[]{:S(2)}) collective-permute-start(bf16[96,768]{1,0:T(8,128)(2,1)} %get-tuple-element.278), channel_id=1, source_target_pairs={{0,1},{1,2},{2,3},{3,0},{4,5},{5,6},{6,7},{7,4},{8,9},{9,10},{10,1... | collective-permute-start | bytes 442376 | tf_op jit(solution)/shard_map/ppermute | solution.py:782
  326.7 40.2 %collective-permute-start.47 = (bf16[96,768]{1,0:T(8,128)(2,1)}, bf16[96,768]{1,0:T(8,128)(2,1)}, u32[]{:S(2)}, u32[]{:S(2)}) collective-permute-start(bf16[96,768]{1,0:T(8,128)(2,1)} %get-tuple-element.279), channel_id=1, source_target_pairs={{0,2},{1,3},{2,0},{3,1},{4,6},{5,7},{6,4},{7,5},{8,10},{9,11},{10,... | collective-permute-start | bytes 442376 | tf_op jit(solution)/shard_map/ppermute | solution.py:782
  330.8 19.2 %collective-permute-start.49 = (bf16[96,768]{1,0:T(8,128)(2,1)S(1)}, bf16[96,768]{1,0:T(8,128)(2,1)S(1)}, u32[]{:S(2)}, u32[]{:S(2)}) collective-permute-start(bf16[96,768]{1,0:T(8,128)(2,1)S(1)} %get-tuple-element.275), channel_id=1, source_target_pairs={{0,1},{1,2},{2,3},{3,0},{4,5},{5,6},{6,7},{7,4},{8,9},{9,10},{10,1... | collective-permute-start | bytes 442376 | tf_op jit(solution)/shard_map/ppermute | solution.py:782
  333.2 18.9 %collective-permute-start.50 = (bf16[96,768]{1,0:T(8,128)(2,1)S(1)}, bf16[96,768]{1,0:T(8,128)(2,1)S(1)}, u32[]{:S(2)}, u32[]{:S(2)}) collective-permute-start(bf16[96,768]{1,0:T(8,128)(2,1)S(1)} %get-tuple-element.276), channel_id=1, source_target_pairs={{0,2},{1,3},{2,0},{3,1},{4,6},{5,7},{6,4},{7,5},{8,10},{9,11},{10,... | collective-permute-start | bytes 442376 | tf_op jit(solution)/shard_map/ppermute | solution.py:782
  334.3 17.7 %collective-permute-start.51 = (bf16[96,768]{1,0:T(8,128)(2,1)S(1)}, bf16[96,768]{1,0:T(8,128)(2,1)S(1)}, u32[]{:S(2)}, u32[]{:S(2)}) collective-permute-start(bf16[96,768]{1,0:T(8,128)(2,1)S(1)} %get-tuple-element.274), channel_id=1, source_target_pairs={{0,3},{1,0},{2,1},{3,2},{4,7},{5,4},{6,5},{7,6},{8,11},{9,8},{10,9... | collective-permute-start | bytes 442376 | tf_op jit(solution)/shard_map/ppermute | solution.py:782
  350.0 16.8 %collective-permute-start.48 = (bf16[96,768]{1,0:T(8,128)(2,1)S(1)}, bf16[96,768]{1,0:T(8,128)(2,1)S(1)}, u32[]{:S(2)}, u32[]{:S(2)}) collective-permute-start(bf16[96,768]{1,0:T(8,128)(2,1)S(1)} %get-tuple-element.277), channel_id=1, source_target_pairs={{0,3},{1,0},{2,1},{3,2},{4,7},{5,4},{6,5},{7,6},{8,11},{9,8},{10,9... | collective-permute-start | bytes 442376 | tf_op jit(solution)/shard_map/ppermute | solution.py:782
  366.8 21.2 %collective-permute-start.52 = (bf16[4,4,96,768]{3,2,1,0:T(8,128)(2,1)}, bf16[4,4,96,768]{3,2,1,0:T(8,128)(2,1)}, u32[]{:S(2)}, u32[]{:S(2)}) collective-permute-start(bf16[4,4,96,768]{3,2,1,0:T(8,128)(2,1)} %get-tuple-element.187), channel_id=1, source_target_pairs={{0,4},{4,0},{8,12},{12,8},{16,20},{20,16},{24,28},{28,24},{1,5},{5... | collective-permute-start | bytes 7077896 | tf_op jit(solution)/shard_map/ppermute | solution.py:777
  366.9 87.1 %all-to-all-start = ((bf16[4,375,768]{2,1,0:T(8,128)(2,1)}), bf16[4,375,768]{2,1,0:T(8,128)(2,1)}, u32[]{:S(2)}, u32[]{:S(2)}) async-start(bf16[4,375,768]{2,1,0:T(8,128)(2,1)} %get-tuple-element.193), calls=%async_computation | async-start | bytes 4620288 | tf_op jit(solution)/shard_map/all_to_all | solution.py:1073
  390.6 15.9 %collective-permute-start.53 = (bf16[2,2,96,768]{3,2,1,0:T(8,128)(2,1)}, bf16[2,2,96,768]{3,2,1,0:T(8,128)(2,1)S(1)}, u32[]{:S(2)}, u32[]{:S(2)}) collective-permute-start(bf16[2,2,96,768]{3,2,1,0:T(8,128)(2,1)} %get-tuple-element.245), channel_id=1, source_target_pairs={{0,16},{4,20},{8,24},{12,28},{16,0},{20,4},{24,8},{28,12},{1,17},{... | collective-permute-start | bytes 1769480 | tf_op jit(solution)/shard_map/ppermute | solution.py:777
  391.9 15.7 %collective-permute-start.54 = (bf16[2,2,96,768]{3,2,1,0:T(8,128)(2,1)}, bf16[2,2,96,768]{3,2,1,0:T(8,128)(2,1)S(1)}, u32[]{:S(2)}, u32[]{:S(2)}) collective-permute-start(bf16[2,2,96,768]{3,2,1,0:T(8,128)(2,1)} %get-tuple-element.244), channel_id=1, source_target_pairs={{0,8},{4,12},{8,0},{12,4},{16,24},{20,28},{24,16},{28,20},{1,9},{5... | collective-permute-start | bytes 1769480 | tf_op jit(solution)/shard_map/ppermute | solution.py:777
  401.6 25.3 %collective-permute-start.55 = (bf16[4,4,96,768]{3,2,1,0:T(8,128)(2,1)}, bf16[4,4,96,768]{3,2,1,0:T(8,128)(2,1)}, u32[]{:S(2)}, u32[]{:S(2)}) collective-permute-start(bf16[4,4,96,768]{3,2,1,0:T(8,128)(2,1)} %get-tuple-element.194), channel_id=1, source_target_pairs={{0,4},{4,0},{8,12},{12,8},{16,20},{20,16},{24,28},{28,24},{1,5},{5... | collective-permute-start | bytes 7077896 | tf_op jit(solution)/shard_map/ppermute | solution.py:777
  409.8 15.2 %collective-permute-start.56 = (bf16[2,96,768]{2,1,0:T(8,128)(2,1)}, bf16[2,96,768]{2,1,0:T(8,128)(2,1)S(1)}, u32[]{:S(2)}, u32[]{:S(2)}) collective-permute-start(bf16[2,96,768]{2,1,0:T(8,128)(2,1)} %get-tuple-element.243), channel_id=1, source_target_pairs={{0,8},{4,12},{8,0},{12,4},{16,24},{20,28},{24,16},{28,20},{1,9},{5... | collective-permute-start | bytes 884744 | tf_op jit(solution)/shard_map/ppermute | solution.py:777
  410.4 14.7 %collective-permute-start.57 = (bf16[2,96,768]{2,1,0:T(8,128)(2,1)}, bf16[2,96,768]{2,1,0:T(8,128)(2,1)}, u32[]{:S(2)}, u32[]{:S(2)}) collective-permute-start(bf16[2,96,768]{2,1,0:T(8,128)(2,1)} %get-tuple-element.242), channel_id=1, source_target_pairs={{0,16},{4,20},{8,24},{12,28},{16,0},{20,4},{24,8},{28,12},{1,17},{... | collective-permute-start | bytes 884744 | tf_op jit(solution)/shard_map/ppermute | solution.py:777
  424.0 10.7 %collective-permute-start.69 = (f32[24,768]{1,0:T(8,128)S(1)}, f32[24,768]{1,0:T(8,128)S(1)}, u32[]{:S(2)}, u32[]{:S(2)}) collective-permute-start(f32[24,768]{1,0:T(8,128)S(1)} %add.518), channel_id=1, source_target_pairs={{0,8},{4,12},{8,0},{12,4},{16,24},{20,28},{24,16},{28,20},{1,9},{5... | collective-permute-start | bytes 221192 | tf_op jit(solution)/shard_map/ppermute | solution.py:777
  428.5 15.7 %collective-permute-start.59 = (bf16[2,2,96,768]{3,2,1,0:T(8,128)(2,1)S(1)}, bf16[2,2,96,768]{3,2,1,0:T(8,128)(2,1)S(1)}, u32[]{:S(2)}, u32[]{:S(2)}) collective-permute-start(bf16[2,2,96,768]{3,2,1,0:T(8,128)(2,1)S(1)} %get-tuple-element.240), channel_id=1, source_target_pairs={{0,8},{4,12},{8,0},{12,4},{16,24},{20,28},{24,16},{28,20},{1,9},{5... | collective-permute-start | bytes 1769480 | tf_op jit(solution)/shard_map/ppermute | solution.py:777
  429.7 15.0 %collective-permute-start.58 = (bf16[2,2,96,768]{3,2,1,0:T(8,128)(2,1)S(1)}, bf16[2,2,96,768]{3,2,1,0:T(8,128)(2,1)S(1)}, u32[]{:S(2)}, u32[]{:S(2)}) collective-permute-start(bf16[2,2,96,768]{3,2,1,0:T(8,128)(2,1)S(1)} %get-tuple-element.241), channel_id=1, source_target_pairs={{0,16},{4,20},{8,24},{12,28},{16,0},{20,4},{24,8},{28,12},{1,17},{... | collective-permute-start | bytes 1769480 | tf_op jit(solution)/shard_map/ppermute | solution.py:777
  432.4 11.7 %collective-permute-start.61 = (bf16[96,768]{1,0:T(8,128)(2,1)S(1)}, bf16[96,768]{1,0:T(8,128)(2,1)S(1)}, u32[]{:S(2)}, u32[]{:S(2)}) collective-permute-start(bf16[96,768]{1,0:T(8,128)(2,1)S(1)} %get-tuple-element.273), channel_id=1, source_target_pairs={{0,2},{1,3},{2,0},{3,1},{4,6},{5,7},{6,4},{7,5},{8,10},{9,11},{10,... | collective-permute-start | bytes 442376 | tf_op jit(solution)/shard_map/ppermute | solution.py:782
  434.8 9.4 %collective-permute-start.62 = (bf16[96,768]{1,0:T(8,128)(2,1)S(1)}, bf16[96,768]{1,0:T(8,128)(2,1)S(1)}, u32[]{:S(2)}, u32[]{:S(2)}) collective-permute-start(bf16[96,768]{1,0:T(8,128)(2,1)S(1)} %get-tuple-element.271), channel_id=1, source_target_pairs={{0,3},{1,0},{2,1},{3,2},{4,7},{5,4},{6,5},{7,6},{8,11},{9,8},{10,9... | collective-permute-start | bytes 442376 | tf_op jit(solution)/shard_map/ppermute | solution.py:782
  446.7 12.8 %collective-permute-start.64 = (bf16[2,96,768]{2,1,0:T(8,128)(2,1)}, bf16[2,96,768]{2,1,0:T(8,128)(2,1)}, u32[]{:S(2)}, u32[]{:S(2)}) collective-permute-start(bf16[2,96,768]{2,1,0:T(8,128)(2,1)} %get-tuple-element.236), channel_id=1, source_target_pairs={{0,16},{4,20},{8,24},{12,28},{16,0},{20,4},{24,8},{28,12},{1,17},{... | collective-permute-start | bytes 884744 | tf_op jit(solution)/shard_map/ppermute | solution.py:777
  447.6 12.0 %collective-permute-start.63 = (bf16[2,96,768]{2,1,0:T(8,128)(2,1)}, bf16[2,96,768]{2,1,0:T(8,128)(2,1)}, u32[]{:S(2)}, u32[]{:S(2)}) collective-permute-start(bf16[2,96,768]{2,1,0:T(8,128)(2,1)} %get-tuple-element.237), channel_id=1, source_target_pairs={{0,8},{4,12},{8,0},{12,4},{16,24},{20,28},{24,16},{28,20},{1,9},{5... | collective-permute-start | bytes 884744 | tf_op jit(solution)/shard_map/ppermute | solution.py:777
  459.6 11.6 %collective-permute-start.73 = (f32[24,768]{1,0:T(8,128)S(1)}, f32[24,768]{1,0:T(8,128)S(1)}, u32[]{:S(2)}, u32[]{:S(2)}) collective-permute-start(f32[24,768]{1,0:T(8,128)S(1)} %add.520), channel_id=1, source_target_pairs={{0,3},{1,0},{2,1},{3,2},{4,7},{5,4},{6,5},{7,6},{8,11},{9,8},{10,9... | collective-permute-start | bytes 221192 | tf_op jit(solution)/shard_map/ppermute | solution.py:782
  470.3 13.3 %collective-permute-start.66 = (bf16[96,768]{1,0:T(8,128)(2,1)S(1)}, bf16[96,768]{1,0:T(8,128)(2,1)S(1)}, u32[]{:S(2)}, u32[]{:S(2)}) collective-permute-start(bf16[96,768]{1,0:T(8,128)(2,1)S(1)} %get-tuple-element.269), channel_id=1, source_target_pairs={{0,2},{1,3},{2,0},{3,1},{4,6},{5,7},{6,4},{7,5},{8,10},{9,11},{10,... | collective-permute-start | bytes 442376 | tf_op jit(solution)/shard_map/ppermute | solution.py:782
  471.1 12.5 %collective-permute-start.65 = (bf16[96,768]{1,0:T(8,128)(2,1)S(1)}, bf16[96,768]{1,0:T(8,128)(2,1)S(1)}, u32[]{:S(2)}, u32[]{:S(2)}) collective-permute-start(bf16[96,768]{1,0:T(8,128)(2,1)S(1)} %get-tuple-element.268), channel_id=1, source_target_pairs={{0,1},{1,2},{2,3},{3,0},{4,5},{5,6},{6,7},{7,4},{8,9},{9,10},{10,1... | collective-permute-start | bytes 442376 | tf_op jit(solution)/shard_map/ppermute | solution.py:782
  (66 other events, 513.4 us)

commit v4 on v3

--- a/solution.py
+++ b/solution.py
@@ -246,13 +246,12 @@
 def frame_keys(place, frames, pack, own, head_bias, piece, dims, deps=()):
     seq, width, blocks, hw = dims
     pieces = len(frames)
-    valid = sum(part.shape[0] for part in frames[0])
-    parts = [part for group in frames for part in group]
+    valid = frames[0].shape[0]
     total = pieces * piece
     edge = valid // 16 * 16
 
     def body(place_ref, *refs):
-        f_refs, refs = list(refs[: len(parts)]), refs[len(parts) :]
+        f_refs, refs = refs[:pieces], refs[pieces:]
         w_refs, refs = refs[: len(pack)], refs[len(pack) :]
         hb_ref, k_ref, v_ref, kt_ref, vt_ref, e_ref, w_scr = refs
         assemble(w_refs, own, place_ref, w_scr)
@@ -261,10 +260,7 @@
         def _():
             for c in range(pieces):
                 e_ref[c, edge:] = jnp.zeros((piece - edge, width), BF)
-                at = 0
-                for part in frames[c]:
-                    e_ref[c, at : at + part.shape[0]] = f_refs.pop(0)[...]
-                    at += part.shape[0]
+                e_ref[c, :valid] = f_refs[c][...]
 
         w = w_scr[:, : 2 * hw]
         for c in range(pieces):
@@ -281,7 +277,7 @@
     padded = sds((pieces, piece, width), BF)
     return call(
         body, "frame_keys", blocks,
-        [(part, whole(part.shape)) for part in parts] + [*pack_in(pack), (head_bias, per_block(head_bias.shape))],
+        [(f, whole(f.shape)) for f in frames] + [*pack_in(pack), (head_bias, per_block(head_bias.shape))],
         [(kv, per_block(kv.shape))] * 2 + [(kvt, per_block(kvt.shape))] * 2 + [(padded, whole(padded.shape))],
         [pack_scratch(width)],
         4 * total * width * width,
@@ -571,11 +567,11 @@
     seq, width, blocks, hw = dims
     _, pieces, piece, _ = dkv.shape
     frames = (pieces, piece, width)
-    kept = (pieces, valid, width)
+    kept = (valid, width)
 
     def body(place_ref, old_ref, dq_ref, dkv_ref, g2_ref, first_ref, *refs):
         w_refs, refs = refs[: len(pack)], refs[len(pack) :]
-        prm_ref, genc_ref, g1_ref, b1_ref, sum_ref, w_scr, genc_scr, acc_scr = refs
+        prm_ref, *genc_refs, g1_ref, b1_ref, sum_ref, w_scr, genc_scr, acc_scr = refs
         t = pl.program_id(0)
         assemble(w_refs, own, place_ref, w_scr)
 
@@ -593,7 +589,7 @@
         @pl.when(t == blocks - 1)
         def _():
             for c in range(pieces):
-                genc_ref[lax.rem(place_ref[1] + pieces - c, pieces)] = genc_scr[c, :valid].astype(BF)
+                genc_refs[c][...] = genc_scr[c, :valid].astype(BF)
             grad = acc_scr[...]
             unit, inverse = layer_norm_parts(first_ref[...])
             sum_ref[1:2] = column_sum(grad * unit)
@@ -609,7 +605,8 @@
         body, "cross_rows_back", blocks,
         [(sums, whole(sums.shape)), (dq, per_block(dq.shape)), (dkv, per_block(dkv.shape)), (g2, full), (first, full), *pack_in(pack),
          (params, whole(params.shape))],
-        [(sds(kept, BF), whole(kept)), (sds((seq, width), F32), full), (sds((seq, width), BF), full),
+        [(sds(kept, BF), whole(kept))] * pieces
+        + [(sds((seq, width), F32), full), (sds((seq, width), BF), full),
          (sds(sums.shape, F32), whole(sums.shape))],
         [pack_scratch(width), pltpu.VMEM(frames, F32), pltpu.VMEM((seq, width), F32)],
         2 * seq * width * width + 4 * pieces * piece * width * width,
@@ -651,19 +648,24 @@
     )
 
 
-def self_attend_back(length, place, sums, b1, queries, keys, values, lse, ot, pack, own, dims, deps=()):
+def self_attend_back(length, place, sums, b1, n1, queries, keys, values, mixed, lse, ot, pack, own, grad_shape, dims,
+                     deps=()):
     seq, width, blocks, hw = dims
     heads = hw // HD
-
-    def body(len_ref, place_ref, old_ref, b1_ref, q_ref, k_ref, v_ref, lse_ref, ot_ref, *refs):
+    grads = grad_outs(grad_shape)
+
+    def body(len_ref, place_ref, old_ref, b1_ref, n1_ref, q_ref, k_ref, v_ref, mix_ref, lse_ref, ot_ref, *refs):
         w_refs, refs = refs[: len(pack)], refs[len(pack) :]
-        dqkv_ref, sum_ref, w_scr, bias_scr, dqt_scr = refs
+        grad_refs, refs = refs[: len(grads)], refs[len(grads) :]
+        dqkv_ref, sum_ref, w_scr, bias_scr, dqt_scr, b1t_scr, n1t_scr = refs
         t = pl.program_id(0)
         assemble(w_refs, own, place_ref, w_scr)
 
         @pl.when(t == 0)
         def _():
             sum_ref[...] = old_ref[...]
+            b1t_scr[...] = b1_ref[...].T
+            n1t_scr[...] = n1_ref[...].T
             key = lax.broadcasted_iota(jnp.int32, (seq, seq), 0)
             query = lax.broadcasted_iota(jnp.int32, (seq, seq), 1)
             bias_scr[...] = jnp.where((key <= query) & (key < len_ref[0]), 0.0, NEGATIVE)
@@ -689,45 +691,22 @@
         dv = dv.astype(BF)
         put_heads(sum_ref, 8, t, blocks, column_sum(dq))
         put_heads(sum_ref, 9, t, blocks, column_sum(dv.astype(F32)))
-        dqkv_ref[0] = jnp.concatenate([dq.astype(BF), dk.astype(BF), dv], 1)
+        dqkv = jnp.concatenate([dq.astype(BF), dk.astype(BF), dv], 1)
+        dqkv_ref[0] = dqkv
+        grad = jnp.concatenate([dot(n1t_scr[...], dqkv), dot(b1t_scr[...], mix_ref[0])], 1)
+        store_pack(grad_refs, grad.astype(BF), place_ref)
 
     hb = per_block((blocks, seq, hw))
     dqkv = (blocks, seq, 3 * hw)
     return call(
         body, "self_attend_back", blocks,
-        [(sums, whole(sums.shape)), (b1, whole((seq, width))), (queries, hb), (keys, hb), (values, hb), (lse, per_block(lse.shape)),
-         (ot, per_block(ot.shape)), *pack_in(pack)],
-        [(sds(dqkv, BF), per_block(dqkv)), (sds(sums.shape, F32), whole(sums.shape))],
-        [pack_scratch(width), pltpu.VMEM((seq, seq), F32), pltpu.VMEM((hw, seq), F32)],
-        2 * seq * width * width + 40 * seq * seq * width,
+        [(sums, whole(sums.shape)), (b1, whole((seq, width))), (n1, whole((seq, width))), (queries, hb), (keys, hb),
+         (values, hb), (mixed, hb), (lse, per_block(lse.shape)), (ot, per_block(ot.shape)), *pack_in(pack)],
+        grads + [(sds(dqkv, BF), per_block(dqkv)), (sds(sums.shape, F32), whole(sums.shape))],
+        [pack_scratch(width), pltpu.VMEM((seq, seq), F32), pltpu.VMEM((hw, seq), F32), pltpu.VMEM((width, seq), BF),
+         pltpu.VMEM((width, seq), BF)],
+        10 * seq * width * width + 40 * seq * seq * width,
         (length, place),
-        deps,
-    )
-
-
-def self_grads(place, dqkv, mixed, b1, n1, grad_shape, dims, deps=()):
-    seq, width, blocks, hw = dims
-
-    def body(place_ref, dqkv_ref, mix_ref, b1_ref, n1_ref, *refs):
-        grad_refs, (b1t_scr, n1t_scr) = refs[:-2], refs[-2:]
-
-        @pl.when(pl.program_id(0) == 0)
-        def _():
-            b1t_scr[...] = b1_ref[...].T
-            n1t_scr[...] = n1_ref[...].T
-
-        grad_qkv = dot(n1t_scr[...], dqkv_ref[0])
-        grad_o = dot(b1t_scr[...], mix_ref[0])
-        store_pack(grad_refs, jnp.concatenate([grad_qkv, grad_o], 1).astype(BF), place_ref)
-
-    full = whole((seq, width))
-    return call(
-        body, "self_grads", blocks,
-        [(dqkv, per_block(dqkv.shape)), (mixed, per_block(mixed.shape)), (b1, full), (n1, full)],
-        grad_outs(grad_shape),
-        [pltpu.VMEM((width, seq), BF), pltpu.VMEM((width, seq), BF)],
-        8 * seq * width * width,
-        (place,),
         deps,
     )
 
@@ -860,21 +839,29 @@
         self.high_y = swap(three(2, high, self.high_x[1]).astype(BF), 4)
         return self.low_x, self.high_y
 
-    def line(self):
+    def sides(self):
         def total(t, more, last):
             return wide(self.kept[0, t]) + wide(self.come[0, t]) + wide(more) + wide(last)
 
         low, high = slice(0, self.half), slice(self.half, self.tp)
-        sums = jnp.concatenate(
+        self.sums = jnp.concatenate(
             [total(low, self.low_y[0], self.low_x), total(high, self.high_x[0], self.high_y)]
         ).astype(BF)
-        here = lax.axis_index("tp")
-        self.own = lax.dynamic_index_in_dim(sums, here, 0, keepdims=False)
-        self.parts = [
-            around(lax.dynamic_index_in_dim(sums, (here + hop) % self.tp, 0, keepdims=False), hop)
-            for hop in range(1, self.tp)
-        ]
+        self.own = lax.dynamic_index_in_dim(self.sums, lax.axis_index("tp"), 0, keepdims=False)
+        self.parts = [self.part(hop) for hop in range(1, self.tp, 2)]
         return tuple(self.parts)
+
+    def across(self):
+        more = [self.part(hop) for hop in range(2, self.tp, 2)]
+        self.parts += more
+        return tuple(more)
+
+    def line(self):
+        return self.sides() + self.across()
+
+    def part(self, hop):
+        place = (lax.axis_index("tp") + hop) % self.tp
+        return around(lax.dynamic_index_in_dim(self.sums, place, 0, keepdims=False), hop)
 
     def total(self):
         result = wide(self.own)
@@ -973,13 +960,9 @@
         turn = move(turn, "self.first", "cross.direct")
         turn = move(turn, "self.second", "in.direct")
         frames[1] = around(gate(frames[1], turn), 1)
-        turn = move(turn, "self.core", "cross.first") + (frames[1],)
-        before = turn
-        edge = frames_own // 32 * 16
-        frames[3] = around(gate(frames[3], turn), 3)
-        near, far = frames[2][:edge], frames[2][edge:]
-        near = around(gate(near, turn), 2)
-        turn = move(turn, "cross.second", "in.first") + (frames[3], near)
+        before = turn = move(turn, "self.core", "cross.first")
+        frames[2] = around(gate(frames[2], turn), 2)
+        turn = move(turn, "cross.second", "in.first") + (frames[1], frames[2])
         w_self = chains["self"].pack
         own_rows = own
         grad_shape = (fsdp // 2, tp, own, width)
@@ -1020,12 +1003,11 @@
     )
     turn += (n2,)
     if chained:
-        far = around(gate(far, turn), 2)
-        turn = move(turn, "cross.core", "in.second") + (far,)
+        frames[3] = around(gate(frames[3], turn), 3)
+        turn = move(turn, "cross.core", "in.second") + (frames[3],)
         w_cross = chains["cross"].pack
-        frames = [(frames[0],), (frames[1],), (near, far), (frames[3],)]
     else:
-        frames = [(around(array, hop) if hop else array,) for hop, array in enumerate(frames)]
+        frames = [around(array, hop) if hop else array for hop, array in enumerate(frames)]
     k2, v2, k2t, v2t, frames = frame_keys(place, frames, w_cross, own_rows, head_bias, piece, dims, turn)
     turn = move(turn, "in.core", "out.direct") + (k2,)
     shared = (w_cross, own_rows, params, head_bias, k2, v2t, frames_own, dims)
@@ -1063,40 +1045,51 @@
     *kept, sums = cross_attend_back(place, 0, half, sums, *shared, step1)
     step3 = go("out", "second") + go("in", "first")
     dq2, dkv2, sums = cross_attend_back(place, half, tp - half, sums, *shared, step2, kept)
+    grad_cross = cross_grads(place, dq2, dkv2, mixed2, b2, n2, frames, grad_shape, dims, step3)
     step4 = go("out", "line") + go("in", "second")
-    grad_frames, g1, b1, sums = cross_rows_back(
-        place, sums, dq2, dkv2, g2, first, w_cross, own_rows, params, frames_own, dims, step3
-    )
-    grad_cross = cross_grads(place, dq2, dkv2, mixed2, b2, n2, frames, grad_shape, dims, step4 + (b1,))
-    step5 = go("in", "line")
     begin("cross", grad_cross)
-    frames_back = lax.all_to_all(gate(grad_frames, (grad_cross[0], *step5)), "tp", 0, 0, tiled=True)
-    step6 = go("cross", "core")
-    dqkv1, sums = self_attend_back(
-        length, place, sums, b1, q1, k1, v1, lse1, ot1, w_self, own_rows, dims, step5 + (grad_cross[0],)
-    )
-    step7 = go("cross", "first")
-    grad_self = self_grads(place, dqkv1, mixed1, b1, n1, grad_shape, dims, step6)
+    step5 = go("cross", "core")
+    *grad_frames, g1, b1, sums = cross_rows_back(
+        place, sums, dq2, dkv2, g2, first, w_cross, own_rows, params, frames_own, dims, step4 + (grad_cross[0],)
+    )
+    step5 += go("in", "line")
+    backs = [around(gate(grad_frames[c], step5), tp - c) if c % 2 else grad_frames[c] for c in range(tp)]
+    step6 = go("cross", "first") + tuple(backs[1::2])
+    *grad_self, dqkv1, sums = self_attend_back(
+        length, place, sums, b1, n1, q1, k1, v1, mixed1, lse1, ot1, w_self, own_rows, grad_shape, dims, step5
+    )
     begin("self", grad_self)
     go("self", "core")
     grad_inputs, sums = self_rows_back(
-        place, sums, dqkv1, g1, x, w_self, own_rows, params, dims, step7 + (grad_self[0],)
-    )
-    turns = [(), (), (), ()]
+        place, sums, dqkv1, g1, x, w_self, own_rows, params, dims, step6 + (grad_self[0],)
+    )
+
+    for c in range(2, tp, 2):
+        backs[c] = around(gate(backs[c], step6 + (grad_self[0],)), tp - c)
+
+    turns = [()]
     if chained:
         scatters["cross"].low_y = gate(scatters["cross"].low_y, (grad_self[0],))
-        step8 = go("cross", "second")
-        scatters["self"].come = gate(scatters["self"].come, (sums, *step8))
-        scatters["cross"].low_x = gate(scatters["cross"].low_x, (sums, *step8))
-        turns[2] = go("self", "first") + go("cross", "line")
-        scatters["self"].low_y = gate(scatters["self"].low_y, turns[2])
-        turns[3] = go("self", "second")
-    step = 1
+        step7 = go("cross", "second")
+        scatters["self"].come = gate(scatters["self"].come, (sums, *step7))
+        turns = [go("self", "first")]
+        scatters["cross"].low_x = gate(scatters["cross"].low_x, (sums, *step7))
+        go("cross", "sides")
+        for name in ("out", "in"):
+            scatters[name].own = gate(scatters[name].own, turns[0])
+        scatters["self"].low_y = gate(scatters["self"].low_y, (backs[2],))
+        turns.append(go("self", "second"))
+        scatters["cross"].sums = gate(scatters["cross"].sums, turns[0])
+        scatters["self"].low_x = gate(scatters["self"].low_x, go("cross", "across"))
+    sums = gate(sums, turns[0])
+    sums = sums + swap(sums, 1)
+    sums = sum([around(sums, hop) for hop in range(1, tp)], sums)
+    sums = gate(sums, turns[-1])
+    step = 2
     while step < fsdp:
-        sums = sums + swap(gate(sums, turns.pop(0) if turns else ()), step)
+        sums = sums + swap(sums, step)
         step *= 2
-    sums = gate(sums, turns.pop(0) if turns else ())
-    sums = sum([around(sums, hop) for hop in range(1, tp)], sums)
+    frames_back = in_order([backs[-hop % tp] for hop in range(tp)], tp_place)
     device = lax.axis_index("fsdp") * tp + tp_place
     mine = lax.dynamic_slice_in_dim(sums[:rows], device * small_own, small_own, 1)
     gains = norm_gain.shape[0]

time: 494 us -> 478 us (0.968)
  starting transfers between devices: 93.1 us -> 84.5 us
    ppermute x31 -> x33, waiting for transfers between devices: 65.5 us -> 69.4 us  [around(): lax.ppermute(array, 'tp', [(i, (i + hop) % count) for i in range(count)])]
    ppermute x31 -> x33, starting transfers between devices: 52.8 us -> 49.6 us  [around(): lax.ppermute(array, 'tp', [(i, (i + hop) % count) for i in range(count)])]
    pallas_call x14 -> x13, Pallas kernels: 224 us -> 221 us  [call(): pl.pallas_call(inner, out_shape=[o for o, _ in outs], grid_spec=pltpu.Pre...]
    unnamed x126 -> x134, local copies, waits for them, and re-layouts: 15.9 us -> 16.4 us
  transfers between devices with their start and end apart: 75 -> 76, of which waited for: 20 -> 21; matrix products, arithmetic and copies ran while one was open for 14% -> 13% of each run, Pallas kernels for 41% -> 42%
where the time goes in v4:
time: 478 us; the launch traced here: 472 us
  Pallas kernels  221 us (46%)
  starting transfers between devices  84.5 us (18%)
  waiting for transfers between devices  81.3 us (17%)
  other arithmetic  48.1 us (10%)
  local copies, waits for them, and re-layouts  34.8 us (7%)
    pallas_call x13, Pallas kernels, call(): pl.pallas_call(inner, out_shape=[o for o, _ in outs], grid_spec=pltpu.Pre...  221 us
    ppermute x33, waiting for transfers between devices, around(): lax.ppermute(array, 'tp', [(i, (i + hop) % count) for i in range(count)])  69.4 us
    ppermute x33, starting transfers between devices, around(): lax.ppermute(array, 'tp', [(i, (i + hop) % count) for i in range(count)])  49.6 us
    ppermute x43, starting transfers between devices, swap(): return lax.ppermute(array, 'fsdp', [(i, i ^ step) for i in range(count)])  34.8 us
    unnamed x134, local copies, waits for them, and re-layouts  16.4 us
    ppermute x43, waiting for transfers between devices, swap(): return lax.ppermute(array, 'fsdp', [(i, i ^ step) for i in range(count)])  11.8 us
  transfers between devices with their start and end apart: 76, of which 21 were waited for; matrix products, arithmetic and copies ran while one was open for 13% of the time, Pallas kernels for 42%

profile of v4, /device:TPU:0, one launch (start us, length us, event | category | flops | bytes accessed | tf_op | source)
XLA Modules:
  0.0 471.9 jit_solution(17632208372498239669)
XLA Ops:
  7.6 5.1 %collective-permute-start.2 = (bf16[112,768]{1,0:T(8,128)(2,1)}, bf16[112,768]{1,0:T(8,128)(2,1)}, u32[]{:S(2)}, u32[]{:S(2)}) collective-permute-start(bf16[112,768]{1,0:T(8,128)(2,1)} %pad_maximum_fusion.16), channel_id=1, source_target_pairs={{0,3},{1,0},{2,1},{3,2},{4,7},{5,4},{6,5},{7,6},{8,11},{9,8},{10,9... | collective-permute-start | bytes 516104 | tf_op jit(solution)/shard_map/ppermute | solution.py:761
  13.7 8.4 %constant_dynamic-slice_fusion.27 = (bf16[1,375,768]{2,0,1:T(2,128)(2,1)S(1)}, bf16[1,375,768]{2,0,1:T(2,128)(2,1)S(1)}, bf16[1,375,768]{2,0,1:T(2,128)(2,1)S(1)}, bf16[1,375,768]{2,0,1:T(2,128)(2,1)}) fusion(bf16[4,375,768]{2,0,1:T(4,128)(2,1)} %param.16, s32[]{:T(128)S(6)} %select_n.201, s32[]{:T(128)S(6)} %select_n.199, s32[]{:T(128)S(6)} %select_n.197, ...), kind=kLoop, calls=%fused_computation.207 | loop fusion | bytes 4608016 | tf_op jit(solution)/shard_map/jit(dynamic_index_in_dim)/dynamic_slice | solution.py:953
  22.1 2.1 copy.67
  28.9 1.6 collective-permute-start.4
  30.5 1.6 collective-permute-start.3
  32.3 2.0 collective-permute-start.5
  35.2 2.8 collective-permute-start.7
  38.1 2.8 collective-permute-done.5
  40.9 4.5 collective-permute-done.6
  47.4 3.6 collective-permute-start.10
  51.0 1.6 collective-permute-start.11
  53.4 3.4 collective-permute-done.10
  56.8 4.6 collective-permute-done.11
  61.4 2.1 collective-permute-done.9
  70.9 1.6 collective-permute-start.14
  73.0 3.9 collective-permute-start.20
  85.1 1.5 collective-permute-start.18
  86.6 1.5 collective-permute-start.19
  90.5 1.6 collective-permute-start.21
  92.1 17.9 %self_forward.1 = (bf16[4,448,192]{2,1,0:T(8,128)(2,1)}, bf16[4,448,192]{2,1,0:T(8,128)(2,1)}, bf16[4,448,192]{2,1,0:T(8,128)(2,1)}, f32[4,8,448]{2,1,0:T(8,128)...) custom-call(s32[1]{0:T(128)} %dynamic_slice.157.refs_0_, ...), custom_call_target="tpu_custom_call" | custom-call | flops 91603599360 | bytes 13918208 | tf_op jit(solution)/shard_map/self_forward/pallas_call | solution.py:80
  110.0 8.2 %collective-permute-done.21.refs_3_ = bf16[375,768]{1,0:T(8,128)(2,1)} collective-permute-done((bf16[375,768]{1,0:T(8,128)(2,1)}, bf16[375,768]{1,0:T(8,128)(2,1)}, u32[]{:S(2)}, u32[]{:S(2)}) %collective-permute-start.21) | collective-permute-done | bytes 576032 | tf_op jit(solution)/shard_map/ppermute | solution.py:761
  119.0 1.7 maximum_maximum_fusion.1.refs_5_.refs_3_.refs_9_.refs_6_
  122.4 1.6 collective-permute-start.23
  124.0 13.3 %collective-permute-done.23.refs_4_.refs_11_ = bf16[375,768]{1,0:T(8,128)(2,1)S(1)} collective-permute-done((bf16[375,768]{1,0:T(8,128)(2,1)S(1)}, bf16[375,768]{1,0:T(8,128)(2,1)S(1)}, u32[]{:S(2)}, u32[]{:S(2)}) %collective-permute-start.23) | collective-permute-done | bytes 576032 | tf_op jit(solution)/shard_map/ppermute | solution.py:761
  137.4 4.0 collective-permute-start.28
  141.7 1.5 maximum_maximum_fusion.2.refs_3_.refs_4_
  143.2 12.5 %frame_keys.1 = (bf16[4,4,384,192]{3,2,1,0:T(8,128)(2,1)}, bf16[4,4,384,192]{3,2,1,0:T(8,128)(2,1)}, bf16[4,192,1536]{2,1,0:T(8,128)(2,1)}, bf16[4,192,1536]{2,1,0:T(8,128)(2,1)}, bf16[4,384,768]{2,1,0:T(8,128)(2,1)}) custom-call(s32[2]{0:T(128)} %pad_add_fusion.refs_1_.refs_0_, bf16[375,768]{1,0:T(8,128)(2,1)} %bitcast.183, ...), custom_call_target="tpu_custom_call" | custom-call | flops 72477573120 | bytes 18843648 | tf_op jit(solution)/shard_map/frame_keys/pallas_call | solution.py:80
  157.0 1.5 collective-permute-start.30
  159.7 19.9 %cross_forward.2 = (bf16[4,448,192]{2,1,0:T(8,128)(2,1)}, f32[4,8,448]{2,1,0:T(8,128)}, f32[4,192,448]{2,1,0:T(8,128)}, bf16[4,448,192]{2,1,0:T(8,128)(2,1)}, f3...) custom-call(s32[2]{0:T(128)} %pad_add_fusion.refs_1_.refs_0_, bf16[448,768]{1,0:T(8,128)(2,1)} %get-tuple-element.126.refs_1_.refs_5_, ...), custom_call_target="tpu_custom_call" | custom-call | flops 95126814720 | bytes 16474112 | tf_op jit(solution)/shard_map/cross_forward/pallas_call | solution.py:80
  181.4 19.9 %cross_forward.3 = (bf16[4,448,192]{2,1,0:T(8,128)(2,1)}, f32[4,8,448]{2,1,0:T(8,128)}, f32[4,192,448]{2,1,0:T(8,128)}, bf16[4,448,192]{2,1,0:T(8,128)(2,1)}, f3...) custom-call(s32[2]{0:T(128)} %pad_add_fusion.refs_1_.refs_0_, ...), custom_call_target="tpu_custom_call", output_to_operand_aliasing={{0}: (9, {}), {1}: (10, {}), {2}: (11, {}), {3}: (12, {})} | custom-call | flops 95126814720 | bytes 16474112 | tf_op jit(solution)/shard_map/cross_forward/pallas_call | solution.py:80
  202.8 4.5 collective-permute-done.34.refs_6_.refs_7_
  208.8 15.5 %feed_forward.1 = (bf16[4,448,768]{2,1,0:T(8,128)(2,1)}, f32[4,448,768]{2,1,0:T(8,128)}, bf16[448,768]{1,0:T(8,128)(2,1)}, f32[448,768]{1,0:T(8,128)}, bf16[448,768]{1,0:T(8,128)(2,1)}, /*index=5*/f32[24,768]{1,0:T(8,128)}) custom-call(s32[2]{0:T(128)} %pad_add_fusion.refs_1_.refs_0_, bf16[448,768]{1,0:T(8,128)(2,1)} %get-tuple-element.151.refs_1_.refs_8_, ...), custom_call_target="tpu_custom_call" | custom-call | flops 84557168640 | bytes 23347200 | tf_op jit(solution)/shard_map/feed_forward/pallas_call | solution.py:80
  224.2 7.8 %feed_out_grads.1 = (bf16[4,4,96,768]{3,2,1,0:T(8,128)(2,1)}, bf16[4,4,96,768]{3,2,1,0:T(8,128)(2,1)}) custom-call(s32[2]{0:T(128)} %pad_add_fusion.refs_1_.refs_0_, bf16[448,768]{1,0:T(8,128)(2,1)} %get-tuple-element.158.refs_1_, bf16[4,448,768]{2,1,0:T(8,128)(2,1)} %get-tuple-element.162.refs_2_), custom_call_target="tpu_custom_call" | custom-call | flops 42278584320 | bytes 8159232 | tf_op jit(solution)/shard_map/feed_out_grads/pallas_call | solution.py:80
  232.2 19.3 %feed_backward.1 = (bf16[4,4,96,768]{3,2,1,0:T(8,128)(2,1)}, bf16[4,4,96,768]{3,2,1,0:T(8,128)(2,1)}, f32[448,768]{1,0:T(8,128)}, bf16[448,768]{1,0:T(8,128)(2,1)}, f32[24,768]{1,0:T(8,128)}) custom-call(s32[2]{0:T(128)} %pad_add_fusion.refs_1_.refs_0_, bf16[448,768]{1,0:T(8,128)(2,1)} %get-tuple-element.158.refs_1_, f32[448,768]{1,0:T(8,128)} %get-tuple-element.159.refs_2_, ...), custom_call_target="tpu_custom_call" | custom-call | flops 126835752960 | bytes 26075136 | tf_op jit(solution)/shard_map/feed_backward/pallas_call | solution.py:80
  252.0 3.1 add_convert_fusion.6
  256.2 1.5 collective-permute-start.37
  257.7 2.5 add_convert_fusion.4
  261.7 23.9 %cross_attend_back.2 = (bf16[4,448,192]{2,1,0:T(8,128)(2,1)}, bf16[4,4,384,384]{3,2,1,0:T(8,128)(2,1)}, f32[24,768]{1,0:T(8,128)}) custom-call(s32[2]{0:T(128)} %pad_add_fusion.refs_1_.refs_0_, f32[24,768]{1,0:T(8,128)} %get-tuple-element.164.refs_1_, bf16[448,768]{1,0:T(8,128)(2,1)} %get-tuple-element.165.refs_2_.refs_4_, ...), custom_call_target="tpu_custom_call" | custom-call | flops 110981283840 | bytes 20160512 | tf_op jit(solution)/shard_map/cross_attend_back/pallas_call | solution.py:80
  285.6 2.4 fusion.9
  290.7 2.5 fusion.11
  294.7 23.7 %cross_attend_back.3 = (bf16[4,448,192]{2,1,0:T(8,128)(2,1)}, bf16[4,4,384,384]{3,2,1,0:T(8,128)(2,1)}, f32[24,768]{1,0:T(8,128)}) custom-call(s32[2]{0:T(128)} %pad_add_fusion.refs_1_.refs_0_, f32[24,768]{1,0:T(8,128)} %get-tuple-element.172.refs_1_, ...), custom_call_target="tpu_custom_call", output_to_operand_aliasing={{0}: (11, {}), {1}: (12, {})} | custom-call | flops 110981283840 | bytes 20160512 | tf_op jit(solution)/shard_map/cross_attend_back/pallas_call | solution.py:80
  318.4 1.9 fusion.6
  321.2 2.0 collective-permute-start.41
  323.2 1.8 collective-permute-start.42
  325.2 14.2 %cross_grads.1 = (bf16[4,4,96,768]{3,2,1,0:T(8,128)(2,1)}, bf16[4,4,96,768]{3,2,1,0:T(8,128)(2,1)}) custom-call(s32[2]{0:T(128)} %pad_add_fusion.refs_1_.refs_0_, bf16[4,448,192]{2,1,0:T(8,128)(2,1)} %get-tuple-element.177.refs_1_.refs_2_, bf16[4,4,384,384]{3,2,1,0:T(8,128)(2,1)} %get-tuple-element.178.refs_2_.refs_3_, ...), custom_call_target="tpu_custom_call" | custom-call | flops 93616865280 | bytes 14548992 | tf_op jit(solution)/shard_map/cross_grads/pallas_call | solution.py:80
  339.5 1.7 fusion.4
  342.6 3.6 collective-permute-start.50
  347.8 14.5 %cross_rows_back.1 = (bf16[375,768]{1,0:T(8,128)(2,1)}, bf16[375,768]{1,0:T(8,128)(2,1)}, bf16[375,768]{1,0:T(8,128)(2,1)}, bf16[375,768]{1,0:T(8,128)(2,1)}, f3...) custom-call(s32[2]{0:T(128)} %pad_add_fusion.refs_1_.refs_0_, ...), custom_call_target="tpu_custom_call" | custom-call | flops 83047219200 | bytes 17467392 | tf_op jit(solution)/shard_map/cross_rows_back/pallas_call | solution.py:80
  362.3 2.6 add_convert_fusion.2
  369.6 22.3 %self_attend_back.1 = (bf16[4,4,96,768]{3,2,1,0:T(8,128)(2,1)}, bf16[4,4,96,768]{3,2,1,0:T(8,128)(2,1)}, bf16[4,448,576]{2,1,0:T(8,128)(2,1)}, f32[24,768]{1,0:T(8,128)}) custom-call(s32[1]{0:T(128)} %dynamic_slice.157.refs_0_, s32[2]{0:T(128)} %pad_add_fusion.refs_1_.refs_0_, f32[24,768]{1,0:T(8,128)} %get-tuple-element.184.refs_2_, ...), custom_call_target="tpu_custom_call" | custom-call | flops 176160768000 | bytes 17997824 | tf_op jit(solution)/shard_map/self_attend_back/pallas_call | solution.py:80
  392.0 3.8 collective-permute-done.55.refs_11_
  396.4 2.3 fusion.13
  400.1 9.4 %self_rows_back.1 = (f32[448,768]{1,0:T(8,128)}, f32[24,768]{1,0:T(8,128)}) custom-call(s32[2]{0:T(128)} %pad_add_fusion.refs_1_.refs_0_, f32[24,768]{1,0:T(8,128)} %get-tuple-element.194.refs_1_, bf16[4,448,576]{2,1,0:T(8,128)(2,1)} %get-tuple-element.195.refs_2_, f32[448,768]{1,0:T(8,128)} %get-tuple-element.196.refs_3_, bf16[448,768]{1,0:T(8,128)(2,1)} %bitcast.215, ...), custom_call_target="tpu_custom_call" | custom-call | flops 31708938240 | bytes 11231232 | tf_op jit(solution)/shard_map/self_rows_back/pallas_call | solution.py:80
  409.5 1.9 fusion.2
  411.5 1.8 collective-permute-start.69
  417.0 9.7 %collective-permute-done.56 = bf16[375,768]{1,0:T(8,128)(2,1)S(1)} collective-permute-done((bf16[375,768]{1,0:T(8,128)(2,1)}, bf16[375,768]{1,0:T(8,128)(2,1)S(1)}, u32[]{:S(2)}, u32[]{:S(2)}) %collective-permute-start.56) | collective-permute-done | bytes 576032 | tf_op jit(solution)/shard_map/ppermute | solution.py:761
  426.6 1.5 pad_maximum_fusion
  428.7 3.9 copy.53
  435.4 2.4 collective-permute-start.73
  438.4 2.0 collective-permute-done.73
  441.1 3.8 collective-permute-done.72
  446.8 8.3 %collective-permute-done.63 = bf16[96,768]{1,0:T(8,128)(2,1)S(1)} collective-permute-done((bf16[96,768]{1,0:T(8,128)(2,1)S(1)}, bf16[96,768]{1,0:T(8,128)(2,1)S(1)}, u32[]{:S(2)}, u32[]{:S(2)}) %collective-permute-start.63) | collective-permute-done | bytes 147488 | tf_op jit(solution)/shard_map/ppermute | solution.py:761
  460.9 2.7 collective-permute-done.74
  464.8 3.0 collective-permute-done.66
  (340 shorter events, 83.2 us)
Async XLA Ops:
  7.6 19.4 %collective-permute-start.2 = (bf16[112,768]{1,0:T(8,128)(2,1)}, bf16[112,768]{1,0:T(8,128)(2,1)}, u32[]{:S(2)}, u32[]{:S(2)}) collective-permute-start(bf16[112,768]{1,0:T(8,128)(2,1)} %pad_maximum_fusion.16), channel_id=1, source_target_pairs={{0,3},{1,0},{2,1},{3,2},{4,7},{5,4},{6,5},{7,6},{8,11},{9,8},{10,9... | collective-permute-start | bytes 516104 | tf_op jit(solution)/shard_map/ppermute | solution.py:761
  12.7 14.9 %collective-permute-start.1 = (bf16[112,768]{1,0:T(8,128)(2,1)}, bf16[112,768]{1,0:T(8,128)(2,1)}, u32[]{:S(2)}, u32[]{:S(2)}) collective-permute-start(bf16[112,768]{1,0:T(8,128)(2,1)} %pad_maximum_fusion.16), channel_id=1, source_target_pairs={{0,2},{1,3},{2,0},{3,1},{4,6},{5,7},{6,4},{7,5},{8,10},{9,11},{10,... | collective-permute-start | bytes 516104 | tf_op jit(solution)/shard_map/ppermute | solution.py:761
  12.7 14.9 %collective-permute-start = (bf16[112,768]{1,0:T(8,128)(2,1)}, bf16[112,768]{1,0:T(8,128)(2,1)}, u32[]{:S(2)}, u32[]{:S(2)}) collective-permute-start(bf16[112,768]{1,0:T(8,128)(2,1)} %pad_maximum_fusion.16), channel_id=1, source_target_pairs={{0,1},{1,2},{2,3},{3,0},{4,5},{5,6},{6,7},{7,4},{8,9},{9,10},{10,1... | collective-permute-start | bytes 516104 | tf_op jit(solution)/shard_map/ppermute | solution.py:761
  28.9 16.5 %collective-permute-start.4 = (bf16[1,2,112,768]{3,2,1,0:T(8,128)(2,1)S(1)}, bf16[1,2,112,768]{3,2,1,0:T(8,128)(2,1)S(1)}, u32[]{:S(2)}, u32[]{:S(2)}) collective-permute-start(bf16[1,2,112,768]{3,2,1,0:T(8,128)(2,1)S(1)} %maximum_bitcast_fusion.1), channel_id=1, source_target_pairs={{0,16},{4,20},{8,24},{12,28},{16,0},{20,4},{24,8},{28,12},{1,17},{... | collective-permute-start | bytes 1032200 | tf_op jit(solution)/shard_map/ppermute | solution.py:756
  30.5 15.6 %collective-permute-start.3 = (bf16[1,2,112,768]{3,2,1,0:T(8,128)(2,1)S(1)}, bf16[1,2,112,768]{3,2,1,0:T(8,128)(2,1)S(1)}, u32[]{:S(2)}, u32[]{:S(2)}) collective-permute-start(bf16[1,2,112,768]{3,2,1,0:T(8,128)(2,1)S(1)} %maximum_bitcast_fusion), channel_id=1, source_target_pairs={{0,8},{4,12},{8,0},{12,4},{16,24},{20,28},{24,16},{28,20},{1,9},{5... | collective-permute-start | bytes 1032200 | tf_op jit(solution)/shard_map/ppermute | solution.py:756
  34.3 11.1 %collective-permute-start.6 = (bf16[96,768]{1,0:T(8,128)(2,1)S(1)}, bf16[96,768]{1,0:T(8,128)(2,1)S(1)}, u32[]{:S(2)}, u32[]{:S(2)}) collective-permute-start(bf16[96,768]{1,0:T(8,128)(2,1)S(1)} %pad_maximum_fusion.17), channel_id=1, source_target_pairs={{0,2},{1,3},{2,0},{3,1},{4,6},{5,7},{6,4},{7,5},{8,10},{9,11},{10,... | collective-permute-start | bytes 442376 | tf_op jit(solution)/shard_map/ppermute | solution.py:761
  35.2 10.2 %collective-permute-start.7 = (bf16[96,768]{1,0:T(8,128)(2,1)S(1)}, bf16[96,768]{1,0:T(8,128)(2,1)S(1)}, u32[]{:S(2)}, u32[]{:S(2)}) collective-permute-start(bf16[96,768]{1,0:T(8,128)(2,1)S(1)} %pad_maximum_fusion.17), channel_id=1, source_target_pairs={{0,3},{1,0},{2,1},{3,2},{4,7},{5,4},{6,5},{7,6},{8,11},{9,8},{10,9... | collective-permute-start | bytes 442376 | tf_op jit(solution)/shard_map/ppermute | solution.py:761
  46.2 17.3 %collective-permute-start.9 = (bf16[2,2,112,768]{3,2,1,0:T(8,128)(2,1)S(1)}, bf16[2,2,112,768]{3,2,1,0:T(8,128)(2,1)S(1)}, u32[]{:S(2)}, u32[]{:S(2)}) collective-permute-start(bf16[2,2,112,768]{3,2,1,0:T(8,128)(2,1)S(1)} %pad_maximum_fusion.4), channel_id=1, source_target_pairs={{0,8},{4,12},{8,0},{12,4},{16,24},{20,28},{24,16},{28,20},{1,9},{5... | collective-permute-start | bytes 2064392 | tf_op jit(solution)/shard_map/ppermute | solution.py:756
  46.9 17.0 %collective-permute-start.8 = (bf16[2,2,112,768]{3,2,1,0:T(8,128)(2,1)S(1)}, bf16[2,2,112,768]{3,2,1,0:T(8,128)(2,1)S(1)}, u32[]{:S(2)}, u32[]{:S(2)}) collective-permute-start(bf16[2,2,112,768]{3,2,1,0:T(8,128)(2,1)S(1)} %pad_maximum_fusion.3), channel_id=1, source_target_pairs={{0,16},{4,20},{8,24},{12,28},{16,0},{20,4},{24,8},{28,12},{1,17},{... | collective-permute-start | bytes 2064392 | tf_op jit(solution)/shard_map/ppermute | solution.py:756
  47.4 9.4 %collective-permute-start.10 = (bf16[96,768]{1,0:T(8,128)(2,1)S(1)}, bf16[96,768]{1,0:T(8,128)(2,1)S(1)}, u32[]{:S(2)}, u32[]{:S(2)}) collective-permute-start(bf16[96,768]{1,0:T(8,128)(2,1)S(1)} %copy-done.29), channel_id=1, source_target_pairs={{0,1},{1,2},{2,3},{3,0},{4,5},{5,6},{6,7},{7,4},{8,9},{9,10},{10,1... | collective-permute-start | bytes 442376 | tf_op jit(solution)/shard_map/ppermute | solution.py:761
  51.0 10.4 %collective-permute-start.11 = (bf16[96,768]{1,0:T(8,128)(2,1)S(1)}, bf16[96,768]{1,0:T(8,128)(2,1)S(1)}, u32[]{:S(2)}, u32[]{:S(2)}) collective-permute-start(bf16[96,768]{1,0:T(8,128)(2,1)S(1)} %copy-done.29), channel_id=1, source_target_pairs={{0,2},{1,3},{2,0},{3,1},{4,6},{5,7},{6,4},{7,5},{8,10},{9,11},{10,... | collective-permute-start | bytes 442376 | tf_op jit(solution)/shard_map/ppermute | solution.py:761
  65.4 11.5 %collective-permute-start.13 = (bf16[4,4,112,768]{3,2,1,0:T(8,128)(2,1)S(1)}, bf16[4,4,112,768]{3,2,1,0:T(8,128)(2,1)}, u32[]{:S(2)}, u32[]{:S(2)}) collective-permute-start(bf16[4,4,112,768]{3,2,1,0:T(8,128)(2,1)S(1)} %maximum_maximum_fusion.refs_4_.refs_11_.refs_5_), channel_id=1, source_target_pairs={{0,4},{4,0},{8,12},{12,8},{16,20},{20,16},{24,28},{28,24},{1,5},{5... | collective-permute-start | bytes 8257544 | tf_op jit(solution)/shard_map/ppermute | solution.py:756
  70.9 9.6 %collective-permute-start.14 = (bf16[1,2,96,768]{3,2,1,0:T(8,128)(2,1)}, bf16[1,2,96,768]{3,2,1,0:T(8,128)(2,1)}, u32[]{:S(2)}, u32[]{:S(2)}) collective-permute-start(bf16[1,2,96,768]{3,2,1,0:T(8,128)(2,1)} %maximum_bitcast_fusion.2), channel_id=1, source_target_pairs={{0,8},{4,12},{8,0},{12,4},{16,24},{20,28},{24,16},{28,20},{1,9},{5... | collective-permute-start | bytes 884744 | tf_op jit(solution)/shard_map/ppermute | solution.py:756
  73.0 17.5 %collective-permute-start.20 = (bf16[375,768]{1,0:T(8,128)(2,1)}, bf16[375,768]{1,0:T(8,128)(2,1)}, u32[]{:S(2)}, u32[]{:S(2)}) collective-permute-start(bf16[375,768]{1,0:T(8,128)(2,1)} %bitcast.178), channel_id=1, source_target_pairs={{0,1},{1,2},{2,3},{3,0},{4,5},{5,6},{6,7},{7,4},{8,9},{9,10},{10,1... | collective-permute-start | bytes 1728008 | tf_op jit(solution)/shard_map/ppermute | solution.py:761
  82.8 35.4 %collective-permute-start.17 = (bf16[2,2,96,768]{3,2,1,0:T(8,128)(2,1)S(1)}, bf16[2,2,96,768]{3,2,1,0:T(8,128)(2,1)S(1)}, u32[]{:S(2)}, u32[]{:S(2)}) collective-permute-start(bf16[2,2,96,768]{3,2,1,0:T(8,128)(2,1)S(1)} %pad_maximum_fusion.7), channel_id=1, source_target_pairs={{0,8},{4,12},{8,0},{12,4},{16,24},{20,28},{24,16},{28,20},{1,9},{5... | collective-permute-start | bytes 1769480 | tf_op jit(solution)/shard_map/ppermute | solution.py:756
  84.6 33.6 %collective-permute-start.16 = (bf16[2,2,96,768]{3,2,1,0:T(8,128)(2,1)S(1)}, bf16[2,2,96,768]{3,2,1,0:T(8,128)(2,1)S(1)}, u32[]{:S(2)}, u32[]{:S(2)}) collective-permute-start(bf16[2,2,96,768]{3,2,1,0:T(8,128)(2,1)S(1)} %pad_maximum_fusion.6), channel_id=1, source_target_pairs={{0,16},{4,20},{8,24},{12,28},{16,0},{20,4},{24,8},{28,12},{1,17},{... | collective-permute-start | bytes 1769480 | tf_op jit(solution)/shard_map/ppermute | solution.py:756
  85.1 24.9 %collective-permute-start.18 = (bf16[1,2,96,768]{3,2,1,0:T(8,128)(2,1)S(1)}, bf16[1,2,96,768]{3,2,1,0:T(8,128)(2,1)S(1)}, u32[]{:S(2)}, u32[]{:S(2)}) collective-permute-start(bf16[1,2,96,768]{3,2,1,0:T(8,128)(2,1)S(1)} %maximum_bitcast_fusion.4), channel_id=1, source_target_pairs={{0,8},{4,12},{8,0},{12,4},{16,24},{20,28},{24,16},{28,20},{1,9},{5... | collective-permute-start | bytes 884744 | tf_op jit(solution)/shard_map/ppermute | solution.py:756
  86.6 23.4 %collective-permute-start.19 = (bf16[1,2,96,768]{3,2,1,0:T(8,128)(2,1)S(1)}, bf16[1,2,96,768]{3,2,1,0:T(8,128)(2,1)S(1)}, u32[]{:S(2)}, u32[]{:S(2)}) collective-permute-start(bf16[1,2,96,768]{3,2,1,0:T(8,128)(2,1)S(1)} %maximum_bitcast_fusion.5), channel_id=1, source_target_pairs={{0,16},{4,20},{8,24},{12,28},{16,0},{20,4},{24,8},{28,12},{1,17},{... | collective-permute-start | bytes 884744 | tf_op jit(solution)/shard_map/ppermute | solution.py:756
  90.5 27.7 %collective-permute-start.21 = (bf16[375,768]{1,0:T(8,128)(2,1)}, bf16[375,768]{1,0:T(8,128)(2,1)}, u32[]{:S(2)}, u32[]{:S(2)}) collective-permute-start(bf16[375,768]{1,0:T(8,128)(2,1)} %bitcast.185), channel_id=1, source_target_pairs={{0,2},{1,3},{2,0},{3,1},{4,6},{5,7},{6,4},{7,5},{8,10},{9,11},{10,... | collective-permute-start | bytes 1728008 | tf_op jit(solution)/shard_map/ppermute | solution.py:761
  120.7 16.6 %collective-permute-start.22 = (bf16[4,4,96,768]{3,2,1,0:T(8,128)(2,1)S(1)}, bf16[4,4,96,768]{3,2,1,0:T(8,128)(2,1)S(1)}, u32[]{:S(2)}, u32[]{:S(2)}) collective-permute-start(bf16[4,4,96,768]{3,2,1,0:T(8,128)(2,1)S(1)} %maximum_maximum_fusion.1.refs_5_.refs_3_.refs_9_.refs_6_), channel_id=1, source_target_pairs={{0,4},{4,0},{8,12},{12,8},{16,20},{20,16},{24,28},{28,24},{1,5},{5... | collective-permute-start | bytes 7077896 | tf_op jit(solution)/shard_map/ppermute | solution.py:756
  120.9 16.4 %collective-permute-start.24 = (bf16[2,2,96,768]{3,2,1,0:T(8,128)(2,1)S(1)}, bf16[2,2,96,768]{3,2,1,0:T(8,128)(2,1)S(1)}, u32[]{:S(2)}, u32[]{:S(2)}) collective-permute-start(bf16[2,2,96,768]{3,2,1,0:T(8,128)(2,1)S(1)} %pad_maximum_fusion.9), channel_id=1, source_target_pairs={{0,16},{4,20},{8,24},{12,28},{16,0},{20,4},{24,8},{28,12},{1,17},{... | collective-permute-start | bytes 1769480 | tf_op jit(solution)/shard_map/ppermute | solution.py:756
  121.8 15.5 %collective-permute-start.25 = (bf16[2,2,96,768]{3,2,1,0:T(8,128)(2,1)S(1)}, bf16[2,2,96,768]{3,2,1,0:T(8,128)(2,1)S(1)}, u32[]{:S(2)}, u32[]{:S(2)}) collective-permute-start(bf16[2,2,96,768]{3,2,1,0:T(8,128)(2,1)S(1)} %pad_maximum_fusion.10), channel_id=1, source_target_pairs={{0,8},{4,12},{8,0},{12,4},{16,24},{20,28},{24,16},{28,20},{1,9},{5... | collective-permute-start | bytes 1769480 | tf_op jit(solution)/shard_map/ppermute | solution.py:756
  122.4 14.9 %collective-permute-start.23 = (bf16[375,768]{1,0:T(8,128)(2,1)S(1)}, bf16[375,768]{1,0:T(8,128)(2,1)S(1)}, u32[]{:S(2)}, u32[]{:S(2)}) collective-permute-start(bf16[375,768]{1,0:T(8,128)(2,1)S(1)} %bitcast.184), channel_id=1, source_target_pairs={{0,3},{1,0},{2,1},{3,2},{4,7},{5,4},{6,5},{7,6},{8,11},{9,8},{10,9... | collective-permute-start | bytes 1728008 | tf_op jit(solution)/shard_map/ppermute | solution.py:761
  137.3 18.5 %collective-permute-start.27 = (bf16[96,768]{1,0:T(8,128)(2,1)S(1)}, bf16[96,768]{1,0:T(8,128)(2,1)S(1)}, u32[]{:S(2)}, u32[]{:S(2)}) collective-permute-start(bf16[96,768]{1,0:T(8,128)(2,1)S(1)} %bitcast.200), channel_id=1, source_target_pairs={{0,1},{1,2},{2,3},{3,0},{4,5},{5,6},{6,7},{7,4},{8,9},{9,10},{10,1... | collective-permute-start | bytes 442376 | tf_op jit(solution)/shard_map/ppermute | solution.py:761
  137.4 18.4 %collective-permute-start.28 = (bf16[96,768]{1,0:T(8,128)(2,1)S(1)}, bf16[96,768]{1,0:T(8,128)(2,1)S(1)}, u32[]{:S(2)}, u32[]{:S(2)}) collective-permute-start(bf16[96,768]{1,0:T(8,128)(2,1)S(1)} %bitcast.201), channel_id=1, source_target_pairs={{0,2},{1,3},{2,0},{3,1},{4,6},{5,7},{6,4},{7,5},{8,10},{9,11},{10,... | collective-permute-start | bytes 442376 | tf_op jit(solution)/shard_map/ppermute | solution.py:761
  141.4 14.5 %collective-permute-start.29 = (bf16[96,768]{1,0:T(8,128)(2,1)S(1)}, bf16[96,768]{1,0:T(8,128)(2,1)}, u32[]{:S(2)}, u32[]{:S(2)}) collective-permute-start(bf16[96,768]{1,0:T(8,128)(2,1)S(1)} %bitcast.202), channel_id=1, source_target_pairs={{0,3},{1,0},{2,1},{3,2},{4,7},{5,4},{6,5},{7,6},{8,11},{9,8},{10,9... | collective-permute-start | bytes 442376 | tf_op jit(solution)/shard_map/ppermute | solution.py:761
  143.2 13.8 %collective-permute-start.26 = (bf16[4,4,96,768]{3,2,1,0:T(8,128)(2,1)}, bf16[4,4,96,768]{3,2,1,0:T(8,128)(2,1)}, u32[]{:S(2)}, u32[]{:S(2)}) collective-permute-start(bf16[4,4,96,768]{3,2,1,0:T(8,128)(2,1)} %maximum_maximum_fusion.2.refs_3_.refs_4_), channel_id=1, source_target_pairs={{0,4},{4,0},{8,12},{12,8},{16,20},{20,16},{24,28},{28,24},{1,5},{5... | collective-permute-start | bytes 7077896 | tf_op jit(solution)/shard_map/ppermute | solution.py:756
  157.0 22.6 %collective-permute-start.30 = (bf16[1,2,96,768]{3,2,1,0:T(8,128)(2,1)S(1)}, bf16[1,2,96,768]{3,2,1,0:T(8,128)(2,1)S(1)}, u32[]{:S(2)}, u32[]{:S(2)}) collective-permute-start(bf16[1,2,96,768]{3,2,1,0:T(8,128)(2,1)S(1)} %maximum_bitcast_fusion.6), channel_id=1, source_target_pairs={{0,8},{4,12},{8,0},{12,4},{16,24},{20,28},{24,16},{28,20},{1,9},{5... | collective-permute-start | bytes 884744 | tf_op jit(solution)/shard_map/ppermute | solution.py:756
  158.6 21.1 %collective-permute-start.31 = (bf16[1,2,96,768]{3,2,1,0:T(8,128)(2,1)S(1)}, bf16[1,2,96,768]{3,2,1,0:T(8,128)(2,1)S(1)}, u32[]{:S(2)}, u32[]{:S(2)}) collective-permute-start(bf16[1,2,96,768]{3,2,1,0:T(8,128)(2,1)S(1)} %maximum_bitcast_fusion.7), channel_id=1, source_target_pairs={{0,16},{4,20},{8,24},{12,28},{16,0},{20,4},{24,8},{28,12},{1,17},{... | collective-permute-start | bytes 884744 | tf_op jit(solution)/shard_map/ppermute | solution.py:756
  179.8 21.6 %collective-permute-start.33 = (bf16[2,2,96,768]{3,2,1,0:T(8,128)(2,1)S(1)}, bf16[2,2,96,768]{3,2,1,0:T(8,128)(2,1)S(1)}, u32[]{:S(2)}, u32[]{:S(2)}) collective-permute-start(bf16[2,2,96,768]{3,2,1,0:T(8,128)(2,1)S(1)} %pad_maximum_fusion.13), channel_id=1, source_target_pairs={{0,8},{4,12},{8,0},{12,4},{16,24},{20,28},{24,16},{28,20},{1,9},{5... | collective-permute-start | bytes 1769480 | tf_op jit(solution)/shard_map/ppermute | solution.py:756
  180.4 20.9 %collective-permute-start.32 = (bf16[2,2,96,768]{3,2,1,0:T(8,128)(2,1)S(1)}, bf16[2,2,96,768]{3,2,1,0:T(8,128)(2,1)S(1)}, u32[]{:S(2)}, u32[]{:S(2)}) collective-permute-start(bf16[2,2,96,768]{3,2,1,0:T(8,128)(2,1)S(1)} %pad_maximum_fusion.12), channel_id=1, source_target_pairs={{0,16},{4,20},{8,24},{12,28},{16,0},{20,4},{24,8},{28,12},{1,17},{... | collective-permute-start | bytes 1769480 | tf_op jit(solution)/shard_map/ppermute | solution.py:756
  232.1 19.9 %collective-permute-start.35 = (bf16[4,4,96,768]{3,2,1,0:T(8,128)(2,1)}, bf16[4,4,96,768]{3,2,1,0:T(8,128)(2,1)}, u32[]{:S(2)}, u32[]{:S(2)}) collective-permute-start(bf16[4,4,96,768]{3,2,1,0:T(8,128)(2,1)} %get-tuple-element.171), channel_id=1, source_target_pairs={{0,4},{4,0},{8,12},{12,8},{16,20},{20,16},{24,28},{28,24},{1,5},{5... | collective-permute-start | bytes 7077896 | tf_op jit(solution)/shard_map/ppermute | solution.py:756
  255.1 30.5 %collective-permute-start.36 = (bf16[2,2,96,768]{3,2,1,0:T(8,128)(2,1)}, bf16[2,2,96,768]{3,2,1,0:T(8,128)(2,1)}, u32[]{:S(2)}, u32[]{:S(2)}) collective-permute-start(bf16[2,2,96,768]{3,2,1,0:T(8,128)(2,1)} %get-tuple-element.273), channel_id=1, source_target_pairs={{0,16},{4,20},{8,24},{12,28},{16,0},{20,4},{24,8},{28,12},{1,17},{... | collective-permute-start | bytes 1769480 | tf_op jit(solution)/shard_map/ppermute | solution.py:756
  256.2 29.4 %collective-permute-start.37 = (bf16[2,2,96,768]{3,2,1,0:T(8,128)(2,1)}, bf16[2,2,96,768]{3,2,1,0:T(8,128)(2,1)}, u32[]{:S(2)}, u32[]{:S(2)}) collective-permute-start(bf16[2,2,96,768]{3,2,1,0:T(8,128)(2,1)} %get-tuple-element.272), channel_id=1, source_target_pairs={{0,8},{4,12},{8,0},{12,4},{16,24},{20,28},{24,16},{28,20},{1,9},{5... | collective-permute-start | bytes 1769480 | tf_op jit(solution)/shard_map/ppermute | solution.py:756
  260.3 30.4 %collective-permute-start.46 = (bf16[2,2,96,768]{3,2,1,0:T(8,128)(2,1)}, bf16[2,2,96,768]{3,2,1,0:T(8,128)(2,1)S(1)}, u32[]{:S(2)}, u32[]{:S(2)}) collective-permute-start(bf16[2,2,96,768]{3,2,1,0:T(8,128)(2,1)} %get-tuple-element.266), channel_id=1, source_target_pairs={{0,8},{4,12},{8,0},{12,4},{16,24},{20,28},{24,16},{28,20},{1,9},{5... | collective-permute-start | bytes 1769480 | tf_op jit(solution)/shard_map/ppermute | solution.py:756
  260.8 29.9 %collective-permute-start.44 = (bf16[2,2,96,768]{3,2,1,0:T(8,128)(2,1)}, bf16[2,2,96,768]{3,2,1,0:T(8,128)(2,1)S(1)}, u32[]{:S(2)}, u32[]{:S(2)}) collective-permute-start(bf16[2,2,96,768]{3,2,1,0:T(8,128)(2,1)} %get-tuple-element.267), channel_id=1, source_target_pairs={{0,16},{4,20},{8,24},{12,28},{16,0},{20,4},{24,8},{28,12},{1,17},{... | collective-permute-start | bytes 1769480 | tf_op jit(solution)/shard_map/ppermute | solution.py:756
  288.1 30.3 %collective-permute-start.40 = (bf16[2,96,768]{2,1,0:T(8,128)(2,1)}, bf16[2,96,768]{2,1,0:T(8,128)(2,1)S(1)}, u32[]{:S(2)}, u32[]{:S(2)}) collective-permute-start(bf16[2,96,768]{2,1,0:T(8,128)(2,1)} %get-tuple-element.270), channel_id=1, source_target_pairs={{0,16},{4,20},{8,24},{12,28},{16,0},{20,4},{24,8},{28,12},{1,17},{... | collective-permute-start | bytes 884744 | tf_op jit(solution)/shard_map/ppermute | solution.py:756
  289.2 29.3 %collective-permute-start.39 = (bf16[2,96,768]{2,1,0:T(8,128)(2,1)}, bf16[2,96,768]{2,1,0:T(8,128)(2,1)}, u32[]{:S(2)}, u32[]{:S(2)}) collective-permute-start(bf16[2,96,768]{2,1,0:T(8,128)(2,1)} %get-tuple-element.271), channel_id=1, source_target_pairs={{0,8},{4,12},{8,0},{12,4},{16,24},{20,28},{24,16},{28,20},{1,9},{5... | collective-permute-start | bytes 884744 | tf_op jit(solution)/shard_map/ppermute | solution.py:756
  293.2 46.2 %collective-permute-start.45 = (bf16[2,96,768]{2,1,0:T(8,128)(2,1)}, bf16[2,96,768]{2,1,0:T(8,128)(2,1)}, u32[]{:S(2)}, u32[]{:S(2)}) collective-permute-start(bf16[2,96,768]{2,1,0:T(8,128)(2,1)} %get-tuple-element.265), channel_id=1, source_target_pairs={{0,8},{4,12},{8,0},{12,4},{16,24},{20,28},{24,16},{28,20},{1,9},{5... | collective-permute-start | bytes 884744 | tf_op jit(solution)/shard_map/ppermute | solution.py:756
  293.7 45.8 %collective-permute-start.47 = (bf16[2,96,768]{2,1,0:T(8,128)(2,1)}, bf16[2,96,768]{2,1,0:T(8,128)(2,1)}, u32[]{:S(2)}, u32[]{:S(2)}) collective-permute-start(bf16[2,96,768]{2,1,0:T(8,128)(2,1)} %get-tuple-element.264), channel_id=1, source_target_pairs={{0,16},{4,20},{8,24},{12,28},{16,0},{20,4},{24,8},{28,12},{1,17},{... | collective-permute-start | bytes 884744 | tf_op jit(solution)/shard_map/ppermute | solution.py:756
  321.2 21.3 %collective-permute-start.41 = (bf16[96,768]{1,0:T(8,128)(2,1)S(1)}, bf16[96,768]{1,0:T(8,128)(2,1)S(1)}, u32[]{:S(2)}, u32[]{:S(2)}) collective-permute-start(bf16[96,768]{1,0:T(8,128)(2,1)S(1)} %get-tuple-element.289), channel_id=1, source_target_pairs={{0,1},{1,2},{2,3},{3,0},{4,5},{5,6},{6,7},{7,4},{8,9},{9,10},{10,1... | collective-permute-start | bytes 442376 | tf_op jit(solution)/shard_map/ppermute | solution.py:761
  323.2 22.9 %collective-permute-start.42 = (bf16[96,768]{1,0:T(8,128)(2,1)S(1)}, bf16[96,768]{1,0:T(8,128)(2,1)S(1)}, u32[]{:S(2)}, u32[]{:S(2)}) collective-permute-start(bf16[96,768]{1,0:T(8,128)(2,1)S(1)} %get-tuple-element.290), channel_id=1, source_target_pairs={{0,3},{1,0},{2,1},{3,2},{4,7},{5,4},{6,5},{7,6},{8,11},{9,8},{10,9... | collective-permute-start | bytes 442376 | tf_op jit(solution)/shard_map/ppermute | solution.py:761
  325.1 22.1 %collective-permute-start.43 = (bf16[96,768]{1,0:T(8,128)(2,1)S(1)}, bf16[96,768]{1,0:T(8,128)(2,1)S(1)}, u32[]{:S(2)}, u32[]{:S(2)}) collective-permute-start(bf16[96,768]{1,0:T(8,128)(2,1)S(1)} %get-tuple-element.291), channel_id=1, source_target_pairs={{0,2},{1,3},{2,0},{3,1},{4,6},{5,7},{6,4},{7,5},{8,10},{9,11},{10,... | collective-permute-start | bytes 442376 | tf_op jit(solution)/shard_map/ppermute | solution.py:761
  339.4 22.9 %collective-permute-start.48 = (bf16[4,4,96,768]{3,2,1,0:T(8,128)(2,1)}, bf16[4,4,96,768]{3,2,1,0:T(8,128)(2,1)}, u32[]{:S(2)}, u32[]{:S(2)}) collective-permute-start(bf16[4,4,96,768]{3,2,1,0:T(8,128)(2,1)} %get-tuple-element.193), channel_id=1, source_target_pairs={{0,4},{4,0},{8,12},{12,8},{16,20},{20,16},{24,28},{28,24},{1,5},{5... | collective-permute-start | bytes 7077896 | tf_op jit(solution)/shard_map/ppermute | solution.py:756
  342.1 25.4 %collective-permute-start.49 = (bf16[96,768]{1,0:T(8,128)(2,1)S(1)}, bf16[96,768]{1,0:T(8,128)(2,1)S(1)}, u32[]{:S(2)}, u32[]{:S(2)}) collective-permute-start(bf16[96,768]{1,0:T(8,128)(2,1)S(1)} %get-tuple-element.293), channel_id=1, source_target_pairs={{0,1},{1,2},{2,3},{3,0},{4,5},{5,6},{6,7},{7,4},{8,9},{9,10},{10,1... | collective-permute-start | bytes 442376 | tf_op jit(solution)/shard_map/ppermute | solution.py:761
  342.6 24.9 %collective-permute-start.50 = (bf16[96,768]{1,0:T(8,128)(2,1)S(1)}, bf16[96,768]{1,0:T(8,128)(2,1)S(1)}, u32[]{:S(2)}, u32[]{:S(2)}) collective-permute-start(bf16[96,768]{1,0:T(8,128)(2,1)S(1)} %get-tuple-element.294), channel_id=1, source_target_pairs={{0,3},{1,0},{2,1},{3,2},{4,7},{5,4},{6,5},{7,6},{8,11},{9,8},{10,9... | collective-permute-start | bytes 442376 | tf_op jit(solution)/shard_map/ppermute | solution.py:761
  346.2 21.4 %collective-permute-start.51 = (bf16[96,768]{1,0:T(8,128)(2,1)S(1)}, bf16[96,768]{1,0:T(8,128)(2,1)S(1)}, u32[]{:S(2)}, u32[]{:S(2)}) collective-permute-start(bf16[96,768]{1,0:T(8,128)(2,1)S(1)} %get-tuple-element.295), channel_id=1, source_target_pairs={{0,2},{1,3},{2,0},{3,1},{4,6},{5,7},{6,4},{7,5},{8,10},{9,11},{10,... | collective-permute-start | bytes 442376 | tf_op jit(solution)/shard_map/ppermute | solution.py:761
  364.9 30.9 %collective-permute-start.52 = (bf16[2,2,96,768]{3,2,1,0:T(8,128)(2,1)}, bf16[2,2,96,768]{3,2,1,0:T(8,128)(2,1)}, u32[]{:S(2)}, u32[]{:S(2)}) collective-permute-start(bf16[2,2,96,768]{3,2,1,0:T(8,128)(2,1)} %get-tuple-element.261), channel_id=1, source_target_pairs={{0,16},{4,20},{8,24},{12,28},{16,0},{20,4},{24,8},{28,12},{1,17},{... | collective-permute-start | bytes 1769480 | tf_op jit(solution)/shard_map/ppermute | solution.py:756
  366.0 29.8 %collective-permute-start.53 = (bf16[2,2,96,768]{3,2,1,0:T(8,128)(2,1)}, bf16[2,2,96,768]{3,2,1,0:T(8,128)(2,1)}, u32[]{:S(2)}, u32[]{:S(2)}) collective-permute-start(bf16[2,2,96,768]{3,2,1,0:T(8,128)(2,1)} %get-tuple-element.260), channel_id=1, source_target_pairs={{0,8},{4,12},{8,0},{12,4},{16,24},{20,28},{24,16},{28,20},{1,9},{5... | collective-permute-start | bytes 1769480 | tf_op jit(solution)/shard_map/ppermute | solution.py:756
  367.5 24.4 %collective-permute-start.54 = (bf16[375,768]{1,0:T(8,128)(2,1)}, bf16[375,768]{1,0:T(8,128)(2,1)}, u32[]{:S(2)}, u32[]{:S(2)}) collective-permute-start(bf16[375,768]{1,0:T(8,128)(2,1)} %get-tuple-element.198), channel_id=1, source_target_pairs={{0,3},{1,0},{2,1},{3,2},{4,7},{5,4},{6,5},{7,6},{8,11},{9,8},{10,9... | collective-permute-start | bytes 1728008 | tf_op jit(solution)/shard_map/ppermute | solution.py:761
  368.6 27.2 %collective-permute-start.55 = (bf16[375,768]{1,0:T(8,128)(2,1)}, bf16[375,768]{1,0:T(8,128)(2,1)}, u32[]{:S(2)}, u32[]{:S(2)}) collective-permute-start(bf16[375,768]{1,0:T(8,128)(2,1)} %get-tuple-element.200), channel_id=1, source_target_pairs={{0,1},{1,2},{2,3},{3,0},{4,5},{5,6},{6,7},{7,4},{8,9},{9,10},{10,1... | collective-permute-start | bytes 1728008 | tf_op jit(solution)/shard_map/ppermute | solution.py:761
  391.9 22.0 %collective-permute-start.57 = (bf16[4,4,96,768]{3,2,1,0:T(8,128)(2,1)}, bf16[4,4,96,768]{3,2,1,0:T(8,128)(2,1)S(1)}, u32[]{:S(2)}, u32[]{:S(2)}) collective-permute-start(bf16[4,4,96,768]{3,2,1,0:T(8,128)(2,1)} %get-tuple-element.206), channel_id=1, source_target_pairs={{0,4},{4,0},{8,12},{12,8},{16,20},{20,16},{24,28},{28,24},{1,5},{5... | collective-permute-start | bytes 7077896 | tf_op jit(solution)/shard_map/ppermute | solution.py:756
  395.8 30.9 %collective-permute-start.56 = (bf16[375,768]{1,0:T(8,128)(2,1)}, bf16[375,768]{1,0:T(8,128)(2,1)S(1)}, u32[]{:S(2)}, u32[]{:S(2)}) collective-permute-start(bf16[375,768]{1,0:T(8,128)(2,1)} %get-tuple-element.205), channel_id=1, source_target_pairs={{0,2},{1,3},{2,0},{3,1},{4,6},{5,7},{6,4},{7,5},{8,10},{9,11},{10,... | collective-permute-start | bytes 1728008 | tf_op jit(solution)/shard_map/ppermute | solution.py:761
  398.7 10.7 %collective-permute-start.58 = (bf16[2,96,768]{2,1,0:T(8,128)(2,1)}, bf16[2,96,768]{2,1,0:T(8,128)(2,1)S(1)}, u32[]{:S(2)}, u32[]{:S(2)}) collective-permute-start(bf16[2,96,768]{2,1,0:T(8,128)(2,1)} %get-tuple-element.259), channel_id=1, source_target_pairs={{0,8},{4,12},{8,0},{12,4},{16,24},{20,28},{24,16},{28,20},{1,9},{5... | collective-permute-start | bytes 884744 | tf_op jit(solution)/shard_map/ppermute | solution.py:756
  399.3 10.2 %collective-permute-start.59 = (bf16[2,96,768]{2,1,0:T(8,128)(2,1)S(1)}, bf16[2,96,768]{2,1,0:T(8,128)(2,1)S(1)}, u32[]{:S(2)}, u32[]{:S(2)}) collective-permute-start(bf16[2,96,768]{2,1,0:T(8,128)(2,1)S(1)} %get-tuple-element.258), channel_id=1, source_target_pairs={{0,16},{4,20},{8,24},{12,28},{16,0},{20,4},{24,8},{28,12},{1,17},{... | collective-permute-start | bytes 884744 | tf_op jit(solution)/shard_map/ppermute | solution.py:756
  411.5 35.2 %collective-permute-start.69 = (bf16[96,768]{1,0:T(8,128)(2,1)S(1)}, bf16[96,768]{1,0:T(8,128)(2,1)S(1)}, u32[]{:S(2)}, u32[]{:S(2)}) collective-permute-start(bf16[96,768]{1,0:T(8,128)(2,1)S(1)} %get-tuple-element.297), channel_id=1, source_target_pairs={{0,3},{1,0},{2,1},{3,2},{4,7},{5,4},{6,5},{7,6},{8,11},{9,8},{10,9... | collective-permute-start | bytes 442376 | tf_op jit(solution)/shard_map/ppermute | solution.py:761
  413.3 33.5 %collective-permute-start.68 = (bf16[96,768]{1,0:T(8,128)(2,1)S(1)}, bf16[96,768]{1,0:T(8,128)(2,1)S(1)}, u32[]{:S(2)}, u32[]{:S(2)}) collective-permute-start(bf16[96,768]{1,0:T(8,128)(2,1)S(1)} %get-tuple-element.296), channel_id=1, source_target_pairs={{0,1},{1,2},{2,3},{3,0},{4,5},{5,6},{6,7},{7,4},{8,9},{9,10},{10,1... | collective-permute-start | bytes 442376 | tf_op jit(solution)/shard_map/ppermute | solution.py:761
  414.2 18.5 %collective-permute-start.62 = (bf16[2,2,96,768]{3,2,1,0:T(8,128)(2,1)S(1)}, bf16[2,2,96,768]{3,2,1,0:T(8,128)(2,1)S(1)}, u32[]{:S(2)}, u32[]{:S(2)}) collective-permute-start(bf16[2,2,96,768]{3,2,1,0:T(8,128)(2,1)S(1)} %get-tuple-element.254), channel_id=1, source_target_pairs={{0,8},{4,12},{8,0},{12,4},{16,24},{20,28},{24,16},{28,20},{1,9},{5... | collective-permute-start | bytes 1769480 | tf_op jit(solution)/shard_map/ppermute | solution.py:756
  415.7 17.1 %collective-permute-start.60 = (bf16[2,2,96,768]{3,2,1,0:T(8,128)(2,1)S(1)}, bf16[2,2,96,768]{3,2,1,0:T(8,128)(2,1)S(1)}, u32[]{:S(2)}, u32[]{:S(2)}) collective-permute-start(bf16[2,2,96,768]{3,2,1,0:T(8,128)(2,1)S(1)} %get-tuple-element.255), channel_id=1, source_target_pairs={{0,16},{4,20},{8,24},{12,28},{16,0},{20,4},{24,8},{28,12},{1,17},{... | collective-permute-start | bytes 1769480 | tf_op jit(solution)/shard_map/ppermute | solution.py:756
  440.5 14.7 %collective-permute-start.64 = (bf16[2,96,768]{2,1,0:T(8,128)(2,1)S(1)}, bf16[2,96,768]{2,1,0:T(8,128)(2,1)S(1)}, u32[]{:S(2)}, u32[]{:S(2)}) collective-permute-start(bf16[2,96,768]{2,1,0:T(8,128)(2,1)S(1)} %get-tuple-element.252), channel_id=1, source_target_pairs={{0,16},{4,20},{8,24},{12,28},{16,0},{20,4},{24,8},{28,12},{1,17},{... | collective-permute-start | bytes 884744 | tf_op jit(solution)/shard_map/ppermute | solution.py:756
  444.9 10.3 %collective-permute-start.61 = (bf16[2,96,768]{2,1,0:T(8,128)(2,1)S(1)}, bf16[2,96,768]{2,1,0:T(8,128)(2,1)S(1)}, u32[]{:S(2)}, u32[]{:S(2)}) collective-permute-start(bf16[2,96,768]{2,1,0:T(8,128)(2,1)S(1)} %get-tuple-element.253), channel_id=1, source_target_pairs={{0,8},{4,12},{8,0},{12,4},{16,24},{20,28},{24,16},{28,20},{1,9},{5... | collective-permute-start | bytes 884744 | tf_op jit(solution)/shard_map/ppermute | solution.py:756
  445.4 9.6 %collective-permute-start.63 = (bf16[96,768]{1,0:T(8,128)(2,1)S(1)}, bf16[96,768]{1,0:T(8,128)(2,1)S(1)}, u32[]{:S(2)}, u32[]{:S(2)}) collective-permute-start(bf16[96,768]{1,0:T(8,128)(2,1)S(1)} %dynamic-slice_bitcast_fusion), channel_id=1, source_target_pairs={{0,2},{1,3},{2,0},{3,1},{4,6},{5,7},{6,4},{7,5},{8,10},{9,11},{10,... | collective-permute-start | bytes 442376 | tf_op jit(solution)/shard_map/ppermute | solution.py:761
  455.8 12.0 %collective-permute-start.66 = (bf16[96,768]{1,0:T(8,128)(2,1)S(1)}, bf16[96,768]{1,0:T(8,128)(2,1)S(1)}, u32[]{:S(2)}, u32[]{:S(2)}) collective-permute-start(bf16[96,768]{1,0:T(8,128)(2,1)S(1)} %get-tuple-element.299), channel_id=1, source_target_pairs={{0,3},{1,0},{2,1},{3,2},{4,7},{5,4},{6,5},{7,6},{8,11},{9,8},{10,9... | collective-permute-start | bytes 442376 | tf_op jit(solution)/shard_map/ppermute | solution.py:761
  457.1 10.7 %collective-permute-start.65 = (bf16[96,768]{1,0:T(8,128)(2,1)S(1)}, bf16[96,768]{1,0:T(8,128)(2,1)S(1)}, u32[]{:S(2)}, u32[]{:S(2)}) collective-permute-start(bf16[96,768]{1,0:T(8,128)(2,1)S(1)} %get-tuple-element.298), channel_id=1, source_target_pairs={{0,1},{1,2},{2,3},{3,0},{4,5},{5,6},{6,7},{7,4},{8,9},{9,10},{10,1... | collective-permute-start | bytes 442376 | tf_op jit(solution)/shard_map/ppermute | solution.py:761
  (71 other events, 463.5 us)

commit v5 on v4

--- a/solution.py
+++ b/solution.py
@@ -1083,7 +1083,10 @@
         scatters["self"].low_x = gate(scatters["self"].low_x, go("cross", "across"))
     sums = gate(sums, turns[0])
     sums = sums + swap(sums, 1)
-    sums = sum([around(sums, hop) for hop in range(1, tp)], sums)
+    step = 1
+    while step < tp:
+        sums = sums + lax.ppermute(sums, "tp", [(i, i ^ step) for i in range(tp)])
+        step *= 2
     sums = gate(sums, turns[-1])
     step = 2
     while step < fsdp:

time: 478 us -> 475 us (level)
    ppermute x33 -> x30, waiting for transfers between devices: 69.4 us -> 61.6 us  [around(): lax.ppermute(array, 'tp', [(i, (i + hop) % count) for i in range(count)])]
    ppermute x33 -> x30, starting transfers between devices: 49.6 us -> 47.1 us  [around(): lax.ppermute(array, 'tp', [(i, (i + hop) % count) for i in range(count)])]
  transfers between devices with their start and end apart: 76 -> 75, of which waited for: 21 -> 21; matrix products, arithmetic and copies ran while one was open for 13% -> 13% of each run, Pallas kernels for 42% -> 42%
where the time goes in v5:
time: 475 us; the launch traced here: 469 us
  Pallas kernels  221 us (47%)
  starting transfers between devices  85.3 us (18%)
  waiting for transfers between devices  77.7 us (16%)
  other arithmetic  48.1 us (10%)
  local copies, waits for them, and re-layouts  34.1 us (7%)
    pallas_call x13, Pallas kernels, call(): pl.pallas_call(inner, out_shape=[o for o, _ in outs], grid_spec=pltpu.Pre...  221 us
    ppermute x30, waiting for transfers between devices, around(): lax.ppermute(array, 'tp', [(i, (i + hop) % count) for i in range(count)])  61.6 us
    ppermute x30, starting transfers between devices, around(): lax.ppermute(array, 'tp', [(i, (i + hop) % count) for i in range(count)])  47.1 us
    ppermute x43, starting transfers between devices, swap(): return lax.ppermute(array, 'fsdp', [(i, i ^ step) for i in range(count)])  36.2 us
    unnamed x134, local copies, waits for them, and re-layouts  15.7 us
    ppermute x43, waiting for transfers between devices, swap(): return lax.ppermute(array, 'fsdp', [(i, i ^ step) for i in range(count)])  11.8 us
  transfers between devices with their start and end apart: 75, of which 21 were waited for; matrix products, arithmetic and copies ran while one was open for 13% of the time, Pallas kernels for 42%

profile of v5, /device:TPU:0, one launch (start us, length us, event | category | flops | bytes accessed | tf_op | source)
XLA Modules:
  0.0 468.5 jit_solution(18179974644927161561)
XLA Ops:
  7.6 5.1 %collective-permute-start.2 = (bf16[112,768]{1,0:T(8,128)(2,1)}, bf16[112,768]{1,0:T(8,128)(2,1)}, u32[]{:S(2)}, u32[]{:S(2)}) collective-permute-start(bf16[112,768]{1,0:T(8,128)(2,1)} %pad_maximum_fusion.16), channel_id=1, source_target_pairs={{0,3},{1,0},{2,1},{3,2},{4,7},{5,4},{6,5},{7,6},{8,11},{9,8},{10,9... | collective-permute-start | bytes 516104 | tf_op jit(solution)/shard_map/ppermute | solution.py:761
  13.7 8.4 %constant_dynamic-slice_fusion.27 = (bf16[1,375,768]{2,0,1:T(2,128)(2,1)S(1)}, bf16[1,375,768]{2,0,1:T(2,128)(2,1)S(1)}, bf16[1,375,768]{2,0,1:T(2,128)(2,1)S(1)}, bf16[1,375,768]{2,0,1:T(2,128)(2,1)}) fusion(bf16[4,375,768]{2,0,1:T(4,128)(2,1)} %param.16, s32[]{:T(128)S(6)} %select_n.201, s32[]{:T(128)S(6)} %select_n.199, s32[]{:T(128)S(6)} %select_n.197, ...), kind=kLoop, calls=%fused_computation.206 | loop fusion | bytes 4608016 | tf_op jit(solution)/shard_map/jit(dynamic_index_in_dim)/dynamic_slice | solution.py:953
  22.1 2.1 copy.67
  28.9 1.6 collective-permute-start.4
  30.5 1.6 collective-permute-start.3
  32.3 2.0 collective-permute-start.5
  35.2 2.8 collective-permute-start.7
  38.1 2.8 collective-permute-done.5
  40.9 4.5 collective-permute-done.6
  47.4 3.6 collective-permute-start.10
  51.0 1.6 collective-permute-start.11
  53.4 3.4 collective-permute-done.10
  56.8 4.6 collective-permute-done.11
  61.4 2.1 collective-permute-done.9
  70.9 1.6 collective-permute-start.14
  73.0 3.9 collective-permute-start.20
  86.6 1.5 collective-permute-start.19
  90.5 1.6 collective-permute-start.21
  92.1 17.8 %self_forward.1 = (bf16[4,448,192]{2,1,0:T(8,128)(2,1)}, bf16[4,448,192]{2,1,0:T(8,128)(2,1)}, bf16[4,448,192]{2,1,0:T(8,128)(2,1)}, f32[4,8,448]{2,1,0:T(8,128)...) custom-call(s32[1]{0:T(128)} %dynamic_slice.157.refs_0_, ...), custom_call_target="tpu_custom_call" | custom-call | flops 91603599360 | bytes 13918208 | tf_op jit(solution)/shard_map/self_forward/pallas_call | solution.py:80
  110.0 8.2 %collective-permute-done.21.refs_3_ = bf16[375,768]{1,0:T(8,128)(2,1)} collective-permute-done((bf16[375,768]{1,0:T(8,128)(2,1)}, bf16[375,768]{1,0:T(8,128)(2,1)}, u32[]{:S(2)}, u32[]{:S(2)}) %collective-permute-start.21) | collective-permute-done | bytes 576032 | tf_op jit(solution)/shard_map/ppermute | solution.py:761
  119.0 1.7 maximum_maximum_fusion.1.refs_5_.refs_3_.refs_9_.refs_6_
  122.4 1.6 collective-permute-start.23
  124.0 13.3 %collective-permute-done.23.refs_4_.refs_11_ = bf16[375,768]{1,0:T(8,128)(2,1)S(1)} collective-permute-done((bf16[375,768]{1,0:T(8,128)(2,1)S(1)}, bf16[375,768]{1,0:T(8,128)(2,1)S(1)}, u32[]{:S(2)}, u32[]{:S(2)}) %collective-permute-start.23) | collective-permute-done | bytes 576032 | tf_op jit(solution)/shard_map/ppermute | solution.py:761
  137.4 4.0 collective-permute-start.28
  141.7 1.5 maximum_maximum_fusion.2.refs_3_.refs_4_
  143.2 12.6 %frame_keys.1 = (bf16[4,4,384,192]{3,2,1,0:T(8,128)(2,1)}, bf16[4,4,384,192]{3,2,1,0:T(8,128)(2,1)}, bf16[4,192,1536]{2,1,0:T(8,128)(2,1)}, bf16[4,192,1536]{2,1,0:T(8,128)(2,1)}, bf16[4,384,768]{2,1,0:T(8,128)(2,1)}) custom-call(s32[2]{0:T(128)} %pad_add_fusion.refs_1_.refs_0_, bf16[375,768]{1,0:T(8,128)(2,1)} %bitcast.183, ...), custom_call_target="tpu_custom_call" | custom-call | flops 72477573120 | bytes 18843648 | tf_op jit(solution)/shard_map/frame_keys/pallas_call | solution.py:80
  157.1 1.5 collective-permute-start.30
  159.7 19.9 %cross_forward.2 = (bf16[4,448,192]{2,1,0:T(8,128)(2,1)}, f32[4,8,448]{2,1,0:T(8,128)}, f32[4,192,448]{2,1,0:T(8,128)}, bf16[4,448,192]{2,1,0:T(8,128)(2,1)}, f3...) custom-call(s32[2]{0:T(128)} %pad_add_fusion.refs_1_.refs_0_, bf16[448,768]{1,0:T(8,128)(2,1)} %get-tuple-element.126.refs_1_.refs_5_, ...), custom_call_target="tpu_custom_call" | custom-call | flops 95126814720 | bytes 16474112 | tf_op jit(solution)/shard_map/cross_forward/pallas_call | solution.py:80
  181.4 20.0 %cross_forward.3 = (bf16[4,448,192]{2,1,0:T(8,128)(2,1)}, f32[4,8,448]{2,1,0:T(8,128)}, f32[4,192,448]{2,1,0:T(8,128)}, bf16[4,448,192]{2,1,0:T(8,128)(2,1)}, f3...) custom-call(s32[2]{0:T(128)} %pad_add_fusion.refs_1_.refs_0_, ...), custom_call_target="tpu_custom_call", output_to_operand_aliasing={{0}: (9, {}), {1}: (10, {}), {2}: (11, {}), {3}: (12, {})} | custom-call | flops 95126814720 | bytes 16474112 | tf_op jit(solution)/shard_map/cross_forward/pallas_call | solution.py:80
  202.9 4.5 collective-permute-done.34.refs_6_.refs_7_
  208.8 15.5 %feed_forward.1 = (bf16[4,448,768]{2,1,0:T(8,128)(2,1)}, f32[4,448,768]{2,1,0:T(8,128)}, bf16[448,768]{1,0:T(8,128)(2,1)}, f32[448,768]{1,0:T(8,128)}, bf16[448,768]{1,0:T(8,128)(2,1)}, /*index=5*/f32[24,768]{1,0:T(8,128)}) custom-call(s32[2]{0:T(128)} %pad_add_fusion.refs_1_.refs_0_, bf16[448,768]{1,0:T(8,128)(2,1)} %get-tuple-element.151.refs_1_.refs_8_, ...), custom_call_target="tpu_custom_call" | custom-call | flops 84557168640 | bytes 23347200 | tf_op jit(solution)/shard_map/feed_forward/pallas_call | solution.py:80
  224.3 7.8 %feed_out_grads.1 = (bf16[4,4,96,768]{3,2,1,0:T(8,128)(2,1)}, bf16[4,4,96,768]{3,2,1,0:T(8,128)(2,1)}) custom-call(s32[2]{0:T(128)} %pad_add_fusion.refs_1_.refs_0_, bf16[448,768]{1,0:T(8,128)(2,1)} %get-tuple-element.158.refs_1_, bf16[4,448,768]{2,1,0:T(8,128)(2,1)} %get-tuple-element.162.refs_2_), custom_call_target="tpu_custom_call" | custom-call | flops 42278584320 | bytes 8159232 | tf_op jit(solution)/shard_map/feed_out_grads/pallas_call | solution.py:80
  232.3 19.4 %feed_backward.1 = (bf16[4,4,96,768]{3,2,1,0:T(8,128)(2,1)}, bf16[4,4,96,768]{3,2,1,0:T(8,128)(2,1)}, f32[448,768]{1,0:T(8,128)}, bf16[448,768]{1,0:T(8,128)(2,1)}, f32[24,768]{1,0:T(8,128)}) custom-call(s32[2]{0:T(128)} %pad_add_fusion.refs_1_.refs_0_, bf16[448,768]{1,0:T(8,128)(2,1)} %get-tuple-element.158.refs_1_, f32[448,768]{1,0:T(8,128)} %get-tuple-element.159.refs_2_, ...), custom_call_target="tpu_custom_call" | custom-call | flops 126835752960 | bytes 26075136 | tf_op jit(solution)/shard_map/feed_backward/pallas_call | solution.py:80
  252.1 3.1 add_convert_fusion.6
  256.3 1.5 collective-permute-start.37
  257.8 2.6 add_convert_fusion.4
  261.8 23.9 %cross_attend_back.2 = (bf16[4,448,192]{2,1,0:T(8,128)(2,1)}, bf16[4,4,384,384]{3,2,1,0:T(8,128)(2,1)}, f32[24,768]{1,0:T(8,128)}) custom-call(s32[2]{0:T(128)} %pad_add_fusion.refs_1_.refs_0_, f32[24,768]{1,0:T(8,128)} %get-tuple-element.164.refs_1_, bf16[448,768]{1,0:T(8,128)(2,1)} %get-tuple-element.165.refs_2_.refs_4_, ...), custom_call_target="tpu_custom_call" | custom-call | flops 110981283840 | bytes 20160512 | tf_op jit(solution)/shard_map/cross_attend_back/pallas_call | solution.py:80
  285.8 2.4 fusion.9
  289.3 1.5 collective-permute-start.39
  290.8 2.5 fusion.11
  294.8 23.7 %cross_attend_back.3 = (bf16[4,448,192]{2,1,0:T(8,128)(2,1)}, bf16[4,4,384,384]{3,2,1,0:T(8,128)(2,1)}, f32[24,768]{1,0:T(8,128)}) custom-call(s32[2]{0:T(128)} %pad_add_fusion.refs_1_.refs_0_, f32[24,768]{1,0:T(8,128)} %get-tuple-element.172.refs_1_, ...), custom_call_target="tpu_custom_call", output_to_operand_aliasing={{0}: (11, {}), {1}: (12, {})} | custom-call | flops 110981283840 | bytes 20160512 | tf_op jit(solution)/shard_map/cross_attend_back/pallas_call | solution.py:80
  318.6 1.9 fusion.6
  321.4 2.0 collective-permute-start.41
  323.4 1.8 collective-permute-start.42
  325.3 14.2 %cross_grads.1 = (bf16[4,4,96,768]{3,2,1,0:T(8,128)(2,1)}, bf16[4,4,96,768]{3,2,1,0:T(8,128)(2,1)}) custom-call(s32[2]{0:T(128)} %pad_add_fusion.refs_1_.refs_0_, bf16[4,448,192]{2,1,0:T(8,128)(2,1)} %get-tuple-element.177.refs_1_.refs_2_, bf16[4,4,384,384]{3,2,1,0:T(8,128)(2,1)} %get-tuple-element.178.refs_2_.refs_3_, ...), custom_call_target="tpu_custom_call" | custom-call | flops 93616865280 | bytes 14548992 | tf_op jit(solution)/shard_map/cross_grads/pallas_call | solution.py:80
  339.6 1.7 fusion.4
  342.7 3.5 collective-permute-start.50
  348.0 14.5 %cross_rows_back.1 = (bf16[375,768]{1,0:T(8,128)(2,1)}, bf16[375,768]{1,0:T(8,128)(2,1)}, bf16[375,768]{1,0:T(8,128)(2,1)}, bf16[375,768]{1,0:T(8,128)(2,1)}, f3...) custom-call(s32[2]{0:T(128)} %pad_add_fusion.refs_1_.refs_0_, ...), custom_call_target="tpu_custom_call" | custom-call | flops 83047219200 | bytes 17467392 | tf_op jit(solution)/shard_map/cross_rows_back/pallas_call | solution.py:80
  362.5 2.6 add_convert_fusion.2
  369.8 22.3 %self_attend_back.1 = (bf16[4,4,96,768]{3,2,1,0:T(8,128)(2,1)}, bf16[4,4,96,768]{3,2,1,0:T(8,128)(2,1)}, bf16[4,448,576]{2,1,0:T(8,128)(2,1)}, f32[24,768]{1,0:T(8,128)}) custom-call(s32[1]{0:T(128)} %dynamic_slice.157.refs_0_, s32[2]{0:T(128)} %pad_add_fusion.refs_1_.refs_0_, f32[24,768]{1,0:T(8,128)} %get-tuple-element.184.refs_2_, ...), custom_call_target="tpu_custom_call" | custom-call | flops 176160768000 | bytes 17997824 | tf_op jit(solution)/shard_map/self_attend_back/pallas_call | solution.py:80
  392.1 3.8 collective-permute-done.55.refs_11_
  396.5 2.3 fusion.13
  400.2 9.4 %self_rows_back.1 = (f32[448,768]{1,0:T(8,128)}, f32[24,768]{1,0:T(8,128)}) custom-call(s32[2]{0:T(128)} %pad_add_fusion.refs_1_.refs_0_, f32[24,768]{1,0:T(8,128)} %get-tuple-element.194.refs_1_, bf16[4,448,576]{2,1,0:T(8,128)(2,1)} %get-tuple-element.195.refs_2_, f32[448,768]{1,0:T(8,128)} %get-tuple-element.196.refs_3_, bf16[448,768]{1,0:T(8,128)(2,1)} %bitcast.215, ...), custom_call_target="tpu_custom_call" | custom-call | flops 31708938240 | bytes 11231232 | tf_op jit(solution)/shard_map/self_rows_back/pallas_call | solution.py:80
  409.6 1.9 fusion.2
  411.6 1.8 collective-permute-start.69
  417.1 9.7 %collective-permute-done.56 = bf16[375,768]{1,0:T(8,128)(2,1)S(1)} collective-permute-done((bf16[375,768]{1,0:T(8,128)(2,1)}, bf16[375,768]{1,0:T(8,128)(2,1)S(1)}, u32[]{:S(2)}, u32[]{:S(2)}) %collective-permute-start.56) | collective-permute-done | bytes 576032 | tf_op jit(solution)/shard_map/ppermute | solution.py:761
  426.8 1.5 pad_maximum_fusion
  428.9 3.9 copy.53
  435.8 4.3 collective-permute-done.71
  442.0 1.9 collective-permute-start.72
  443.9 6.9 %collective-permute-done.63 = bf16[96,768]{1,0:T(8,128)(2,1)S(1)} collective-permute-done((bf16[96,768]{1,0:T(8,128)(2,1)S(1)}, bf16[96,768]{1,0:T(8,128)(2,1)S(1)}, u32[]{:S(2)}, u32[]{:S(2)}) %collective-permute-start.63) | collective-permute-done | bytes 147488 | tf_op jit(solution)/shard_map/ppermute | solution.py:761
  451.6 2.3 collective-permute-start.66
  458.0 2.2 collective-permute-done.73
  461.9 2.5 collective-permute-done.66
  (339 shorter events, 81.7 us)
Async XLA Ops:
  7.6 19.4 %collective-permute-start.2 = (bf16[112,768]{1,0:T(8,128)(2,1)}, bf16[112,768]{1,0:T(8,128)(2,1)}, u32[]{:S(2)}, u32[]{:S(2)}) collective-permute-start(bf16[112,768]{1,0:T(8,128)(2,1)} %pad_maximum_fusion.16), channel_id=1, source_target_pairs={{0,3},{1,0},{2,1},{3,2},{4,7},{5,4},{6,5},{7,6},{8,11},{9,8},{10,9... | collective-permute-start | bytes 516104 | tf_op jit(solution)/shard_map/ppermute | solution.py:761
  12.7 14.9 %collective-permute-start.1 = (bf16[112,768]{1,0:T(8,128)(2,1)}, bf16[112,768]{1,0:T(8,128)(2,1)}, u32[]{:S(2)}, u32[]{:S(2)}) collective-permute-start(bf16[112,768]{1,0:T(8,128)(2,1)} %pad_maximum_fusion.16), channel_id=1, source_target_pairs={{0,2},{1,3},{2,0},{3,1},{4,6},{5,7},{6,4},{7,5},{8,10},{9,11},{10,... | collective-permute-start | bytes 516104 | tf_op jit(solution)/shard_map/ppermute | solution.py:761
  12.7 14.9 %collective-permute-start = (bf16[112,768]{1,0:T(8,128)(2,1)}, bf16[112,768]{1,0:T(8,128)(2,1)}, u32[]{:S(2)}, u32[]{:S(2)}) collective-permute-start(bf16[112,768]{1,0:T(8,128)(2,1)} %pad_maximum_fusion.16), channel_id=1, source_target_pairs={{0,1},{1,2},{2,3},{3,0},{4,5},{5,6},{6,7},{7,4},{8,9},{9,10},{10,1... | collective-permute-start | bytes 516104 | tf_op jit(solution)/shard_map/ppermute | solution.py:761
  28.9 16.5 %collective-permute-start.4 = (bf16[1,2,112,768]{3,2,1,0:T(8,128)(2,1)S(1)}, bf16[1,2,112,768]{3,2,1,0:T(8,128)(2,1)S(1)}, u32[]{:S(2)}, u32[]{:S(2)}) collective-permute-start(bf16[1,2,112,768]{3,2,1,0:T(8,128)(2,1)S(1)} %maximum_bitcast_fusion.1), channel_id=1, source_target_pairs={{0,16},{4,20},{8,24},{12,28},{16,0},{20,4},{24,8},{28,12},{1,17},{... | collective-permute-start | bytes 1032200 | tf_op jit(solution)/shard_map/ppermute | solution.py:756
  30.5 15.6 %collective-permute-start.3 = (bf16[1,2,112,768]{3,2,1,0:T(8,128)(2,1)S(1)}, bf16[1,2,112,768]{3,2,1,0:T(8,128)(2,1)S(1)}, u32[]{:S(2)}, u32[]{:S(2)}) collective-permute-start(bf16[1,2,112,768]{3,2,1,0:T(8,128)(2,1)S(1)} %maximum_bitcast_fusion), channel_id=1, source_target_pairs={{0,8},{4,12},{8,0},{12,4},{16,24},{20,28},{24,16},{28,20},{1,9},{5... | collective-permute-start | bytes 1032200 | tf_op jit(solution)/shard_map/ppermute | solution.py:756
  34.3 11.1 %collective-permute-start.6 = (bf16[96,768]{1,0:T(8,128)(2,1)S(1)}, bf16[96,768]{1,0:T(8,128)(2,1)S(1)}, u32[]{:S(2)}, u32[]{:S(2)}) collective-permute-start(bf16[96,768]{1,0:T(8,128)(2,1)S(1)} %pad_maximum_fusion.17), channel_id=1, source_target_pairs={{0,2},{1,3},{2,0},{3,1},{4,6},{5,7},{6,4},{7,5},{8,10},{9,11},{10,... | collective-permute-start | bytes 442376 | tf_op jit(solution)/shard_map/ppermute | solution.py:761
  35.2 10.2 %collective-permute-start.7 = (bf16[96,768]{1,0:T(8,128)(2,1)S(1)}, bf16[96,768]{1,0:T(8,128)(2,1)S(1)}, u32[]{:S(2)}, u32[]{:S(2)}) collective-permute-start(bf16[96,768]{1,0:T(8,128)(2,1)S(1)} %pad_maximum_fusion.17), channel_id=1, source_target_pairs={{0,3},{1,0},{2,1},{3,2},{4,7},{5,4},{6,5},{7,6},{8,11},{9,8},{10,9... | collective-permute-start | bytes 442376 | tf_op jit(solution)/shard_map/ppermute | solution.py:761
  46.2 17.3 %collective-permute-start.9 = (bf16[2,2,112,768]{3,2,1,0:T(8,128)(2,1)S(1)}, bf16[2,2,112,768]{3,2,1,0:T(8,128)(2,1)S(1)}, u32[]{:S(2)}, u32[]{:S(2)}) collective-permute-start(bf16[2,2,112,768]{3,2,1,0:T(8,128)(2,1)S(1)} %pad_maximum_fusion.4), channel_id=1, source_target_pairs={{0,8},{4,12},{8,0},{12,4},{16,24},{20,28},{24,16},{28,20},{1,9},{5... | collective-permute-start | bytes 2064392 | tf_op jit(solution)/shard_map/ppermute | solution.py:756
  46.9 17.0 %collective-permute-start.8 = (bf16[2,2,112,768]{3,2,1,0:T(8,128)(2,1)S(1)}, bf16[2,2,112,768]{3,2,1,0:T(8,128)(2,1)S(1)}, u32[]{:S(2)}, u32[]{:S(2)}) collective-permute-start(bf16[2,2,112,768]{3,2,1,0:T(8,128)(2,1)S(1)} %pad_maximum_fusion.3), channel_id=1, source_target_pairs={{0,16},{4,20},{8,24},{12,28},{16,0},{20,4},{24,8},{28,12},{1,17},{... | collective-permute-start | bytes 2064392 | tf_op jit(solution)/shard_map/ppermute | solution.py:756
  51.0 10.4 %collective-permute-start.11 = (bf16[96,768]{1,0:T(8,128)(2,1)S(1)}, bf16[96,768]{1,0:T(8,128)(2,1)S(1)}, u32[]{:S(2)}, u32[]{:S(2)}) collective-permute-start(bf16[96,768]{1,0:T(8,128)(2,1)S(1)} %copy-done.29), channel_id=1, source_target_pairs={{0,2},{1,3},{2,0},{3,1},{4,6},{5,7},{6,4},{7,5},{8,10},{9,11},{10,... | collective-permute-start | bytes 442376 | tf_op jit(solution)/shard_map/ppermute | solution.py:761
  65.4 11.5 %collective-permute-start.13 = (bf16[4,4,112,768]{3,2,1,0:T(8,128)(2,1)S(1)}, bf16[4,4,112,768]{3,2,1,0:T(8,128)(2,1)}, u32[]{:S(2)}, u32[]{:S(2)}) collective-permute-start(bf16[4,4,112,768]{3,2,1,0:T(8,128)(2,1)S(1)} %maximum_maximum_fusion.refs_4_.refs_11_.refs_5_), channel_id=1, source_target_pairs={{0,4},{4,0},{8,12},{12,8},{16,20},{20,16},{24,28},{28,24},{1,5},{5... | collective-permute-start | bytes 8257544 | tf_op jit(solution)/shard_map/ppermute | solution.py:756
  73.0 17.5 %collective-permute-start.20 = (bf16[375,768]{1,0:T(8,128)(2,1)}, bf16[375,768]{1,0:T(8,128)(2,1)}, u32[]{:S(2)}, u32[]{:S(2)}) collective-permute-start(bf16[375,768]{1,0:T(8,128)(2,1)} %bitcast.178), channel_id=1, source_target_pairs={{0,1},{1,2},{2,3},{3,0},{4,5},{5,6},{6,7},{7,4},{8,9},{9,10},{10,1... | collective-permute-start | bytes 1728008 | tf_op jit(solution)/shard_map/ppermute | solution.py:761
  82.8 35.4 %collective-permute-start.17 = (bf16[2,2,96,768]{3,2,1,0:T(8,128)(2,1)S(1)}, bf16[2,2,96,768]{3,2,1,0:T(8,128)(2,1)S(1)}, u32[]{:S(2)}, u32[]{:S(2)}) collective-permute-start(bf16[2,2,96,768]{3,2,1,0:T(8,128)(2,1)S(1)} %pad_maximum_fusion.7), channel_id=1, source_target_pairs={{0,8},{4,12},{8,0},{12,4},{16,24},{20,28},{24,16},{28,20},{1,9},{5... | collective-permute-start | bytes 1769480 | tf_op jit(solution)/shard_map/ppermute | solution.py:756
  84.6 33.7 %collective-permute-start.16 = (bf16[2,2,96,768]{3,2,1,0:T(8,128)(2,1)S(1)}, bf16[2,2,96,768]{3,2,1,0:T(8,128)(2,1)S(1)}, u32[]{:S(2)}, u32[]{:S(2)}) collective-permute-start(bf16[2,2,96,768]{3,2,1,0:T(8,128)(2,1)S(1)} %pad_maximum_fusion.6), channel_id=1, source_target_pairs={{0,16},{4,20},{8,24},{12,28},{16,0},{20,4},{24,8},{28,12},{1,17},{... | collective-permute-start | bytes 1769480 | tf_op jit(solution)/shard_map/ppermute | solution.py:756
  85.1 24.8 %collective-permute-start.18 = (bf16[1,2,96,768]{3,2,1,0:T(8,128)(2,1)S(1)}, bf16[1,2,96,768]{3,2,1,0:T(8,128)(2,1)S(1)}, u32[]{:S(2)}, u32[]{:S(2)}) collective-permute-start(bf16[1,2,96,768]{3,2,1,0:T(8,128)(2,1)S(1)} %maximum_bitcast_fusion.4), channel_id=1, source_target_pairs={{0,8},{4,12},{8,0},{12,4},{16,24},{20,28},{24,16},{28,20},{1,9},{5... | collective-permute-start | bytes 884744 | tf_op jit(solution)/shard_map/ppermute | solution.py:756
  86.6 23.3 %collective-permute-start.19 = (bf16[1,2,96,768]{3,2,1,0:T(8,128)(2,1)S(1)}, bf16[1,2,96,768]{3,2,1,0:T(8,128)(2,1)S(1)}, u32[]{:S(2)}, u32[]{:S(2)}) collective-permute-start(bf16[1,2,96,768]{3,2,1,0:T(8,128)(2,1)S(1)} %maximum_bitcast_fusion.5), channel_id=1, source_target_pairs={{0,16},{4,20},{8,24},{12,28},{16,0},{20,4},{24,8},{28,12},{1,17},{... | collective-permute-start | bytes 884744 | tf_op jit(solution)/shard_map/ppermute | solution.py:756
  90.5 27.7 %collective-permute-start.21 = (bf16[375,768]{1,0:T(8,128)(2,1)}, bf16[375,768]{1,0:T(8,128)(2,1)}, u32[]{:S(2)}, u32[]{:S(2)}) collective-permute-start(bf16[375,768]{1,0:T(8,128)(2,1)} %bitcast.185), channel_id=1, source_target_pairs={{0,2},{1,3},{2,0},{3,1},{4,6},{5,7},{6,4},{7,5},{8,10},{9,11},{10,... | collective-permute-start | bytes 1728008 | tf_op jit(solution)/shard_map/ppermute | solution.py:761
  120.7 16.6 %collective-permute-start.22 = (bf16[4,4,96,768]{3,2,1,0:T(8,128)(2,1)S(1)}, bf16[4,4,96,768]{3,2,1,0:T(8,128)(2,1)S(1)}, u32[]{:S(2)}, u32[]{:S(2)}) collective-permute-start(bf16[4,4,96,768]{3,2,1,0:T(8,128)(2,1)S(1)} %maximum_maximum_fusion.1.refs_5_.refs_3_.refs_9_.refs_6_), channel_id=1, source_target_pairs={{0,4},{4,0},{8,12},{12,8},{16,20},{20,16},{24,28},{28,24},{1,5},{5... | collective-permute-start | bytes 7077896 | tf_op jit(solution)/shard_map/ppermute | solution.py:756
  120.9 16.4 %collective-permute-start.24 = (bf16[2,2,96,768]{3,2,1,0:T(8,128)(2,1)S(1)}, bf16[2,2,96,768]{3,2,1,0:T(8,128)(2,1)S(1)}, u32[]{:S(2)}, u32[]{:S(2)}) collective-permute-start(bf16[2,2,96,768]{3,2,1,0:T(8,128)(2,1)S(1)} %pad_maximum_fusion.9), channel_id=1, source_target_pairs={{0,16},{4,20},{8,24},{12,28},{16,0},{20,4},{24,8},{28,12},{1,17},{... | collective-permute-start | bytes 1769480 | tf_op jit(solution)/shard_map/ppermute | solution.py:756
  121.8 15.5 %collective-permute-start.25 = (bf16[2,2,96,768]{3,2,1,0:T(8,128)(2,1)S(1)}, bf16[2,2,96,768]{3,2,1,0:T(8,128)(2,1)S(1)}, u32[]{:S(2)}, u32[]{:S(2)}) collective-permute-start(bf16[2,2,96,768]{3,2,1,0:T(8,128)(2,1)S(1)} %pad_maximum_fusion.10), channel_id=1, source_target_pairs={{0,8},{4,12},{8,0},{12,4},{16,24},{20,28},{24,16},{28,20},{1,9},{5... | collective-permute-start | bytes 1769480 | tf_op jit(solution)/shard_map/ppermute | solution.py:756
  122.4 14.9 %collective-permute-start.23 = (bf16[375,768]{1,0:T(8,128)(2,1)S(1)}, bf16[375,768]{1,0:T(8,128)(2,1)S(1)}, u32[]{:S(2)}, u32[]{:S(2)}) collective-permute-start(bf16[375,768]{1,0:T(8,128)(2,1)S(1)} %bitcast.184), channel_id=1, source_target_pairs={{0,3},{1,0},{2,1},{3,2},{4,7},{5,4},{6,5},{7,6},{8,11},{9,8},{10,9... | collective-permute-start | bytes 1728008 | tf_op jit(solution)/shard_map/ppermute | solution.py:761
  137.3 18.5 %collective-permute-start.27 = (bf16[96,768]{1,0:T(8,128)(2,1)S(1)}, bf16[96,768]{1,0:T(8,128)(2,1)S(1)}, u32[]{:S(2)}, u32[]{:S(2)}) collective-permute-start(bf16[96,768]{1,0:T(8,128)(2,1)S(1)} %bitcast.200), channel_id=1, source_target_pairs={{0,1},{1,2},{2,3},{3,0},{4,5},{5,6},{6,7},{7,4},{8,9},{9,10},{10,1... | collective-permute-start | bytes 442376 | tf_op jit(solution)/shard_map/ppermute | solution.py:761
  137.4 18.4 %collective-permute-start.28 = (bf16[96,768]{1,0:T(8,128)(2,1)S(1)}, bf16[96,768]{1,0:T(8,128)(2,1)S(1)}, u32[]{:S(2)}, u32[]{:S(2)}) collective-permute-start(bf16[96,768]{1,0:T(8,128)(2,1)S(1)} %bitcast.201), channel_id=1, source_target_pairs={{0,2},{1,3},{2,0},{3,1},{4,6},{5,7},{6,4},{7,5},{8,10},{9,11},{10,... | collective-permute-start | bytes 442376 | tf_op jit(solution)/shard_map/ppermute | solution.py:761
  141.4 14.5 %collective-permute-start.29 = (bf16[96,768]{1,0:T(8,128)(2,1)S(1)}, bf16[96,768]{1,0:T(8,128)(2,1)}, u32[]{:S(2)}, u32[]{:S(2)}) collective-permute-start(bf16[96,768]{1,0:T(8,128)(2,1)S(1)} %bitcast.202), channel_id=1, source_target_pairs={{0,3},{1,0},{2,1},{3,2},{4,7},{5,4},{6,5},{7,6},{8,11},{9,8},{10,9... | collective-permute-start | bytes 442376 | tf_op jit(solution)/shard_map/ppermute | solution.py:761
  143.2 13.8 %collective-permute-start.26 = (bf16[4,4,96,768]{3,2,1,0:T(8,128)(2,1)}, bf16[4,4,96,768]{3,2,1,0:T(8,128)(2,1)}, u32[]{:S(2)}, u32[]{:S(2)}) collective-permute-start(bf16[4,4,96,768]{3,2,1,0:T(8,128)(2,1)} %maximum_maximum_fusion.2.refs_3_.refs_4_), channel_id=1, source_target_pairs={{0,4},{4,0},{8,12},{12,8},{16,20},{20,16},{24,28},{28,24},{1,5},{5... | collective-permute-start | bytes 7077896 | tf_op jit(solution)/shard_map/ppermute | solution.py:756
  157.1 22.6 %collective-permute-start.30 = (bf16[1,2,96,768]{3,2,1,0:T(8,128)(2,1)S(1)}, bf16[1,2,96,768]{3,2,1,0:T(8,128)(2,1)S(1)}, u32[]{:S(2)}, u32[]{:S(2)}) collective-permute-start(bf16[1,2,96,768]{3,2,1,0:T(8,128)(2,1)S(1)} %maximum_bitcast_fusion.6), channel_id=1, source_target_pairs={{0,8},{4,12},{8,0},{12,4},{16,24},{20,28},{24,16},{28,20},{1,9},{5... | collective-permute-start | bytes 884744 | tf_op jit(solution)/shard_map/ppermute | solution.py:756
  158.6 21.1 %collective-permute-start.31 = (bf16[1,2,96,768]{3,2,1,0:T(8,128)(2,1)S(1)}, bf16[1,2,96,768]{3,2,1,0:T(8,128)(2,1)S(1)}, u32[]{:S(2)}, u32[]{:S(2)}) collective-permute-start(bf16[1,2,96,768]{3,2,1,0:T(8,128)(2,1)S(1)} %maximum_bitcast_fusion.7), channel_id=1, source_target_pairs={{0,16},{4,20},{8,24},{12,28},{16,0},{20,4},{24,8},{28,12},{1,17},{... | collective-permute-start | bytes 884744 | tf_op jit(solution)/shard_map/ppermute | solution.py:756
  179.8 21.6 %collective-permute-start.33 = (bf16[2,2,96,768]{3,2,1,0:T(8,128)(2,1)S(1)}, bf16[2,2,96,768]{3,2,1,0:T(8,128)(2,1)S(1)}, u32[]{:S(2)}, u32[]{:S(2)}) collective-permute-start(bf16[2,2,96,768]{3,2,1,0:T(8,128)(2,1)S(1)} %pad_maximum_fusion.13), channel_id=1, source_target_pairs={{0,8},{4,12},{8,0},{12,4},{16,24},{20,28},{24,16},{28,20},{1,9},{5... | collective-permute-start | bytes 1769480 | tf_op jit(solution)/shard_map/ppermute | solution.py:756
  180.4 21.0 %collective-permute-start.32 = (bf16[2,2,96,768]{3,2,1,0:T(8,128)(2,1)S(1)}, bf16[2,2,96,768]{3,2,1,0:T(8,128)(2,1)S(1)}, u32[]{:S(2)}, u32[]{:S(2)}) collective-permute-start(bf16[2,2,96,768]{3,2,1,0:T(8,128)(2,1)S(1)} %pad_maximum_fusion.12), channel_id=1, source_target_pairs={{0,16},{4,20},{8,24},{12,28},{16,0},{20,4},{24,8},{28,12},{1,17},{... | collective-permute-start | bytes 1769480 | tf_op jit(solution)/shard_map/ppermute | solution.py:756
  232.1 20.0 %collective-permute-start.35 = (bf16[4,4,96,768]{3,2,1,0:T(8,128)(2,1)}, bf16[4,4,96,768]{3,2,1,0:T(8,128)(2,1)}, u32[]{:S(2)}, u32[]{:S(2)}) collective-permute-start(bf16[4,4,96,768]{3,2,1,0:T(8,128)(2,1)} %get-tuple-element.171), channel_id=1, source_target_pairs={{0,4},{4,0},{8,12},{12,8},{16,20},{20,16},{24,28},{28,24},{1,5},{5... | collective-permute-start | bytes 7077896 | tf_op jit(solution)/shard_map/ppermute | solution.py:756
  255.2 30.5 %collective-permute-start.36 = (bf16[2,2,96,768]{3,2,1,0:T(8,128)(2,1)}, bf16[2,2,96,768]{3,2,1,0:T(8,128)(2,1)}, u32[]{:S(2)}, u32[]{:S(2)}) collective-permute-start(bf16[2,2,96,768]{3,2,1,0:T(8,128)(2,1)} %get-tuple-element.273), channel_id=1, source_target_pairs={{0,16},{4,20},{8,24},{12,28},{16,0},{20,4},{24,8},{28,12},{1,17},{... | collective-permute-start | bytes 1769480 | tf_op jit(solution)/shard_map/ppermute | solution.py:756
  256.3 29.4 %collective-permute-start.37 = (bf16[2,2,96,768]{3,2,1,0:T(8,128)(2,1)}, bf16[2,2,96,768]{3,2,1,0:T(8,128)(2,1)}, u32[]{:S(2)}, u32[]{:S(2)}) collective-permute-start(bf16[2,2,96,768]{3,2,1,0:T(8,128)(2,1)} %get-tuple-element.272), channel_id=1, source_target_pairs={{0,8},{4,12},{8,0},{12,4},{16,24},{20,28},{24,16},{28,20},{1,9},{5... | collective-permute-start | bytes 1769480 | tf_op jit(solution)/shard_map/ppermute | solution.py:756
  260.4 30.4 %collective-permute-start.46 = (bf16[2,2,96,768]{3,2,1,0:T(8,128)(2,1)}, bf16[2,2,96,768]{3,2,1,0:T(8,128)(2,1)S(1)}, u32[]{:S(2)}, u32[]{:S(2)}) collective-permute-start(bf16[2,2,96,768]{3,2,1,0:T(8,128)(2,1)} %get-tuple-element.266), channel_id=1, source_target_pairs={{0,8},{4,12},{8,0},{12,4},{16,24},{20,28},{24,16},{28,20},{1,9},{5... | collective-permute-start | bytes 1769480 | tf_op jit(solution)/shard_map/ppermute | solution.py:756
  260.9 29.9 %collective-permute-start.44 = (bf16[2,2,96,768]{3,2,1,0:T(8,128)(2,1)}, bf16[2,2,96,768]{3,2,1,0:T(8,128)(2,1)S(1)}, u32[]{:S(2)}, u32[]{:S(2)}) collective-permute-start(bf16[2,2,96,768]{3,2,1,0:T(8,128)(2,1)} %get-tuple-element.267), channel_id=1, source_target_pairs={{0,16},{4,20},{8,24},{12,28},{16,0},{20,4},{24,8},{28,12},{1,17},{... | collective-permute-start | bytes 1769480 | tf_op jit(solution)/shard_map/ppermute | solution.py:756
  288.2 30.3 %collective-permute-start.40 = (bf16[2,96,768]{2,1,0:T(8,128)(2,1)}, bf16[2,96,768]{2,1,0:T(8,128)(2,1)S(1)}, u32[]{:S(2)}, u32[]{:S(2)}) collective-permute-start(bf16[2,96,768]{2,1,0:T(8,128)(2,1)} %get-tuple-element.270), channel_id=1, source_target_pairs={{0,16},{4,20},{8,24},{12,28},{16,0},{20,4},{24,8},{28,12},{1,17},{... | collective-permute-start | bytes 884744 | tf_op jit(solution)/shard_map/ppermute | solution.py:756
  289.3 29.2 %collective-permute-start.39 = (bf16[2,96,768]{2,1,0:T(8,128)(2,1)}, bf16[2,96,768]{2,1,0:T(8,128)(2,1)}, u32[]{:S(2)}, u32[]{:S(2)}) collective-permute-start(bf16[2,96,768]{2,1,0:T(8,128)(2,1)} %get-tuple-element.271), channel_id=1, source_target_pairs={{0,8},{4,12},{8,0},{12,4},{16,24},{20,28},{24,16},{28,20},{1,9},{5... | collective-permute-start | bytes 884744 | tf_op jit(solution)/shard_map/ppermute | solution.py:756
  293.3 46.2 %collective-permute-start.45 = (bf16[2,96,768]{2,1,0:T(8,128)(2,1)}, bf16[2,96,768]{2,1,0:T(8,128)(2,1)}, u32[]{:S(2)}, u32[]{:S(2)}) collective-permute-start(bf16[2,96,768]{2,1,0:T(8,128)(2,1)} %get-tuple-element.265), channel_id=1, source_target_pairs={{0,8},{4,12},{8,0},{12,4},{16,24},{20,28},{24,16},{28,20},{1,9},{5... | collective-permute-start | bytes 884744 | tf_op jit(solution)/shard_map/ppermute | solution.py:756
  293.9 45.7 %collective-permute-start.47 = (bf16[2,96,768]{2,1,0:T(8,128)(2,1)}, bf16[2,96,768]{2,1,0:T(8,128)(2,1)}, u32[]{:S(2)}, u32[]{:S(2)}) collective-permute-start(bf16[2,96,768]{2,1,0:T(8,128)(2,1)} %get-tuple-element.264), channel_id=1, source_target_pairs={{0,16},{4,20},{8,24},{12,28},{16,0},{20,4},{24,8},{28,12},{1,17},{... | collective-permute-start | bytes 884744 | tf_op jit(solution)/shard_map/ppermute | solution.py:756
  321.4 21.3 %collective-permute-start.41 = (bf16[96,768]{1,0:T(8,128)(2,1)S(1)}, bf16[96,768]{1,0:T(8,128)(2,1)S(1)}, u32[]{:S(2)}, u32[]{:S(2)}) collective-permute-start(bf16[96,768]{1,0:T(8,128)(2,1)S(1)} %get-tuple-element.289), channel_id=1, source_target_pairs={{0,1},{1,2},{2,3},{3,0},{4,5},{5,6},{6,7},{7,4},{8,9},{9,10},{10,1... | collective-permute-start | bytes 442376 | tf_op jit(solution)/shard_map/ppermute | solution.py:761
  323.4 22.9 %collective-permute-start.42 = (bf16[96,768]{1,0:T(8,128)(2,1)S(1)}, bf16[96,768]{1,0:T(8,128)(2,1)S(1)}, u32[]{:S(2)}, u32[]{:S(2)}) collective-permute-start(bf16[96,768]{1,0:T(8,128)(2,1)S(1)} %get-tuple-element.290), channel_id=1, source_target_pairs={{0,3},{1,0},{2,1},{3,2},{4,7},{5,4},{6,5},{7,6},{8,11},{9,8},{10,9... | collective-permute-start | bytes 442376 | tf_op jit(solution)/shard_map/ppermute | solution.py:761
  325.2 22.1 %collective-permute-start.43 = (bf16[96,768]{1,0:T(8,128)(2,1)S(1)}, bf16[96,768]{1,0:T(8,128)(2,1)S(1)}, u32[]{:S(2)}, u32[]{:S(2)}) collective-permute-start(bf16[96,768]{1,0:T(8,128)(2,1)S(1)} %get-tuple-element.291), channel_id=1, source_target_pairs={{0,2},{1,3},{2,0},{3,1},{4,6},{5,7},{6,4},{7,5},{8,10},{9,11},{10,... | collective-permute-start | bytes 442376 | tf_op jit(solution)/shard_map/ppermute | solution.py:761
  339.5 22.9 %collective-permute-start.48 = (bf16[4,4,96,768]{3,2,1,0:T(8,128)(2,1)}, bf16[4,4,96,768]{3,2,1,0:T(8,128)(2,1)}, u32[]{:S(2)}, u32[]{:S(2)}) collective-permute-start(bf16[4,4,96,768]{3,2,1,0:T(8,128)(2,1)} %get-tuple-element.193), channel_id=1, source_target_pairs={{0,4},{4,0},{8,12},{12,8},{16,20},{20,16},{24,28},{28,24},{1,5},{5... | collective-permute-start | bytes 7077896 | tf_op jit(solution)/shard_map/ppermute | solution.py:756
  342.2 25.4 %collective-permute-start.49 = (bf16[96,768]{1,0:T(8,128)(2,1)S(1)}, bf16[96,768]{1,0:T(8,128)(2,1)S(1)}, u32[]{:S(2)}, u32[]{:S(2)}) collective-permute-start(bf16[96,768]{1,0:T(8,128)(2,1)S(1)} %get-tuple-element.293), channel_id=1, source_target_pairs={{0,1},{1,2},{2,3},{3,0},{4,5},{5,6},{6,7},{7,4},{8,9},{9,10},{10,1... | collective-permute-start | bytes 442376 | tf_op jit(solution)/shard_map/ppermute | solution.py:761
  342.7 24.9 %collective-permute-start.50 = (bf16[96,768]{1,0:T(8,128)(2,1)S(1)}, bf16[96,768]{1,0:T(8,128)(2,1)S(1)}, u32[]{:S(2)}, u32[]{:S(2)}) collective-permute-start(bf16[96,768]{1,0:T(8,128)(2,1)S(1)} %get-tuple-element.294), channel_id=1, source_target_pairs={{0,3},{1,0},{2,1},{3,2},{4,7},{5,4},{6,5},{7,6},{8,11},{9,8},{10,9... | collective-permute-start | bytes 442376 | tf_op jit(solution)/shard_map/ppermute | solution.py:761
  346.3 21.4 %collective-permute-start.51 = (bf16[96,768]{1,0:T(8,128)(2,1)S(1)}, bf16[96,768]{1,0:T(8,128)(2,1)S(1)}, u32[]{:S(2)}, u32[]{:S(2)}) collective-permute-start(bf16[96,768]{1,0:T(8,128)(2,1)S(1)} %get-tuple-element.295), channel_id=1, source_target_pairs={{0,2},{1,3},{2,0},{3,1},{4,6},{5,7},{6,4},{7,5},{8,10},{9,11},{10,... | collective-permute-start | bytes 442376 | tf_op jit(solution)/shard_map/ppermute | solution.py:761
  365.0 30.9 %collective-permute-start.52 = (bf16[2,2,96,768]{3,2,1,0:T(8,128)(2,1)}, bf16[2,2,96,768]{3,2,1,0:T(8,128)(2,1)}, u32[]{:S(2)}, u32[]{:S(2)}) collective-permute-start(bf16[2,2,96,768]{3,2,1,0:T(8,128)(2,1)} %get-tuple-element.261), channel_id=1, source_target_pairs={{0,16},{4,20},{8,24},{12,28},{16,0},{20,4},{24,8},{28,12},{1,17},{... | collective-permute-start | bytes 1769480 | tf_op jit(solution)/shard_map/ppermute | solution.py:756
  366.1 29.8 %collective-permute-start.53 = (bf16[2,2,96,768]{3,2,1,0:T(8,128)(2,1)}, bf16[2,2,96,768]{3,2,1,0:T(8,128)(2,1)}, u32[]{:S(2)}, u32[]{:S(2)}) collective-permute-start(bf16[2,2,96,768]{3,2,1,0:T(8,128)(2,1)} %get-tuple-element.260), channel_id=1, source_target_pairs={{0,8},{4,12},{8,0},{12,4},{16,24},{20,28},{24,16},{28,20},{1,9},{5... | collective-permute-start | bytes 1769480 | tf_op jit(solution)/shard_map/ppermute | solution.py:756
  367.7 24.4 %collective-permute-start.54 = (bf16[375,768]{1,0:T(8,128)(2,1)}, bf16[375,768]{1,0:T(8,128)(2,1)}, u32[]{:S(2)}, u32[]{:S(2)}) collective-permute-start(bf16[375,768]{1,0:T(8,128)(2,1)} %get-tuple-element.198), channel_id=1, source_target_pairs={{0,3},{1,0},{2,1},{3,2},{4,7},{5,4},{6,5},{7,6},{8,11},{9,8},{10,9... | collective-permute-start | bytes 1728008 | tf_op jit(solution)/shard_map/ppermute | solution.py:761
  368.7 27.2 %collective-permute-start.55 = (bf16[375,768]{1,0:T(8,128)(2,1)}, bf16[375,768]{1,0:T(8,128)(2,1)}, u32[]{:S(2)}, u32[]{:S(2)}) collective-permute-start(bf16[375,768]{1,0:T(8,128)(2,1)} %get-tuple-element.200), channel_id=1, source_target_pairs={{0,1},{1,2},{2,3},{3,0},{4,5},{5,6},{6,7},{7,4},{8,9},{9,10},{10,1... | collective-permute-start | bytes 1728008 | tf_op jit(solution)/shard_map/ppermute | solution.py:761
  392.0 21.9 %collective-permute-start.57 = (bf16[4,4,96,768]{3,2,1,0:T(8,128)(2,1)}, bf16[4,4,96,768]{3,2,1,0:T(8,128)(2,1)S(1)}, u32[]{:S(2)}, u32[]{:S(2)}) collective-permute-start(bf16[4,4,96,768]{3,2,1,0:T(8,128)(2,1)} %get-tuple-element.206), channel_id=1, source_target_pairs={{0,4},{4,0},{8,12},{12,8},{16,20},{20,16},{24,28},{28,24},{1,5},{5... | collective-permute-start | bytes 7077896 | tf_op jit(solution)/shard_map/ppermute | solution.py:756
  395.9 30.9 %collective-permute-start.56 = (bf16[375,768]{1,0:T(8,128)(2,1)}, bf16[375,768]{1,0:T(8,128)(2,1)S(1)}, u32[]{:S(2)}, u32[]{:S(2)}) collective-permute-start(bf16[375,768]{1,0:T(8,128)(2,1)} %get-tuple-element.205), channel_id=1, source_target_pairs={{0,2},{1,3},{2,0},{3,1},{4,6},{5,7},{6,4},{7,5},{8,10},{9,11},{10,... | collective-permute-start | bytes 1728008 | tf_op jit(solution)/shard_map/ppermute | solution.py:761
  398.9 10.7 %collective-permute-start.58 = (bf16[2,96,768]{2,1,0:T(8,128)(2,1)}, bf16[2,96,768]{2,1,0:T(8,128)(2,1)S(1)}, u32[]{:S(2)}, u32[]{:S(2)}) collective-permute-start(bf16[2,96,768]{2,1,0:T(8,128)(2,1)} %get-tuple-element.259), channel_id=1, source_target_pairs={{0,8},{4,12},{8,0},{12,4},{16,24},{20,28},{24,16},{28,20},{1,9},{5... | collective-permute-start | bytes 884744 | tf_op jit(solution)/shard_map/ppermute | solution.py:756
  399.4 10.2 %collective-permute-start.59 = (bf16[2,96,768]{2,1,0:T(8,128)(2,1)S(1)}, bf16[2,96,768]{2,1,0:T(8,128)(2,1)S(1)}, u32[]{:S(2)}, u32[]{:S(2)}) collective-permute-start(bf16[2,96,768]{2,1,0:T(8,128)(2,1)S(1)} %get-tuple-element.258), channel_id=1, source_target_pairs={{0,16},{4,20},{8,24},{12,28},{16,0},{20,4},{24,8},{28,12},{1,17},{... | collective-permute-start | bytes 884744 | tf_op jit(solution)/shard_map/ppermute | solution.py:756
  411.6 30.4 %collective-permute-start.69 = (bf16[96,768]{1,0:T(8,128)(2,1)S(1)}, bf16[96,768]{1,0:T(8,128)(2,1)S(1)}, u32[]{:S(2)}, u32[]{:S(2)}) collective-permute-start(bf16[96,768]{1,0:T(8,128)(2,1)S(1)} %get-tuple-element.297), channel_id=1, source_target_pairs={{0,3},{1,0},{2,1},{3,2},{4,7},{5,4},{6,5},{7,6},{8,11},{9,8},{10,9... | collective-permute-start | bytes 442376 | tf_op jit(solution)/shard_map/ppermute | solution.py:761
  413.4 30.5 %collective-permute-start.68 = (bf16[96,768]{1,0:T(8,128)(2,1)S(1)}, bf16[96,768]{1,0:T(8,128)(2,1)S(1)}, u32[]{:S(2)}, u32[]{:S(2)}) collective-permute-start(bf16[96,768]{1,0:T(8,128)(2,1)S(1)} %get-tuple-element.296), channel_id=1, source_target_pairs={{0,1},{1,2},{2,3},{3,0},{4,5},{5,6},{6,7},{7,4},{8,9},{9,10},{10,1... | collective-permute-start | bytes 442376 | tf_op jit(solution)/shard_map/ppermute | solution.py:761
  414.3 18.6 %collective-permute-start.62 = (bf16[2,2,96,768]{3,2,1,0:T(8,128)(2,1)S(1)}, bf16[2,2,96,768]{3,2,1,0:T(8,128)(2,1)S(1)}, u32[]{:S(2)}, u32[]{:S(2)}) collective-permute-start(bf16[2,2,96,768]{3,2,1,0:T(8,128)(2,1)S(1)} %get-tuple-element.254), channel_id=1, source_target_pairs={{0,8},{4,12},{8,0},{12,4},{16,24},{20,28},{24,16},{28,20},{1,9},{5... | collective-permute-start | bytes 1769480 | tf_op jit(solution)/shard_map/ppermute | solution.py:756
  415.8 17.1 %collective-permute-start.60 = (bf16[2,2,96,768]{3,2,1,0:T(8,128)(2,1)S(1)}, bf16[2,2,96,768]{3,2,1,0:T(8,128)(2,1)S(1)}, u32[]{:S(2)}, u32[]{:S(2)}) collective-permute-start(bf16[2,2,96,768]{3,2,1,0:T(8,128)(2,1)S(1)} %get-tuple-element.255), channel_id=1, source_target_pairs={{0,16},{4,20},{8,24},{12,28},{16,0},{20,4},{24,8},{28,12},{1,17},{... | collective-permute-start | bytes 1769480 | tf_op jit(solution)/shard_map/ppermute | solution.py:756
  433.1 17.9 %collective-permute-start.64 = (bf16[2,96,768]{2,1,0:T(8,128)(2,1)S(1)}, bf16[2,96,768]{2,1,0:T(8,128)(2,1)S(1)}, u32[]{:S(2)}, u32[]{:S(2)}) collective-permute-start(bf16[2,96,768]{2,1,0:T(8,128)(2,1)S(1)} %get-tuple-element.252), channel_id=1, source_target_pairs={{0,16},{4,20},{8,24},{12,28},{16,0},{20,4},{24,8},{28,12},{1,17},{... | collective-permute-start | bytes 884744 | tf_op jit(solution)/shard_map/ppermute | solution.py:756
  433.9 17.1 %collective-permute-start.61 = (bf16[2,96,768]{2,1,0:T(8,128)(2,1)S(1)}, bf16[2,96,768]{2,1,0:T(8,128)(2,1)S(1)}, u32[]{:S(2)}, u32[]{:S(2)}) collective-permute-start(bf16[2,96,768]{2,1,0:T(8,128)(2,1)S(1)} %get-tuple-element.253), channel_id=1, source_target_pairs={{0,8},{4,12},{8,0},{12,4},{16,24},{20,28},{24,16},{28,20},{1,9},{5... | collective-permute-start | bytes 884744 | tf_op jit(solution)/shard_map/ppermute | solution.py:756
  440.1 10.8 %collective-permute-start.63 = (bf16[96,768]{1,0:T(8,128)(2,1)S(1)}, bf16[96,768]{1,0:T(8,128)(2,1)S(1)}, u32[]{:S(2)}, u32[]{:S(2)}) collective-permute-start(bf16[96,768]{1,0:T(8,128)(2,1)S(1)} %dynamic-slice_bitcast_fusion), channel_id=1, source_target_pairs={{0,2},{1,3},{2,0},{3,1},{4,6},{5,7},{6,4},{7,5},{8,10},{9,11},{10,... | collective-permute-start | bytes 442376 | tf_op jit(solution)/shard_map/ppermute | solution.py:761
  442.0 13.8 %collective-permute-start.72 = (f32[24,768]{1,0:T(8,128)S(1)}, f32[24,768]{1,0:T(8,128)S(1)}, u32[]{:S(2)}, u32[]{:S(2)}) collective-permute-start(f32[24,768]{1,0:T(8,128)S(1)} %add.524), channel_id=1, source_target_pairs={{0,2},{1,3},{2,0},{3,1},{4,6},{5,7},{6,4},{7,5},{8,10},{9,11},{10,... | collective-permute-start | bytes 221192 | tf_op jit(solution)/shard_map/ppermute | solution.py:1088
  451.5 10.3 %collective-permute-start.67 = (bf16[96,768]{1,0:T(8,128)(2,1)S(1)}, bf16[96,768]{1,0:T(8,128)(2,1)S(1)}, u32[]{:S(2)}, u32[]{:S(2)}) collective-permute-start(bf16[96,768]{1,0:T(8,128)(2,1)S(1)} %get-tuple-element.300), channel_id=1, source_target_pairs={{0,2},{1,3},{2,0},{3,1},{4,6},{5,7},{6,4},{7,5},{8,10},{9,11},{10,... | collective-permute-start | bytes 442376 | tf_op jit(solution)/shard_map/ppermute | solution.py:761
  451.6 12.8 %collective-permute-start.66 = (bf16[96,768]{1,0:T(8,128)(2,1)S(1)}, bf16[96,768]{1,0:T(8,128)(2,1)S(1)}, u32[]{:S(2)}, u32[]{:S(2)}) collective-permute-start(bf16[96,768]{1,0:T(8,128)(2,1)S(1)} %get-tuple-element.299), channel_id=1, source_target_pairs={{0,3},{1,0},{2,1},{3,2},{4,7},{5,4},{6,5},{7,6},{8,11},{9,8},{10,9... | collective-permute-start | bytes 442376 | tf_op jit(solution)/shard_map/ppermute | solution.py:761
  453.9 10.5 %collective-permute-start.65 = (bf16[96,768]{1,0:T(8,128)(2,1)S(1)}, bf16[96,768]{1,0:T(8,128)(2,1)S(1)}, u32[]{:S(2)}, u32[]{:S(2)}) collective-permute-start(bf16[96,768]{1,0:T(8,128)(2,1)S(1)} %get-tuple-element.298), channel_id=1, source_target_pairs={{0,1},{1,2},{2,3},{3,0},{4,5},{5,6},{6,7},{7,4},{8,9},{9,10},{10,1... | collective-permute-start | bytes 442376 | tf_op jit(solution)/shard_map/ppermute | solution.py:761
  (70 other events, 482.9 us)
